TPU v7x, 32 devices: a whole 2x2x4 slice. The times are simulated.
32 devices in a mesh: groups: 2 (over y), tensor: 4 (over x, core), task: 4 (over z).
Axes of the slice: x: 2, y: 2, z: 4, core: 2. Of those that a mesh axis runs over, the one named last changes fastest.
Arguments:
- tokens: bfloat16 [3072, 8192], P(('groups', 'task'), 'tensor'), parts along dimension 0, may hold values from -6 to 6
- task_counts: int32 [512], P(('groups', 'task')), parts along dimension 0, may hold values from 0 to 96, as said below
- task_embeddings: bfloat16 [512, 1024], P(('groups', 'task')), parts along dimension 0, may hold values from -6 to 6
- embedding_weight: bfloat16 [1024, 512], replicated, may hold values from -0.1875 to 0.1875
- down_factor_head: bfloat16 [512, 16, 8192], P('task', None, 'tensor'), may hold values from -0.0029296875 to 0.0029296875
- query_up_head: bfloat16 [512, 8, 4096], P('task', None, 'tensor'), may hold values from -0.09375 to 0.09375
- value_up_head: bfloat16 [512, 8, 1024], P('task', None, 'tensor'), may hold values from -0.09375 to 0.09375
- w_query: bfloat16 [8192, 4096], P('tensor'), may hold values from -0.0625 to 0.0625
- w_value: bfloat16 [8192, 1024], P('tensor'), may hold values from -0.0625 to 0.0625
Outputs:
- query: bfloat16 [3072, 4096], P(('groups', 'task', 'tensor')), parts along dimension 0
- value: bfloat16 [3072, 1024], P(('groups', 'task', 'tensor')), parts along dimension 0
- down_factors: bfloat16 [512, 16, 8192], P(('groups', 'task'), None, 'tensor'), parts along dimension 0
- query_up_factors: bfloat16 [512, 8, 4096], P(('groups', 'task'), None, 'tensor'), parts along dimension 0
- value_up_factors: bfloat16 [512, 8, 1024], P(('groups', 'task'), None, 'tensor'), parts along dimension 0
There are 2 independent parts, one for each index of `groups`. A program takes and returns all parts, laid end to end along the dimension named above; an argument that names none is the same for every part. Nothing has to cross between parts.
Inputs may be any that keep to these rules, and one draw needn't show every extreme that they name: For every k the task_counts of tasks k * 16 to k * 16 + 15 sum to at most 96; in every draw at least one task has exactly 96 tokens.
All inputs are finite; a program needn't handle non-finite values.
Results may differ from a plain program's by a relative error of at most 0.0059.
Values may be sent and summed in bfloat16 or wider, within the bound.
No kernel may reach another device: no remote copies, remote signals or barrier semaphores. Data moves between devices by JAX's collectives and lax.ppermute only.
A program may use at most 128 MiB of HBM per device.

v0:
```python
import functools

import jax
import jax.numpy as jnp
from jax import lax
from jax.experimental import pallas as pl
from jax.experimental.pallas import tpu as pltpu
from jax.sharding import PartitionSpec as P


ADAPTER_SCALE = 2.0
LANES = 128
PLACES = ("groups", "task")


def swap(x, axes, shift):
    total = lax.axis_size(axes)
    return lax.ppermute(x, axes, [(a, a ^ shift) for a in range(total)])


def place():
    return lax.axis_index("groups") * lax.axis_size("task") + lax.axis_index("task")


def through_vmem(moves, scratch, arrived, left):
    fetches = [
        pltpu.make_async_copy(source, scratch.at[k], arrived.at[k])
        for k, (source, _) in enumerate(moves)
    ]
    stores = [
        pltpu.make_async_copy(scratch.at[k], target, left.at[k])
        for k, (_, target) in enumerate(moves)
    ]
    for fetch in fetches:
        fetch.start()
    for fetch, store in zip(fetches, stores):
        fetch.wait()
        store.start()
    for store in stores:
        store.wait()


def vmem_scratch(count, shape, dtype):
    return [
        pltpu.VMEM((count,) + shape, dtype),
        pltpu.SemaphoreType.DMA((count,)),
        pltpu.SemaphoreType.DMA((count,)),
    ]


def cut_kernel(shifts, stride, start, width, source, *rest):
    moves = []
    for k, shift in enumerate(shifts):
        column = pl.multiple_of((place() ^ shift) * stride + start, LANES)
        moves.append((source.at[:, :, pl.ds(column, width)], rest[k]))
    through_vmem(moves, *rest[len(shifts) :])


def cut(head, shifts, stride, start, width):
    shape = head.shape[:2] + (width,)
    return pl.pallas_call(
        functools.partial(cut_kernel, shifts, stride, start, width),
        in_specs=[pl.BlockSpec(memory_space=pl.ANY)],
        out_specs=[pl.BlockSpec(memory_space=pl.ANY)] * len(shifts),
        out_shape=[jax.ShapeDtypeStruct(shape, head.dtype)] * len(shifts),
        scratch_shapes=vmem_scratch(len(shifts), shape, head.dtype),
        name="cut",
    )(head)


def join_kernel(shifts, stride, start, width, *refs):
    whole = refs[-4]
    moves = []
    for k, shift in enumerate(shifts):
        column = pl.multiple_of((place() ^ shift) * stride + start, LANES)
        moves.append((refs[k], whole.at[:, :, pl.ds(column, width)]))
    through_vmem(moves, *refs[-3:])


def join(pieces, shifts, stride, start, width, columns, whole):
    operands = list(pieces) + ([] if whole is None else [whole])
    return pl.pallas_call(
        functools.partial(join_kernel, shifts, stride, start, width),
        in_specs=[pl.BlockSpec(memory_space=pl.ANY)] * len(operands),
        out_specs=pl.BlockSpec(memory_space=pl.ANY),
        out_shape=jax.ShapeDtypeStruct(pieces[0].shape[:2] + (columns,), pieces[0].dtype),
        scratch_shapes=vmem_scratch(len(pieces), pieces[0].shape, pieces[0].dtype),
        input_output_aliases={} if whole is None else {len(pieces): 0},
        name="join",
    )(*operands)


def stack_kernel(shifts, *refs):
    count = len(shifts)
    moves = [(refs[k], refs[count].at[place() ^ s]) for k, s in enumerate(shifts)]
    through_vmem(moves, *refs[count + 1 :])


def stack(pieces, shifts):
    shape, dtype = pieces[0].shape, pieces[0].dtype
    return pl.pallas_call(
        functools.partial(stack_kernel, shifts),
        in_specs=[pl.BlockSpec(memory_space=pl.ANY)] * len(pieces),
        out_specs=pl.BlockSpec(memory_space=pl.ANY),
        out_shape=jax.ShapeDtypeStruct((len(pieces),) + shape, dtype),
        scratch_shapes=vmem_scratch(len(pieces), shape, dtype),
        name="stack",
    )(*pieces)


def in_order(pieces, shifts):
    stack = jnp.zeros((len(pieces),) + pieces[0].shape, pieces[0].dtype)
    for piece, shift in zip(pieces, shifts):
        stack = lax.dynamic_update_index_in_dim(stack, piece, place() ^ shift, 0)
    return stack


class Head:
    def __init__(self, head, chunks):
        self.rank, self.columns = head.shape[1:]
        self.head = head
        self.places = lax.axis_size("groups") * lax.axis_size("task")
        self.stride = self.columns // self.places
        self.by_lane = self.stride % (LANES * chunks) == 0
        self.by_row = not self.by_lane and self.rank % self.places == 0
        self.chunks = chunks if self.by_lane else 1
        self.width = self.stride // self.chunks

    def cut(self, chunk, shifts):
        if self.by_lane:
            return cut(self.head, shifts, self.stride, chunk * self.width, self.width)
        rows = self.head.shape[0]
        if self.by_row:
            shares = self.head.reshape(rows, self.places, -1).transpose(1, 0, 2)
        else:
            shares = self.head.reshape(rows, self.rank, self.places, -1).transpose(2, 0, 1, 3)
        return [lax.dynamic_index_in_dim(shares, place() ^ s, 0, keepdims=False) for s in shifts]

    def join(self, pieces, shifts, chunk=0, whole=None):
        if self.by_lane:
            start = chunk * self.width
            return join(pieces, shifts, self.stride, start, self.width, self.columns, whole)
        if self.by_row:
            whole = stack(pieces, shifts).transpose(1, 0, 2)
        else:
            whole = in_order(pieces, shifts).transpose(1, 2, 0, 3)
        return whole.reshape(whole.shape[0], self.rank, self.columns)


def project_kernel(shifts, parts, stride, start, width, tokens, inside, *refs):
    pieces, refs = refs[: len(shifts)], refs[len(shifts) :]
    before, after = refs[:-parts], refs[-parts:]
    rows = tokens.shape[0] // parts
    tasks = pieces[0].shape[0] // parts
    for turn in range(parts):
        block = lax.axis_index("tensor") ^ turn
        total = before[turn][...] if before else None
        found = jnp.zeros(after[turn].shape, jnp.float32)
        for k, shift in enumerate(shifts):
            column = pl.multiple_of((place() ^ shift) * stride + start, LANES)
            found += lax.dot_general(
                tokens[pl.ds(pl.multiple_of(block * rows, 8), rows), pl.ds(column, width)],
                pieces[k][pl.ds(block * tasks, tasks)].reshape(-1, width),
                (((1,), (1,)), ((), ())),
                preferred_element_type=jnp.float32,
            )
        found = found * inside[block]
        after[turn][...] = found if total is None else total + found


def project(pieces, shifts, stride, start, width, tokens, inside, before):
    parts = inside.shape[0]
    return pl.pallas_call(
        functools.partial(project_kernel, shifts, parts, stride, start, width),
        out_shape=[jax.ShapeDtypeStruct(inside.shape[1:], jnp.float32)] * parts,
        name="project",
    )(tokens, inside, *pieces, *before)


def finish_kernel(count, *refs):
    low_rank = refs[0][...]
    for k in range(1, count):
        low_rank = low_rank + refs[k][...]
    high = low_rank.astype(jnp.bfloat16)
    low = (low_rank - high.astype(jnp.float32)).astype(jnp.bfloat16)
    refs = refs[count:]
    for kept, came, up, out in (refs[0:3] + refs[6:7], refs[3:6] + refs[7:8]):
        update = jnp.dot(high, up[...], preferred_element_type=jnp.float32)
        update = update + jnp.dot(low, up[...], preferred_element_type=jnp.float32)
        out[...] = (kept[...] + came[...] + ADAPTER_SCALE * update).astype(out.dtype)


def finish(shares, query, value, steps):
    rows = query[0].shape[0]

    def columns(x):
        return pl.BlockSpec((x.shape[0], x.shape[1] // steps), lambda i: (0, i))

    return pl.pallas_call(
        functools.partial(finish_kernel, len(shares)),
        grid=(steps,),
        in_specs=[pl.BlockSpec(x.shape, lambda i: (0, 0)) for x in shares]
        + [columns(x) for x in query + value],
        out_specs=[columns(query[0]), columns(value[0])],
        out_shape=[
            jax.ShapeDtypeStruct((rows, query[0].shape[1]), jnp.bfloat16),
            jax.ShapeDtypeStruct((rows, value[0].shape[1]), jnp.bfloat16),
        ],
        name="finish",
    )(*shares, *query, *value)


def halving_order(total):
    bits = total.bit_length() - 1
    return [int(format(o, "b").zfill(bits)[::-1], 2) if bits else 0 for o in range(total)]


def reduce_blocks(partial, axis):
    step = 1
    came = jnp.zeros_like(partial)
    while partial.shape[0] > 1:
        half = partial.shape[0] // 2
        came = swap(partial[half:], axis, step)
        partial = partial[:half]
        step *= 2
        if half > 1:
            partial = partial + came
    return partial[0], came[0]


def gather_blocks(x, axis):
    x = x[None]
    step = 1
    while step < lax.axis_size(axis):
        came = swap(x, axis, step)
        upper = (lax.axis_index(axis) & step) > 0
        x = jnp.concatenate([jnp.where(upper, came, x), jnp.where(upper, x, came)])
        step *= 2
    return x


def local(
    tokens,
    task_counts,
    task_embeddings,
    embedding_weight,
    down_factor_head,
    query_up_head,
    value_up_head,
    w_query,
    w_value,
):
    groups, ring, parts = lax.axis_size("groups"), lax.axis_size("task"), lax.axis_size("tensor")
    places = groups * ring
    tok_rows, shard_width = tokens.shape
    block_rows = tok_rows // parts
    own_tasks = task_counts.shape[0]
    block_tasks = own_tasks // parts
    rank = query_up_head.shape[1]
    hidden_rows = down_factor_head.shape[0]
    tensor = lax.axis_index("tensor")
    ring_shifts = list(range(ring))
    far_first = sorted(ring_shifts[1:], reverse=True)
    shifts = list(range(places))

    heads = {
        "value": Head(value_up_head, 1),
        "query": Head(query_up_head, 1),
        "down": Head(down_factor_head, 2),
    }

    def fetch(name, chunk):
        pieces = heads[name].cut(chunk, ring_shifts)
        got = {0: pieces[0]}
        for s in far_first:
            got[s] = swap(pieces[s], "task", s)
        return jnp.concatenate([got[s] for s in ring_shifts], axis=0)

    fetched = {}
    fetched["query", 0] = fetch("query", 0)

    share = own_tasks // parts
    embeddings = lax.dynamic_index_in_dim(
        task_embeddings.reshape(parts, share, -1), tensor, 0, keepdims=False
    )
    hidden = jax.nn.silu(
        jnp.dot(embeddings, embedding_weight, preferred_element_type=jnp.float32)
    ).astype(jnp.bfloat16)
    group_hidden = jnp.concatenate([hidden] + [swap(hidden, "groups", s) for s in range(1, groups)])
    ring_hidden = jnp.stack(
        [group_hidden] + [swap(group_hidden, "task", s) for s in ring_shifts[1:]]
    )
    every_hidden = gather_blocks(ring_hidden.reshape(places * share, -1), "tensor")
    every_hidden = every_hidden.reshape(parts, ring, groups, share, ring, hidden_rows)
    every_hidden = every_hidden.transpose(4, 2, 1, 0, 3, 5)
    every_hidden = every_hidden.reshape(ring, places * own_tasks, hidden_rows)
    every_hidden = jnp.concatenate(
        [
            lax.dynamic_index_in_dim(every_hidden, lax.axis_index("task") ^ s, 0, keepdims=False)
            for s in ring_shifts
        ],
        axis=1,
    )

    chunks = heads["down"].chunks
    for chunk in range(chunks):
        fetched["down", chunk] = fetch("down", chunk)
    fetched["value", 0] = fetch("value", 0)

    def emit(name, chunk):
        matrix = fetched[name, chunk]
        flat = jnp.dot(
            every_hidden, matrix.reshape(matrix.shape[0], -1), preferred_element_type=jnp.float32
        ).astype(jnp.bfloat16)
        made = flat.reshape((places, own_tasks) + matrix.shape[1:])
        got = {0: made[0]}
        for s in reversed(shifts[1:]):
            got[s] = swap(made[s], PLACES, s)
        return [got[s] for s in shifts]

    emitted = {}
    for name, chunk in [("query", 0), ("value", 0)] + [("down", c) for c in range(chunks)]:
        emitted[name, chunk] = emit(name, chunk)

    token_blocks = tokens.reshape(parts, block_rows, shard_width)
    order = halving_order(parts)
    turned = jnp.concatenate(
        [lax.dynamic_index_in_dim(token_blocks, tensor ^ s, 0, keepdims=False) for s in order]
    )
    base_query = jnp.dot(turned, w_query, preferred_element_type=jnp.float32)
    base_value = jnp.dot(turned, w_value, preferred_element_type=jnp.float32)
    base_query = reduce_blocks(base_query.reshape(parts, block_rows, -1), "tensor")
    base_value = reduce_blocks(base_value.reshape(parts, block_rows, -1), "tensor")

    def own_block(factors, above, below):
        moved = lax.all_to_all(factors, "tensor", split_axis=0, concat_axis=0, tiled=True)
        moved = moved.reshape(parts, block_tasks, rank, -1).transpose(1, 2, 0, 3)
        moved = moved.reshape(block_tasks, rank, -1)
        moved = jnp.pad(moved, ((0, 0), (above, below), (0, 0)))
        return moved.reshape(block_tasks * 2 * rank, -1)

    query_up_factors = heads["query"].join(emitted["query", 0], shifts)
    own_query = own_block(query_up_factors, 0, rank)
    value_up_factors = heads["value"].join(emitted["value", 0], shifts)
    own_value = own_block(value_up_factors, rank, 0)

    tallies = task_counts.reshape(parts, block_tasks)
    ends = jnp.cumsum(tallies, axis=1)
    starts = ends - tallies
    positions = jnp.arange(block_rows, dtype=jnp.int32)
    inside = (
        (positions[None, :, None] >= starts[:, None, :])
        & (positions[None, :, None] < ends[:, None, :])
    ).astype(jnp.float32)
    inside = jnp.repeat(inside, 2 * rank, axis=2)

    down_factors, spread = None, []
    for chunk in range(chunks):
        head, pieces = heads["down"], emitted["down", chunk]
        if head.by_lane:
            start = chunk * head.width
            spread = project(pieces, shifts, head.stride, start, head.width, tokens, inside, spread)
        down_factors = head.join(pieces, shifts, chunk, down_factors)
    if not spread:
        projected = jnp.einsum(
            "bpd,bmd->bpm",
            token_blocks,
            down_factors.reshape(parts, block_tasks * 2 * rank, shard_width),
            preferred_element_type=jnp.float32,
        )
        projected = projected * inside
        spread = [
            lax.dynamic_index_in_dim(projected, tensor ^ s, 0, keepdims=False)
            for s in range(parts)
        ]
    shares = [spread[0]] + [swap(spread[s], "tensor", s) for s in range(1, parts)]
    query, value = finish(
        shares, [*base_query, own_query], [*base_value, own_value], steps=4
    )
    return query, value, down_factors, query_up_factors, value_up_factors


def solution(mesh):
    return jax.shard_map(
        local,
        mesh=mesh,
        in_specs=(
            P(("groups", "task"), "tensor"),
            P(("groups", "task")),
            P(("groups", "task"), None),
            P(),
            P("task", None, "tensor"),
            P("task", None, "tensor"),
            P("task", None, "tensor"),
            P("tensor", None),
            P("tensor", None),
        ),
        out_specs=(
            P(("groups", "task", "tensor"), None),
            P(("groups", "task", "tensor"), None),
            P(("groups", "task"), None, "tensor"),
            P(("groups", "task"), None, "tensor"),
            P(("groups", "task"), None, "tensor"),
        ),
        check_vma=False,
    )
```

profile of v0, /device:TPU:0, one launch (start us, length us, event | category | flops | bytes accessed | tf_op | source)
XLA Modules:
  0.0 313.0 jit_solution(17416092640127400305)
XLA Ops:
  2.9 3.1 collective-permute-start
  7.7 4.1 %collective-permute-start.3 = (bf16[32,512]{1,0:T(8,128)(2,1)S(1)}, bf16[32,512]{1,0:T(8,128)(2,1)S(1)}, u32[]{:S(2)}, u32[]{:S(2)}) collective-permute-start(bf16[32,512]{1,0:T(8,128)(2,1)S(1)} %get-tuple-element.126), channel_id=1, source_target_pairs={{0,3},{1,2},{2,1},{3,0},{4,7},{5,6},{6,5},{7,4},{8,11},{9,10},{10,... | collective-permute-start | bytes 98312 | tf_op jit(solution)/shard_map/ppermute | solution.py:18
  12.4 10.2 %fusion.7 = f32[384,4096]{1,0:T(8,128)S(1)} fusion(bf16[2048,4096]{1,0:T(8,128)(2,1)} %param.16, bf16[96,2048]{1,0:T(8,128)(2,1)S(1)} %get-tuple-element.92, bf16[96,2048]{1,0:T(8,128)(2,1)S(1)} %get-tuple-element.93, bf16[96,2048]{1,0:T(8,128)(2,1)S(1)} %get-tuple-element.94, bf16[96,2048]{1,0:T(8,128)(2,1)S(1)} %get-tuple-element.91), kind=kOutput, calls=%fused_computation.23 | convolution fusion | flops 6448742400 | bytes 24641536 | tf_op jit(solution)/shard_map/dot_general | solution.py:330
  22.8 2.2 fusion.27
  25.6 2.0 cut.5
  27.6 3.8 %collective-permute-start.33 = (bf16[128,8,128]{2,1,0:T(8,128)(2,1)}, bf16[128,8,128]{2,1,0:T(8,128)(2,1)}, u32[]{:S(2)}, u32[]{:S(2)}) collective-permute-start(bf16[128,8,128]{2,1,0:T(8,128)(2,1)} %get-tuple-element.46), channel_id=1, source_target_pairs={{0,3},{1,2},{2,1},{3,0},{4,7},{5,6},{6,5},{7,4},{8,11},{9,10},{10,... | collective-permute-start | bytes 786440 | tf_op jit(solution)/shard_map/ppermute | solution.py:18
  31.4 3.0 constant_dynamic-slice_fusion.3
  39.4 5.7 %fusion.6 = f32[384,1024]{1,0:T(8,128)} fusion(bf16[2048,1024]{1,0:T(8,128)(2,1)} %param.17, bf16[96,2048]{1,0:T(8,128)(2,1)} %copy-done.14, bf16[96,2048]{1,0:T(8,128)(2,1)} %copy-done.15, bf16[96,2048]{1,0:T(8,128)(2,1)} %copy-done.16, bf16[96,2048]{1,0:T(8,128)(2,1)} %copy-done.13), kind=kOutput, calls=%fused_computation.22 | convolution fusion | flops 1616904192 | bytes 7340032 | tf_op jit(solution)/shard_map/dot_general | solution.py:331
  47.2 3.8 %collective-permute-start.43 = (bf16[128,256]{1,0:T(8,128)(2,1)}, bf16[128,256]{1,0:T(8,128)(2,1)}, u32[]{:S(2)}, u32[]{:S(2)}) collective-permute-start(bf16[128,256]{1,0:T(8,128)(2,1)} %bitcast.193), channel_id=1, source_target_pairs={{0,1},{1,0},{2,3},{3,2},{4,5},{5,4},{6,7},{7,6},{8,9},{9,8},{10,11... | collective-permute-start | bytes 196616 | tf_op jit(solution)/shard_map/ppermute | solution.py:18
  52.9 2.0 reshape.148
  61.5 2.5 cut.3
  64.0 2.5 cut.4
  66.6 2.9 collective-permute-start.47
  73.1 3.7 %collective-permute-start.8 = (bf16[128,16,128]{2,1,0:T(8,128)(2,1)}, bf16[128,16,128]{2,1,0:T(8,128)(2,1)}, u32[]{:S(2)}, u32[]{:S(2)}) collective-permute-start(bf16[128,16,128]{2,1,0:T(8,128)(2,1)} %get-tuple-element.30), channel_id=1, source_target_pairs={{0,3},{1,2},{2,1},{3,0},{4,7},{5,6},{6,5},{7,4},{8,11},{9,10},{10,... | collective-permute-start | bytes 1572872 | tf_op jit(solution)/shard_map/ppermute | solution.py:18
  77.9 3.9 %collective-permute-start.51 = (bf16[64,256]{1,0:T(8,128)(2,1)S(1)}, bf16[64,256]{1,0:T(8,128)(2,1)S(1)}, u32[]{:S(2)}, u32[]{:S(2)}) collective-permute-start(bf16[64,256]{1,0:T(8,128)(2,1)S(1)} %copy-done.48), channel_id=1, source_target_pairs={{0,18},{1,19},{2,16},{3,17},{16,2},{17,3},{18,0},{19,1},{4,22},{5,... | collective-permute-start | bytes 98312 | tf_op jit(solution)/shard_map/ppermute | solution.py:18
  82.6 41.3 %collective-permute-done.51.refs_6_ = bf16[64,256]{1,0:T(8,128)(2,1)S(1)} collective-permute-done((bf16[64,256]{1,0:T(8,128)(2,1)S(1)}, bf16[64,256]{1,0:T(8,128)(2,1)S(1)}, u32[]{:S(2)}, u32[]{:S(2)}) %collective-permute-start.51) | collective-permute-done | bytes 32800 | tf_op jit(solution)/shard_map/ppermute | solution.py:18
  124.5 3.5 %collective-permute-start.52 = (bf16[64,256]{1,0:T(8,128)(2,1)S(1)}, bf16[64,256]{1,0:T(8,128)(2,1)S(1)}, u32[]{:S(2)}, u32[]{:S(2)}) collective-permute-start(bf16[64,256]{1,0:T(8,128)(2,1)S(1)} %copy-done.45), channel_id=1, source_target_pairs={{0,19},{1,18},{2,17},{3,16},{16,3},{17,2},{18,1},{19,0},{4,23},{5,... | collective-permute-start | bytes 98312 | tf_op jit(solution)/shard_map/ppermute | solution.py:18
  134.9 1.6 stack.21
  136.5 1.8 copy.45
  138.3 4.2 %all-to-all-start.1 = ((bf16[64,8,256]{2,1,0:T(8,128)(2,1)}), bf16[64,8,256]{2,1,0:T(8,128)(2,1)}, u32[]{:S(2)}, u32[]{:S(2)}) async-start(bf16[64,8,256]{2,1,0:T(8,128)(2,1)} %copy.45), calls=%async_computation.1 | async-start | bytes 524288 | tf_op jit(solution)/shard_map/all_to_all | solution.py:336
  142.6 2.9 collective-permute-start.16
  145.6 1.8 pad_maximum_fusion
  149.9 2.0 collective-permute-start.35
  151.9 2.2 add.70
  155.6 2.4 collective-permute-start.36
  157.9 26.2 %collective-permute-done.17 = bf16[128,16,128]{2,1,0:T(8,128)(2,1)S(1)} collective-permute-done((bf16[128,16,128]{2,1,0:T(8,128)(2,1)}, bf16[128,16,128]{2,1,0:T(8,128)(2,1)S(1)}, u32[]{:S(2)}, u32[]{:S(2)}) %collective-permute-start.17) | collective-permute-done | bytes 524320 | tf_op jit(solution)/shard_map/ppermute | solution.py:18
  187.8 3.6 %collective-permute-start.39 = (bf16[64,8,128]{2,1,0:T(8,128)(2,1)S(1)}, bf16[64,8,128]{2,1,0:T(8,128)(2,1)S(1)}, u32[]{:S(2)}, u32[]{:S(2)}) collective-permute-start(bf16[64,8,128]{2,1,0:T(8,128)(2,1)S(1)} %bitcast.186), channel_id=1, source_target_pairs={{0,18},{1,19},{2,16},{3,17},{16,2},{17,3},{18,0},{19,1},{4,22},{5,... | collective-permute-start | bytes 393224 | tf_op jit(solution)/shard_map/ppermute | solution.py:18
  191.5 1.6 collective-permute-start.40
  194.5 7.2 %collective-permute-done.39.refs_6_ = bf16[64,8,128]{2,1,0:T(8,128)(2,1)S(1)} collective-permute-done((bf16[64,8,128]{2,1,0:T(8,128)(2,1)S(1)}, bf16[64,8,128]{2,1,0:T(8,128)(2,1)S(1)}, u32[]{:S(2)}, u32[]{:S(2)}) %collective-permute-start.39) | collective-permute-done | bytes 131104 | tf_op jit(solution)/shard_map/ppermute | solution.py:18
  201.8 2.2 collective-permute-start.11
  204.0 2.5 collective-permute-done.9.refs_1_
  210.4 11.8 %collective-permute-done.10.refs_2_ = bf16[64,16,128]{2,1,0:T(8,128)(2,1)} collective-permute-done((bf16[64,16,128]{2,1,0:T(8,128)(2,1)S(1)}, bf16[64,16,128]{2,1,0:T(8,128)(2,1)}, u32[]{:S(2)}, u32[]{:S(2)}) %collective-permute-start.10) | collective-permute-done | bytes 262176 | tf_op jit(solution)/shard_map/ppermute | solution.py:18
  222.2 5.8 %collective-permute-start.20 = (bf16[64,16,128]{2,1,0:T(8,128)(2,1)}, bf16[64,16,128]{2,1,0:T(8,128)(2,1)}, u32[]{:S(2)}, u32[]{:S(2)}) collective-permute-start(bf16[64,16,128]{2,1,0:T(8,128)(2,1)} %bitcast.67), channel_id=1, source_target_pairs={{0,2},{1,3},{2,0},{3,1},{16,18},{17,19},{18,16},{19,17},{4,6},{5,7... | collective-permute-start | bytes 786440 | tf_op jit(solution)/shard_map/ppermute | solution.py:18
  228.0 1.9 collective-permute-start.21
  230.6 2.1 join.3
  232.7 3.7 %all-to-all-start = ((bf16[64,8,1024]{2,1,0:T(8,128)(2,1)}), bf16[64,8,1024]{2,1,0:T(8,128)(2,1)S(1)}, u32[]{:S(2)}, u32[]{:S(2)}) async-start(bf16[64,8,1024]{2,1,0:T(8,128)(2,1)} %join.3), calls=%async_computation | async-start | bytes 2097152 | tf_op jit(solution)/shard_map/all_to_all | solution.py:336
  243.0 3.7 %collective-permute-done.20.refs_2_ = bf16[64,16,128]{2,1,0:T(8,128)(2,1)} collective-permute-done((bf16[64,16,128]{2,1,0:T(8,128)(2,1)}, bf16[64,16,128]{2,1,0:T(8,128)(2,1)}, u32[]{:S(2)}, u32[]{:S(2)}) %collective-permute-start.20) | collective-permute-done | bytes 262176 | tf_op jit(solution)/shard_map/ppermute | solution.py:18
  247.1 2.1 collective-permute-start.25
  253.9 16.1 %collective-permute-start.13 = (bf16[64,16,128]{2,1,0:T(8,128)(2,1)}, bf16[64,16,128]{2,1,0:T(8,128)(2,1)}, u32[]{:S(2)}, u32[]{:S(2)}) collective-permute-start(bf16[64,16,128]{2,1,0:T(8,128)(2,1)} %bitcast.55), channel_id=1, source_target_pairs={{0,17},{1,16},{2,19},{3,18},{16,1},{17,0},{18,3},{19,2},{4,21},{5,... | collective-permute-start | bytes 786440 | tf_op jit(solution)/shard_map/ppermute | solution.py:18
  270.7 3.0 collective-permute-start.15
  275.0 1.7 copy.53
  276.7 1.7 copy.62
  278.4 3.6 %project.2 = (f32[96,256]{1,0:T(8,128)}, f32[96,256]{1,0:T(8,128)}, f32[96,256]{1,0:T(8,128)}, f32[96,256]{1,0:T(8,128)}) custom-call(bf16[384,2048]{1,0:T(8,128)(2,1)} %tokens.3, f32[4,96,256]{2,1,0:T(8,128)} %copy.39.inside, bf16[64,16,128]{2,1,0:T(8,128)(2,1)} %bitcast.163, bf16[64,16,128]{2,1,0:T(8,128)(2,1)} %collective-permute-done.19.refs_1_, ...), custom_call_target="tpu_custom_call" | custom-call | tf_op jit(solution)/shard_map/project/pallas_call | solution.py:173
  282.0 11.0 %collective-permute-done.14.refs_6_ = bf16[64,16,128]{2,1,0:T(8,128)(2,1)} collective-permute-done((bf16[64,16,128]{2,1,0:T(8,128)(2,1)}, bf16[64,16,128]{2,1,0:T(8,128)(2,1)}, u32[]{:S(2)}, u32[]{:S(2)}) %collective-permute-start.14) | collective-permute-done | bytes 262176 | tf_op jit(solution)/shard_map/ppermute | solution.py:18
  293.0 3.7 %project.3 = (f32[96,256]{1,0:T(8,128)}, f32[96,256]{1,0:T(8,128)}, f32[96,256]{1,0:T(8,128)}, f32[96,256]{1,0:T(8,128)}) custom-call(bf16[384,2048]{1,0:T(8,128)(2,1)} %tokens.3, f32[4,96,256]{2,1,0:T(8,128)} %copy.39.inside, bf16[64,16,128]{2,1,0:T(8,128)(2,1)} %bitcast.161, bf16[64,16,128]{2,1,0:T(8,128)(2,1)} %copy-done.4, ...), custom_call_target="tpu_custom_call" | custom-call | tf_op jit(solution)/shard_map/project/pallas_call | solution.py:173
  300.4 2.4 join.4.refs_8_
  302.8 2.4 join.5
  307.5 5.3 %finish.1 = (bf16[96,4096]{1,0:T(8,128)(2,1)}, bf16[96,1024]{1,0:T(8,128)(2,1)}) custom-call(f32[96,256]{1,0:T(8,128)} %get-tuple-element.39.refs_0_, f32[96,256]{1,0:T(8,128)} %copy-done.42, f32[96,256]{1,0:T(8,128)} %copy-done.43, f32[96,256]{1,0:T(8,128)} %copy-done.44, f32[96,4096]{1,0:T(8,128)} %get-tuple-element.72.refs_4_, ...), custom_call_target="tpu_custom_call" | custom-call | tf_op jit(solution)/shard_map/finish/pallas_call | solution.py:199
  (250 shorter events, 67.1 us)
Async XLA Ops:
  7.7 15.0 %collective-permute-start.3 = (bf16[32,512]{1,0:T(8,128)(2,1)S(1)}, bf16[32,512]{1,0:T(8,128)(2,1)S(1)}, u32[]{:S(2)}, u32[]{:S(2)}) collective-permute-start(bf16[32,512]{1,0:T(8,128)(2,1)S(1)} %get-tuple-element.126), channel_id=1, source_target_pairs={{0,3},{1,2},{2,1},{3,0},{4,7},{5,6},{6,5},{7,4},{8,11},{9,10},{10,... | collective-permute-start | bytes 98312 | tf_op jit(solution)/shard_map/ppermute | solution.py:18
  11.8 10.9 %collective-permute-start.2 = (bf16[32,512]{1,0:T(8,128)(2,1)S(1)}, bf16[32,512]{1,0:T(8,128)(2,1)S(1)}, u32[]{:S(2)}, u32[]{:S(2)}) collective-permute-start(bf16[32,512]{1,0:T(8,128)(2,1)S(1)} %get-tuple-element.126), channel_id=1, source_target_pairs={{0,2},{1,3},{2,0},{3,1},{4,6},{5,7},{6,4},{7,5},{8,10},{9,11},{10,... | collective-permute-start | bytes 98312 | tf_op jit(solution)/shard_map/ppermute | solution.py:18
  11.8 10.9 %collective-permute-start.1 = (bf16[32,512]{1,0:T(8,128)(2,1)S(1)}, bf16[32,512]{1,0:T(8,128)(2,1)S(1)}, u32[]{:S(2)}, u32[]{:S(2)}) collective-permute-start(bf16[32,512]{1,0:T(8,128)(2,1)S(1)} %get-tuple-element.126), channel_id=1, source_target_pairs={{0,1},{1,0},{2,3},{3,2},{4,5},{5,4},{6,7},{7,6},{8,9},{9,8},{10,11... | collective-permute-start | bytes 98312 | tf_op jit(solution)/shard_map/ppermute | solution.py:18
  22.8 13.5 %collective-permute-start.4 = (bf16[1,128,512]{2,1,0:T(8,128)(2,1)S(1)}, bf16[1,128,512]{2,1,0:T(8,128)(2,1)}, u32[]{:S(2)}, u32[]{:S(2)}) collective-permute-start(bf16[1,128,512]{2,1,0:T(8,128)(2,1)S(1)} %bitcast.174), channel_id=1, source_target_pairs={{0,4},{4,0},{8,12},{12,8},{1,5},{5,1},{9,13},{13,9},{2,6},{6,2},{1... | collective-permute-start | bytes 393224 | tf_op jit(solution)/shard_map/ppermute | solution.py:18
  25.1 124.8 %collective-permute-start.29 = (f32[2,96,4096]{2,1,0:T(8,128)}, f32[2,96,4096]{2,1,0:T(8,128)}, u32[]{:S(2)}, u32[]{:S(2)}) collective-permute-start(f32[2,96,4096]{2,1,0:T(8,128)} %bitcast.20), channel_id=1, source_target_pairs={{0,4},{4,0},{8,12},{12,8},{1,5},{5,1},{9,13},{13,9},{2,6},{6,2},{1... | collective-permute-start | bytes 9437192 | tf_op jit(solution)/shard_map/ppermute | solution.py:18
  27.6 39.0 %collective-permute-start.33 = (bf16[128,8,128]{2,1,0:T(8,128)(2,1)}, bf16[128,8,128]{2,1,0:T(8,128)(2,1)}, u32[]{:S(2)}, u32[]{:S(2)}) collective-permute-start(bf16[128,8,128]{2,1,0:T(8,128)(2,1)} %get-tuple-element.46), channel_id=1, source_target_pairs={{0,3},{1,2},{2,1},{3,0},{4,7},{5,6},{6,5},{7,4},{8,11},{9,10},{10,... | collective-permute-start | bytes 786440 | tf_op jit(solution)/shard_map/ppermute | solution.py:18
  35.0 21.1 %collective-permute-start.45 = (bf16[128,256]{1,0:T(8,128)(2,1)}, bf16[128,256]{1,0:T(8,128)(2,1)}, u32[]{:S(2)}, u32[]{:S(2)}) collective-permute-start(bf16[128,256]{1,0:T(8,128)(2,1)} %bitcast.150), channel_id=1, source_target_pairs={{0,3},{1,2},{2,1},{3,0},{4,7},{5,6},{6,5},{7,4},{8,11},{9,10},{10,... | collective-permute-start | bytes 196616 | tf_op jit(solution)/shard_map/ppermute | solution.py:18
  35.7 20.5 %collective-permute-start.44 = (bf16[128,256]{1,0:T(8,128)(2,1)}, bf16[128,256]{1,0:T(8,128)(2,1)}, u32[]{:S(2)}, u32[]{:S(2)}) collective-permute-start(bf16[128,256]{1,0:T(8,128)(2,1)} %bitcast.151), channel_id=1, source_target_pairs={{0,2},{1,3},{2,0},{3,1},{4,6},{5,7},{6,4},{7,5},{8,10},{9,11},{10,... | collective-permute-start | bytes 196616 | tf_op jit(solution)/shard_map/ppermute | solution.py:18
  37.9 9.3 %collective-permute-start.5 = (bf16[2,128,512]{2,1,0:T(8,128)(2,1)}, bf16[2,128,512]{2,1,0:T(8,128)(2,1)}, u32[]{:S(2)}, u32[]{:S(2)}) collective-permute-start(bf16[2,128,512]{2,1,0:T(8,128)(2,1)} %pad_maximum_fusion.8), channel_id=1, source_target_pairs={{0,8},{4,12},{8,0},{12,4},{1,9},{5,13},{9,1},{13,5},{2,10},{6,14},... | collective-permute-start | bytes 786440 | tf_op jit(solution)/shard_map/ppermute | solution.py:18
  47.2 9.7 %collective-permute-start.43 = (bf16[128,256]{1,0:T(8,128)(2,1)}, bf16[128,256]{1,0:T(8,128)(2,1)}, u32[]{:S(2)}, u32[]{:S(2)}) collective-permute-start(bf16[128,256]{1,0:T(8,128)(2,1)} %bitcast.193), channel_id=1, source_target_pairs={{0,1},{1,0},{2,3},{3,2},{4,5},{5,4},{6,7},{7,6},{8,9},{9,8},{10,11... | collective-permute-start | bytes 196616 | tf_op jit(solution)/shard_map/ppermute | solution.py:18
  56.1 13.9 %collective-permute-start.32 = (bf16[128,8,128]{2,1,0:T(8,128)(2,1)}, bf16[128,8,128]{2,1,0:T(8,128)(2,1)}, u32[]{:S(2)}, u32[]{:S(2)}) collective-permute-start(bf16[128,8,128]{2,1,0:T(8,128)(2,1)} %get-tuple-element.45), channel_id=1, source_target_pairs={{0,2},{1,3},{2,0},{3,1},{4,6},{5,7},{6,4},{7,5},{8,10},{9,11},{10,... | collective-permute-start | bytes 786440 | tf_op jit(solution)/shard_map/ppermute | solution.py:18
  56.2 14.1 %collective-permute-start.31 = (bf16[128,8,128]{2,1,0:T(8,128)(2,1)}, bf16[128,8,128]{2,1,0:T(8,128)(2,1)}, u32[]{:S(2)}, u32[]{:S(2)}) collective-permute-start(bf16[128,8,128]{2,1,0:T(8,128)(2,1)} %get-tuple-element.44), channel_id=1, source_target_pairs={{0,1},{1,0},{2,3},{3,2},{4,5},{5,4},{6,7},{7,6},{8,9},{9,8},{10,11... | collective-permute-start | bytes 786440 | tf_op jit(solution)/shard_map/ppermute | solution.py:18
  58.9 12.9 %collective-permute-start.46 = (bf16[64,256]{1,0:T(8,128)(2,1)}, bf16[64,256]{1,0:T(8,128)(2,1)}, u32[]{:S(2)}, u32[]{:S(2)}) collective-permute-start(bf16[64,256]{1,0:T(8,128)(2,1)} %get-tuple-element.121), channel_id=1, source_target_pairs={{0,1},{1,0},{2,3},{3,2},{16,17},{17,16},{18,19},{19,18},{4,5},{5,4... | collective-permute-start | bytes 98312 | tf_op jit(solution)/shard_map/ppermute | solution.py:18
  73.1 69.4 %collective-permute-start.8 = (bf16[128,16,128]{2,1,0:T(8,128)(2,1)}, bf16[128,16,128]{2,1,0:T(8,128)(2,1)}, u32[]{:S(2)}, u32[]{:S(2)}) collective-permute-start(bf16[128,16,128]{2,1,0:T(8,128)(2,1)} %get-tuple-element.30), channel_id=1, source_target_pairs={{0,3},{1,2},{2,1},{3,0},{4,7},{5,6},{6,5},{7,4},{8,11},{9,10},{10,... | collective-permute-start | bytes 1572872 | tf_op jit(solution)/shard_map/ppermute | solution.py:18
  76.8 65.9 %collective-permute-start.7 = (bf16[128,16,128]{2,1,0:T(8,128)(2,1)}, bf16[128,16,128]{2,1,0:T(8,128)(2,1)}, u32[]{:S(2)}, u32[]{:S(2)}) collective-permute-start(bf16[128,16,128]{2,1,0:T(8,128)(2,1)} %get-tuple-element.29), channel_id=1, source_target_pairs={{0,2},{1,3},{2,0},{3,1},{4,6},{5,7},{6,4},{7,5},{8,10},{9,11},{10,... | collective-permute-start | bytes 1572872 | tf_op jit(solution)/shard_map/ppermute | solution.py:18
  77.4 68.2 %collective-permute-start.6 = (bf16[128,16,128]{2,1,0:T(8,128)(2,1)}, bf16[128,16,128]{2,1,0:T(8,128)(2,1)}, u32[]{:S(2)}, u32[]{:S(2)}) collective-permute-start(bf16[128,16,128]{2,1,0:T(8,128)(2,1)} %get-tuple-element.28), channel_id=1, source_target_pairs={{0,1},{1,0},{2,3},{3,2},{4,5},{5,4},{6,7},{7,6},{8,9},{9,8},{10,11... | collective-permute-start | bytes 1572872 | tf_op jit(solution)/shard_map/ppermute | solution.py:18
  77.9 45.9 %collective-permute-start.51 = (bf16[64,256]{1,0:T(8,128)(2,1)S(1)}, bf16[64,256]{1,0:T(8,128)(2,1)S(1)}, u32[]{:S(2)}, u32[]{:S(2)}) collective-permute-start(bf16[64,256]{1,0:T(8,128)(2,1)S(1)} %copy-done.48), channel_id=1, source_target_pairs={{0,18},{1,19},{2,16},{3,17},{16,2},{17,3},{18,0},{19,1},{4,22},{5,... | collective-permute-start | bytes 98312 | tf_op jit(solution)/shard_map/ppermute | solution.py:18
  124.5 8.3 %collective-permute-start.52 = (bf16[64,256]{1,0:T(8,128)(2,1)S(1)}, bf16[64,256]{1,0:T(8,128)(2,1)S(1)}, u32[]{:S(2)}, u32[]{:S(2)}) collective-permute-start(bf16[64,256]{1,0:T(8,128)(2,1)S(1)} %copy-done.45), channel_id=1, source_target_pairs={{0,19},{1,18},{2,17},{3,16},{16,3},{17,2},{18,1},{19,0},{4,23},{5,... | collective-permute-start | bytes 98312 | tf_op jit(solution)/shard_map/ppermute | solution.py:18
  133.4 22.2 %collective-permute-start.18 = (bf16[128,16,128]{2,1,0:T(8,128)(2,1)}, bf16[128,16,128]{2,1,0:T(8,128)(2,1)}, u32[]{:S(2)}, u32[]{:S(2)}) collective-permute-start(bf16[128,16,128]{2,1,0:T(8,128)(2,1)} %get-tuple-element.34), channel_id=1, source_target_pairs={{0,3},{1,2},{2,1},{3,0},{4,7},{5,6},{6,5},{7,4},{8,11},{9,10},{10,... | collective-permute-start | bytes 1572872 | tf_op jit(solution)/shard_map/ppermute | solution.py:18
  138.3 94.4 %all-to-all-start.1 = ((bf16[64,8,256]{2,1,0:T(8,128)(2,1)}), bf16[64,8,256]{2,1,0:T(8,128)(2,1)}, u32[]{:S(2)}, u32[]{:S(2)}) async-start(bf16[64,8,256]{2,1,0:T(8,128)(2,1)} %copy.45), calls=%async_computation.1 | async-start | bytes 524288 | tf_op jit(solution)/shard_map/all_to_all | solution.py:336
  142.5 41.5 %collective-permute-start.17 = (bf16[128,16,128]{2,1,0:T(8,128)(2,1)}, bf16[128,16,128]{2,1,0:T(8,128)(2,1)S(1)}, u32[]{:S(2)}, u32[]{:S(2)}) collective-permute-start(bf16[128,16,128]{2,1,0:T(8,128)(2,1)} %get-tuple-element.33), channel_id=1, source_target_pairs={{0,2},{1,3},{2,0},{3,1},{4,6},{5,7},{6,4},{7,5},{8,10},{9,11},{10,... | collective-permute-start | bytes 1572872 | tf_op jit(solution)/shard_map/ppermute | solution.py:18
  142.6 42.5 %collective-permute-start.16 = (bf16[128,16,128]{2,1,0:T(8,128)(2,1)}, bf16[128,16,128]{2,1,0:T(8,128)(2,1)S(1)}, u32[]{:S(2)}, u32[]{:S(2)}) collective-permute-start(bf16[128,16,128]{2,1,0:T(8,128)(2,1)} %get-tuple-element.32), channel_id=1, source_target_pairs={{0,1},{1,0},{2,3},{3,2},{4,5},{5,4},{6,7},{7,6},{8,9},{9,8},{10,11... | collective-permute-start | bytes 1572872 | tf_op jit(solution)/shard_map/ppermute | solution.py:18
  145.5 40.2 %collective-permute-start.34 = (bf16[64,8,128]{2,1,0:T(8,128)(2,1)}, bf16[64,8,128]{2,1,0:T(8,128)(2,1)S(1)}, u32[]{:S(2)}, u32[]{:S(2)}) collective-permute-start(bf16[64,8,128]{2,1,0:T(8,128)(2,1)} %bitcast.191), channel_id=1, source_target_pairs={{0,1},{1,0},{2,3},{3,2},{16,17},{17,16},{18,19},{19,18},{4,5},{5,4... | collective-permute-start | bytes 393224 | tf_op jit(solution)/shard_map/ppermute | solution.py:18
  149.9 37.8 %collective-permute-start.35 = (bf16[64,8,128]{2,1,0:T(8,128)(2,1)S(1)}, bf16[64,8,128]{2,1,0:T(8,128)(2,1)S(1)}, u32[]{:S(2)}, u32[]{:S(2)}) collective-permute-start(bf16[64,8,128]{2,1,0:T(8,128)(2,1)S(1)} %bitcast.190), channel_id=1, source_target_pairs={{0,2},{1,3},{2,0},{3,1},{16,18},{17,19},{18,16},{19,17},{4,6},{5,7... | collective-permute-start | bytes 393224 | tf_op jit(solution)/shard_map/ppermute | solution.py:18
  155.6 32.3 %collective-permute-start.36 = (bf16[64,8,128]{2,1,0:T(8,128)(2,1)S(1)}, bf16[64,8,128]{2,1,0:T(8,128)(2,1)S(1)}, u32[]{:S(2)}, u32[]{:S(2)}) collective-permute-start(bf16[64,8,128]{2,1,0:T(8,128)(2,1)S(1)} %bitcast.189), channel_id=1, source_target_pairs={{0,3},{1,2},{2,1},{3,0},{16,19},{17,18},{18,17},{19,16},{4,7},{5,6... | collective-permute-start | bytes 393224 | tf_op jit(solution)/shard_map/ppermute | solution.py:18
  185.8 121.1 %collective-permute-start.30 = (f32[1,96,4096]{2,1,0:T(8,128)S(1)}, f32[1,96,4096]{2,1,0:T(8,128)}, u32[]{:S(2)}, u32[]{:S(2)}) collective-permute-start(f32[1,96,4096]{2,1,0:T(8,128)S(1)} %get-tuple-element.71), channel_id=1, source_target_pairs={{0,8},{4,12},{8,0},{12,4},{1,9},{5,13},{9,1},{13,5},{2,10},{6,14},... | collective-permute-start | bytes 4718600 | tf_op jit(solution)/shard_map/ppermute | solution.py:18
  187.7 49.6 %collective-permute-start.41 = (f32[2,96,1024]{2,1,0:T(8,128)}, f32[2,96,1024]{2,1,0:T(8,128)}, u32[]{:S(2)}, u32[]{:S(2)}) collective-permute-start(f32[2,96,1024]{2,1,0:T(8,128)} %bitcast.28), channel_id=1, source_target_pairs={{0,4},{4,0},{8,12},{12,8},{1,5},{5,1},{9,13},{13,9},{2,6},{6,2},{1... | collective-permute-start | bytes 2359304 | tf_op jit(solution)/shard_map/ppermute | solution.py:18
  187.8 13.9 %collective-permute-start.39 = (bf16[64,8,128]{2,1,0:T(8,128)(2,1)S(1)}, bf16[64,8,128]{2,1,0:T(8,128)(2,1)S(1)}, u32[]{:S(2)}, u32[]{:S(2)}) collective-permute-start(bf16[64,8,128]{2,1,0:T(8,128)(2,1)S(1)} %bitcast.186), channel_id=1, source_target_pairs={{0,18},{1,19},{2,16},{3,17},{16,2},{17,3},{18,0},{19,1},{4,22},{5,... | collective-permute-start | bytes 393224 | tf_op jit(solution)/shard_map/ppermute | solution.py:18
  191.5 10.3 %collective-permute-start.40 = (bf16[64,8,128]{2,1,0:T(8,128)(2,1)S(1)}, bf16[64,8,128]{2,1,0:T(8,128)(2,1)S(1)}, u32[]{:S(2)}, u32[]{:S(2)}) collective-permute-start(bf16[64,8,128]{2,1,0:T(8,128)(2,1)S(1)} %bitcast.185), channel_id=1, source_target_pairs={{0,19},{1,18},{2,17},{3,16},{16,3},{17,2},{18,1},{19,0},{4,23},{5,... | collective-permute-start | bytes 393224 | tf_op jit(solution)/shard_map/ppermute | solution.py:18
  193.1 13.5 %collective-permute-start.9 = (bf16[64,16,128]{2,1,0:T(8,128)(2,1)S(1)}, bf16[64,16,128]{2,1,0:T(8,128)(2,1)S(1)}, u32[]{:S(2)}, u32[]{:S(2)}) collective-permute-start(bf16[64,16,128]{2,1,0:T(8,128)(2,1)S(1)} %bitcast.178), channel_id=1, source_target_pairs={{0,1},{1,0},{2,3},{3,2},{16,17},{17,16},{18,19},{19,18},{4,5},{5,4... | collective-permute-start | bytes 786440 | tf_op jit(solution)/shard_map/ppermute | solution.py:18
  201.7 20.5 %collective-permute-start.10 = (bf16[64,16,128]{2,1,0:T(8,128)(2,1)S(1)}, bf16[64,16,128]{2,1,0:T(8,128)(2,1)}, u32[]{:S(2)}, u32[]{:S(2)}) collective-permute-start(bf16[64,16,128]{2,1,0:T(8,128)(2,1)S(1)} %bitcast.184), channel_id=1, source_target_pairs={{0,2},{1,3},{2,0},{3,1},{16,18},{17,19},{18,16},{19,17},{4,6},{5,7... | collective-permute-start | bytes 786440 | tf_op jit(solution)/shard_map/ppermute | solution.py:18
  201.8 20.5 %collective-permute-start.11 = (bf16[64,16,128]{2,1,0:T(8,128)(2,1)S(1)}, bf16[64,16,128]{2,1,0:T(8,128)(2,1)}, u32[]{:S(2)}, u32[]{:S(2)}) collective-permute-start(bf16[64,16,128]{2,1,0:T(8,128)(2,1)S(1)} %bitcast.181), channel_id=1, source_target_pairs={{0,3},{1,2},{2,1},{3,0},{16,19},{17,18},{18,17},{19,16},{4,7},{5,6... | collective-permute-start | bytes 786440 | tf_op jit(solution)/shard_map/ppermute | solution.py:18
  206.5 21.5 %collective-permute-start.12 = (bf16[64,16,128]{2,1,0:T(8,128)(2,1)S(1)}, bf16[64,16,128]{2,1,0:T(8,128)(2,1)}, u32[]{:S(2)}, u32[]{:S(2)}) collective-permute-start(bf16[64,16,128]{2,1,0:T(8,128)(2,1)S(1)} %bitcast.179), channel_id=1, source_target_pairs={{0,16},{1,17},{2,18},{3,19},{16,0},{17,1},{18,2},{19,3},{4,20},{5,... | collective-permute-start | bytes 786440 | tf_op jit(solution)/shard_map/ppermute | solution.py:18
  222.2 20.7 %collective-permute-start.19 = (bf16[64,16,128]{2,1,0:T(8,128)(2,1)}, bf16[64,16,128]{2,1,0:T(8,128)(2,1)}, u32[]{:S(2)}, u32[]{:S(2)}) collective-permute-start(bf16[64,16,128]{2,1,0:T(8,128)(2,1)} %bitcast.65), channel_id=1, source_target_pairs={{0,1},{1,0},{2,3},{3,2},{16,17},{17,16},{18,19},{19,18},{4,5},{5,4... | collective-permute-start | bytes 786440 | tf_op jit(solution)/shard_map/ppermute | solution.py:18
  222.2 24.5 %collective-permute-start.20 = (bf16[64,16,128]{2,1,0:T(8,128)(2,1)}, bf16[64,16,128]{2,1,0:T(8,128)(2,1)}, u32[]{:S(2)}, u32[]{:S(2)}) collective-permute-start(bf16[64,16,128]{2,1,0:T(8,128)(2,1)} %bitcast.67), channel_id=1, source_target_pairs={{0,2},{1,3},{2,0},{3,1},{16,18},{17,19},{18,16},{19,17},{4,6},{5,7... | collective-permute-start | bytes 786440 | tf_op jit(solution)/shard_map/ppermute | solution.py:18
  228.0 19.1 %collective-permute-start.21 = (bf16[64,16,128]{2,1,0:T(8,128)(2,1)}, bf16[64,16,128]{2,1,0:T(8,128)(2,1)}, u32[]{:S(2)}, u32[]{:S(2)}) collective-permute-start(bf16[64,16,128]{2,1,0:T(8,128)(2,1)} %bitcast.69), channel_id=1, source_target_pairs={{0,3},{1,2},{2,1},{3,0},{16,19},{17,18},{18,17},{19,16},{4,7},{5,6... | collective-permute-start | bytes 786440 | tf_op jit(solution)/shard_map/ppermute | solution.py:18
  232.7 72.5 %all-to-all-start = ((bf16[64,8,1024]{2,1,0:T(8,128)(2,1)}), bf16[64,8,1024]{2,1,0:T(8,128)(2,1)S(1)}, u32[]{:S(2)}, u32[]{:S(2)}) async-start(bf16[64,8,1024]{2,1,0:T(8,128)(2,1)} %join.3), calls=%async_computation | async-start | bytes 2097152 | tf_op jit(solution)/shard_map/all_to_all | solution.py:336
  237.3 12.8 %collective-permute-start.22 = (bf16[64,16,128]{2,1,0:T(8,128)(2,1)S(1)}, bf16[64,16,128]{2,1,0:T(8,128)(2,1)}, u32[]{:S(2)}, u32[]{:S(2)}) collective-permute-start(bf16[64,16,128]{2,1,0:T(8,128)(2,1)S(1)} %bitcast.183), channel_id=1, source_target_pairs={{0,16},{1,17},{2,18},{3,19},{16,0},{17,1},{18,2},{19,3},{4,20},{5,... | collective-permute-start | bytes 786440 | tf_op jit(solution)/shard_map/ppermute | solution.py:18
  242.9 11.0 %collective-permute-start.23 = (bf16[64,16,128]{2,1,0:T(8,128)(2,1)S(1)}, bf16[64,16,128]{2,1,0:T(8,128)(2,1)S(1)}, u32[]{:S(2)}, u32[]{:S(2)}) collective-permute-start(bf16[64,16,128]{2,1,0:T(8,128)(2,1)S(1)} %bitcast.182), channel_id=1, source_target_pairs={{0,17},{1,16},{2,19},{3,18},{16,1},{17,0},{18,3},{19,2},{4,21},{5,... | collective-permute-start | bytes 786440 | tf_op jit(solution)/shard_map/ppermute | solution.py:18
  246.7 23.2 %collective-permute-start.24 = (bf16[64,16,128]{2,1,0:T(8,128)(2,1)S(1)}, bf16[64,16,128]{2,1,0:T(8,128)(2,1)S(1)}, u32[]{:S(2)}, u32[]{:S(2)}) collective-permute-start(bf16[64,16,128]{2,1,0:T(8,128)(2,1)S(1)} %bitcast.180), channel_id=1, source_target_pairs={{0,18},{1,19},{2,16},{3,17},{16,2},{17,3},{18,0},{19,1},{4,22},{5,... | collective-permute-start | bytes 786440 | tf_op jit(solution)/shard_map/ppermute | solution.py:18
  247.1 23.6 %collective-permute-start.25 = (bf16[64,16,128]{2,1,0:T(8,128)(2,1)S(1)}, bf16[64,16,128]{2,1,0:T(8,128)(2,1)S(1)}, u32[]{:S(2)}, u32[]{:S(2)}) collective-permute-start(bf16[64,16,128]{2,1,0:T(8,128)(2,1)S(1)} %bitcast.177), channel_id=1, source_target_pairs={{0,19},{1,18},{2,17},{3,16},{16,3},{17,2},{18,1},{19,0},{4,23},{5,... | collective-permute-start | bytes 786440 | tf_op jit(solution)/shard_map/ppermute | solution.py:18
  250.1 56.7 %collective-permute-start.42 = (f32[1,96,1024]{2,1,0:T(8,128)}, f32[1,96,1024]{2,1,0:T(8,128)}, u32[]{:S(2)}, u32[]{:S(2)}) collective-permute-start(f32[1,96,1024]{2,1,0:T(8,128)} %get-tuple-element.103), channel_id=1, source_target_pairs={{0,8},{4,12},{8,0},{12,4},{1,9},{5,13},{9,1},{13,5},{2,10},{6,14},... | collective-permute-start | bytes 1179656 | tf_op jit(solution)/shard_map/ppermute | solution.py:18
  253.9 28.1 %collective-permute-start.13 = (bf16[64,16,128]{2,1,0:T(8,128)(2,1)}, bf16[64,16,128]{2,1,0:T(8,128)(2,1)}, u32[]{:S(2)}, u32[]{:S(2)}) collective-permute-start(bf16[64,16,128]{2,1,0:T(8,128)(2,1)} %bitcast.55), channel_id=1, source_target_pairs={{0,17},{1,16},{2,19},{3,18},{16,1},{17,0},{18,3},{19,2},{4,21},{5,... | collective-permute-start | bytes 786440 | tf_op jit(solution)/shard_map/ppermute | solution.py:18
  269.9 23.0 %collective-permute-start.14 = (bf16[64,16,128]{2,1,0:T(8,128)(2,1)}, bf16[64,16,128]{2,1,0:T(8,128)(2,1)}, u32[]{:S(2)}, u32[]{:S(2)}) collective-permute-start(bf16[64,16,128]{2,1,0:T(8,128)(2,1)} %bitcast.57), channel_id=1, source_target_pairs={{0,18},{1,19},{2,16},{3,17},{16,2},{17,3},{18,0},{19,1},{4,22},{5,... | collective-permute-start | bytes 786440 | tf_op jit(solution)/shard_map/ppermute | solution.py:18
  270.7 22.3 %collective-permute-start.15 = (bf16[64,16,128]{2,1,0:T(8,128)(2,1)}, bf16[64,16,128]{2,1,0:T(8,128)(2,1)}, u32[]{:S(2)}, u32[]{:S(2)}) collective-permute-start(bf16[64,16,128]{2,1,0:T(8,128)(2,1)} %bitcast.59), channel_id=1, source_target_pairs={{0,19},{1,18},{2,17},{3,16},{16,3},{17,2},{18,1},{19,0},{4,23},{5,... | collective-permute-start | bytes 786440 | tf_op jit(solution)/shard_map/ppermute | solution.py:18
  296.7 10.1 %collective-permute-start.26 = (f32[96,256]{1,0:T(8,128)}, f32[96,256]{1,0:T(8,128)S(1)}, u32[]{:S(2)}, u32[]{:S(2)}) collective-permute-start(f32[96,256]{1,0:T(8,128)} %get-tuple-element.40), channel_id=1, source_target_pairs={{0,4},{4,0},{8,12},{12,8},{1,5},{5,1},{9,13},{13,9},{2,6},{6,2},{1... | collective-permute-start | bytes 294920 | tf_op jit(solution)/shard_map/ppermute | solution.py:18
  296.7 10.1 %collective-permute-start.27 = (f32[96,256]{1,0:T(8,128)}, f32[96,256]{1,0:T(8,128)S(1)}, u32[]{:S(2)}, u32[]{:S(2)}) collective-permute-start(f32[96,256]{1,0:T(8,128)} %get-tuple-element.41), channel_id=1, source_target_pairs={{0,8},{4,12},{8,0},{12,4},{1,9},{5,13},{9,1},{13,5},{2,10},{6,14},... | collective-permute-start | bytes 294920 | tf_op jit(solution)/shard_map/ppermute | solution.py:18
  297.8 9.0 %collective-permute-start.28 = (f32[96,256]{1,0:T(8,128)}, f32[96,256]{1,0:T(8,128)S(1)}, u32[]{:S(2)}, u32[]{:S(2)}) collective-permute-start(f32[96,256]{1,0:T(8,128)} %get-tuple-element.42), channel_id=1, source_target_pairs={{0,12},{4,8},{8,4},{12,0},{1,13},{5,9},{9,5},{13,1},{2,14},{6,10},... | collective-permute-start | bytes 294920 | tf_op jit(solution)/shard_map/ppermute | solution.py:18
  (61 other events, 550.5 us)
where the time goes:
time: 317 us; the launch traced here: 313 us
  waiting for transfers between devices  105 us (33%)
  starting transfers between devices  98.5 us (31%)
  local copies, waits for them, and re-layouts  46.9 us (15%)
  Pallas kernels  28.1 us (9%)
  matrix products  21.4 us (7%)
  other arithmetic  11.7 us (4%)
    ppermute x53, waiting for transfers between devices, swap(): return lax.ppermute(x, axes, [(a, a ^ shift) for a in range(total)])  105 us
    ppermute x53, starting transfers between devices, swap(): return lax.ppermute(x, axes, [(a, a ^ shift) for a in range(total)])  90.7 us
    unnamed x139, local copies, waits for them, and re-layouts  26.5 us
    dot_general x1, matrix products, local(): base_query = jnp.dot(turned, w_query, preferred_element_type=jnp.float32)  10.2 us
    all_to_all x2, starting transfers between devices, own_block(): lax.all_to_all(factors, 'tensor', split_axis=0, concat_axis=0, tiled=True)  7.88 us
    pallas_call x2, Pallas kernels, project(): pl.pallas_call(functools.partial(project_kernel, shifts, parts, stride, s...  7.3 us
    pallas_call x3, Pallas kernels, cut(): pl.pallas_call(functools.partial(cut_kernel, shifts, stride, start, width...  7 us
    pallas_call x3, Pallas kernels, join(): pl.pallas_call(functools.partial(join_kernel, shifts, stride, start, widt...  6.88 us
  transfers between devices with their start and end apart: 55, of which 9 were waited for; matrix products, arithmetic and copies ran while one was open for 24% of the time, Pallas kernels for 7%

commit v1 on v0

--- a/solution.py
+++ b/solution.py
@@ -147,15 +147,39 @@
         return whole.reshape(whole.shape[0], self.rank, self.columns)
 
 
-def project_kernel(shifts, parts, stride, start, width, tokens, inside, *refs):
-    pieces, refs = refs[: len(shifts)], refs[len(shifts) :]
+def rank_columns(shape, rank_axis, column_axis, rank):
+    of_column = lax.broadcasted_iota(jnp.int32, shape, column_axis) % rank
+    return of_column == lax.broadcasted_iota(jnp.int32, shape, rank_axis)
+
+
+def inside(bounds, rows):
+    row = lax.broadcasted_iota(jnp.int32, (rows, bounds.shape[1]), 0)
+    return (row >= bounds[0:1]) & (row < bounds[1:2])
+
+
+def turned(x, square):
+    square[...] = jnp.zeros(square.shape, square.dtype)
+    square[0 : x.shape[0], 0 : x.shape[1]] = x
+    return square[...].T
+
+
+def terms(x, count):
+    parts = []
+    for _ in range(count):
+        parts.append(x.astype(jnp.bfloat16))
+        x = x - parts[-1].astype(jnp.float32)
+    return jnp.concatenate(parts)
+
+
+def project_kernel(shifts, parts, stride, start, width, tokens, bounds, *refs):
+    pieces, refs, square = refs[: len(shifts)], refs[len(shifts) : -1], refs[-1]
     before, after = refs[:-parts], refs[-parts:]
     rows = tokens.shape[0] // parts
-    tasks = pieces[0].shape[0] // parts
+    tasks, rank = pieces[0].shape[0] // parts, pieces[0].shape[1]
+    every = []
     for turn in range(parts):
         block = lax.axis_index("tensor") ^ turn
-        total = before[turn][...] if before else None
-        found = jnp.zeros(after[turn].shape, jnp.float32)
+        found = jnp.zeros((rows, tasks * rank), jnp.float32)
         for k, shift in enumerate(shifts):
             column = pl.multiple_of((place() ^ shift) * stride + start, LANES)
             found += lax.dot_general(
@@ -164,34 +188,54 @@
                 (((1,), (1,)), ((), ())),
                 preferred_element_type=jnp.float32,
             )
-        found = found * inside[block]
-        after[turn][...] = found if total is None else total + found
-
-
-def project(pieces, shifts, stride, start, width, tokens, inside, before):
-    parts = inside.shape[0]
+        every.append(jnp.where(inside(bounds[block], rows), found, 0.0))
+    pick = rank_columns((tasks * rank, LANES), 1, 0, rank).astype(jnp.bfloat16)
+    count = 3
+    summed = jnp.dot(
+        terms(jnp.concatenate(every), count), pick, preferred_element_type=jnp.float32
+    ).reshape(count, parts, rows, LANES)
+    for turn in range(parts):
+        low_rank = turned(sum(summed[k, turn] for k in range(count)), square)[0:rank, 0:rows]
+        after[turn][...] = low_rank + before[turn][...] if before else low_rank
+
+
+def project(pieces, shifts, stride, start, width, tokens, bounds, before):
+    parts, rank = bounds.shape[0], pieces[0].shape[1]
+    rows = tokens.shape[0] // parts
     return pl.pallas_call(
         functools.partial(project_kernel, shifts, parts, stride, start, width),
-        out_shape=[jax.ShapeDtypeStruct(inside.shape[1:], jnp.float32)] * parts,
+        out_shape=[jax.ShapeDtypeStruct((rank, rows), jnp.float32)] * parts,
+        scratch_shapes=[pltpu.VMEM((LANES, LANES), jnp.float32)],
         name="project",
-    )(tokens, inside, *pieces, *before)
-
-
-def finish_kernel(count, *refs):
-    low_rank = refs[0][...]
-    for k in range(1, count):
-        low_rank = low_rank + refs[k][...]
-    high = low_rank.astype(jnp.bfloat16)
-    low = (low_rank - high.astype(jnp.float32)).astype(jnp.bfloat16)
-    refs = refs[count:]
-    for kept, came, up, out in (refs[0:3] + refs[6:7], refs[3:6] + refs[7:8]):
-        update = jnp.dot(high, up[...], preferred_element_type=jnp.float32)
-        update = update + jnp.dot(low, up[...], preferred_element_type=jnp.float32)
-        out[...] = (kept[...] + came[...] + ADAPTER_SCALE * update).astype(out.dtype)
-
-
-def finish(shares, query, value, steps):
-    rows = query[0].shape[0]
+    )(tokens, bounds, *pieces, *before)
+
+
+def finish_kernel(count, bounds, *refs):
+    shares, rest = refs[:count], refs[count:]
+    base_query, base_value, up_query, up_value, query, value, square, spread = rest
+    rank, rows = shares[0].shape
+
+    @pl.when(pl.program_id(0) == 0)
+    def _():
+        low_rank = shares[0][...]
+        for share in shares[1:]:
+            low_rank = low_rank + share[...]
+        low_rank = turned(low_rank, square)[0:rows]
+        own = bounds[lax.axis_index("tensor")]
+        pick = rank_columns((LANES, own.shape[1]), 0, 1, rank).astype(jnp.bfloat16)
+        each = jnp.dot(terms(low_rank, 2), pick, preferred_element_type=jnp.float32)
+        own = inside(own, rows)
+        each = jnp.where(jnp.concatenate([own, own]), each, 0.0)
+        spread[...] = each.astype(jnp.bfloat16)
+
+    for base, up, out in ((base_query, up_query, query), (base_value, up_value, value)):
+        update = jnp.dot(spread[...], up[...], preferred_element_type=jnp.float32)
+        update = update[0:rows] + update[rows:]
+        out[...] = (base[...] + ADAPTER_SCALE * update).astype(out.dtype)
+
+
+def finish(shares, bounds, operands, steps):
+    rows = operands[0].shape[0]
 
     def columns(x):
         return pl.BlockSpec((x.shape[0], x.shape[1] // steps), lambda i: (0, i))
@@ -199,15 +243,17 @@
     return pl.pallas_call(
         functools.partial(finish_kernel, len(shares)),
         grid=(steps,),
-        in_specs=[pl.BlockSpec(x.shape, lambda i: (0, 0)) for x in shares]
-        + [columns(x) for x in query + value],
-        out_specs=[columns(query[0]), columns(value[0])],
-        out_shape=[
-            jax.ShapeDtypeStruct((rows, query[0].shape[1]), jnp.bfloat16),
-            jax.ShapeDtypeStruct((rows, value[0].shape[1]), jnp.bfloat16),
+        in_specs=[pl.BlockSpec(bounds.shape, lambda i: (0, 0, 0))]
+        + [pl.BlockSpec(x.shape, lambda i: (0, 0)) for x in shares]
+        + [columns(x) for x in operands],
+        out_specs=[columns(x) for x in operands[:2]],
+        out_shape=[jax.ShapeDtypeStruct(x.shape, jnp.bfloat16) for x in operands[:2]],
+        scratch_shapes=[
+            pltpu.VMEM((LANES, LANES), jnp.float32),
+            pltpu.VMEM((2 * rows, bounds.shape[2]), jnp.bfloat16),
         ],
         name="finish",
-    )(*shares, *query, *value)
+    )(bounds, *shares, *operands)
 
 
 def halving_order(total):
@@ -217,15 +263,13 @@
 
 def reduce_blocks(partial, axis):
     step = 1
-    came = jnp.zeros_like(partial)
-    while partial.shape[0] > 1:
+    while True:
         half = partial.shape[0] // 2
         came = swap(partial[half:], axis, step)
-        partial = partial[:half]
+        if half == 1:
+            return partial[0] + came[0]
+        partial = partial[:half] + came
         step *= 2
-        if half > 1:
-            partial = partial + came
-    return partial[0], came[0]
 
 
 def gather_blocks(x, axis):
@@ -312,15 +356,21 @@
         flat = jnp.dot(
             every_hidden, matrix.reshape(matrix.shape[0], -1), preferred_element_type=jnp.float32
         ).astype(jnp.bfloat16)
-        made = flat.reshape((places, own_tasks) + matrix.shape[1:])
-        got = {0: made[0]}
-        for s in reversed(shifts[1:]):
-            got[s] = swap(made[s], PLACES, s)
-        return [got[s] for s in shifts]
-
+        return flat.reshape((places, own_tasks) + matrix.shape[1:])
+
+    def send(made, sent):
+        return {s: swap(made[s], PLACES, s) if s else made[s] for s in sent}
+
+    late = [s for s in far_first if s >= ring // 2]
+    early = [s for s in reversed(shifts) if s not in late]
     emitted = {}
     for name, chunk in [("query", 0), ("value", 0)] + [("down", c) for c in range(chunks)]:
-        emitted[name, chunk] = emit(name, chunk)
+        made = emit(name, chunk)
+        emitted[name, chunk] = send(made, early)
+        emitted[name, chunk].update(send(made, late))
+
+    def ordered(pieces):
+        return [pieces[s] for s in shifts]
 
     token_blocks = tokens.reshape(parts, block_rows, shard_width)
     order = halving_order(parts)
@@ -339,44 +389,44 @@
         moved = jnp.pad(moved, ((0, 0), (above, below), (0, 0)))
         return moved.reshape(block_tasks * 2 * rank, -1)
 
-    query_up_factors = heads["query"].join(emitted["query", 0], shifts)
+    query_up_factors = heads["query"].join(ordered(emitted["query", 0]), shifts)
     own_query = own_block(query_up_factors, 0, rank)
-    value_up_factors = heads["value"].join(emitted["value", 0], shifts)
+    value_up_factors = heads["value"].join(ordered(emitted["value", 0]), shifts)
     own_value = own_block(value_up_factors, rank, 0)
 
     tallies = task_counts.reshape(parts, block_tasks)
     ends = jnp.cumsum(tallies, axis=1)
-    starts = ends - tallies
-    positions = jnp.arange(block_rows, dtype=jnp.int32)
-    inside = (
-        (positions[None, :, None] >= starts[:, None, :])
-        & (positions[None, :, None] < ends[:, None, :])
-    ).astype(jnp.float32)
-    inside = jnp.repeat(inside, 2 * rank, axis=2)
-
-    down_factors, spread = None, []
-    for chunk in range(chunks):
-        head, pieces = heads["down"], emitted["down", chunk]
-        if head.by_lane:
-            start = chunk * head.width
-            spread = project(pieces, shifts, head.stride, start, head.width, tokens, inside, spread)
-        down_factors = head.join(pieces, shifts, chunk, down_factors)
-    if not spread:
+    bounds = jnp.stack([ends - tallies, ends], axis=1)
+    bounds = jnp.repeat(bounds, 2 * rank, axis=2)
+
+    down_factors, low_rank = None, []
+    head = heads["down"]
+    if head.by_lane:
+        for chunk in range(chunks):
+            pieces, start = emitted["down", chunk], chunk * head.width
+            for half in [early, late] if chunk + 1 == chunks else [early + late]:
+                some = [pieces[s] for s in half]
+                low_rank = project(
+                    some, half, head.stride, start, head.width, tokens, bounds, low_rank
+                )
+                down_factors = head.join(some, half, chunk, down_factors)
+    else:
+        down_factors = head.join(ordered(emitted["down", 0]), shifts)
         projected = jnp.einsum(
             "bpd,bmd->bpm",
             token_blocks,
             down_factors.reshape(parts, block_tasks * 2 * rank, shard_width),
             preferred_element_type=jnp.float32,
         )
-        projected = projected * inside
-        spread = [
+        projected = jnp.where(jax.vmap(lambda b: inside(b, block_rows))(bounds), projected, 0.0)
+        projected = projected.reshape(parts, block_rows, block_tasks, 2 * rank).sum(axis=2)
+        projected = projected.transpose(0, 2, 1)
+        low_rank = [
             lax.dynamic_index_in_dim(projected, tensor ^ s, 0, keepdims=False)
             for s in range(parts)
         ]
-    shares = [spread[0]] + [swap(spread[s], "tensor", s) for s in range(1, parts)]
-    query, value = finish(
-        shares, [*base_query, own_query], [*base_value, own_value], steps=4
-    )
+    shares = [low_rank[0]] + [swap(low_rank[s], "tensor", s) for s in range(1, parts)]
+    query, value = finish(shares, bounds, [base_query, base_value, own_query, own_value], steps=4)
     return query, value, down_factors, query_up_factors, value_up_factors
 
 

time: 317 us -> 329 us (1.038)
  waiting for transfers between devices: 105 us -> 121 us
  local copies, waits for them, and re-layouts: 46.9 us -> 37 us
  other arithmetic: 11.7 us -> 16.6 us
  Pallas kernels: 28.1 us -> 31.8 us
    ppermute x53, waiting for transfers between devices: 105 us -> 121 us  [swap(): return lax.ppermute(x, axes, [(a, a ^ shift) for a in range(total)])]
    unnamed x139 -> x133, local copies, waits for them, and re-layouts: 26.5 us -> 18.5 us
    add x2 -> x4, other arithmetic: 3.51 us -> 8.17 us  [the longest x2 4.65 us: reduce_blocks(): return partial[0] + came[0]]
    pallas_call x2 -> x3, Pallas kernels: 7.3 us -> 10 us  [project(): pl.pallas_call(functools.partial(project_kernel, shifts, parts, stride, s...]
    pallas_call x3 -> x4, Pallas kernels: 6.88 us -> 8.51 us  [join(): pl.pallas_call(functools.partial(join_kernel, shifts, stride, start, widt...]
  transfers between devices with their start and end apart: 55 -> 55, of which waited for: 9 -> 12; matrix products, arithmetic and copies ran while one was open for 24% -> 20% of each run, Pallas kernels for 7% -> 8%
where the time goes in v1:
time: 329 us; the launch traced here: 328 us
  waiting for transfers between devices  121 us (37%)
  starting transfers between devices  98.6 us (30%)
  local copies, waits for them, and re-layouts  37 us (11%)
  Pallas kernels  31.8 us (10%)
  matrix products  20.6 us (6%)
  other arithmetic  16.6 us (5%)
    ppermute x53, waiting for transfers between devices, swap(): return lax.ppermute(x, axes, [(a, a ^ shift) for a in range(total)])  121 us
    ppermute x53, starting transfers between devices, swap(): return lax.ppermute(x, axes, [(a, a ^ shift) for a in range(total)])  91.5 us
    unnamed x133, local copies, waits for them, and re-layouts  18.5 us
    dot_general x1, matrix products, local(): base_query = jnp.dot(turned, w_query, preferred_element_type=jnp.float32)  10.8 us
    pallas_call x3, Pallas kernels, project(): pl.pallas_call(functools.partial(project_kernel, shifts, parts, stride, s...  10 us
    pallas_call x4, Pallas kernels, join(): pl.pallas_call(functools.partial(join_kernel, shifts, stride, start, widt...  8.51 us
    all_to_all x2, starting transfers between devices, own_block(): lax.all_to_all(factors, 'tensor', split_axis=0, concat_axis=0, tiled=True)  7.16 us
    pallas_call x3, Pallas kernels, cut(): pl.pallas_call(functools.partial(cut_kernel, shifts, stride, start, width...  6.95 us
  transfers between devices with their start and end apart: 55, of which 12 were waited for; matrix products, arithmetic and copies ran while one was open for 20% of the time, Pallas kernels for 8%

profile of v1, /device:TPU:0, one launch (start us, length us, event | category | flops | bytes accessed | tf_op | source)
XLA Modules:
  0.0 327.5 jit_solution(8540359396793177968)
XLA Ops:
  2.9 3.1 collective-permute-start
  7.4 10.8 %fusion.9 = f32[384,4096]{1,0:T(8,128)S(1)} fusion(bf16[2048,4096]{1,0:T(8,128)(2,1)} %param.16, bf16[96,2048]{1,0:T(8,128)(2,1)S(1)} %get-tuple-element.98, bf16[96,2048]{1,0:T(8,128)(2,1)S(1)} %get-tuple-element.99, bf16[96,2048]{1,0:T(8,128)(2,1)S(1)} %get-tuple-element.100, bf16[96,2048]{1,0:T(8,128)(2,1)S(1)} %get-tuple-element.97), kind=kOutput, calls=%fused_computation.25 | convolution fusion | flops 6448742400 | bytes 24641536 | tf_op jit(solution)/shard_map/dot_general | solution.py:380
  18.3 2.2 fusion.27
  20.5 2.0 cut.5
  22.6 3.7 %collective-permute-start.35 = (bf16[128,8,128]{2,1,0:T(8,128)(2,1)}, bf16[128,8,128]{2,1,0:T(8,128)(2,1)}, u32[]{:S(2)}, u32[]{:S(2)}) collective-permute-start(bf16[128,8,128]{2,1,0:T(8,128)(2,1)} %get-tuple-element.54), channel_id=1, source_target_pairs={{0,3},{1,2},{2,1},{3,0},{4,7},{5,6},{6,5},{7,4},{8,11},{9,10},{10,... | collective-permute-start | bytes 786440 | tf_op jit(solution)/shard_map/ppermute | solution.py:18
  28.0 3.4 %collective-permute-start.1 = (bf16[32,512]{1,0:T(8,128)(2,1)S(1)}, bf16[32,512]{1,0:T(8,128)(2,1)S(1)}, u32[]{:S(2)}, u32[]{:S(2)}) collective-permute-start(bf16[32,512]{1,0:T(8,128)(2,1)S(1)} %get-tuple-element.130), channel_id=1, source_target_pairs={{0,1},{1,0},{2,3},{3,2},{4,5},{5,4},{6,7},{7,6},{8,9},{9,8},{10,11... | collective-permute-start | bytes 98312 | tf_op jit(solution)/shard_map/ppermute | solution.py:18
  31.3 4.3 %fusion.8 = f32[384,1024]{1,0:T(8,128)S(1)} fusion(bf16[2048,1024]{1,0:T(8,128)(2,1)} %param.17, bf16[96,2048]{1,0:T(8,128)(2,1)} %copy-done.24, bf16[96,2048]{1,0:T(8,128)(2,1)} %copy-done.25, bf16[96,2048]{1,0:T(8,128)(2,1)} %copy-done.26, bf16[96,2048]{1,0:T(8,128)(2,1)S(1)} %get-tuple-element.97), kind=kOutput, calls=%fused_computation.24 | convolution fusion | flops 1616904192 | bytes 7340032 | tf_op jit(solution)/shard_map/dot_general | solution.py:381
  35.7 6.5 %collective-permute-start.34 = (bf16[128,8,128]{2,1,0:T(8,128)(2,1)}, bf16[128,8,128]{2,1,0:T(8,128)(2,1)}, u32[]{:S(2)}, u32[]{:S(2)}) collective-permute-start(bf16[128,8,128]{2,1,0:T(8,128)(2,1)} %get-tuple-element.53), channel_id=1, source_target_pairs={{0,2},{1,3},{2,0},{3,1},{4,6},{5,7},{6,4},{7,5},{8,10},{9,11},{10,... | collective-permute-start | bytes 786440 | tf_op jit(solution)/shard_map/ppermute | solution.py:18
  43.6 2.5 cut.3
  46.1 2.5 cut.4
  52.4 2.2 constant_dynamic-slice_fusion.3
  57.5 2.4 collective-permute-start.45
  60.0 2.3 pad_maximum_fusion.3
  69.3 5.1 %collective-permute-done.45 = bf16[128,256]{1,0:T(8,128)(2,1)} collective-permute-done((bf16[128,256]{1,0:T(8,128)(2,1)}, bf16[128,256]{1,0:T(8,128)(2,1)}, u32[]{:S(2)}, u32[]{:S(2)}) %collective-permute-start.45) | collective-permute-done | bytes 65568 | tf_op jit(solution)/shard_map/ppermute | solution.py:18
  74.4 13.8 %collective-permute-start.7 = (bf16[128,16,128]{2,1,0:T(8,128)(2,1)S(1)}, bf16[128,16,128]{2,1,0:T(8,128)(2,1)S(1)}, u32[]{:S(2)}, u32[]{:S(2)}) collective-permute-start(bf16[128,16,128]{2,1,0:T(8,128)(2,1)S(1)} %copy-done.50), channel_id=1, source_target_pairs={{0,2},{1,3},{2,0},{3,1},{4,6},{5,7},{6,4},{7,5},{8,10},{9,11},{10,... | collective-permute-start | bytes 1572872 | tf_op jit(solution)/shard_map/ppermute | solution.py:18
  91.0 2.0 collective-permute-start.46
  94.0 18.2 %collective-permute-done.46.refs_1_ = bf16[64,256]{1,0:T(8,128)(2,1)S(1)} collective-permute-done((bf16[64,256]{1,0:T(8,128)(2,1)S(1)}, bf16[64,256]{1,0:T(8,128)(2,1)S(1)}, u32[]{:S(2)}, u32[]{:S(2)}) %collective-permute-start.46) | collective-permute-done | bytes 32800 | tf_op jit(solution)/shard_map/ppermute | solution.py:18
  112.2 2.1 collective-permute-start.47
  118.6 2.2 collective-permute-start.18
  123.2 5.7 %collective-permute-done.50.refs_5_ = bf16[64,256]{1,0:T(8,128)(2,1)S(1)} collective-permute-done((bf16[64,256]{1,0:T(8,128)(2,1)S(1)}, bf16[64,256]{1,0:T(8,128)(2,1)S(1)}, u32[]{:S(2)}, u32[]{:S(2)}) %collective-permute-start.50) | collective-permute-done | bytes 32800 | tf_op jit(solution)/shard_map/ppermute | solution.py:18
  130.8 35.4 %collective-permute-done.51.refs_6_ = bf16[64,256]{1,0:T(8,128)(2,1)S(1)} collective-permute-done((bf16[64,256]{1,0:T(8,128)(2,1)S(1)}, bf16[64,256]{1,0:T(8,128)(2,1)S(1)}, u32[]{:S(2)}, u32[]{:S(2)}) %collective-permute-start.51) | collective-permute-done | bytes 32800 | tf_op jit(solution)/shard_map/ppermute | solution.py:18
  166.2 3.1 collective-permute-start.52
  170.5 2.4 collective-permute-done.52.refs_7_
  173.5 3.0 collective-permute-start.37
  179.7 2.2 add.80
  184.8 2.2 collective-permute-start.41
  188.7 3.1 collective-permute-start.11
  193.8 12.8 %collective-permute-done.41.refs_6_ = bf16[64,8,128]{2,1,0:T(8,128)(2,1)S(1)} collective-permute-done((bf16[64,8,128]{2,1,0:T(8,128)(2,1)S(1)}, bf16[64,8,128]{2,1,0:T(8,128)(2,1)S(1)}, u32[]{:S(2)}, u32[]{:S(2)}) %collective-permute-start.41) | collective-permute-done | bytes 131104 | tf_op jit(solution)/shard_map/ppermute | solution.py:18
  206.6 4.9 %collective-permute-start.13 = (bf16[64,16,128]{2,1,0:T(8,128)(2,1)S(1)}, bf16[64,16,128]{2,1,0:T(8,128)(2,1)S(1)}, u32[]{:S(2)}, u32[]{:S(2)}) collective-permute-start(bf16[64,16,128]{2,1,0:T(8,128)(2,1)S(1)} %bitcast.182), channel_id=1, source_target_pairs={{0,17},{1,16},{2,19},{3,18},{16,1},{17,0},{18,3},{19,2},{4,21},{5,... | collective-permute-start | bytes 786440 | tf_op jit(solution)/shard_map/ppermute | solution.py:18
  212.6 14.0 %collective-permute-done.12.refs_1_ = bf16[64,16,128]{2,1,0:T(8,128)(2,1)S(1)} collective-permute-done((bf16[64,16,128]{2,1,0:T(8,128)(2,1)S(1)}, bf16[64,16,128]{2,1,0:T(8,128)(2,1)S(1)}, u32[]{:S(2)}, u32[]{:S(2)}) %collective-permute-start.12) | collective-permute-done | bytes 262176 | tf_op jit(solution)/shard_map/ppermute | solution.py:18
  228.3 4.1 %collective-permute-start.21 = (bf16[64,16,128]{2,1,0:T(8,128)(2,1)S(1)}, bf16[64,16,128]{2,1,0:T(8,128)(2,1)S(1)}, u32[]{:S(2)}, u32[]{:S(2)}) collective-permute-start(bf16[64,16,128]{2,1,0:T(8,128)(2,1)S(1)} %bitcast.179), channel_id=1, source_target_pairs={{0,17},{1,16},{2,19},{3,18},{16,1},{17,0},{18,3},{19,2},{4,21},{5,... | collective-permute-start | bytes 786440 | tf_op jit(solution)/shard_map/ppermute | solution.py:18
  235.9 3.6 %all-to-all-start.1 = ((bf16[64,8,256]{2,1,0:T(8,128)(2,1)}), bf16[64,8,256]{2,1,0:T(8,128)(2,1)S(1)}, u32[]{:S(2)}, u32[]{:S(2)}) async-start(bf16[64,8,256]{2,1,0:T(8,128)(2,1)} %copy.44), calls=%async_computation.1 | async-start | bytes 524288 | tf_op jit(solution)/shard_map/all_to_all | solution.py:386
  244.2 5.2 %collective-permute-done.20.refs_1_ = bf16[64,16,128]{2,1,0:T(8,128)(2,1)S(1)} collective-permute-done((bf16[64,16,128]{2,1,0:T(8,128)(2,1)S(1)}, bf16[64,16,128]{2,1,0:T(8,128)(2,1)S(1)}, u32[]{:S(2)}, u32[]{:S(2)}) %collective-permute-start.20) | collective-permute-done | bytes 262176 | tf_op jit(solution)/shard_map/ppermute | solution.py:18
  249.4 2.4 collective-permute-start.23
  251.8 2.0 collective-permute-start.24
  254.4 2.2 join.4
  256.6 3.5 %all-to-all-start = ((bf16[64,8,1024]{2,1,0:T(8,128)(2,1)}), bf16[64,8,1024]{2,1,0:T(8,128)(2,1)S(1)}, u32[]{:S(2)}, u32[]{:S(2)}) async-start(bf16[64,8,1024]{2,1,0:T(8,128)(2,1)} %join.4), calls=%async_computation | async-start | bytes 2097152 | tf_op jit(solution)/shard_map/all_to_all | solution.py:386
  262.3 2.0 collective-permute-start.32
  269.7 2.0 collective-permute-start.10
  271.7 15.7 %collective-permute-done.25.refs_7_ = bf16[64,16,128]{2,1,0:T(8,128)(2,1)} collective-permute-done((bf16[64,16,128]{2,1,0:T(8,128)(2,1)}, bf16[64,16,128]{2,1,0:T(8,128)(2,1)}, u32[]{:S(2)}, u32[]{:S(2)}) %collective-permute-start.25) | collective-permute-done | bytes 262176 | tf_op jit(solution)/shard_map/ppermute | solution.py:18
  290.6 3.8 %project.3 = (f32[16,96]{1,0:T(8,128)}, f32[16,96]{1,0:T(8,128)}, f32[16,96]{1,0:T(8,128)}, f32[16,96]{1,0:T(8,128)}) custom-call(bf16[384,2048]{1,0:T(8,128)(2,1)} %tokens.5, s32[4,2,256]{2,1,0:T(2,128)} %reshape.157.bounds, bf16[64,16,128]{2,1,0:T(8,128)(2,1)} %copy-done.5, bf16[64,16,128]{2,1,0:T(8,128)(2,1)} %copy-done.6, ...), custom_call_target="tpu_custom_call" | custom-call | tf_op jit(solution)/shard_map/project/pallas_call | solution.py:205
  294.4 4.2 %collective-permute-done.15.refs_4_ = bf16[64,16,128]{2,1,0:T(8,128)(2,1)S(1)} collective-permute-done((bf16[64,16,128]{2,1,0:T(8,128)(2,1)}, bf16[64,16,128]{2,1,0:T(8,128)(2,1)S(1)}, u32[]{:S(2)}, u32[]{:S(2)}) %collective-permute-start.15) | collective-permute-done | bytes 262176 | tf_op jit(solution)/shard_map/ppermute | solution.py:18
  299.3 3.5 %project.4 = (f32[16,96]{1,0:T(8,128)}, f32[16,96]{1,0:T(8,128)}, f32[16,96]{1,0:T(8,128)}, f32[16,96]{1,0:T(8,128)}) custom-call(bf16[384,2048]{1,0:T(8,128)(2,1)} %tokens.5, s32[4,2,256]{2,1,0:T(2,128)} %reshape.157.bounds, bf16[64,16,128]{2,1,0:T(8,128)(2,1)} %copy-done.8, bf16[64,16,128]{2,1,0:T(8,128)(2,1)} %copy-done.9, ...), custom_call_target="tpu_custom_call" | custom-call | tf_op jit(solution)/shard_map/project/pallas_call | solution.py:205
  303.6 2.8 project.5
  308.2 2.4 join.5.refs_6_
  310.6 2.2 join.6.refs_2_
  319.1 2.9 fusion.4.refs_4_
  322.6 4.7 %finish.1 = (bf16[96,4096]{1,0:T(8,128)(2,1)}, bf16[96,1024]{1,0:T(8,128)(2,1)}) custom-call(s32[4,2,256]{2,1,0:T(2,128)} %reshape.157.bounds, f32[16,96]{1,0:T(8,128)} %get-tuple-element.47.refs_0_, f32[16,96]{1,0:T(8,128)} %copy-done.42, f32[16,96]{1,0:T(8,128)} %copy-done.43, f32[16,96]{1,0:T(8,128)} %copy-done.44, f32[96,4096]{1,0:T(8,128)} %fusion.4.refs_4_, ...), custom_call_target="tpu_custom_call" | custom-call | tf_op jit(solution)/shard_map/finish/pallas_call | solution.py:243
  (250 shorter events, 76.5 us)
Async XLA Ops:
  2.9 23.3 %collective-permute-start = (bf16[16,512]{1,0:T(8,128)(2,1)S(1)}, bf16[16,512]{1,0:T(8,128)(2,1)}, u32[]{:S(2)}, u32[]{:S(2)}) collective-permute-start(bf16[16,512]{1,0:T(8,128)(2,1)S(1)} %multiply_convert_fusion), channel_id=1, source_target_pairs={{0,16},{16,0},{1,17},{17,1},{2,18},{18,2},{3,19},{19,3},{4,20},{20... | collective-permute-start | bytes 49160 | tf_op jit(solution)/shard_map/ppermute | solution.py:18
  20.5 158.9 %collective-permute-start.29 = (f32[2,96,4096]{2,1,0:T(8,128)}, f32[2,96,4096]{2,1,0:T(8,128)}, u32[]{:S(2)}, u32[]{:S(2)}) collective-permute-start(f32[2,96,4096]{2,1,0:T(8,128)} %bitcast.20), channel_id=1, source_target_pairs={{0,4},{4,0},{8,12},{12,8},{1,5},{5,1},{9,13},{13,9},{2,6},{6,2},{1... | collective-permute-start | bytes 9437192 | tf_op jit(solution)/shard_map/ppermute | solution.py:18
  22.6 33.4 %collective-permute-start.35 = (bf16[128,8,128]{2,1,0:T(8,128)(2,1)}, bf16[128,8,128]{2,1,0:T(8,128)(2,1)}, u32[]{:S(2)}, u32[]{:S(2)}) collective-permute-start(bf16[128,8,128]{2,1,0:T(8,128)(2,1)} %get-tuple-element.54), channel_id=1, source_target_pairs={{0,3},{1,2},{2,1},{3,0},{4,7},{5,6},{6,5},{7,4},{8,11},{9,10},{10,... | collective-permute-start | bytes 786440 | tf_op jit(solution)/shard_map/ppermute | solution.py:18
  27.2 15.0 %collective-permute-start.2 = (bf16[32,512]{1,0:T(8,128)(2,1)S(1)}, bf16[32,512]{1,0:T(8,128)(2,1)S(1)}, u32[]{:S(2)}, u32[]{:S(2)}) collective-permute-start(bf16[32,512]{1,0:T(8,128)(2,1)S(1)} %get-tuple-element.130), channel_id=1, source_target_pairs={{0,2},{1,3},{2,0},{3,1},{4,6},{5,7},{6,4},{7,5},{8,10},{9,11},{10,... | collective-permute-start | bytes 98312 | tf_op jit(solution)/shard_map/ppermute | solution.py:18
  28.0 14.3 %collective-permute-start.1 = (bf16[32,512]{1,0:T(8,128)(2,1)S(1)}, bf16[32,512]{1,0:T(8,128)(2,1)S(1)}, u32[]{:S(2)}, u32[]{:S(2)}) collective-permute-start(bf16[32,512]{1,0:T(8,128)(2,1)S(1)} %get-tuple-element.130), channel_id=1, source_target_pairs={{0,1},{1,0},{2,3},{3,2},{4,5},{5,4},{6,7},{7,6},{8,9},{9,8},{10,11... | collective-permute-start | bytes 98312 | tf_op jit(solution)/shard_map/ppermute | solution.py:18
  35.7 21.8 %collective-permute-start.34 = (bf16[128,8,128]{2,1,0:T(8,128)(2,1)}, bf16[128,8,128]{2,1,0:T(8,128)(2,1)}, u32[]{:S(2)}, u32[]{:S(2)}) collective-permute-start(bf16[128,8,128]{2,1,0:T(8,128)(2,1)} %get-tuple-element.53), channel_id=1, source_target_pairs={{0,2},{1,3},{2,0},{3,1},{4,6},{5,7},{6,4},{7,5},{8,10},{9,11},{10,... | collective-permute-start | bytes 786440 | tf_op jit(solution)/shard_map/ppermute | solution.py:18
  42.2 17.6 %collective-permute-start.33 = (bf16[128,8,128]{2,1,0:T(8,128)(2,1)}, bf16[128,8,128]{2,1,0:T(8,128)(2,1)}, u32[]{:S(2)}, u32[]{:S(2)}) collective-permute-start(bf16[128,8,128]{2,1,0:T(8,128)(2,1)} %get-tuple-element.52), channel_id=1, source_target_pairs={{0,1},{1,0},{2,3},{3,2},{4,5},{5,4},{6,7},{7,6},{8,9},{9,8},{10,11... | collective-permute-start | bytes 786440 | tf_op jit(solution)/shard_map/ppermute | solution.py:18
  50.9 11.3 %collective-permute-start.5 = (bf16[2,128,512]{2,1,0:T(8,128)(2,1)}, bf16[2,128,512]{2,1,0:T(8,128)(2,1)}, u32[]{:S(2)}, u32[]{:S(2)}) collective-permute-start(bf16[2,128,512]{2,1,0:T(8,128)(2,1)} %pad_maximum_fusion.8), channel_id=1, source_target_pairs={{0,8},{4,12},{8,0},{12,4},{1,9},{5,13},{9,1},{13,5},{2,10},{6,14},... | collective-permute-start | bytes 786440 | tf_op jit(solution)/shard_map/ppermute | solution.py:18
  56.0 58.3 %collective-permute-start.8 = (bf16[128,16,128]{2,1,0:T(8,128)(2,1)}, bf16[128,16,128]{2,1,0:T(8,128)(2,1)}, u32[]{:S(2)}, u32[]{:S(2)}) collective-permute-start(bf16[128,16,128]{2,1,0:T(8,128)(2,1)} %get-tuple-element.34), channel_id=1, source_target_pairs={{0,3},{1,2},{2,1},{3,0},{4,7},{5,6},{6,5},{7,4},{8,11},{9,10},{10,... | collective-permute-start | bytes 1572872 | tf_op jit(solution)/shard_map/ppermute | solution.py:18
  57.5 17.0 %collective-permute-start.45 = (bf16[128,256]{1,0:T(8,128)(2,1)}, bf16[128,256]{1,0:T(8,128)(2,1)}, u32[]{:S(2)}, u32[]{:S(2)}) collective-permute-start(bf16[128,256]{1,0:T(8,128)(2,1)} %bitcast.195), channel_id=1, source_target_pairs={{0,3},{1,2},{2,1},{3,0},{4,7},{5,6},{6,5},{7,4},{8,11},{9,10},{10,... | collective-permute-start | bytes 196616 | tf_op jit(solution)/shard_map/ppermute | solution.py:18
  59.8 29.3 %collective-permute-start.44 = (bf16[128,256]{1,0:T(8,128)(2,1)}, bf16[128,256]{1,0:T(8,128)(2,1)}, u32[]{:S(2)}, u32[]{:S(2)}) collective-permute-start(bf16[128,256]{1,0:T(8,128)(2,1)} %bitcast.194), channel_id=1, source_target_pairs={{0,2},{1,3},{2,0},{3,1},{4,6},{5,7},{6,4},{7,5},{8,10},{9,11},{10,... | collective-permute-start | bytes 196616 | tf_op jit(solution)/shard_map/ppermute | solution.py:18
  62.2 26.9 %collective-permute-start.43 = (bf16[128,256]{1,0:T(8,128)(2,1)S(1)}, bf16[128,256]{1,0:T(8,128)(2,1)}, u32[]{:S(2)}, u32[]{:S(2)}) collective-permute-start(bf16[128,256]{1,0:T(8,128)(2,1)S(1)} %bitcast.193), channel_id=1, source_target_pairs={{0,1},{1,0},{2,3},{3,2},{4,5},{5,4},{6,7},{7,6},{8,9},{9,8},{10,11... | collective-permute-start | bytes 196616 | tf_op jit(solution)/shard_map/ppermute | solution.py:18
  74.4 41.0 %collective-permute-start.7 = (bf16[128,16,128]{2,1,0:T(8,128)(2,1)S(1)}, bf16[128,16,128]{2,1,0:T(8,128)(2,1)S(1)}, u32[]{:S(2)}, u32[]{:S(2)}) collective-permute-start(bf16[128,16,128]{2,1,0:T(8,128)(2,1)S(1)} %copy-done.50), channel_id=1, source_target_pairs={{0,2},{1,3},{2,0},{3,1},{4,6},{5,7},{6,4},{7,5},{8,10},{9,11},{10,... | collective-permute-start | bytes 1572872 | tf_op jit(solution)/shard_map/ppermute | solution.py:18
  89.1 26.9 %collective-permute-start.6 = (bf16[128,16,128]{2,1,0:T(8,128)(2,1)S(1)}, bf16[128,16,128]{2,1,0:T(8,128)(2,1)S(1)}, u32[]{:S(2)}, u32[]{:S(2)}) collective-permute-start(bf16[128,16,128]{2,1,0:T(8,128)(2,1)S(1)} %copy-done.49), channel_id=1, source_target_pairs={{0,1},{1,0},{2,3},{3,2},{4,5},{5,4},{6,7},{7,6},{8,9},{9,8},{10,11... | collective-permute-start | bytes 1572872 | tf_op jit(solution)/shard_map/ppermute | solution.py:18
  91.0 21.2 %collective-permute-start.46 = (bf16[64,256]{1,0:T(8,128)(2,1)S(1)}, bf16[64,256]{1,0:T(8,128)(2,1)S(1)}, u32[]{:S(2)}, u32[]{:S(2)}) collective-permute-start(bf16[64,256]{1,0:T(8,128)(2,1)S(1)} %get-tuple-element.125), channel_id=1, source_target_pairs={{0,1},{1,0},{2,3},{3,2},{16,17},{17,16},{18,19},{19,18},{4,5},{5,4... | collective-permute-start | bytes 98312 | tf_op jit(solution)/shard_map/ppermute | solution.py:18
  116.0 12.9 %collective-permute-start.50 = (bf16[64,256]{1,0:T(8,128)(2,1)S(1)}, bf16[64,256]{1,0:T(8,128)(2,1)S(1)}, u32[]{:S(2)}, u32[]{:S(2)}) collective-permute-start(bf16[64,256]{1,0:T(8,128)(2,1)S(1)} %get-tuple-element.121), channel_id=1, source_target_pairs={{0,17},{1,16},{2,19},{3,18},{16,1},{17,0},{18,3},{19,2},{4,21},{5,... | collective-permute-start | bytes 98312 | tf_op jit(solution)/shard_map/ppermute | solution.py:18
  118.6 54.9 %collective-permute-start.18 = (bf16[128,16,128]{2,1,0:T(8,128)(2,1)S(1)}, bf16[128,16,128]{2,1,0:T(8,128)(2,1)S(1)}, u32[]{:S(2)}, u32[]{:S(2)}) collective-permute-start(bf16[128,16,128]{2,1,0:T(8,128)(2,1)S(1)} %copy-done.48), channel_id=1, source_target_pairs={{0,3},{1,2},{2,1},{3,0},{4,7},{5,6},{6,5},{7,4},{8,11},{9,10},{10,... | collective-permute-start | bytes 1572872 | tf_op jit(solution)/shard_map/ppermute | solution.py:18
  120.8 55.7 %collective-permute-start.17 = (bf16[128,16,128]{2,1,0:T(8,128)(2,1)S(1)}, bf16[128,16,128]{2,1,0:T(8,128)(2,1)S(1)}, u32[]{:S(2)}, u32[]{:S(2)}) collective-permute-start(bf16[128,16,128]{2,1,0:T(8,128)(2,1)S(1)} %copy-done.47), channel_id=1, source_target_pairs={{0,2},{1,3},{2,0},{3,1},{4,6},{5,7},{6,4},{7,5},{8,10},{9,11},{10,... | collective-permute-start | bytes 1572872 | tf_op jit(solution)/shard_map/ppermute | solution.py:18
  122.1 55.8 %collective-permute-start.16 = (bf16[128,16,128]{2,1,0:T(8,128)(2,1)S(1)}, bf16[128,16,128]{2,1,0:T(8,128)(2,1)S(1)}, u32[]{:S(2)}, u32[]{:S(2)}) collective-permute-start(bf16[128,16,128]{2,1,0:T(8,128)(2,1)S(1)} %copy-done.46), channel_id=1, source_target_pairs={{0,1},{1,0},{2,3},{3,2},{4,5},{5,4},{6,7},{7,6},{8,9},{9,8},{10,11... | collective-permute-start | bytes 1572872 | tf_op jit(solution)/shard_map/ppermute | solution.py:18
  128.9 37.3 %collective-permute-start.51 = (bf16[64,256]{1,0:T(8,128)(2,1)S(1)}, bf16[64,256]{1,0:T(8,128)(2,1)S(1)}, u32[]{:S(2)}, u32[]{:S(2)}) collective-permute-start(bf16[64,256]{1,0:T(8,128)(2,1)S(1)} %get-tuple-element.120), channel_id=1, source_target_pairs={{0,18},{1,19},{2,16},{3,17},{16,2},{17,3},{18,0},{19,1},{4,22},{5,... | collective-permute-start | bytes 98312 | tf_op jit(solution)/shard_map/ppermute | solution.py:18
  173.5 11.4 %collective-permute-start.37 = (bf16[64,8,128]{2,1,0:T(8,128)(2,1)S(1)}, bf16[64,8,128]{2,1,0:T(8,128)(2,1)S(1)}, u32[]{:S(2)}, u32[]{:S(2)}) collective-permute-start(bf16[64,8,128]{2,1,0:T(8,128)(2,1)S(1)} %bitcast.190), channel_id=1, source_target_pairs={{0,2},{1,3},{2,0},{3,1},{16,18},{17,19},{18,16},{19,17},{4,6},{5,7... | collective-permute-start | bytes 393224 | tf_op jit(solution)/shard_map/ppermute | solution.py:18
  176.5 10.5 %collective-permute-start.38 = (bf16[64,8,128]{2,1,0:T(8,128)(2,1)S(1)}, bf16[64,8,128]{2,1,0:T(8,128)(2,1)S(1)}, u32[]{:S(2)}, u32[]{:S(2)}) collective-permute-start(bf16[64,8,128]{2,1,0:T(8,128)(2,1)S(1)} %bitcast.189), channel_id=1, source_target_pairs={{0,3},{1,2},{2,1},{3,0},{16,19},{17,18},{18,17},{19,16},{4,7},{5,6... | collective-permute-start | bytes 393224 | tf_op jit(solution)/shard_map/ppermute | solution.py:18
  177.9 10.8 %collective-permute-start.39 = (bf16[64,8,128]{2,1,0:T(8,128)(2,1)S(1)}, bf16[64,8,128]{2,1,0:T(8,128)(2,1)S(1)}, u32[]{:S(2)}, u32[]{:S(2)}) collective-permute-start(bf16[64,8,128]{2,1,0:T(8,128)(2,1)S(1)} %bitcast.188), channel_id=1, source_target_pairs={{0,16},{1,17},{2,18},{3,19},{16,0},{17,1},{18,2},{19,3},{4,20},{5,... | collective-permute-start | bytes 393224 | tf_op jit(solution)/shard_map/ppermute | solution.py:18
  179.4 12.4 %collective-permute-start.40 = (bf16[64,8,128]{2,1,0:T(8,128)(2,1)S(1)}, bf16[64,8,128]{2,1,0:T(8,128)(2,1)S(1)}, u32[]{:S(2)}, u32[]{:S(2)}) collective-permute-start(bf16[64,8,128]{2,1,0:T(8,128)(2,1)S(1)} %bitcast.187), channel_id=1, source_target_pairs={{0,17},{1,16},{2,19},{3,18},{16,1},{17,0},{18,3},{19,2},{4,21},{5,... | collective-permute-start | bytes 393224 | tf_op jit(solution)/shard_map/ppermute | solution.py:18
  183.4 70.4 %collective-permute-start.31 = (f32[2,96,1024]{2,1,0:T(8,128)}, f32[2,96,1024]{2,1,0:T(8,128)}, u32[]{:S(2)}, u32[]{:S(2)}) collective-permute-start(f32[2,96,1024]{2,1,0:T(8,128)} %bitcast.23), channel_id=1, source_target_pairs={{0,4},{4,0},{8,12},{12,8},{1,5},{5,1},{9,13},{13,9},{2,6},{6,2},{1... | collective-permute-start | bytes 2359304 | tf_op jit(solution)/shard_map/ppermute | solution.py:18
  184.8 21.8 %collective-permute-start.41 = (bf16[64,8,128]{2,1,0:T(8,128)(2,1)S(1)}, bf16[64,8,128]{2,1,0:T(8,128)(2,1)S(1)}, u32[]{:S(2)}, u32[]{:S(2)}) collective-permute-start(bf16[64,8,128]{2,1,0:T(8,128)(2,1)S(1)} %bitcast.186), channel_id=1, source_target_pairs={{0,18},{1,19},{2,16},{3,17},{16,2},{17,3},{18,0},{19,1},{4,22},{5,... | collective-permute-start | bytes 393224 | tf_op jit(solution)/shard_map/ppermute | solution.py:18
  187.1 19.6 %collective-permute-start.42 = (bf16[64,8,128]{2,1,0:T(8,128)(2,1)S(1)}, bf16[64,8,128]{2,1,0:T(8,128)(2,1)S(1)}, u32[]{:S(2)}, u32[]{:S(2)}) collective-permute-start(bf16[64,8,128]{2,1,0:T(8,128)(2,1)S(1)} %bitcast.185), channel_id=1, source_target_pairs={{0,19},{1,18},{2,17},{3,16},{16,3},{17,2},{18,1},{19,0},{4,23},{5,... | collective-permute-start | bytes 393224 | tf_op jit(solution)/shard_map/ppermute | solution.py:18
  188.7 22.9 %collective-permute-start.11 = (bf16[64,16,128]{2,1,0:T(8,128)(2,1)S(1)}, bf16[64,16,128]{2,1,0:T(8,128)(2,1)S(1)}, u32[]{:S(2)}, u32[]{:S(2)}) collective-permute-start(bf16[64,16,128]{2,1,0:T(8,128)(2,1)S(1)} %bitcast.178), channel_id=1, source_target_pairs={{0,19},{1,18},{2,17},{3,16},{16,3},{17,2},{18,1},{19,0},{4,23},{5,... | collective-permute-start | bytes 786440 | tf_op jit(solution)/shard_map/ppermute | solution.py:18
  191.8 126.3 %collective-permute-start.30 = (f32[1,96,4096]{2,1,0:T(8,128)}, f32[1,96,4096]{2,1,0:T(8,128)}, u32[]{:S(2)}, u32[]{:S(2)}) collective-permute-start(f32[1,96,4096]{2,1,0:T(8,128)} %slice.227), channel_id=1, source_target_pairs={{0,8},{4,12},{8,0},{12,4},{1,9},{5,13},{9,1},{13,5},{2,10},{6,14},... | collective-permute-start | bytes 4718600 | tf_op jit(solution)/shard_map/ppermute | solution.py:18
  206.6 20.0 %collective-permute-start.12 = (bf16[64,16,128]{2,1,0:T(8,128)(2,1)S(1)}, bf16[64,16,128]{2,1,0:T(8,128)(2,1)S(1)}, u32[]{:S(2)}, u32[]{:S(2)}) collective-permute-start(bf16[64,16,128]{2,1,0:T(8,128)(2,1)S(1)} %bitcast.184), channel_id=1, source_target_pairs={{0,18},{1,19},{2,16},{3,17},{16,2},{17,3},{18,0},{19,1},{4,22},{5,... | collective-permute-start | bytes 786440 | tf_op jit(solution)/shard_map/ppermute | solution.py:18
  206.6 20.9 %collective-permute-start.13 = (bf16[64,16,128]{2,1,0:T(8,128)(2,1)S(1)}, bf16[64,16,128]{2,1,0:T(8,128)(2,1)S(1)}, u32[]{:S(2)}, u32[]{:S(2)}) collective-permute-start(bf16[64,16,128]{2,1,0:T(8,128)(2,1)S(1)} %bitcast.182), channel_id=1, source_target_pairs={{0,17},{1,16},{2,19},{3,18},{16,1},{17,0},{18,3},{19,2},{4,21},{5,... | collective-permute-start | bytes 786440 | tf_op jit(solution)/shard_map/ppermute | solution.py:18
  211.6 16.1 %collective-permute-start.14 = (bf16[64,16,128]{2,1,0:T(8,128)(2,1)S(1)}, bf16[64,16,128]{2,1,0:T(8,128)(2,1)S(1)}, u32[]{:S(2)}, u32[]{:S(2)}) collective-permute-start(bf16[64,16,128]{2,1,0:T(8,128)(2,1)S(1)} %bitcast.180), channel_id=1, source_target_pairs={{0,16},{1,17},{2,18},{3,19},{16,0},{17,1},{18,2},{19,3},{4,20},{5,... | collective-permute-start | bytes 786440 | tf_op jit(solution)/shard_map/ppermute | solution.py:18
  226.7 13.6 %collective-permute-start.19 = (bf16[64,16,128]{2,1,0:T(8,128)(2,1)S(1)}, bf16[64,16,128]{2,1,0:T(8,128)(2,1)S(1)}, u32[]{:S(2)}, u32[]{:S(2)}) collective-permute-start(bf16[64,16,128]{2,1,0:T(8,128)(2,1)S(1)} %bitcast.183), channel_id=1, source_target_pairs={{0,19},{1,18},{2,17},{3,16},{16,3},{17,2},{18,1},{19,0},{4,23},{5,... | collective-permute-start | bytes 786440 | tf_op jit(solution)/shard_map/ppermute | solution.py:18
  227.6 21.8 %collective-permute-start.20 = (bf16[64,16,128]{2,1,0:T(8,128)(2,1)S(1)}, bf16[64,16,128]{2,1,0:T(8,128)(2,1)S(1)}, u32[]{:S(2)}, u32[]{:S(2)}) collective-permute-start(bf16[64,16,128]{2,1,0:T(8,128)(2,1)S(1)} %bitcast.181), channel_id=1, source_target_pairs={{0,18},{1,19},{2,16},{3,17},{16,2},{17,3},{18,0},{19,1},{4,22},{5,... | collective-permute-start | bytes 786440 | tf_op jit(solution)/shard_map/ppermute | solution.py:18
  228.3 23.5 %collective-permute-start.21 = (bf16[64,16,128]{2,1,0:T(8,128)(2,1)S(1)}, bf16[64,16,128]{2,1,0:T(8,128)(2,1)S(1)}, u32[]{:S(2)}, u32[]{:S(2)}) collective-permute-start(bf16[64,16,128]{2,1,0:T(8,128)(2,1)S(1)} %bitcast.179), channel_id=1, source_target_pairs={{0,17},{1,16},{2,19},{3,18},{16,1},{17,0},{18,3},{19,2},{4,21},{5,... | collective-permute-start | bytes 786440 | tf_op jit(solution)/shard_map/ppermute | solution.py:18
  235.9 20.7 %all-to-all-start.1 = ((bf16[64,8,256]{2,1,0:T(8,128)(2,1)}), bf16[64,8,256]{2,1,0:T(8,128)(2,1)S(1)}, u32[]{:S(2)}, u32[]{:S(2)}) async-start(bf16[64,8,256]{2,1,0:T(8,128)(2,1)} %copy.44), calls=%async_computation.1 | async-start | bytes 524288 | tf_op jit(solution)/shard_map/all_to_all | solution.py:386
  240.3 22.1 %collective-permute-start.22 = (bf16[64,16,128]{2,1,0:T(8,128)(2,1)}, bf16[64,16,128]{2,1,0:T(8,128)(2,1)}, u32[]{:S(2)}, u32[]{:S(2)}) collective-permute-start(bf16[64,16,128]{2,1,0:T(8,128)(2,1)} %bitcast.68), channel_id=1, source_target_pairs={{0,16},{1,17},{2,18},{3,19},{16,0},{17,1},{18,2},{19,3},{4,20},{5,... | collective-permute-start | bytes 786440 | tf_op jit(solution)/shard_map/ppermute | solution.py:18
  249.4 18.4 %collective-permute-start.23 = (bf16[64,16,128]{2,1,0:T(8,128)(2,1)}, bf16[64,16,128]{2,1,0:T(8,128)(2,1)}, u32[]{:S(2)}, u32[]{:S(2)}) collective-permute-start(bf16[64,16,128]{2,1,0:T(8,128)(2,1)} %bitcast.70), channel_id=1, source_target_pairs={{0,1},{1,0},{2,3},{3,2},{16,17},{17,16},{18,19},{19,18},{4,5},{5,4... | collective-permute-start | bytes 786440 | tf_op jit(solution)/shard_map/ppermute | solution.py:18
  251.8 17.9 %collective-permute-start.24 = (bf16[64,16,128]{2,1,0:T(8,128)(2,1)}, bf16[64,16,128]{2,1,0:T(8,128)(2,1)}, u32[]{:S(2)}, u32[]{:S(2)}) collective-permute-start(bf16[64,16,128]{2,1,0:T(8,128)(2,1)} %bitcast.74), channel_id=1, source_target_pairs={{0,3},{1,2},{2,1},{3,0},{16,19},{17,18},{18,17},{19,16},{4,7},{5,6... | collective-permute-start | bytes 786440 | tf_op jit(solution)/shard_map/ppermute | solution.py:18
  253.7 33.6 %collective-permute-start.25 = (bf16[64,16,128]{2,1,0:T(8,128)(2,1)}, bf16[64,16,128]{2,1,0:T(8,128)(2,1)}, u32[]{:S(2)}, u32[]{:S(2)}) collective-permute-start(bf16[64,16,128]{2,1,0:T(8,128)(2,1)} %bitcast.76), channel_id=1, source_target_pairs={{0,2},{1,3},{2,0},{3,1},{16,18},{17,19},{18,16},{19,17},{4,6},{5,7... | collective-permute-start | bytes 786440 | tf_op jit(solution)/shard_map/ppermute | solution.py:18
  256.6 59.8 %all-to-all-start = ((bf16[64,8,1024]{2,1,0:T(8,128)(2,1)}), bf16[64,8,1024]{2,1,0:T(8,128)(2,1)S(1)}, u32[]{:S(2)}, u32[]{:S(2)}) async-start(bf16[64,8,1024]{2,1,0:T(8,128)(2,1)} %join.4), calls=%async_computation | async-start | bytes 2097152 | tf_op jit(solution)/shard_map/all_to_all | solution.py:386
  262.3 52.3 %collective-permute-start.32 = (f32[1,96,1024]{2,1,0:T(8,128)}, f32[1,96,1024]{2,1,0:T(8,128)}, u32[]{:S(2)}, u32[]{:S(2)}) collective-permute-start(f32[1,96,1024]{2,1,0:T(8,128)} %slice.231), channel_id=1, source_target_pairs={{0,8},{4,12},{8,0},{12,4},{1,9},{5,13},{9,1},{13,5},{2,10},{6,14},... | collective-permute-start | bytes 1179656 | tf_op jit(solution)/shard_map/ppermute | solution.py:18
  267.8 34.9 %collective-permute-start.9 = (bf16[64,16,128]{2,1,0:T(8,128)(2,1)}, bf16[64,16,128]{2,1,0:T(8,128)(2,1)S(1)}, u32[]{:S(2)}, u32[]{:S(2)}) collective-permute-start(bf16[64,16,128]{2,1,0:T(8,128)(2,1)} %bitcast.44), channel_id=1, source_target_pairs={{0,3},{1,2},{2,1},{3,0},{16,19},{17,18},{18,17},{19,16},{4,7},{5,6... | collective-permute-start | bytes 786440 | tf_op jit(solution)/shard_map/ppermute | solution.py:18
  269.7 33.1 %collective-permute-start.10 = (bf16[64,16,128]{2,1,0:T(8,128)(2,1)}, bf16[64,16,128]{2,1,0:T(8,128)(2,1)S(1)}, u32[]{:S(2)}, u32[]{:S(2)}) collective-permute-start(bf16[64,16,128]{2,1,0:T(8,128)(2,1)} %bitcast.46), channel_id=1, source_target_pairs={{0,2},{1,3},{2,0},{3,1},{16,18},{17,19},{18,16},{19,17},{4,6},{5,7... | collective-permute-start | bytes 786440 | tf_op jit(solution)/shard_map/ppermute | solution.py:18
  287.4 11.2 %collective-permute-start.15 = (bf16[64,16,128]{2,1,0:T(8,128)(2,1)}, bf16[64,16,128]{2,1,0:T(8,128)(2,1)S(1)}, u32[]{:S(2)}, u32[]{:S(2)}) collective-permute-start(bf16[64,16,128]{2,1,0:T(8,128)(2,1)} %bitcast.56), channel_id=1, source_target_pairs={{0,1},{1,0},{2,3},{3,2},{16,17},{17,16},{18,19},{19,18},{4,5},{5,4... | collective-permute-start | bytes 786440 | tf_op jit(solution)/shard_map/ppermute | solution.py:18
  306.4 15.6 %collective-permute-start.26 = (f32[16,96]{1,0:T(8,128)}, f32[16,96]{1,0:T(8,128)S(1)}, u32[]{:S(2)}, u32[]{:S(2)}) collective-permute-start(f32[16,96]{1,0:T(8,128)} %get-tuple-element.48), channel_id=1, source_target_pairs={{0,4},{4,0},{8,12},{12,8},{1,5},{5,1},{9,13},{13,9},{2,6},{6,2},{1... | collective-permute-start | bytes 18440 | tf_op jit(solution)/shard_map/ppermute | solution.py:18
  306.4 15.6 %collective-permute-start.27 = (f32[16,96]{1,0:T(8,128)}, f32[16,96]{1,0:T(8,128)S(1)}, u32[]{:S(2)}, u32[]{:S(2)}) collective-permute-start(f32[16,96]{1,0:T(8,128)} %get-tuple-element.49), channel_id=1, source_target_pairs={{0,8},{4,12},{8,0},{12,4},{1,9},{5,13},{9,1},{13,5},{2,10},{6,14},... | collective-permute-start | bytes 18440 | tf_op jit(solution)/shard_map/ppermute | solution.py:18
  307.0 15.1 %collective-permute-start.28 = (f32[16,96]{1,0:T(8,128)}, f32[16,96]{1,0:T(8,128)S(1)}, u32[]{:S(2)}, u32[]{:S(2)}) collective-permute-start(f32[16,96]{1,0:T(8,128)} %get-tuple-element.50), channel_id=1, source_target_pairs={{0,12},{4,8},{8,4},{12,0},{1,13},{5,9},{9,5},{13,1},{2,14},{6,10},... | collective-permute-start | bytes 18440 | tf_op jit(solution)/shard_map/ppermute | solution.py:18
  (58 other events, 441.9 us)

commit v2 on v1

--- a/solution.py
+++ b/solution.py
@@ -11,6 +11,7 @@
 ADAPTER_SCALE = 2.0
 LANES = 128
 PLACES = ("groups", "task")
+SMALL = pltpu.CompilerParams(vmem_limit_bytes=16 * 1024 * 1024)
 
 
 def swap(x, axes, shift):
@@ -64,6 +65,7 @@
         out_specs=[pl.BlockSpec(memory_space=pl.ANY)] * len(shifts),
         out_shape=[jax.ShapeDtypeStruct(shape, head.dtype)] * len(shifts),
         scratch_shapes=vmem_scratch(len(shifts), shape, head.dtype),
+        compiler_params=SMALL,
         name="cut",
     )(head)
 
@@ -86,6 +88,7 @@
         out_shape=jax.ShapeDtypeStruct(pieces[0].shape[:2] + (columns,), pieces[0].dtype),
         scratch_shapes=vmem_scratch(len(pieces), pieces[0].shape, pieces[0].dtype),
         input_output_aliases={} if whole is None else {len(pieces): 0},
+        compiler_params=SMALL,
         name="join",
     )(*operands)
 
@@ -104,6 +107,7 @@
         out_specs=pl.BlockSpec(memory_space=pl.ANY),
         out_shape=jax.ShapeDtypeStruct((len(pieces),) + shape, dtype),
         scratch_shapes=vmem_scratch(len(pieces), shape, dtype),
+        compiler_params=SMALL,
         name="stack",
     )(*pieces)
 
@@ -172,7 +176,7 @@
 
 
 def project_kernel(shifts, parts, stride, start, width, tokens, bounds, *refs):
-    pieces, refs, square = refs[: len(shifts)], refs[len(shifts) : -1], refs[-1]
+    pieces, refs = refs[: len(shifts)], refs[len(shifts) :]
     before, after = refs[:-parts], refs[-parts:]
     rows = tokens.shape[0] // parts
     tasks, rank = pieces[0].shape[0] // parts, pieces[0].shape[1]
@@ -193,67 +197,74 @@
     count = 3
     summed = jnp.dot(
         terms(jnp.concatenate(every), count), pick, preferred_element_type=jnp.float32
-    ).reshape(count, parts, rows, LANES)
+    ).reshape(count, parts * rows, LANES)
+    low_rank = sum(summed[k] for k in range(count)).T
     for turn in range(parts):
-        low_rank = turned(sum(summed[k, turn] for k in range(count)), square)[0:rank, 0:rows]
-        after[turn][...] = low_rank + before[turn][...] if before else low_rank
-
-
-def project(pieces, shifts, stride, start, width, tokens, bounds, before):
+        share = low_rank[0:rank, turn * rows : (turn + 1) * rows]
+        after[turn][...] = share + before[turn][...] if before else share
+
+
+def in_vmem(x):
+    return pltpu.with_memory_space_constraint(x, pltpu.VMEM)
+
+
+def project(pieces, shifts, stride, start, width, tokens, bounds, before, near):
     parts, rank = bounds.shape[0], pieces[0].shape[1]
     rows = tokens.shape[0] // parts
+    if near:
+        tokens, bounds = in_vmem(tokens), in_vmem(bounds)
+        before = [in_vmem(x) for x in before]
     return pl.pallas_call(
         functools.partial(project_kernel, shifts, parts, stride, start, width),
+        in_specs=[pl.BlockSpec(memory_space=pltpu.VMEM)] * (2 + len(pieces) + len(before)),
         out_shape=[jax.ShapeDtypeStruct((rank, rows), jnp.float32)] * parts,
-        scratch_shapes=[pltpu.VMEM((LANES, LANES), jnp.float32)],
+        compiler_params=SMALL,
         name="project",
     )(tokens, bounds, *pieces, *before)
 
 
-def finish_kernel(count, bounds, *refs):
+def finish_kernel(count, steps, bounds, *refs):
     shares, rest = refs[:count], refs[count:]
-    base_query, base_value, up_query, up_value, query, value, square, spread = rest
+    bases, ups, outs, makes, square, sems = rest[0:2], rest[2:4], rest[4:6], rest[6:8], *rest[8:]
     rank, rows = shares[0].shape
-
-    @pl.when(pl.program_id(0) == 0)
-    def _():
-        low_rank = shares[0][...]
-        for share in shares[1:]:
-            low_rank = low_rank + share[...]
-        low_rank = turned(low_rank, square)[0:rows]
-        own = bounds[lax.axis_index("tensor")]
-        pick = rank_columns((LANES, own.shape[1]), 0, 1, rank).astype(jnp.bfloat16)
-        each = jnp.dot(terms(low_rank, 2), pick, preferred_element_type=jnp.float32)
-        own = inside(own, rows)
-        each = jnp.where(jnp.concatenate([own, own]), each, 0.0)
-        spread[...] = each.astype(jnp.bfloat16)
-
-    for base, up, out in ((base_query, up_query, query), (base_value, up_value, value)):
-        update = jnp.dot(spread[...], up[...], preferred_element_type=jnp.float32)
-        update = update[0:rows] + update[rows:]
-        out[...] = (base[...] + ADAPTER_SCALE * update).astype(out.dtype)
+    low_rank = shares[0][...]
+    for share in shares[1:]:
+        low_rank = low_rank + share[...]
+    low_rank = turned(low_rank, square)[0:rows]
+    own = bounds[lax.axis_index("tensor")]
+    pick = rank_columns((LANES, own.shape[1]), 0, 1, rank).astype(jnp.bfloat16)
+    spread = jnp.dot(terms(low_rank, 2), pick, preferred_element_type=jnp.float32)
+    own = inside(own, rows)
+    spread = jnp.where(jnp.concatenate([own, own]), spread, 0.0).astype(jnp.bfloat16)
+    copies = []
+    for step in range(steps):
+        for k, (base, up, out, made) in enumerate(zip(bases, ups, outs, makes)):
+            width = base.shape[1] // steps
+            columns = pl.ds(step * width, width)
+            update = jnp.dot(spread, up[:, columns], preferred_element_type=jnp.float32)
+            update = update[0:rows] + update[rows:]
+            made[:, columns] = (base[:, columns] + ADAPTER_SCALE * update).astype(made.dtype)
+            copies.append(
+                pltpu.make_async_copy(made.at[:, columns], out.at[:, columns], sems.at[k, step])
+            )
+            copies[-1].start()
+    for copy in copies:
+        copy.wait()
 
 
 def finish(shares, bounds, operands, steps):
-    rows = operands[0].shape[0]
-
-    def columns(x):
-        return pl.BlockSpec((x.shape[0], x.shape[1] // steps), lambda i: (0, i))
-
+    operands = [in_vmem(x) for x in (bounds, *shares, *operands)]
+    shapes = [x.shape for x in operands[-4:-2]]
     return pl.pallas_call(
-        functools.partial(finish_kernel, len(shares)),
-        grid=(steps,),
-        in_specs=[pl.BlockSpec(bounds.shape, lambda i: (0, 0, 0))]
-        + [pl.BlockSpec(x.shape, lambda i: (0, 0)) for x in shares]
-        + [columns(x) for x in operands],
-        out_specs=[columns(x) for x in operands[:2]],
-        out_shape=[jax.ShapeDtypeStruct(x.shape, jnp.bfloat16) for x in operands[:2]],
-        scratch_shapes=[
-            pltpu.VMEM((LANES, LANES), jnp.float32),
-            pltpu.VMEM((2 * rows, bounds.shape[2]), jnp.bfloat16),
-        ],
+        functools.partial(finish_kernel, len(shares), steps),
+        in_specs=[pl.BlockSpec(memory_space=pltpu.VMEM)] * len(operands),
+        out_specs=[pl.BlockSpec(memory_space=pl.ANY)] * 2,
+        out_shape=[jax.ShapeDtypeStruct(shape, jnp.bfloat16) for shape in shapes],
+        scratch_shapes=[pltpu.VMEM(shape, jnp.bfloat16) for shape in shapes]
+        + [pltpu.VMEM((LANES, LANES), jnp.float32), pltpu.SemaphoreType.DMA((2, steps))],
+        compiler_params=SMALL,
         name="finish",
-    )(bounds, *shares, *operands)
+    )(*operands)
 
 
 def halving_order(total):
@@ -396,8 +407,8 @@
 
     tallies = task_counts.reshape(parts, block_tasks)
     ends = jnp.cumsum(tallies, axis=1)
-    bounds = jnp.stack([ends - tallies, ends], axis=1)
-    bounds = jnp.repeat(bounds, 2 * rank, axis=2)
+    begins = ends - tallies
+    bounds = jnp.repeat(jnp.stack([begins, ends], axis=1), 2 * rank, axis=2)
 
     down_factors, low_rank = None, []
     head = heads["down"]
@@ -407,7 +418,8 @@
             for half in [early, late] if chunk + 1 == chunks else [early + late]:
                 some = [pieces[s] for s in half]
                 low_rank = project(
-                    some, half, head.stride, start, head.width, tokens, bounds, low_rank
+                    some, half, head.stride, start, head.width, tokens, bounds, low_rank,
+                    half is late,
                 )
                 down_factors = head.join(some, half, chunk, down_factors)
     else:

time: 329 us -> 326 us (level); the launches traced: 328 us -> 321 us
  Pallas kernels: 31.8 us -> 19.2 us
  local copies, waits for them, and re-layouts: 37 us -> 47.3 us
  starting transfers between devices: 98.6 us -> 106 us
  matrix products: 20.6 us -> 16.6 us
  waiting for transfers between devices: 121 us -> 117 us
    unnamed x133 -> x91, local copies, waits for them, and re-layouts: 18.5 us -> 30.7 us
    ppermute x53, starting transfers between devices: 91.5 us -> 97 us  [swap(): return lax.ppermute(x, axes, [(a, a ^ shift) for a in range(total)])]
    pallas_call x3, Pallas kernels: 10 us -> 4.89 us  [project(): pl.pallas_call(functools.partial(project_kernel, shifts, parts, stride, s...]
    ppermute x53, waiting for transfers between devices: 121 us -> 117 us  [swap(): return lax.ppermute(x, axes, [(a, a ^ shift) for a in range(total)])]
  transfers between devices with their start and end apart: 55 -> 55, of which waited for: 12 -> 13; matrix products, arithmetic and copies ran while one was open for 20% -> 20% of each run, Pallas kernels for 8% -> 5%
where the time goes in v2:
time: 326 us; the launch traced here: 321 us
  waiting for transfers between devices  117 us (36%)
  starting transfers between devices  106 us (33%)
  local copies, waits for them, and re-layouts  47.3 us (15%)
  Pallas kernels  19.2 us (6%)
  matrix products  16.6 us (5%)
  other arithmetic  13.6 us (4%)
    ppermute x53, waiting for transfers between devices, swap(): return lax.ppermute(x, axes, [(a, a ^ shift) for a in range(total)])  117 us
    ppermute x53, starting transfers between devices, swap(): return lax.ppermute(x, axes, [(a, a ^ shift) for a in range(total)])  97 us
    unnamed x91, local copies, waits for them, and re-layouts  30.7 us
    dot_general x1, matrix products, local(): base_query = jnp.dot(turned, w_query, preferred_element_type=jnp.float32)  10.2 us
    all_to_all x2, starting transfers between devices, own_block(): lax.all_to_all(factors, 'tensor', split_axis=0, concat_axis=0, tiled=True)  8.65 us
    pallas_call x4, Pallas kernels, join(): pl.pallas_call(functools.partial(join_kernel, shifts, stride, start, widt...  7.93 us
    slice x4, local copies, waits for them, and re-layouts, reduce_blocks(): came = swap(partial[half:], axis, step)  7.08 us
  transfers between devices with their start and end apart: 55, of which 13 were waited for; matrix products, arithmetic and copies ran while one was open for 20% of the time, Pallas kernels for 5%

profile of v2, /device:TPU:0, one launch (start us, length us, event | category | flops | bytes accessed | tf_op | source)
XLA Modules:
  0.0 321.0 jit_solution(12847221687238717565)
XLA Ops:
  2.9 3.1 collective-permute-start
  7.4 10.2 %fusion.9 = f32[384,4096]{1,0:T(8,128)S(1)} fusion(bf16[2048,4096]{1,0:T(8,128)(2,1)} %param.16, bf16[96,2048]{1,0:T(8,128)(2,1)S(1)} %get-tuple-element.98, bf16[96,2048]{1,0:T(8,128)(2,1)S(1)} %get-tuple-element.99, bf16[96,2048]{1,0:T(8,128)(2,1)S(1)} %get-tuple-element.100, bf16[96,2048]{1,0:T(8,128)(2,1)S(1)} %get-tuple-element.97), kind=kOutput, calls=%fused_computation.25 | convolution fusion | flops 6448742400 | bytes 24641536 | tf_op jit(solution)/shard_map/dot_general | solution.py:391
  17.7 3.6 %fusion.27 = (f32[192,4096]{1,0:T(8,128)}, f32[192,4096]{1,0:T(8,128)}) fusion(f32[384,4096]{1,0:T(8,128)S(1)} %fusion.9), kind=kLoop, calls=%fused_computation.87 | loop fusion | bytes 12582912 | tf_op jit(solution)/shard_map/slice | solution.py:279
  22.4 3.7 %collective-permute-start.35 = (bf16[128,8,128]{2,1,0:T(8,128)(2,1)}, bf16[128,8,128]{2,1,0:T(8,128)(2,1)}, u32[]{:S(2)}, u32[]{:S(2)}) collective-permute-start(bf16[128,8,128]{2,1,0:T(8,128)(2,1)} %get-tuple-element.54), channel_id=1, source_target_pairs={{0,3},{1,2},{2,1},{3,0},{4,7},{5,6},{6,5},{7,4},{8,11},{9,10},{10,... | collective-permute-start | bytes 786440 | tf_op jit(solution)/shard_map/ppermute | solution.py:19
  27.2 3.4 %collective-permute-start.1 = (bf16[32,512]{1,0:T(8,128)(2,1)S(1)}, bf16[32,512]{1,0:T(8,128)(2,1)S(1)}, u32[]{:S(2)}, u32[]{:S(2)}) collective-permute-start(bf16[32,512]{1,0:T(8,128)(2,1)S(1)} %get-tuple-element.130), channel_id=1, source_target_pairs={{0,1},{1,0},{2,3},{3,2},{4,5},{5,4},{6,7},{7,6},{8,9},{9,8},{10,11... | collective-permute-start | bytes 98312 | tf_op jit(solution)/shard_map/ppermute | solution.py:19
  30.5 1.8 fusion.8
  32.4 2.1 collective-permute-done.3
  34.5 7.6 %collective-permute-start.34 = (bf16[128,8,128]{2,1,0:T(8,128)(2,1)S(1)}, bf16[128,8,128]{2,1,0:T(8,128)(2,1)}, u32[]{:S(2)}, u32[]{:S(2)}) collective-permute-start(bf16[128,8,128]{2,1,0:T(8,128)(2,1)S(1)} %get-tuple-element.53), channel_id=1, source_target_pairs={{0,2},{1,3},{2,0},{3,1},{4,6},{5,7},{6,4},{7,5},{8,10},{9,11},{10,... | collective-permute-start | bytes 786440 | tf_op jit(solution)/shard_map/ppermute | solution.py:19
  44.0 3.4 %copy-done.2 = bf16[128,16,2048]{2,1,0:T(8,128)(2,1)S(1)} copy-done((bf16[128,16,2048]{2,1,0:T(8,128)(2,1)S(1)}, bf16[128,16,2048]{2,1,0:T(8,128)(2,1)}, u32[]{:S(2)}) %copy-start.2) | copy-done | bytes 8388632
  47.4 1.8 cut.3
  54.9 2.2 constant_dynamic-slice_fusion.3
  61.0 2.4 collective-permute-start.45
  63.5 2.2 pad_maximum_fusion.3
  65.7 1.9 collective-permute-start.43
  70.9 7.0 %collective-permute-done.45 = bf16[128,256]{1,0:T(8,128)(2,1)S(1)} collective-permute-done((bf16[128,256]{1,0:T(8,128)(2,1)}, bf16[128,256]{1,0:T(8,128)(2,1)S(1)}, u32[]{:S(2)}, u32[]{:S(2)}) %collective-permute-start.45) | collective-permute-done | bytes 65568 | tf_op jit(solution)/shard_map/ppermute | solution.py:19
  77.9 13.9 %collective-permute-start.7 = (bf16[128,16,128]{2,1,0:T(8,128)(2,1)}, bf16[128,16,128]{2,1,0:T(8,128)(2,1)S(1)}, u32[]{:S(2)}, u32[]{:S(2)}) collective-permute-start(bf16[128,16,128]{2,1,0:T(8,128)(2,1)} %get-tuple-element.33), channel_id=1, source_target_pairs={{0,2},{1,3},{2,0},{3,1},{4,6},{5,7},{6,4},{7,5},{8,10},{9,11},{10,... | collective-permute-start | bytes 1572872 | tf_op jit(solution)/shard_map/ppermute | solution.py:19
  92.8 2.1 collective-permute-start.46
  95.9 19.8 %collective-permute-done.46.refs_1_ = bf16[64,256]{1,0:T(8,128)(2,1)S(1)} collective-permute-done((bf16[64,256]{1,0:T(8,128)(2,1)S(1)}, bf16[64,256]{1,0:T(8,128)(2,1)S(1)}, u32[]{:S(2)}, u32[]{:S(2)}) %collective-permute-start.46) | collective-permute-done | bytes 32800 | tf_op jit(solution)/shard_map/ppermute | solution.py:19
  115.7 2.2 collective-permute-start.47
  122.0 2.3 collective-permute-start.18
  126.5 6.2 %collective-permute-done.50.refs_5_ = bf16[64,256]{1,0:T(8,128)(2,1)S(1)} collective-permute-done((bf16[64,256]{1,0:T(8,128)(2,1)S(1)}, bf16[64,256]{1,0:T(8,128)(2,1)S(1)}, u32[]{:S(2)}, u32[]{:S(2)}) %collective-permute-start.50) | collective-permute-done | bytes 32800 | tf_op jit(solution)/shard_map/ppermute | solution.py:19
  134.7 35.2 %collective-permute-done.51.refs_6_ = bf16[64,256]{1,0:T(8,128)(2,1)S(1)} collective-permute-done((bf16[64,256]{1,0:T(8,128)(2,1)S(1)}, bf16[64,256]{1,0:T(8,128)(2,1)S(1)}, u32[]{:S(2)}, u32[]{:S(2)}) %collective-permute-start.51) | collective-permute-done | bytes 32800 | tf_op jit(solution)/shard_map/ppermute | solution.py:19
  169.9 2.9 collective-permute-start.52
  173.9 2.6 collective-permute-done.52.refs_7_
  176.5 2.9 collective-permute-start.37
  184.3 2.3 add.80
  188.1 3.5 %collective-permute-start.41 = (bf16[64,8,128]{2,1,0:T(8,128)(2,1)S(1)}, bf16[64,8,128]{2,1,0:T(8,128)(2,1)S(1)}, u32[]{:S(2)}, u32[]{:S(2)}) collective-permute-start(bf16[64,8,128]{2,1,0:T(8,128)(2,1)S(1)} %bitcast.179), channel_id=1, source_target_pairs={{0,18},{1,19},{2,16},{3,17},{16,2},{17,3},{18,0},{19,1},{4,22},{5,... | collective-permute-start | bytes 393224 | tf_op jit(solution)/shard_map/ppermute | solution.py:19
  191.6 1.8 collective-permute-start.42
  193.4 2.9 collective-permute-start.11
  198.3 12.1 %collective-permute-done.41.refs_6_ = bf16[64,8,128]{2,1,0:T(8,128)(2,1)S(1)} collective-permute-done((bf16[64,8,128]{2,1,0:T(8,128)(2,1)S(1)}, bf16[64,8,128]{2,1,0:T(8,128)(2,1)S(1)}, u32[]{:S(2)}, u32[]{:S(2)}) %collective-permute-start.41) | collective-permute-done | bytes 131104 | tf_op jit(solution)/shard_map/ppermute | solution.py:19
  210.3 4.8 %collective-permute-start.13 = (bf16[64,16,128]{2,1,0:T(8,128)(2,1)S(1)}, bf16[64,16,128]{2,1,0:T(8,128)(2,1)S(1)}, u32[]{:S(2)}, u32[]{:S(2)}) collective-permute-start(bf16[64,16,128]{2,1,0:T(8,128)(2,1)S(1)} %bitcast.176), channel_id=1, source_target_pairs={{0,17},{1,16},{2,19},{3,18},{16,1},{17,0},{18,3},{19,2},{4,21},{5,... | collective-permute-start | bytes 786440 | tf_op jit(solution)/shard_map/ppermute | solution.py:19
  215.1 3.1 collective-permute-start.14
  219.8 10.7 %collective-permute-done.12.refs_1_ = bf16[64,16,128]{2,1,0:T(8,128)(2,1)S(1)} collective-permute-done((bf16[64,16,128]{2,1,0:T(8,128)(2,1)S(1)}, bf16[64,16,128]{2,1,0:T(8,128)(2,1)S(1)}, u32[]{:S(2)}, u32[]{:S(2)}) %collective-permute-start.12) | collective-permute-done | bytes 262176 | tf_op jit(solution)/shard_map/ppermute | solution.py:19
  233.8 4.7 %collective-permute-start.21 = (bf16[64,16,128]{2,1,0:T(8,128)(2,1)}, bf16[64,16,128]{2,1,0:T(8,128)(2,1)S(1)}, u32[]{:S(2)}, u32[]{:S(2)}) collective-permute-start(bf16[64,16,128]{2,1,0:T(8,128)(2,1)} %bitcast.66), channel_id=1, source_target_pairs={{0,17},{1,16},{2,19},{3,18},{16,1},{17,0},{18,3},{19,2},{4,21},{5,... | collective-permute-start | bytes 786440 | tf_op jit(solution)/shard_map/ppermute | solution.py:19
  240.1 4.0 %all-to-all-start.1 = ((bf16[64,8,256]{2,1,0:T(8,128)(2,1)}), bf16[64,8,256]{2,1,0:T(8,128)(2,1)}, u32[]{:S(2)}, u32[]{:S(2)}) async-start(bf16[64,8,256]{2,1,0:T(8,128)(2,1)} %copy.44), calls=%async_computation.1 | async-start | bytes 524288 | tf_op jit(solution)/shard_map/all_to_all | solution.py:397
  244.9 2.5 collective-permute-start.22
  249.7 5.9 %collective-permute-done.20.refs_1_ = bf16[64,16,128]{2,1,0:T(8,128)(2,1)S(1)} collective-permute-done((bf16[64,16,128]{2,1,0:T(8,128)(2,1)}, bf16[64,16,128]{2,1,0:T(8,128)(2,1)S(1)}, u32[]{:S(2)}, u32[]{:S(2)}) %collective-permute-start.20) | collective-permute-done | bytes 262176 | tf_op jit(solution)/shard_map/ppermute | solution.py:19
  255.6 1.8 collective-permute-start.23
  257.4 2.7 collective-permute-start.24
  260.2 2.5 join.4
  262.6 4.6 %all-to-all-start = ((bf16[64,8,1024]{2,1,0:T(8,128)(2,1)}), bf16[64,8,1024]{2,1,0:T(8,128)(2,1)}, u32[]{:S(2)}, u32[]{:S(2)}) async-start(bf16[64,8,1024]{2,1,0:T(8,128)(2,1)} %join.4), calls=%async_computation | async-start | bytes 2097152 | tf_op jit(solution)/shard_map/all_to_all | solution.py:397
  270.2 1.7 collective-permute-start.32
  288.3 7.9 %collective-permute-done.15.refs_4_ = bf16[64,16,128]{2,1,0:T(8,128)(2,1)} collective-permute-done((bf16[64,16,128]{2,1,0:T(8,128)(2,1)}, bf16[64,16,128]{2,1,0:T(8,128)(2,1)}, u32[]{:S(2)}, u32[]{:S(2)}) %collective-permute-start.15) | collective-permute-done | bytes 262176 | tf_op jit(solution)/shard_map/ppermute | solution.py:19
  296.2 2.0 project.4
  298.2 5.8 %collective-permute-done.10.refs_1_ = bf16[64,16,128]{2,1,0:T(8,128)(2,1)} collective-permute-done((bf16[64,16,128]{2,1,0:T(8,128)(2,1)}, bf16[64,16,128]{2,1,0:T(8,128)(2,1)}, u32[]{:S(2)}, u32[]{:S(2)}) %collective-permute-start.10) | collective-permute-done | bytes 262176 | tf_op jit(solution)/shard_map/ppermute | solution.py:19
  309.2 2.0 join.6.refs_2_
  311.3 1.8 join.7
  319.1 1.7 finish.1
  (208 shorter events, 80.2 us)
Async XLA Ops:
  2.9 23.2 %collective-permute-start = (bf16[16,512]{1,0:T(8,128)(2,1)S(1)}, bf16[16,512]{1,0:T(8,128)(2,1)S(1)}, u32[]{:S(2)}, u32[]{:S(2)}) collective-permute-start(bf16[16,512]{1,0:T(8,128)(2,1)S(1)} %multiply_convert_fusion), channel_id=1, source_target_pairs={{0,16},{16,0},{1,17},{17,1},{2,18},{18,2},{3,19},{19,3},{4,20},{20... | collective-permute-start | bytes 49160 | tf_op jit(solution)/shard_map/ppermute | solution.py:19
  21.3 161.2 %collective-permute-start.29 = (f32[2,96,4096]{2,1,0:T(8,128)}, f32[2,96,4096]{2,1,0:T(8,128)}, u32[]{:S(2)}, u32[]{:S(2)}) collective-permute-start(f32[2,96,4096]{2,1,0:T(8,128)} %bitcast.20), channel_id=1, source_target_pairs={{0,4},{4,0},{8,12},{12,8},{1,5},{5,1},{9,13},{13,9},{2,6},{6,2},{1... | collective-permute-start | bytes 9437192 | tf_op jit(solution)/shard_map/ppermute | solution.py:19
  22.4 37.2 %collective-permute-start.35 = (bf16[128,8,128]{2,1,0:T(8,128)(2,1)}, bf16[128,8,128]{2,1,0:T(8,128)(2,1)}, u32[]{:S(2)}, u32[]{:S(2)}) collective-permute-start(bf16[128,8,128]{2,1,0:T(8,128)(2,1)} %get-tuple-element.54), channel_id=1, source_target_pairs={{0,3},{1,2},{2,1},{3,0},{4,7},{5,6},{6,5},{7,4},{8,11},{9,10},{10,... | collective-permute-start | bytes 786440 | tf_op jit(solution)/shard_map/ppermute | solution.py:19
  26.4 15.7 %collective-permute-start.2 = (bf16[32,512]{1,0:T(8,128)(2,1)S(1)}, bf16[32,512]{1,0:T(8,128)(2,1)S(1)}, u32[]{:S(2)}, u32[]{:S(2)}) collective-permute-start(bf16[32,512]{1,0:T(8,128)(2,1)S(1)} %get-tuple-element.130), channel_id=1, source_target_pairs={{0,2},{1,3},{2,0},{3,1},{4,6},{5,7},{6,4},{7,5},{8,10},{9,11},{10,... | collective-permute-start | bytes 98312 | tf_op jit(solution)/shard_map/ppermute | solution.py:19
  27.2 14.9 %collective-permute-start.1 = (bf16[32,512]{1,0:T(8,128)(2,1)S(1)}, bf16[32,512]{1,0:T(8,128)(2,1)S(1)}, u32[]{:S(2)}, u32[]{:S(2)}) collective-permute-start(bf16[32,512]{1,0:T(8,128)(2,1)S(1)} %get-tuple-element.130), channel_id=1, source_target_pairs={{0,1},{1,0},{2,3},{3,2},{4,5},{5,4},{6,7},{7,6},{8,9},{9,8},{10,11... | collective-permute-start | bytes 98312 | tf_op jit(solution)/shard_map/ppermute | solution.py:19
  34.5 26.6 %collective-permute-start.34 = (bf16[128,8,128]{2,1,0:T(8,128)(2,1)S(1)}, bf16[128,8,128]{2,1,0:T(8,128)(2,1)}, u32[]{:S(2)}, u32[]{:S(2)}) collective-permute-start(bf16[128,8,128]{2,1,0:T(8,128)(2,1)S(1)} %get-tuple-element.53), channel_id=1, source_target_pairs={{0,2},{1,3},{2,0},{3,1},{4,6},{5,7},{6,4},{7,5},{8,10},{9,11},{10,... | collective-permute-start | bytes 786440 | tf_op jit(solution)/shard_map/ppermute | solution.py:19
  42.1 21.3 %collective-permute-start.33 = (bf16[128,8,128]{2,1,0:T(8,128)(2,1)S(1)}, bf16[128,8,128]{2,1,0:T(8,128)(2,1)}, u32[]{:S(2)}, u32[]{:S(2)}) collective-permute-start(bf16[128,8,128]{2,1,0:T(8,128)(2,1)S(1)} %get-tuple-element.52), channel_id=1, source_target_pairs={{0,1},{1,0},{2,3},{3,2},{4,5},{5,4},{6,7},{7,6},{8,9},{9,8},{10,11... | collective-permute-start | bytes 786440 | tf_op jit(solution)/shard_map/ppermute | solution.py:19
  53.4 12.3 %collective-permute-start.5 = (bf16[2,128,512]{2,1,0:T(8,128)(2,1)}, bf16[2,128,512]{2,1,0:T(8,128)(2,1)}, u32[]{:S(2)}, u32[]{:S(2)}) collective-permute-start(bf16[2,128,512]{2,1,0:T(8,128)(2,1)} %pad_maximum_fusion.8), channel_id=1, source_target_pairs={{0,8},{4,12},{8,0},{12,4},{1,9},{5,13},{9,1},{13,5},{2,10},{6,14},... | collective-permute-start | bytes 786440 | tf_op jit(solution)/shard_map/ppermute | solution.py:19
  59.6 58.3 %collective-permute-start.8 = (bf16[128,16,128]{2,1,0:T(8,128)(2,1)}, bf16[128,16,128]{2,1,0:T(8,128)(2,1)}, u32[]{:S(2)}, u32[]{:S(2)}) collective-permute-start(bf16[128,16,128]{2,1,0:T(8,128)(2,1)} %copy-done.17), channel_id=1, source_target_pairs={{0,3},{1,2},{2,1},{3,0},{4,7},{5,6},{6,5},{7,4},{8,11},{9,10},{10,... | collective-permute-start | bytes 1572872 | tf_op jit(solution)/shard_map/ppermute | solution.py:19
  61.0 16.9 %collective-permute-start.45 = (bf16[128,256]{1,0:T(8,128)(2,1)}, bf16[128,256]{1,0:T(8,128)(2,1)S(1)}, u32[]{:S(2)}, u32[]{:S(2)}) collective-permute-start(bf16[128,256]{1,0:T(8,128)(2,1)} %bitcast.187), channel_id=1, source_target_pairs={{0,3},{1,2},{2,1},{3,0},{4,7},{5,6},{6,5},{7,4},{8,11},{9,10},{10,... | collective-permute-start | bytes 196616 | tf_op jit(solution)/shard_map/ppermute | solution.py:19
  63.4 29.1 %collective-permute-start.44 = (bf16[128,256]{1,0:T(8,128)(2,1)}, bf16[128,256]{1,0:T(8,128)(2,1)S(1)}, u32[]{:S(2)}, u32[]{:S(2)}) collective-permute-start(bf16[128,256]{1,0:T(8,128)(2,1)} %bitcast.186), channel_id=1, source_target_pairs={{0,2},{1,3},{2,0},{3,1},{4,6},{5,7},{6,4},{7,5},{8,10},{9,11},{10,... | collective-permute-start | bytes 196616 | tf_op jit(solution)/shard_map/ppermute | solution.py:19
  65.7 26.8 %collective-permute-start.43 = (bf16[128,256]{1,0:T(8,128)(2,1)}, bf16[128,256]{1,0:T(8,128)(2,1)S(1)}, u32[]{:S(2)}, u32[]{:S(2)}) collective-permute-start(bf16[128,256]{1,0:T(8,128)(2,1)} %bitcast.153), channel_id=1, source_target_pairs={{0,1},{1,0},{2,3},{3,2},{4,5},{5,4},{6,7},{7,6},{8,9},{9,8},{10,11... | collective-permute-start | bytes 196616 | tf_op jit(solution)/shard_map/ppermute | solution.py:19
  77.9 41.3 %collective-permute-start.7 = (bf16[128,16,128]{2,1,0:T(8,128)(2,1)}, bf16[128,16,128]{2,1,0:T(8,128)(2,1)S(1)}, u32[]{:S(2)}, u32[]{:S(2)}) collective-permute-start(bf16[128,16,128]{2,1,0:T(8,128)(2,1)} %get-tuple-element.33), channel_id=1, source_target_pairs={{0,2},{1,3},{2,0},{3,1},{4,6},{5,7},{6,4},{7,5},{8,10},{9,11},{10,... | collective-permute-start | bytes 1572872 | tf_op jit(solution)/shard_map/ppermute | solution.py:19
  92.5 27.2 %collective-permute-start.6 = (bf16[128,16,128]{2,1,0:T(8,128)(2,1)}, bf16[128,16,128]{2,1,0:T(8,128)(2,1)S(1)}, u32[]{:S(2)}, u32[]{:S(2)}) collective-permute-start(bf16[128,16,128]{2,1,0:T(8,128)(2,1)} %get-tuple-element.32), channel_id=1, source_target_pairs={{0,1},{1,0},{2,3},{3,2},{4,5},{5,4},{6,7},{7,6},{8,9},{9,8},{10,11... | collective-permute-start | bytes 1572872 | tf_op jit(solution)/shard_map/ppermute | solution.py:19
  92.8 22.9 %collective-permute-start.46 = (bf16[64,256]{1,0:T(8,128)(2,1)S(1)}, bf16[64,256]{1,0:T(8,128)(2,1)S(1)}, u32[]{:S(2)}, u32[]{:S(2)}) collective-permute-start(bf16[64,256]{1,0:T(8,128)(2,1)S(1)} %get-tuple-element.125), channel_id=1, source_target_pairs={{0,1},{1,0},{2,3},{3,2},{16,17},{17,16},{18,19},{19,18},{4,5},{5,4... | collective-permute-start | bytes 98312 | tf_op jit(solution)/shard_map/ppermute | solution.py:19
  119.7 13.0 %collective-permute-start.50 = (bf16[64,256]{1,0:T(8,128)(2,1)S(1)}, bf16[64,256]{1,0:T(8,128)(2,1)S(1)}, u32[]{:S(2)}, u32[]{:S(2)}) collective-permute-start(bf16[64,256]{1,0:T(8,128)(2,1)S(1)} %get-tuple-element.121), channel_id=1, source_target_pairs={{0,17},{1,16},{2,19},{3,18},{16,1},{17,0},{18,3},{19,2},{4,21},{5,... | collective-permute-start | bytes 98312 | tf_op jit(solution)/shard_map/ppermute | solution.py:19
  122.0 54.5 %collective-permute-start.18 = (bf16[128,16,128]{2,1,0:T(8,128)(2,1)S(1)}, bf16[128,16,128]{2,1,0:T(8,128)(2,1)S(1)}, u32[]{:S(2)}, u32[]{:S(2)}) collective-permute-start(bf16[128,16,128]{2,1,0:T(8,128)(2,1)S(1)} %get-tuple-element.38), channel_id=1, source_target_pairs={{0,3},{1,2},{2,1},{3,0},{4,7},{5,6},{6,5},{7,4},{8,11},{9,10},{10,... | collective-permute-start | bytes 1572872 | tf_op jit(solution)/shard_map/ppermute | solution.py:19
  124.3 55.1 %collective-permute-start.17 = (bf16[128,16,128]{2,1,0:T(8,128)(2,1)S(1)}, bf16[128,16,128]{2,1,0:T(8,128)(2,1)S(1)}, u32[]{:S(2)}, u32[]{:S(2)}) collective-permute-start(bf16[128,16,128]{2,1,0:T(8,128)(2,1)S(1)} %get-tuple-element.37), channel_id=1, source_target_pairs={{0,2},{1,3},{2,0},{3,1},{4,6},{5,7},{6,4},{7,5},{8,10},{9,11},{10,... | collective-permute-start | bytes 1572872 | tf_op jit(solution)/shard_map/ppermute | solution.py:19
  125.5 55.4 %collective-permute-start.16 = (bf16[128,16,128]{2,1,0:T(8,128)(2,1)S(1)}, bf16[128,16,128]{2,1,0:T(8,128)(2,1)S(1)}, u32[]{:S(2)}, u32[]{:S(2)}) collective-permute-start(bf16[128,16,128]{2,1,0:T(8,128)(2,1)S(1)} %get-tuple-element.36), channel_id=1, source_target_pairs={{0,1},{1,0},{2,3},{3,2},{4,5},{5,4},{6,7},{7,6},{8,9},{9,8},{10,11... | collective-permute-start | bytes 1572872 | tf_op jit(solution)/shard_map/ppermute | solution.py:19
  132.6 37.3 %collective-permute-start.51 = (bf16[64,256]{1,0:T(8,128)(2,1)S(1)}, bf16[64,256]{1,0:T(8,128)(2,1)S(1)}, u32[]{:S(2)}, u32[]{:S(2)}) collective-permute-start(bf16[64,256]{1,0:T(8,128)(2,1)S(1)} %get-tuple-element.120), channel_id=1, source_target_pairs={{0,18},{1,19},{2,16},{3,17},{16,2},{17,3},{18,0},{19,1},{4,22},{5,... | collective-permute-start | bytes 98312 | tf_op jit(solution)/shard_map/ppermute | solution.py:19
  176.5 11.5 %collective-permute-start.36 = (bf16[64,8,128]{2,1,0:T(8,128)(2,1)S(1)}, bf16[64,8,128]{2,1,0:T(8,128)(2,1)S(1)}, u32[]{:S(2)}, u32[]{:S(2)}) collective-permute-start(bf16[64,8,128]{2,1,0:T(8,128)(2,1)S(1)} %bitcast.184), channel_id=1, source_target_pairs={{0,1},{1,0},{2,3},{3,2},{16,17},{17,16},{18,19},{19,18},{4,5},{5,4... | collective-permute-start | bytes 393224 | tf_op jit(solution)/shard_map/ppermute | solution.py:19
  179.4 12.2 %collective-permute-start.38 = (bf16[64,8,128]{2,1,0:T(8,128)(2,1)S(1)}, bf16[64,8,128]{2,1,0:T(8,128)(2,1)S(1)}, u32[]{:S(2)}, u32[]{:S(2)}) collective-permute-start(bf16[64,8,128]{2,1,0:T(8,128)(2,1)S(1)} %bitcast.182), channel_id=1, source_target_pairs={{0,3},{1,2},{2,1},{3,0},{16,19},{17,18},{18,17},{19,16},{4,7},{5,6... | collective-permute-start | bytes 393224 | tf_op jit(solution)/shard_map/ppermute | solution.py:19
  180.9 12.4 %collective-permute-start.39 = (bf16[64,8,128]{2,1,0:T(8,128)(2,1)S(1)}, bf16[64,8,128]{2,1,0:T(8,128)(2,1)S(1)}, u32[]{:S(2)}, u32[]{:S(2)}) collective-permute-start(bf16[64,8,128]{2,1,0:T(8,128)(2,1)S(1)} %bitcast.181), channel_id=1, source_target_pairs={{0,16},{1,17},{2,18},{3,19},{16,0},{17,1},{18,2},{19,3},{4,20},{5,... | collective-permute-start | bytes 393224 | tf_op jit(solution)/shard_map/ppermute | solution.py:19
  182.4 13.9 %collective-permute-start.40 = (bf16[64,8,128]{2,1,0:T(8,128)(2,1)S(1)}, bf16[64,8,128]{2,1,0:T(8,128)(2,1)S(1)}, u32[]{:S(2)}, u32[]{:S(2)}) collective-permute-start(bf16[64,8,128]{2,1,0:T(8,128)(2,1)S(1)} %bitcast.180), channel_id=1, source_target_pairs={{0,17},{1,16},{2,19},{3,18},{16,1},{17,0},{18,3},{19,2},{4,21},{5,... | collective-permute-start | bytes 393224 | tf_op jit(solution)/shard_map/ppermute | solution.py:19
  188.1 72.1 %collective-permute-start.31 = (f32[2,96,1024]{2,1,0:T(8,128)}, f32[2,96,1024]{2,1,0:T(8,128)}, u32[]{:S(2)}, u32[]{:S(2)}) collective-permute-start(f32[2,96,1024]{2,1,0:T(8,128)} %bitcast.23), channel_id=1, source_target_pairs={{0,4},{4,0},{8,12},{12,8},{1,5},{5,1},{9,13},{13,9},{2,6},{6,2},{1... | collective-permute-start | bytes 2359304 | tf_op jit(solution)/shard_map/ppermute | solution.py:19
  188.1 22.3 %collective-permute-start.41 = (bf16[64,8,128]{2,1,0:T(8,128)(2,1)S(1)}, bf16[64,8,128]{2,1,0:T(8,128)(2,1)S(1)}, u32[]{:S(2)}, u32[]{:S(2)}) collective-permute-start(bf16[64,8,128]{2,1,0:T(8,128)(2,1)S(1)} %bitcast.179), channel_id=1, source_target_pairs={{0,18},{1,19},{2,16},{3,17},{16,2},{17,3},{18,0},{19,1},{4,22},{5,... | collective-permute-start | bytes 393224 | tf_op jit(solution)/shard_map/ppermute | solution.py:19
  191.6 18.8 %collective-permute-start.42 = (bf16[64,8,128]{2,1,0:T(8,128)(2,1)S(1)}, bf16[64,8,128]{2,1,0:T(8,128)(2,1)S(1)}, u32[]{:S(2)}, u32[]{:S(2)}) collective-permute-start(bf16[64,8,128]{2,1,0:T(8,128)(2,1)S(1)} %bitcast.178), channel_id=1, source_target_pairs={{0,19},{1,18},{2,17},{3,16},{16,3},{17,2},{18,1},{19,0},{4,23},{5,... | collective-permute-start | bytes 393224 | tf_op jit(solution)/shard_map/ppermute | solution.py:19
  193.4 21.8 %collective-permute-start.11 = (bf16[64,16,128]{2,1,0:T(8,128)(2,1)S(1)}, bf16[64,16,128]{2,1,0:T(8,128)(2,1)S(1)}, u32[]{:S(2)}, u32[]{:S(2)}) collective-permute-start(bf16[64,16,128]{2,1,0:T(8,128)(2,1)S(1)} %bitcast.174), channel_id=1, source_target_pairs={{0,19},{1,18},{2,17},{3,16},{16,3},{17,2},{18,1},{19,0},{4,23},{5,... | collective-permute-start | bytes 786440 | tf_op jit(solution)/shard_map/ppermute | solution.py:19
  196.3 119.4 %collective-permute-start.30 = (f32[1,96,4096]{2,1,0:T(8,128)}, f32[1,96,4096]{2,1,0:T(8,128)}, u32[]{:S(2)}, u32[]{:S(2)}) collective-permute-start(f32[1,96,4096]{2,1,0:T(8,128)} %slice.227), channel_id=1, source_target_pairs={{0,8},{4,12},{8,0},{12,4},{1,9},{5,13},{9,1},{13,5},{2,10},{6,14},... | collective-permute-start | bytes 4718600 | tf_op jit(solution)/shard_map/ppermute | solution.py:19
  210.3 20.1 %collective-permute-start.12 = (bf16[64,16,128]{2,1,0:T(8,128)(2,1)S(1)}, bf16[64,16,128]{2,1,0:T(8,128)(2,1)S(1)}, u32[]{:S(2)}, u32[]{:S(2)}) collective-permute-start(bf16[64,16,128]{2,1,0:T(8,128)(2,1)S(1)} %bitcast.177), channel_id=1, source_target_pairs={{0,18},{1,19},{2,16},{3,17},{16,2},{17,3},{18,0},{19,1},{4,22},{5,... | collective-permute-start | bytes 786440 | tf_op jit(solution)/shard_map/ppermute | solution.py:19
  210.3 21.8 %collective-permute-start.13 = (bf16[64,16,128]{2,1,0:T(8,128)(2,1)S(1)}, bf16[64,16,128]{2,1,0:T(8,128)(2,1)S(1)}, u32[]{:S(2)}, u32[]{:S(2)}) collective-permute-start(bf16[64,16,128]{2,1,0:T(8,128)(2,1)S(1)} %bitcast.176), channel_id=1, source_target_pairs={{0,17},{1,16},{2,19},{3,18},{16,1},{17,0},{18,3},{19,2},{4,21},{5,... | collective-permute-start | bytes 786440 | tf_op jit(solution)/shard_map/ppermute | solution.py:19
  215.1 18.0 %collective-permute-start.14 = (bf16[64,16,128]{2,1,0:T(8,128)(2,1)S(1)}, bf16[64,16,128]{2,1,0:T(8,128)(2,1)S(1)}, u32[]{:S(2)}, u32[]{:S(2)}) collective-permute-start(bf16[64,16,128]{2,1,0:T(8,128)(2,1)S(1)} %bitcast.175), channel_id=1, source_target_pairs={{0,16},{1,17},{2,18},{3,19},{16,0},{17,1},{18,2},{19,3},{4,20},{5,... | collective-permute-start | bytes 786440 | tf_op jit(solution)/shard_map/ppermute | solution.py:19
  230.5 14.5 %collective-permute-start.19 = (bf16[64,16,128]{2,1,0:T(8,128)(2,1)}, bf16[64,16,128]{2,1,0:T(8,128)(2,1)S(1)}, u32[]{:S(2)}, u32[]{:S(2)}) collective-permute-start(bf16[64,16,128]{2,1,0:T(8,128)(2,1)} %bitcast.62), channel_id=1, source_target_pairs={{0,19},{1,18},{2,17},{3,16},{16,3},{17,2},{18,1},{19,0},{4,23},{5,... | collective-permute-start | bytes 786440 | tf_op jit(solution)/shard_map/ppermute | solution.py:19
  232.8 22.7 %collective-permute-start.20 = (bf16[64,16,128]{2,1,0:T(8,128)(2,1)}, bf16[64,16,128]{2,1,0:T(8,128)(2,1)S(1)}, u32[]{:S(2)}, u32[]{:S(2)}) collective-permute-start(bf16[64,16,128]{2,1,0:T(8,128)(2,1)} %bitcast.64), channel_id=1, source_target_pairs={{0,18},{1,19},{2,16},{3,17},{16,2},{17,3},{18,0},{19,1},{4,22},{5,... | collective-permute-start | bytes 786440 | tf_op jit(solution)/shard_map/ppermute | solution.py:19
  233.8 23.6 %collective-permute-start.21 = (bf16[64,16,128]{2,1,0:T(8,128)(2,1)}, bf16[64,16,128]{2,1,0:T(8,128)(2,1)S(1)}, u32[]{:S(2)}, u32[]{:S(2)}) collective-permute-start(bf16[64,16,128]{2,1,0:T(8,128)(2,1)} %bitcast.66), channel_id=1, source_target_pairs={{0,17},{1,16},{2,19},{3,18},{16,1},{17,0},{18,3},{19,2},{4,21},{5,... | collective-permute-start | bytes 786440 | tf_op jit(solution)/shard_map/ppermute | solution.py:19
  240.1 22.5 %all-to-all-start.1 = ((bf16[64,8,256]{2,1,0:T(8,128)(2,1)}), bf16[64,8,256]{2,1,0:T(8,128)(2,1)}, u32[]{:S(2)}, u32[]{:S(2)}) async-start(bf16[64,8,256]{2,1,0:T(8,128)(2,1)} %copy.44), calls=%async_computation.1 | async-start | bytes 524288 | tf_op jit(solution)/shard_map/all_to_all | solution.py:397
  244.9 25.3 %collective-permute-start.22 = (bf16[64,16,128]{2,1,0:T(8,128)(2,1)}, bf16[64,16,128]{2,1,0:T(8,128)(2,1)S(1)}, u32[]{:S(2)}, u32[]{:S(2)}) collective-permute-start(bf16[64,16,128]{2,1,0:T(8,128)(2,1)} %bitcast.68), channel_id=1, source_target_pairs={{0,16},{1,17},{2,18},{3,19},{16,0},{17,1},{18,2},{19,3},{4,20},{5,... | collective-permute-start | bytes 786440 | tf_op jit(solution)/shard_map/ppermute | solution.py:19
  255.6 21.9 %collective-permute-start.23 = (bf16[64,16,128]{2,1,0:T(8,128)(2,1)}, bf16[64,16,128]{2,1,0:T(8,128)(2,1)S(1)}, u32[]{:S(2)}, u32[]{:S(2)}) collective-permute-start(bf16[64,16,128]{2,1,0:T(8,128)(2,1)} %bitcast.70), channel_id=1, source_target_pairs={{0,1},{1,0},{2,3},{3,2},{16,17},{17,16},{18,19},{19,18},{4,5},{5,4... | collective-permute-start | bytes 786440 | tf_op jit(solution)/shard_map/ppermute | solution.py:19
  257.4 21.6 %collective-permute-start.24 = (bf16[64,16,128]{2,1,0:T(8,128)(2,1)}, bf16[64,16,128]{2,1,0:T(8,128)(2,1)S(1)}, u32[]{:S(2)}, u32[]{:S(2)}) collective-permute-start(bf16[64,16,128]{2,1,0:T(8,128)(2,1)} %bitcast.74), channel_id=1, source_target_pairs={{0,3},{1,2},{2,1},{3,0},{16,19},{17,18},{18,17},{19,16},{4,7},{5,6... | collective-permute-start | bytes 786440 | tf_op jit(solution)/shard_map/ppermute | solution.py:19
  260.1 21.4 %collective-permute-start.25 = (bf16[64,16,128]{2,1,0:T(8,128)(2,1)}, bf16[64,16,128]{2,1,0:T(8,128)(2,1)S(1)}, u32[]{:S(2)}, u32[]{:S(2)}) collective-permute-start(bf16[64,16,128]{2,1,0:T(8,128)(2,1)} %bitcast.76), channel_id=1, source_target_pairs={{0,2},{1,3},{2,0},{3,1},{16,18},{17,19},{18,16},{19,17},{4,6},{5,7... | collective-permute-start | bytes 786440 | tf_op jit(solution)/shard_map/ppermute | solution.py:19
  262.6 51.5 %all-to-all-start = ((bf16[64,8,1024]{2,1,0:T(8,128)(2,1)}), bf16[64,8,1024]{2,1,0:T(8,128)(2,1)}, u32[]{:S(2)}, u32[]{:S(2)}) async-start(bf16[64,8,1024]{2,1,0:T(8,128)(2,1)} %join.4), calls=%async_computation | async-start | bytes 2097152 | tf_op jit(solution)/shard_map/all_to_all | solution.py:397
  270.2 42.9 %collective-permute-start.32 = (f32[1,96,1024]{2,1,0:T(8,128)}, f32[1,96,1024]{2,1,0:T(8,128)}, u32[]{:S(2)}, u32[]{:S(2)}) collective-permute-start(f32[1,96,1024]{2,1,0:T(8,128)} %slice.231), channel_id=1, source_target_pairs={{0,8},{4,12},{8,0},{12,4},{1,9},{5,13},{9,1},{13,5},{2,10},{6,14},... | collective-permute-start | bytes 1179656 | tf_op jit(solution)/shard_map/ppermute | solution.py:19
  277.4 20.8 %collective-permute-start.9 = (bf16[64,16,128]{2,1,0:T(8,128)(2,1)}, bf16[64,16,128]{2,1,0:T(8,128)(2,1)}, u32[]{:S(2)}, u32[]{:S(2)}) collective-permute-start(bf16[64,16,128]{2,1,0:T(8,128)(2,1)} %bitcast.44), channel_id=1, source_target_pairs={{0,3},{1,2},{2,1},{3,0},{16,19},{17,18},{18,17},{19,16},{4,7},{5,6... | collective-permute-start | bytes 786440 | tf_op jit(solution)/shard_map/ppermute | solution.py:19
  279.0 25.0 %collective-permute-start.10 = (bf16[64,16,128]{2,1,0:T(8,128)(2,1)}, bf16[64,16,128]{2,1,0:T(8,128)(2,1)}, u32[]{:S(2)}, u32[]{:S(2)}) collective-permute-start(bf16[64,16,128]{2,1,0:T(8,128)(2,1)} %bitcast.46), channel_id=1, source_target_pairs={{0,2},{1,3},{2,0},{3,1},{16,18},{17,19},{18,16},{19,17},{4,6},{5,7... | collective-permute-start | bytes 786440 | tf_op jit(solution)/shard_map/ppermute | solution.py:19
  281.5 14.7 %collective-permute-start.15 = (bf16[64,16,128]{2,1,0:T(8,128)(2,1)}, bf16[64,16,128]{2,1,0:T(8,128)(2,1)}, u32[]{:S(2)}, u32[]{:S(2)}) collective-permute-start(bf16[64,16,128]{2,1,0:T(8,128)(2,1)} %bitcast.56), channel_id=1, source_target_pairs={{0,1},{1,0},{2,3},{3,2},{16,17},{17,16},{18,19},{19,18},{4,5},{5,4... | collective-permute-start | bytes 786440 | tf_op jit(solution)/shard_map/ppermute | solution.py:19
  305.7 13.3 %collective-permute-start.26 = (f32[16,96]{1,0:T(8,128)S(1)}, f32[16,96]{1,0:T(8,128)S(1)}, u32[]{:S(2)}, u32[]{:S(2)}) collective-permute-start(f32[16,96]{1,0:T(8,128)S(1)} %get-tuple-element.48), channel_id=1, source_target_pairs={{0,4},{4,0},{8,12},{12,8},{1,5},{5,1},{9,13},{13,9},{2,6},{6,2},{1... | collective-permute-start | bytes 18440 | tf_op jit(solution)/shard_map/ppermute | solution.py:19
  305.8 13.3 %collective-permute-start.27 = (f32[16,96]{1,0:T(8,128)S(1)}, f32[16,96]{1,0:T(8,128)S(1)}, u32[]{:S(2)}, u32[]{:S(2)}) collective-permute-start(f32[16,96]{1,0:T(8,128)S(1)} %get-tuple-element.49), channel_id=1, source_target_pairs={{0,8},{4,12},{8,0},{12,4},{1,9},{5,13},{9,1},{13,5},{2,10},{6,14},... | collective-permute-start | bytes 18440 | tf_op jit(solution)/shard_map/ppermute | solution.py:19
  306.4 12.7 %collective-permute-start.28 = (f32[16,96]{1,0:T(8,128)S(1)}, f32[16,96]{1,0:T(8,128)S(1)}, u32[]{:S(2)}, u32[]{:S(2)}) collective-permute-start(f32[16,96]{1,0:T(8,128)S(1)} %get-tuple-element.50), channel_id=1, source_target_pairs={{0,12},{4,8},{8,4},{12,0},{1,13},{5,9},{9,5},{13,1},{2,14},{6,10},... | collective-permute-start | bytes 18440 | tf_op jit(solution)/shard_map/ppermute | solution.py:19
  (37 other events, 238.3 us)

commit v3 on v2

--- a/solution.py
+++ b/solution.py
@@ -67,7 +67,27 @@
         scratch_shapes=vmem_scratch(len(shifts), shape, head.dtype),
         compiler_params=SMALL,
         name="cut",
-    )(head)
+    )(pltpu.with_memory_space_constraint(head, pltpu.HBM))
+
+
+def cut_row_kernel(shifts, rank, source, *pieces):
+    rows = source.shape[0] // rank
+    at = lax.broadcasted_iota(jnp.int32, (rows, source.shape[0]), 1)
+    at = at - rank * lax.broadcasted_iota(jnp.int32, (rows, source.shape[0]), 0)
+    for shift, piece in zip(shifts, pieces):
+        pick = jnp.where(at == (place() ^ shift), 1.0, 0.0).astype(source.dtype)
+        picked = jnp.dot(pick, source[...], preferred_element_type=jnp.float32)
+        piece[...] = picked.astype(piece.dtype)
+
+
+def cut_row(head, shifts):
+    rows, rank, columns = head.shape
+    return pl.pallas_call(
+        functools.partial(cut_row_kernel, shifts, rank),
+        out_shape=[jax.ShapeDtypeStruct((rows, columns), head.dtype)] * len(shifts),
+        compiler_params=SMALL,
+        name="cut_row",
+    )(head.reshape(rows * rank, columns))
 
 
 def join_kernel(shifts, stride, start, width, *refs):
@@ -126,18 +146,16 @@
         self.places = lax.axis_size("groups") * lax.axis_size("task")
         self.stride = self.columns // self.places
         self.by_lane = self.stride % (LANES * chunks) == 0
-        self.by_row = not self.by_lane and self.rank % self.places == 0
+        self.by_row = not self.by_lane and self.rank == self.places
         self.chunks = chunks if self.by_lane else 1
         self.width = self.stride // self.chunks
 
     def cut(self, chunk, shifts):
         if self.by_lane:
             return cut(self.head, shifts, self.stride, chunk * self.width, self.width)
-        rows = self.head.shape[0]
         if self.by_row:
-            shares = self.head.reshape(rows, self.places, -1).transpose(1, 0, 2)
-        else:
-            shares = self.head.reshape(rows, self.rank, self.places, -1).transpose(2, 0, 1, 3)
+            return cut_row(self.head, shifts)
+        shares = self.head.reshape(-1, self.rank, self.places, self.stride).transpose(2, 0, 1, 3)
         return [lax.dynamic_index_in_dim(shares, place() ^ s, 0, keepdims=False) for s in shifts]
 
     def join(self, pieces, shifts, chunk=0, whole=None):
@@ -372,8 +390,10 @@
     def send(made, sent):
         return {s: swap(made[s], PLACES, s) if s else made[s] for s in sent}
 
-    late = [s for s in far_first if s >= ring // 2]
-    early = [s for s in reversed(shifts) if s not in late]
+    crossing = [s for s in reversed(shifts) if s % ring >= ring // 2]
+    early = [s for s in crossing if s >= ring] + [s for s in reversed(shifts) if s % ring == 0]
+    late = [s for s in crossing if s < ring]
+    late = late + [s for s in reversed(shifts) if 0 < s % ring < ring // 2]
     emitted = {}
     for name, chunk in [("query", 0), ("value", 0)] + [("down", c) for c in range(chunks)]:
         made = emit(name, chunk)

time: 326 us -> 316 us (0.969); the launches traced: 321 us -> 315 us
  starting transfers between devices: 106 us -> 97.8 us
  waiting for transfers between devices: 117 us -> 122 us
  local copies, waits for them, and re-layouts: 47.3 us -> 43.2 us
    ppermute x53, starting transfers between devices: 97 us -> 89.2 us  [swap(): return lax.ppermute(x, axes, [(a, a ^ shift) for a in range(total)])]
    ppermute x53, waiting for transfers between devices: 117 us -> 122 us  [swap(): return lax.ppermute(x, axes, [(a, a ^ shift) for a in range(total)])]
    unnamed x91 -> x95, local copies, waits for them, and re-layouts: 30.7 us -> 27.8 us
  transfers between devices with their start and end apart: 55 -> 55, of which waited for: 13 -> 11; matrix products, arithmetic and copies ran while one was open for 20% -> 19% of each run, Pallas kernels for 5% -> 6%
where the time goes in v3:
time: 316 us; the launch traced here: 315 us
  waiting for transfers between devices  122 us (39%)
  starting transfers between devices  97.8 us (31%)
  local copies, waits for them, and re-layouts  43.2 us (14%)
  Pallas kernels  19.8 us (6%)
  matrix products  17.5 us (6%)
  other arithmetic  12.9 us (4%)
    ppermute x53, waiting for transfers between devices, swap(): return lax.ppermute(x, axes, [(a, a ^ shift) for a in range(total)])  122 us
    ppermute x53, starting transfers between devices, swap(): return lax.ppermute(x, axes, [(a, a ^ shift) for a in range(total)])  89.2 us
    unnamed x95, local copies, waits for them, and re-layouts  27.8 us
    dot_general x1, matrix products, local(): base_query = jnp.dot(turned, w_query, preferred_element_type=jnp.float32)  10.2 us
    all_to_all x2, starting transfers between devices, own_block(): lax.all_to_all(factors, 'tensor', split_axis=0, concat_axis=0, tiled=True)  8.64 us
    pallas_call x4, Pallas kernels, join(): pl.pallas_call(functools.partial(join_kernel, shifts, stride, start, widt...  7.24 us
    slice x4, local copies, waits for them, and re-layouts, reduce_blocks(): came = swap(partial[half:], axis, step)  6.98 us
  transfers between devices with their start and end apart: 55, of which 11 were waited for; matrix products, arithmetic and copies ran while one was open for 19% of the time, Pallas kernels for 6%

profile of v3, /device:TPU:0, one launch (start us, length us, event | category | flops | bytes accessed | tf_op | source)
XLA Modules:
  0.0 314.7 jit_solution(16698116631019002218)
XLA Ops:
  2.9 3.1 collective-permute-start
  7.4 10.2 %fusion.9 = f32[384,4096]{1,0:T(8,128)S(1)} fusion(bf16[2048,4096]{1,0:T(8,128)(2,1)} %param.16, bf16[96,2048]{1,0:T(8,128)(2,1)S(1)} %get-tuple-element.106, bf16[96,2048]{1,0:T(8,128)(2,1)S(1)} %get-tuple-element.107, bf16[96,2048]{1,0:T(8,128)(2,1)S(1)} %get-tuple-element.108, bf16[96,2048]{1,0:T(8,128)(2,1)S(1)} %get-tuple-element.105), kind=kOutput, calls=%fused_computation.25 | convolution fusion | flops 6448742400 | bytes 24641536 | tf_op jit(solution)/shard_map/dot_general | solution.py:411
  17.7 3.7 %collective-permute-start.3 = (bf16[32,512]{1,0:T(8,128)(2,1)S(1)}, bf16[32,512]{1,0:T(8,128)(2,1)S(1)}, u32[]{:S(2)}, u32[]{:S(2)}) collective-permute-start(bf16[32,512]{1,0:T(8,128)(2,1)S(1)} %get-tuple-element.134), channel_id=1, source_target_pairs={{0,3},{1,2},{2,1},{3,0},{4,7},{5,6},{6,5},{7,4},{8,11},{9,10},{10,... | collective-permute-start | bytes 98312 | tf_op jit(solution)/shard_map/ppermute | solution.py:19
  22.1 3.5 %fusion.27 = (f32[192,4096]{1,0:T(8,128)}, f32[192,4096]{1,0:T(8,128)}) fusion(f32[384,4096]{1,0:T(8,128)S(1)} %fusion.9), kind=kLoop, calls=%fused_computation.79 | loop fusion | bytes 12582912 | tf_op jit(solution)/shard_map/slice | solution.py:297
  25.7 2.0 cut.5
  27.6 3.7 %collective-permute-start.35 = (bf16[128,8,128]{2,1,0:T(8,128)(2,1)}, bf16[128,8,128]{2,1,0:T(8,128)(2,1)}, u32[]{:S(2)}, u32[]{:S(2)}) collective-permute-start(bf16[128,8,128]{2,1,0:T(8,128)(2,1)} %get-tuple-element.58), channel_id=1, source_target_pairs={{0,3},{1,2},{2,1},{3,0},{4,7},{5,6},{6,5},{7,4},{8,11},{9,10},{10,... | collective-permute-start | bytes 786440 | tf_op jit(solution)/shard_map/ppermute | solution.py:19
  32.2 1.8 fusion.8
  42.4 1.9 cut.4
  46.1 3.6 %collective-permute-start.8 = (bf16[128,16,128]{2,1,0:T(8,128)(2,1)}, bf16[128,16,128]{2,1,0:T(8,128)(2,1)}, u32[]{:S(2)}, u32[]{:S(2)}) collective-permute-start(bf16[128,16,128]{2,1,0:T(8,128)(2,1)} %copy-done.20), channel_id=1, source_target_pairs={{0,3},{1,2},{2,1},{3,0},{4,7},{5,6},{6,5},{7,4},{8,11},{9,10},{10,... | collective-permute-start | bytes 1572872 | tf_op jit(solution)/shard_map/ppermute | solution.py:19
  49.7 16.3 %collective-permute-done.34 = bf16[128,8,128]{2,1,0:T(8,128)(2,1)} collective-permute-done((bf16[128,8,128]{2,1,0:T(8,128)(2,1)}, bf16[128,8,128]{2,1,0:T(8,128)(2,1)}, u32[]{:S(2)}, u32[]{:S(2)}) %collective-permute-start.34) | collective-permute-done | bytes 262176 | tf_op jit(solution)/shard_map/ppermute | solution.py:19
  66.0 2.4 collective-permute-start.45
  68.3 2.2 pad_maximum_fusion.3
  70.6 2.0 collective-permute-start.43
  74.5 2.0 reshape.154
  77.8 5.1 %collective-permute-start.7 = (bf16[128,16,128]{2,1,0:T(8,128)(2,1)S(1)}, bf16[128,16,128]{2,1,0:T(8,128)(2,1)S(1)}, u32[]{:S(2)}, u32[]{:S(2)}) collective-permute-start(bf16[128,16,128]{2,1,0:T(8,128)(2,1)S(1)} %copy-done.19), channel_id=1, source_target_pairs={{0,2},{1,3},{2,0},{3,1},{4,6},{5,7},{6,4},{7,5},{8,10},{9,11},{10,... | collective-permute-start | bytes 1572872 | tf_op jit(solution)/shard_map/ppermute | solution.py:19
  84.1 2.1 collective-permute-start.46
  87.2 19.3 %collective-permute-done.46.refs_1_ = bf16[64,256]{1,0:T(8,128)(2,1)S(1)} collective-permute-done((bf16[64,256]{1,0:T(8,128)(2,1)S(1)}, bf16[64,256]{1,0:T(8,128)(2,1)S(1)}, u32[]{:S(2)}, u32[]{:S(2)}) %collective-permute-start.46) | collective-permute-done | bytes 32800 | tf_op jit(solution)/shard_map/ppermute | solution.py:19
  107.9 2.4 collective-permute-start.48
  112.8 1.8 collective-permute-start.18
  114.5 2.1 collective-permute-start.17
  117.2 7.1 %collective-permute-done.50.refs_5_ = bf16[64,256]{1,0:T(8,128)(2,1)S(1)} collective-permute-done((bf16[64,256]{1,0:T(8,128)(2,1)S(1)}, bf16[64,256]{1,0:T(8,128)(2,1)S(1)}, u32[]{:S(2)}, u32[]{:S(2)}) %collective-permute-start.50) | collective-permute-done | bytes 32800 | tf_op jit(solution)/shard_map/ppermute | solution.py:19
  125.6 35.1 %collective-permute-done.51.refs_6_ = bf16[64,256]{1,0:T(8,128)(2,1)S(1)} collective-permute-done((bf16[64,256]{1,0:T(8,128)(2,1)S(1)}, bf16[64,256]{1,0:T(8,128)(2,1)S(1)}, u32[]{:S(2)}, u32[]{:S(2)}) %collective-permute-start.51) | collective-permute-done | bytes 32800 | tf_op jit(solution)/shard_map/ppermute | solution.py:19
  160.7 2.5 collective-permute-start.52
  164.3 3.0 collective-permute-done.52.refs_7_
  167.3 2.1 collective-permute-start.37
  169.4 2.3 collective-permute-start.38
  174.8 2.3 add.61
  178.5 3.4 %collective-permute-start.41 = (bf16[64,8,128]{2,1,0:T(8,128)(2,1)S(1)}, bf16[64,8,128]{2,1,0:T(8,128)(2,1)S(1)}, u32[]{:S(2)}, u32[]{:S(2)}) collective-permute-start(bf16[64,8,128]{2,1,0:T(8,128)(2,1)S(1)} %bitcast.171), channel_id=1, source_target_pairs={{0,18},{1,19},{2,16},{3,17},{16,2},{17,3},{18,0},{19,1},{4,22},{5,... | collective-permute-start | bytes 393224 | tf_op jit(solution)/shard_map/ppermute | solution.py:19
  181.9 2.2 collective-permute-start.42
  188.6 9.4 %collective-permute-done.41.refs_6_ = bf16[64,8,128]{2,1,0:T(8,128)(2,1)S(1)} collective-permute-done((bf16[64,8,128]{2,1,0:T(8,128)(2,1)S(1)}, bf16[64,8,128]{2,1,0:T(8,128)(2,1)S(1)}, u32[]{:S(2)}, u32[]{:S(2)}) %collective-permute-start.41) | collective-permute-done | bytes 131104 | tf_op jit(solution)/shard_map/ppermute | solution.py:19
  198.0 2.8 collective-permute-start.13
  200.8 10.3 %collective-permute-start.14 = (bf16[64,16,128]{2,1,0:T(8,128)(2,1)S(1)}, bf16[64,16,128]{2,1,0:T(8,128)(2,1)S(1)}, u32[]{:S(2)}, u32[]{:S(2)}) collective-permute-start(bf16[64,16,128]{2,1,0:T(8,128)(2,1)S(1)} %bitcast.168), channel_id=1, source_target_pairs={{0,18},{1,19},{2,16},{3,17},{16,2},{17,3},{18,0},{19,1},{4,22},{5,... | collective-permute-start | bytes 786440 | tf_op jit(solution)/shard_map/ppermute | solution.py:19
  212.8 6.2 %collective-permute-start.19 = (bf16[64,16,128]{2,1,0:T(8,128)(2,1)}, bf16[64,16,128]{2,1,0:T(8,128)(2,1)S(1)}, u32[]{:S(2)}, u32[]{:S(2)}) collective-permute-start(bf16[64,16,128]{2,1,0:T(8,128)(2,1)} %bitcast.59), channel_id=1, source_target_pairs={{0,19},{1,18},{2,17},{3,16},{16,3},{17,2},{18,1},{19,0},{4,23},{5,... | collective-permute-start | bytes 786440 | tf_op jit(solution)/shard_map/ppermute | solution.py:19
  220.5 14.0 %collective-permute-done.14.refs_1_ = bf16[64,16,128]{2,1,0:T(8,128)(2,1)S(1)} collective-permute-done((bf16[64,16,128]{2,1,0:T(8,128)(2,1)S(1)}, bf16[64,16,128]{2,1,0:T(8,128)(2,1)S(1)}, u32[]{:S(2)}, u32[]{:S(2)}) %collective-permute-start.14) | collective-permute-done | bytes 262176 | tf_op jit(solution)/shard_map/ppermute | solution.py:19
  239.2 4.0 %all-to-all-start.1 = ((bf16[64,8,256]{2,1,0:T(8,128)(2,1)}), bf16[64,8,256]{2,1,0:T(8,128)(2,1)}, u32[]{:S(2)}, u32[]{:S(2)}) async-start(bf16[64,8,256]{2,1,0:T(8,128)(2,1)} %copy.32), calls=%async_computation.1 | async-start | bytes 524288 | tf_op jit(solution)/shard_map/all_to_all | solution.py:417
  244.0 1.8 collective-permute-start.22
  248.0 9.0 %collective-permute-done.20.refs_1_ = bf16[64,16,128]{2,1,0:T(8,128)(2,1)S(1)} collective-permute-done((bf16[64,16,128]{2,1,0:T(8,128)(2,1)}, bf16[64,16,128]{2,1,0:T(8,128)(2,1)S(1)}, u32[]{:S(2)}, u32[]{:S(2)}) %collective-permute-start.20) | collective-permute-done | bytes 262176 | tf_op jit(solution)/shard_map/ppermute | solution.py:19
  257.1 3.1 collective-permute-start.24
  260.2 2.5 join.4
  262.7 4.6 %all-to-all-start = ((bf16[64,8,1024]{2,1,0:T(8,128)(2,1)}), bf16[64,8,1024]{2,1,0:T(8,128)(2,1)}, u32[]{:S(2)}, u32[]{:S(2)}) async-start(bf16[64,8,1024]{2,1,0:T(8,128)(2,1)} %join.4), calls=%async_computation | async-start | bytes 2097152 | tf_op jit(solution)/shard_map/all_to_all | solution.py:417
  270.3 1.7 collective-permute-start.32
  277.5 2.8 collective-permute-start.10
  280.4 1.9 collective-permute-start.12
  289.6 3.0 collective-permute-done.10.refs_1_
  292.6 2.1 collective-permute-done.11.refs_2_
  294.8 3.4 %collective-permute-done.12.refs_3_ = bf16[64,16,128]{2,1,0:T(8,128)(2,1)} collective-permute-done((bf16[64,16,128]{2,1,0:T(8,128)(2,1)}, bf16[64,16,128]{2,1,0:T(8,128)(2,1)}, u32[]{:S(2)}, u32[]{:S(2)}) %collective-permute-start.12) | collective-permute-done | bytes 262176 | tf_op jit(solution)/shard_map/ppermute | solution.py:19
  298.2 2.0 project.5
  304.8 2.1 join.7
  (212 shorter events, 75.2 us)
Async XLA Ops:
  2.9 14.8 %collective-permute-start = (bf16[16,512]{1,0:T(8,128)(2,1)S(1)}, bf16[16,512]{1,0:T(8,128)(2,1)S(1)}, u32[]{:S(2)}, u32[]{:S(2)}) collective-permute-start(bf16[16,512]{1,0:T(8,128)(2,1)S(1)} %multiply_convert_fusion), channel_id=1, source_target_pairs={{0,16},{16,0},{1,17},{17,1},{2,18},{18,2},{3,19},{19,3},{4,20},{20... | collective-permute-start | bytes 49160 | tf_op jit(solution)/shard_map/ppermute | solution.py:19
  17.7 13.6 %collective-permute-start.3 = (bf16[32,512]{1,0:T(8,128)(2,1)S(1)}, bf16[32,512]{1,0:T(8,128)(2,1)S(1)}, u32[]{:S(2)}, u32[]{:S(2)}) collective-permute-start(bf16[32,512]{1,0:T(8,128)(2,1)S(1)} %get-tuple-element.134), channel_id=1, source_target_pairs={{0,3},{1,2},{2,1},{3,0},{4,7},{5,6},{6,5},{7,4},{8,11},{9,10},{10,... | collective-permute-start | bytes 98312 | tf_op jit(solution)/shard_map/ppermute | solution.py:19
  25.7 147.3 %collective-permute-start.29 = (f32[2,96,4096]{2,1,0:T(8,128)}, f32[2,96,4096]{2,1,0:T(8,128)}, u32[]{:S(2)}, u32[]{:S(2)}) collective-permute-start(f32[2,96,4096]{2,1,0:T(8,128)} %bitcast.20), channel_id=1, source_target_pairs={{0,4},{4,0},{8,12},{12,8},{1,5},{5,1},{9,13},{13,9},{2,6},{6,2},{1... | collective-permute-start | bytes 9437192 | tf_op jit(solution)/shard_map/ppermute | solution.py:19
  27.6 18.4 %collective-permute-start.35 = (bf16[128,8,128]{2,1,0:T(8,128)(2,1)}, bf16[128,8,128]{2,1,0:T(8,128)(2,1)}, u32[]{:S(2)}, u32[]{:S(2)}) collective-permute-start(bf16[128,8,128]{2,1,0:T(8,128)(2,1)} %get-tuple-element.58), channel_id=1, source_target_pairs={{0,3},{1,2},{2,1},{3,0},{4,7},{5,6},{6,5},{7,4},{8,11},{9,10},{10,... | collective-permute-start | bytes 786440 | tf_op jit(solution)/shard_map/ppermute | solution.py:19
  31.3 34.7 %collective-permute-start.34 = (bf16[128,8,128]{2,1,0:T(8,128)(2,1)}, bf16[128,8,128]{2,1,0:T(8,128)(2,1)}, u32[]{:S(2)}, u32[]{:S(2)}) collective-permute-start(bf16[128,8,128]{2,1,0:T(8,128)(2,1)} %get-tuple-element.57), channel_id=1, source_target_pairs={{0,2},{1,3},{2,0},{3,1},{4,6},{5,7},{6,4},{7,5},{8,10},{9,11},{10,... | collective-permute-start | bytes 786440 | tf_op jit(solution)/shard_map/ppermute | solution.py:19
  31.3 37.0 %collective-permute-start.33 = (bf16[128,8,128]{2,1,0:T(8,128)(2,1)}, bf16[128,8,128]{2,1,0:T(8,128)(2,1)}, u32[]{:S(2)}, u32[]{:S(2)}) collective-permute-start(bf16[128,8,128]{2,1,0:T(8,128)(2,1)} %get-tuple-element.56), channel_id=1, source_target_pairs={{0,1},{1,0},{2,3},{3,2},{4,5},{5,4},{6,7},{7,6},{8,9},{9,8},{10,11... | collective-permute-start | bytes 786440 | tf_op jit(solution)/shard_map/ppermute | solution.py:19
  35.5 35.1 %collective-permute-start.5 = (bf16[2,128,512]{2,1,0:T(8,128)(2,1)}, bf16[2,128,512]{2,1,0:T(8,128)(2,1)}, u32[]{:S(2)}, u32[]{:S(2)}) collective-permute-start(bf16[2,128,512]{2,1,0:T(8,128)(2,1)} %pad_maximum_fusion.8), channel_id=1, source_target_pairs={{0,8},{4,12},{8,0},{12,4},{1,9},{5,13},{9,1},{13,5},{2,10},{6,14},... | collective-permute-start | bytes 786440 | tf_op jit(solution)/shard_map/ppermute | solution.py:19
  46.1 61.8 %collective-permute-start.8 = (bf16[128,16,128]{2,1,0:T(8,128)(2,1)}, bf16[128,16,128]{2,1,0:T(8,128)(2,1)}, u32[]{:S(2)}, u32[]{:S(2)}) collective-permute-start(bf16[128,16,128]{2,1,0:T(8,128)(2,1)} %copy-done.20), channel_id=1, source_target_pairs={{0,3},{1,2},{2,1},{3,0},{4,7},{5,6},{6,5},{7,4},{8,11},{9,10},{10,... | collective-permute-start | bytes 1572872 | tf_op jit(solution)/shard_map/ppermute | solution.py:19
  66.0 11.8 %collective-permute-start.45 = (bf16[128,256]{1,0:T(8,128)(2,1)}, bf16[128,256]{1,0:T(8,128)(2,1)}, u32[]{:S(2)}, u32[]{:S(2)}) collective-permute-start(bf16[128,256]{1,0:T(8,128)(2,1)} %copy-done.22), channel_id=1, source_target_pairs={{0,3},{1,2},{2,1},{3,0},{4,7},{5,6},{6,5},{7,4},{8,11},{9,10},{10,... | collective-permute-start | bytes 196616 | tf_op jit(solution)/shard_map/ppermute | solution.py:19
  68.3 14.6 %collective-permute-start.44 = (bf16[128,256]{1,0:T(8,128)(2,1)}, bf16[128,256]{1,0:T(8,128)(2,1)}, u32[]{:S(2)}, u32[]{:S(2)}) collective-permute-start(bf16[128,256]{1,0:T(8,128)(2,1)} %copy-done.21), channel_id=1, source_target_pairs={{0,2},{1,3},{2,0},{3,1},{4,6},{5,7},{6,4},{7,5},{8,10},{9,11},{10,... | collective-permute-start | bytes 196616 | tf_op jit(solution)/shard_map/ppermute | solution.py:19
  70.6 12.3 %collective-permute-start.43 = (bf16[128,256]{1,0:T(8,128)(2,1)S(1)}, bf16[128,256]{1,0:T(8,128)(2,1)}, u32[]{:S(2)}, u32[]{:S(2)}) collective-permute-start(bf16[128,256]{1,0:T(8,128)(2,1)S(1)} %get-tuple-element.60), channel_id=1, source_target_pairs={{0,1},{1,0},{2,3},{3,2},{4,5},{5,4},{6,7},{7,6},{8,9},{9,8},{10,11... | collective-permute-start | bytes 196616 | tf_op jit(solution)/shard_map/ppermute | solution.py:19
  77.8 32.5 %collective-permute-start.7 = (bf16[128,16,128]{2,1,0:T(8,128)(2,1)S(1)}, bf16[128,16,128]{2,1,0:T(8,128)(2,1)S(1)}, u32[]{:S(2)}, u32[]{:S(2)}) collective-permute-start(bf16[128,16,128]{2,1,0:T(8,128)(2,1)S(1)} %copy-done.19), channel_id=1, source_target_pairs={{0,2},{1,3},{2,0},{3,1},{4,6},{5,7},{6,4},{7,5},{8,10},{9,11},{10,... | collective-permute-start | bytes 1572872 | tf_op jit(solution)/shard_map/ppermute | solution.py:19
  82.9 27.9 %collective-permute-start.6 = (bf16[128,16,128]{2,1,0:T(8,128)(2,1)S(1)}, bf16[128,16,128]{2,1,0:T(8,128)(2,1)S(1)}, u32[]{:S(2)}, u32[]{:S(2)}) collective-permute-start(bf16[128,16,128]{2,1,0:T(8,128)(2,1)S(1)} %copy-done.17), channel_id=1, source_target_pairs={{0,1},{1,0},{2,3},{3,2},{4,5},{5,4},{6,7},{7,6},{8,9},{9,8},{10,11... | collective-permute-start | bytes 1572872 | tf_op jit(solution)/shard_map/ppermute | solution.py:19
  84.1 22.4 %collective-permute-start.46 = (bf16[64,256]{1,0:T(8,128)(2,1)S(1)}, bf16[64,256]{1,0:T(8,128)(2,1)S(1)}, u32[]{:S(2)}, u32[]{:S(2)}) collective-permute-start(bf16[64,256]{1,0:T(8,128)(2,1)S(1)} %get-tuple-element.129), channel_id=1, source_target_pairs={{0,1},{1,0},{2,3},{3,2},{16,17},{17,16},{18,19},{19,18},{4,5},{5,4... | collective-permute-start | bytes 98312 | tf_op jit(solution)/shard_map/ppermute | solution.py:19
  110.8 13.6 %collective-permute-start.50 = (bf16[64,256]{1,0:T(8,128)(2,1)S(1)}, bf16[64,256]{1,0:T(8,128)(2,1)S(1)}, u32[]{:S(2)}, u32[]{:S(2)}) collective-permute-start(bf16[64,256]{1,0:T(8,128)(2,1)S(1)} %get-tuple-element.125), channel_id=1, source_target_pairs={{0,17},{1,16},{2,19},{3,18},{16,1},{17,0},{18,3},{19,2},{4,21},{5,... | collective-permute-start | bytes 98312 | tf_op jit(solution)/shard_map/ppermute | solution.py:19
  112.8 54.5 %collective-permute-start.18 = (bf16[128,16,128]{2,1,0:T(8,128)(2,1)S(1)}, bf16[128,16,128]{2,1,0:T(8,128)(2,1)S(1)}, u32[]{:S(2)}, u32[]{:S(2)}) collective-permute-start(bf16[128,16,128]{2,1,0:T(8,128)(2,1)S(1)} %get-tuple-element.42), channel_id=1, source_target_pairs={{0,3},{1,2},{2,1},{3,0},{4,7},{5,6},{6,5},{7,4},{8,11},{9,10},{10,... | collective-permute-start | bytes 1572872 | tf_op jit(solution)/shard_map/ppermute | solution.py:19
  114.5 54.9 %collective-permute-start.17 = (bf16[128,16,128]{2,1,0:T(8,128)(2,1)S(1)}, bf16[128,16,128]{2,1,0:T(8,128)(2,1)S(1)}, u32[]{:S(2)}, u32[]{:S(2)}) collective-permute-start(bf16[128,16,128]{2,1,0:T(8,128)(2,1)S(1)} %get-tuple-element.41), channel_id=1, source_target_pairs={{0,2},{1,3},{2,0},{3,1},{4,6},{5,7},{6,4},{7,5},{8,10},{9,11},{10,... | collective-permute-start | bytes 1572872 | tf_op jit(solution)/shard_map/ppermute | solution.py:19
  116.6 55.1 %collective-permute-start.16 = (bf16[128,16,128]{2,1,0:T(8,128)(2,1)S(1)}, bf16[128,16,128]{2,1,0:T(8,128)(2,1)S(1)}, u32[]{:S(2)}, u32[]{:S(2)}) collective-permute-start(bf16[128,16,128]{2,1,0:T(8,128)(2,1)S(1)} %get-tuple-element.40), channel_id=1, source_target_pairs={{0,1},{1,0},{2,3},{3,2},{4,5},{5,4},{6,7},{7,6},{8,9},{9,8},{10,11... | collective-permute-start | bytes 1572872 | tf_op jit(solution)/shard_map/ppermute | solution.py:19
  124.4 36.4 %collective-permute-start.51 = (bf16[64,256]{1,0:T(8,128)(2,1)S(1)}, bf16[64,256]{1,0:T(8,128)(2,1)S(1)}, u32[]{:S(2)}, u32[]{:S(2)}) collective-permute-start(bf16[64,256]{1,0:T(8,128)(2,1)S(1)} %get-tuple-element.124), channel_id=1, source_target_pairs={{0,18},{1,19},{2,16},{3,17},{16,2},{17,3},{18,0},{19,1},{4,22},{5,... | collective-permute-start | bytes 98312 | tf_op jit(solution)/shard_map/ppermute | solution.py:19
  167.3 11.2 %collective-permute-start.36 = (bf16[64,8,128]{2,1,0:T(8,128)(2,1)S(1)}, bf16[64,8,128]{2,1,0:T(8,128)(2,1)S(1)}, u32[]{:S(2)}, u32[]{:S(2)}) collective-permute-start(bf16[64,8,128]{2,1,0:T(8,128)(2,1)S(1)} %bitcast.176), channel_id=1, source_target_pairs={{0,1},{1,0},{2,3},{3,2},{16,17},{17,16},{18,19},{19,18},{4,5},{5,4... | collective-permute-start | bytes 393224 | tf_op jit(solution)/shard_map/ppermute | solution.py:19
  167.3 11.2 %collective-permute-start.37 = (bf16[64,8,128]{2,1,0:T(8,128)(2,1)S(1)}, bf16[64,8,128]{2,1,0:T(8,128)(2,1)S(1)}, u32[]{:S(2)}, u32[]{:S(2)}) collective-permute-start(bf16[64,8,128]{2,1,0:T(8,128)(2,1)S(1)} %bitcast.175), channel_id=1, source_target_pairs={{0,2},{1,3},{2,0},{3,1},{16,18},{17,19},{18,16},{19,17},{4,6},{5,7... | collective-permute-start | bytes 393224 | tf_op jit(solution)/shard_map/ppermute | solution.py:19
  169.4 12.5 %collective-permute-start.38 = (bf16[64,8,128]{2,1,0:T(8,128)(2,1)S(1)}, bf16[64,8,128]{2,1,0:T(8,128)(2,1)S(1)}, u32[]{:S(2)}, u32[]{:S(2)}) collective-permute-start(bf16[64,8,128]{2,1,0:T(8,128)(2,1)S(1)} %bitcast.174), channel_id=1, source_target_pairs={{0,3},{1,2},{2,1},{3,0},{16,19},{17,18},{18,17},{19,16},{4,7},{5,6... | collective-permute-start | bytes 393224 | tf_op jit(solution)/shard_map/ppermute | solution.py:19
  171.7 12.4 %collective-permute-start.39 = (bf16[64,8,128]{2,1,0:T(8,128)(2,1)S(1)}, bf16[64,8,128]{2,1,0:T(8,128)(2,1)S(1)}, u32[]{:S(2)}, u32[]{:S(2)}) collective-permute-start(bf16[64,8,128]{2,1,0:T(8,128)(2,1)S(1)} %bitcast.173), channel_id=1, source_target_pairs={{0,16},{1,17},{2,18},{3,19},{16,0},{17,1},{18,2},{19,3},{4,20},{5,... | collective-permute-start | bytes 393224 | tf_op jit(solution)/shard_map/ppermute | solution.py:19
  172.9 12.8 %collective-permute-start.40 = (bf16[64,8,128]{2,1,0:T(8,128)(2,1)S(1)}, bf16[64,8,128]{2,1,0:T(8,128)(2,1)S(1)}, u32[]{:S(2)}, u32[]{:S(2)}) collective-permute-start(bf16[64,8,128]{2,1,0:T(8,128)(2,1)S(1)} %bitcast.172), channel_id=1, source_target_pairs={{0,17},{1,16},{2,19},{3,18},{16,1},{17,0},{18,3},{19,2},{4,21},{5,... | collective-permute-start | bytes 393224 | tf_op jit(solution)/shard_map/ppermute | solution.py:19
  178.5 81.7 %collective-permute-start.31 = (f32[2,96,1024]{2,1,0:T(8,128)}, f32[2,96,1024]{2,1,0:T(8,128)}, u32[]{:S(2)}, u32[]{:S(2)}) collective-permute-start(f32[2,96,1024]{2,1,0:T(8,128)} %bitcast.23), channel_id=1, source_target_pairs={{0,4},{4,0},{8,12},{12,8},{1,5},{5,1},{9,13},{13,9},{2,6},{6,2},{1... | collective-permute-start | bytes 2359304 | tf_op jit(solution)/shard_map/ppermute | solution.py:19
  178.5 19.5 %collective-permute-start.41 = (bf16[64,8,128]{2,1,0:T(8,128)(2,1)S(1)}, bf16[64,8,128]{2,1,0:T(8,128)(2,1)S(1)}, u32[]{:S(2)}, u32[]{:S(2)}) collective-permute-start(bf16[64,8,128]{2,1,0:T(8,128)(2,1)S(1)} %bitcast.171), channel_id=1, source_target_pairs={{0,18},{1,19},{2,16},{3,17},{16,2},{17,3},{18,0},{19,1},{4,22},{5,... | collective-permute-start | bytes 393224 | tf_op jit(solution)/shard_map/ppermute | solution.py:19
  181.9 18.9 %collective-permute-start.42 = (bf16[64,8,128]{2,1,0:T(8,128)(2,1)S(1)}, bf16[64,8,128]{2,1,0:T(8,128)(2,1)S(1)}, u32[]{:S(2)}, u32[]{:S(2)}) collective-permute-start(bf16[64,8,128]{2,1,0:T(8,128)(2,1)S(1)} %bitcast.170), channel_id=1, source_target_pairs={{0,19},{1,18},{2,17},{3,16},{16,3},{17,2},{18,1},{19,0},{4,23},{5,... | collective-permute-start | bytes 393224 | tf_op jit(solution)/shard_map/ppermute | solution.py:19
  184.2 27.0 %collective-permute-start.9 = (bf16[64,16,128]{2,1,0:T(8,128)(2,1)S(1)}, bf16[64,16,128]{2,1,0:T(8,128)(2,1)S(1)}, u32[]{:S(2)}, u32[]{:S(2)}) collective-permute-start(bf16[64,16,128]{2,1,0:T(8,128)(2,1)S(1)} %bitcast.166), channel_id=1, source_target_pairs={{0,3},{1,2},{2,1},{3,0},{16,19},{17,18},{18,17},{19,16},{4,7},{5,6... | collective-permute-start | bytes 786440 | tf_op jit(solution)/shard_map/ppermute | solution.py:19
  185.7 123.8 %collective-permute-start.30 = (f32[1,96,4096]{2,1,0:T(8,128)}, f32[1,96,4096]{2,1,0:T(8,128)}, u32[]{:S(2)}, u32[]{:S(2)}) collective-permute-start(f32[1,96,4096]{2,1,0:T(8,128)} %slice.227), channel_id=1, source_target_pairs={{0,8},{4,12},{8,0},{12,4},{1,9},{5,13},{9,1},{13,5},{2,10},{6,14},... | collective-permute-start | bytes 4718600 | tf_op jit(solution)/shard_map/ppermute | solution.py:19
  198.0 14.8 %collective-permute-start.13 = (bf16[64,16,128]{2,1,0:T(8,128)(2,1)S(1)}, bf16[64,16,128]{2,1,0:T(8,128)(2,1)S(1)}, u32[]{:S(2)}, u32[]{:S(2)}) collective-permute-start(bf16[64,16,128]{2,1,0:T(8,128)(2,1)S(1)} %bitcast.169), channel_id=1, source_target_pairs={{0,19},{1,18},{2,17},{3,16},{16,3},{17,2},{18,1},{19,0},{4,23},{5,... | collective-permute-start | bytes 786440 | tf_op jit(solution)/shard_map/ppermute | solution.py:19
  200.8 33.7 %collective-permute-start.14 = (bf16[64,16,128]{2,1,0:T(8,128)(2,1)S(1)}, bf16[64,16,128]{2,1,0:T(8,128)(2,1)S(1)}, u32[]{:S(2)}, u32[]{:S(2)}) collective-permute-start(bf16[64,16,128]{2,1,0:T(8,128)(2,1)S(1)} %bitcast.168), channel_id=1, source_target_pairs={{0,18},{1,19},{2,16},{3,17},{16,2},{17,3},{18,0},{19,1},{4,22},{5,... | collective-permute-start | bytes 786440 | tf_op jit(solution)/shard_map/ppermute | solution.py:19
  211.2 24.1 %collective-permute-start.15 = (bf16[64,16,128]{2,1,0:T(8,128)(2,1)S(1)}, bf16[64,16,128]{2,1,0:T(8,128)(2,1)S(1)}, u32[]{:S(2)}, u32[]{:S(2)}) collective-permute-start(bf16[64,16,128]{2,1,0:T(8,128)(2,1)S(1)} %bitcast.167), channel_id=1, source_target_pairs={{0,16},{1,17},{2,18},{3,19},{16,0},{17,1},{18,2},{19,3},{4,20},{5,... | collective-permute-start | bytes 786440 | tf_op jit(solution)/shard_map/ppermute | solution.py:19
  212.8 31.2 %collective-permute-start.19 = (bf16[64,16,128]{2,1,0:T(8,128)(2,1)}, bf16[64,16,128]{2,1,0:T(8,128)(2,1)S(1)}, u32[]{:S(2)}, u32[]{:S(2)}) collective-permute-start(bf16[64,16,128]{2,1,0:T(8,128)(2,1)} %bitcast.59), channel_id=1, source_target_pairs={{0,19},{1,18},{2,17},{3,16},{16,3},{17,2},{18,1},{19,0},{4,23},{5,... | collective-permute-start | bytes 786440 | tf_op jit(solution)/shard_map/ppermute | solution.py:19
  235.3 21.8 %collective-permute-start.20 = (bf16[64,16,128]{2,1,0:T(8,128)(2,1)}, bf16[64,16,128]{2,1,0:T(8,128)(2,1)S(1)}, u32[]{:S(2)}, u32[]{:S(2)}) collective-permute-start(bf16[64,16,128]{2,1,0:T(8,128)(2,1)} %bitcast.61), channel_id=1, source_target_pairs={{0,18},{1,19},{2,16},{3,17},{16,2},{17,3},{18,0},{19,1},{4,22},{5,... | collective-permute-start | bytes 786440 | tf_op jit(solution)/shard_map/ppermute | solution.py:19
  236.0 21.1 %collective-permute-start.21 = (bf16[64,16,128]{2,1,0:T(8,128)(2,1)}, bf16[64,16,128]{2,1,0:T(8,128)(2,1)S(1)}, u32[]{:S(2)}, u32[]{:S(2)}) collective-permute-start(bf16[64,16,128]{2,1,0:T(8,128)(2,1)} %bitcast.63), channel_id=1, source_target_pairs={{0,16},{1,17},{2,18},{3,19},{16,0},{17,1},{18,2},{19,3},{4,20},{5,... | collective-permute-start | bytes 786440 | tf_op jit(solution)/shard_map/ppermute | solution.py:19
  239.2 23.5 %all-to-all-start.1 = ((bf16[64,8,256]{2,1,0:T(8,128)(2,1)}), bf16[64,8,256]{2,1,0:T(8,128)(2,1)}, u32[]{:S(2)}, u32[]{:S(2)}) async-start(bf16[64,8,256]{2,1,0:T(8,128)(2,1)} %copy.32), calls=%async_computation.1 | async-start | bytes 524288 | tf_op jit(solution)/shard_map/all_to_all | solution.py:417
  244.0 26.3 %collective-permute-start.22 = (bf16[64,16,128]{2,1,0:T(8,128)(2,1)}, bf16[64,16,128]{2,1,0:T(8,128)(2,1)S(1)}, u32[]{:S(2)}, u32[]{:S(2)}) collective-permute-start(bf16[64,16,128]{2,1,0:T(8,128)(2,1)} %bitcast.67), channel_id=1, source_target_pairs={{0,3},{1,2},{2,1},{3,0},{16,19},{17,18},{18,17},{19,16},{4,7},{5,6... | collective-permute-start | bytes 786440 | tf_op jit(solution)/shard_map/ppermute | solution.py:19
  257.1 20.4 %collective-permute-start.23 = (bf16[64,16,128]{2,1,0:T(8,128)(2,1)}, bf16[64,16,128]{2,1,0:T(8,128)(2,1)S(1)}, u32[]{:S(2)}, u32[]{:S(2)}) collective-permute-start(bf16[64,16,128]{2,1,0:T(8,128)(2,1)} %bitcast.69), channel_id=1, source_target_pairs={{0,2},{1,3},{2,0},{3,1},{16,18},{17,19},{18,16},{19,17},{4,6},{5,7... | collective-permute-start | bytes 786440 | tf_op jit(solution)/shard_map/ppermute | solution.py:19
  257.1 23.2 %collective-permute-start.24 = (bf16[64,16,128]{2,1,0:T(8,128)(2,1)}, bf16[64,16,128]{2,1,0:T(8,128)(2,1)S(1)}, u32[]{:S(2)}, u32[]{:S(2)}) collective-permute-start(bf16[64,16,128]{2,1,0:T(8,128)(2,1)} %bitcast.71), channel_id=1, source_target_pairs={{0,17},{1,16},{2,19},{3,18},{16,1},{17,0},{18,3},{19,2},{4,21},{5,... | collective-permute-start | bytes 786440 | tf_op jit(solution)/shard_map/ppermute | solution.py:19
  260.2 20.2 %collective-permute-start.25 = (bf16[64,16,128]{2,1,0:T(8,128)(2,1)}, bf16[64,16,128]{2,1,0:T(8,128)(2,1)S(1)}, u32[]{:S(2)}, u32[]{:S(2)}) collective-permute-start(bf16[64,16,128]{2,1,0:T(8,128)(2,1)} %bitcast.73), channel_id=1, source_target_pairs={{0,1},{1,0},{2,3},{3,2},{16,17},{17,16},{18,19},{19,18},{4,5},{5,4... | collective-permute-start | bytes 786440 | tf_op jit(solution)/shard_map/ppermute | solution.py:19
  262.7 45.2 %all-to-all-start = ((bf16[64,8,1024]{2,1,0:T(8,128)(2,1)}), bf16[64,8,1024]{2,1,0:T(8,128)(2,1)}, u32[]{:S(2)}, u32[]{:S(2)}) async-start(bf16[64,8,1024]{2,1,0:T(8,128)(2,1)} %join.4), calls=%async_computation | async-start | bytes 2097152 | tf_op jit(solution)/shard_map/all_to_all | solution.py:417
  270.3 36.6 %collective-permute-start.32 = (f32[1,96,1024]{2,1,0:T(8,128)}, f32[1,96,1024]{2,1,0:T(8,128)}, u32[]{:S(2)}, u32[]{:S(2)}) collective-permute-start(f32[1,96,1024]{2,1,0:T(8,128)} %slice.231), channel_id=1, source_target_pairs={{0,8},{4,12},{8,0},{12,4},{1,9},{5,13},{9,1},{13,5},{2,10},{6,14},... | collective-permute-start | bytes 1179656 | tf_op jit(solution)/shard_map/ppermute | solution.py:19
  277.5 15.2 %collective-permute-start.10 = (bf16[64,16,128]{2,1,0:T(8,128)(2,1)}, bf16[64,16,128]{2,1,0:T(8,128)(2,1)}, u32[]{:S(2)}, u32[]{:S(2)}) collective-permute-start(bf16[64,16,128]{2,1,0:T(8,128)(2,1)} %bitcast.43), channel_id=1, source_target_pairs={{0,2},{1,3},{2,0},{3,1},{16,18},{17,19},{18,16},{19,17},{4,6},{5,7... | collective-permute-start | bytes 786440 | tf_op jit(solution)/shard_map/ppermute | solution.py:19
  280.3 14.5 %collective-permute-start.11 = (bf16[64,16,128]{2,1,0:T(8,128)(2,1)}, bf16[64,16,128]{2,1,0:T(8,128)(2,1)}, u32[]{:S(2)}, u32[]{:S(2)}) collective-permute-start(bf16[64,16,128]{2,1,0:T(8,128)(2,1)} %bitcast.45), channel_id=1, source_target_pairs={{0,17},{1,16},{2,19},{3,18},{16,1},{17,0},{18,3},{19,2},{4,21},{5,... | collective-permute-start | bytes 786440 | tf_op jit(solution)/shard_map/ppermute | solution.py:19
  280.4 17.8 %collective-permute-start.12 = (bf16[64,16,128]{2,1,0:T(8,128)(2,1)}, bf16[64,16,128]{2,1,0:T(8,128)(2,1)}, u32[]{:S(2)}, u32[]{:S(2)}) collective-permute-start(bf16[64,16,128]{2,1,0:T(8,128)(2,1)} %bitcast.47), channel_id=1, source_target_pairs={{0,1},{1,0},{2,3},{3,2},{16,17},{17,16},{18,19},{19,18},{4,5},{5,4... | collective-permute-start | bytes 786440 | tf_op jit(solution)/shard_map/ppermute | solution.py:19
  300.1 12.6 %collective-permute-start.26 = (f32[16,96]{1,0:T(8,128)S(1)}, f32[16,96]{1,0:T(8,128)S(1)}, u32[]{:S(2)}, u32[]{:S(2)}) collective-permute-start(f32[16,96]{1,0:T(8,128)S(1)} %get-tuple-element.52), channel_id=1, source_target_pairs={{0,4},{4,0},{8,12},{12,8},{1,5},{5,1},{9,13},{13,9},{2,6},{6,2},{1... | collective-permute-start | bytes 18440 | tf_op jit(solution)/shard_map/ppermute | solution.py:19
  300.2 12.6 %collective-permute-start.27 = (f32[16,96]{1,0:T(8,128)S(1)}, f32[16,96]{1,0:T(8,128)S(1)}, u32[]{:S(2)}, u32[]{:S(2)}) collective-permute-start(f32[16,96]{1,0:T(8,128)S(1)} %get-tuple-element.53), channel_id=1, source_target_pairs={{0,8},{4,12},{8,0},{12,4},{1,9},{5,13},{9,1},{13,5},{2,10},{6,14},... | collective-permute-start | bytes 18440 | tf_op jit(solution)/shard_map/ppermute | solution.py:19
  300.7 12.1 %collective-permute-start.28 = (f32[16,96]{1,0:T(8,128)S(1)}, f32[16,96]{1,0:T(8,128)S(1)}, u32[]{:S(2)}, u32[]{:S(2)}) collective-permute-start(f32[16,96]{1,0:T(8,128)S(1)} %get-tuple-element.54), channel_id=1, source_target_pairs={{0,12},{4,8},{8,4},{12,0},{1,13},{5,9},{9,5},{13,1},{2,14},{6,10},... | collective-permute-start | bytes 18440 | tf_op jit(solution)/shard_map/ppermute | solution.py:19
  (41 other events, 189.4 us)

commit v4 on v3

--- a/solution.py
+++ b/solution.py
@@ -342,15 +342,15 @@
         "down": Head(down_factor_head, 2),
     }
 
-    def fetch(name, chunk):
-        pieces = heads[name].cut(chunk, ring_shifts)
-        got = {0: pieces[0]}
-        for s in far_first:
-            got[s] = swap(pieces[s], "task", s)
+    def fetch(name, chunk, cuts):
+        got = {}
+        for cut_shifts in cuts:
+            for s, piece in zip(cut_shifts, heads[name].cut(chunk, cut_shifts)):
+                got[s] = swap(piece, "task", s) if s else piece
         return jnp.concatenate([got[s] for s in ring_shifts], axis=0)
 
     fetched = {}
-    fetched["query", 0] = fetch("query", 0)
+    fetched["query", 0] = fetch("query", 0, [far_first[: ring // 2], far_first[ring // 2 :] + [0]])
 
     share = own_tasks // parts
     embeddings = lax.dynamic_index_in_dim(
@@ -359,13 +359,13 @@
     hidden = jax.nn.silu(
         jnp.dot(embeddings, embedding_weight, preferred_element_type=jnp.float32)
     ).astype(jnp.bfloat16)
-    group_hidden = jnp.concatenate([hidden] + [swap(hidden, "groups", s) for s in range(1, groups)])
-    ring_hidden = jnp.stack(
-        [group_hidden] + [swap(group_hidden, "task", s) for s in ring_shifts[1:]]
+    ring_hidden = jnp.stack([hidden] + [swap(hidden, "task", s) for s in ring_shifts[1:]])
+    group_hidden = jnp.concatenate(
+        [ring_hidden] + [swap(ring_hidden, "groups", s) for s in range(1, groups)]
     )
-    every_hidden = gather_blocks(ring_hidden.reshape(places * share, -1), "tensor")
-    every_hidden = every_hidden.reshape(parts, ring, groups, share, ring, hidden_rows)
-    every_hidden = every_hidden.transpose(4, 2, 1, 0, 3, 5)
+    every_hidden = gather_blocks(group_hidden.reshape(places * share, -1), "tensor")
+    every_hidden = every_hidden.reshape(parts, places, share, ring, hidden_rows)
+    every_hidden = every_hidden.transpose(3, 1, 0, 2, 4)
     every_hidden = every_hidden.reshape(ring, places * own_tasks, hidden_rows)
     every_hidden = jnp.concatenate(
         [
@@ -377,8 +377,8 @@
 
     chunks = heads["down"].chunks
     for chunk in range(chunks):
-        fetched["down", chunk] = fetch("down", chunk)
-    fetched["value", 0] = fetch("value", 0)
+        fetched["down", chunk] = fetch("down", chunk, [far_first + [0]])
+    fetched["value", 0] = fetch("value", 0, [far_first + [0]])
 
     def emit(name, chunk):
         matrix = fetched[name, chunk]

time: 316 us -> 315 us (level)
  waiting for transfers between devices: 122 us -> 115 us
  starting transfers between devices: 97.8 us -> 103 us
    ppermute x53, waiting for transfers between devices: 122 us -> 115 us  [swap(): return lax.ppermute(x, axes, [(a, a ^ shift) for a in range(total)])]
    ppermute x53, starting transfers between devices: 89.2 us -> 94.4 us  [swap(): return lax.ppermute(x, axes, [(a, a ^ shift) for a in range(total)])]
    pallas_call x3 -> x4, Pallas kernels: 5.57 us -> 7.2 us  [cut(): pl.pallas_call(functools.partial(cut_kernel, shifts, stride, start, width...]
    unnamed x95 -> x98, local copies, waits for them, and re-layouts: 27.8 us -> 27.8 us
  transfers between devices with their start and end apart: 55 -> 55, of which waited for: 11 -> 13; matrix products, arithmetic and copies ran while one was open for 19% -> 19% of each run, Pallas kernels for 6% -> 6%
where the time goes in v4:
time: 315 us; the launch traced here: 314 us
  waiting for transfers between devices  115 us (37%)
  starting transfers between devices  103 us (33%)
  local copies, waits for them, and re-layouts  42.7 us (14%)
  Pallas kernels  21.4 us (7%)
  matrix products  17.5 us (6%)
  other arithmetic  12.9 us (4%)
    ppermute x53, waiting for transfers between devices, swap(): return lax.ppermute(x, axes, [(a, a ^ shift) for a in range(total)])  115 us
    ppermute x53, starting transfers between devices, swap(): return lax.ppermute(x, axes, [(a, a ^ shift) for a in range(total)])  94.4 us
    unnamed x98, local copies, waits for them, and re-layouts  27.8 us
    dot_general x1, matrix products, local(): base_query = jnp.dot(turned, w_query, preferred_element_type=jnp.float32)  10.2 us
    all_to_all x2, starting transfers between devices, own_block(): lax.all_to_all(factors, 'tensor', split_axis=0, concat_axis=0, tiled=True)  8.7 us
    pallas_call x4, Pallas kernels, join(): pl.pallas_call(functools.partial(join_kernel, shifts, stride, start, widt...  7.24 us
    pallas_call x4, Pallas kernels, cut(): pl.pallas_call(functools.partial(cut_kernel, shifts, stride, start, width...  7.2 us
    slice x4, local copies, waits for them, and re-layouts, reduce_blocks(): came = swap(partial[half:], axis, step)  6.5 us
  transfers between devices with their start and end apart: 55, of which 13 were waited for; matrix products, arithmetic and copies ran while one was open for 19% of the time, Pallas kernels for 6%

profile of v4, /device:TPU:0, one launch (start us, length us, event | category | flops | bytes accessed | tf_op | source)
XLA Modules:
  0.0 314.0 jit_solution(12246787386089362158)
XLA Ops:
  2.9 3.1 collective-permute-start
  6.0 2.6 collective-permute-start.1
  10.1 10.2 %fusion.9 = f32[384,4096]{1,0:T(8,128)S(1)} fusion(bf16[2048,4096]{1,0:T(8,128)(2,1)} %param.16, bf16[96,2048]{1,0:T(8,128)(2,1)S(1)} %get-tuple-element.106, bf16[96,2048]{1,0:T(8,128)(2,1)S(1)} %get-tuple-element.107, bf16[96,2048]{1,0:T(8,128)(2,1)S(1)} %get-tuple-element.108, bf16[96,2048]{1,0:T(8,128)(2,1)S(1)} %get-tuple-element.105), kind=kOutput, calls=%fused_computation.25 | convolution fusion | flops 6448742400 | bytes 24641536 | tf_op jit(solution)/shard_map/dot_general | solution.py:411
  20.3 3.1 fusion.26
  23.4 1.9 cut.7
  25.3 3.9 %collective-permute-start.35 = (bf16[128,8,128]{2,1,0:T(8,128)(2,1)}, bf16[128,8,128]{2,1,0:T(8,128)(2,1)}, u32[]{:S(2)}, u32[]{:S(2)}) collective-permute-start(bf16[128,8,128]{2,1,0:T(8,128)(2,1)} %get-tuple-element.58), channel_id=1, source_target_pairs={{0,3},{1,2},{2,1},{3,0},{4,7},{5,6},{6,5},{7,4},{8,11},{9,10},{10,... | collective-permute-start | bytes 786440 | tf_op jit(solution)/shard_map/ppermute | solution.py:19
  31.6 1.8 collective-permute-start.3
  33.4 2.5 collective-permute-done.3
  35.9 1.8 fusion.8
  46.3 1.9 cut.5
  49.9 3.6 %collective-permute-start.8 = (bf16[128,16,128]{2,1,0:T(8,128)(2,1)}, bf16[128,16,128]{2,1,0:T(8,128)(2,1)}, u32[]{:S(2)}, u32[]{:S(2)}) collective-permute-start(bf16[128,16,128]{2,1,0:T(8,128)(2,1)} %copy-done.20), channel_id=1, source_target_pairs={{0,3},{1,2},{2,1},{3,0},{4,7},{5,6},{6,5},{7,4},{8,11},{9,10},{10,... | collective-permute-start | bytes 1572872 | tf_op jit(solution)/shard_map/ppermute | solution.py:19
  54.1 2.2 pad_maximum_fusion.3
  56.3 3.8 %collective-permute-start.43 = (bf16[128,256]{1,0:T(8,128)(2,1)S(1)}, bf16[128,256]{1,0:T(8,128)(2,1)}, u32[]{:S(2)}, u32[]{:S(2)}) collective-permute-start(bf16[128,256]{1,0:T(8,128)(2,1)S(1)} %get-tuple-element.60), channel_id=1, source_target_pairs={{0,1},{1,0},{2,3},{3,2},{4,5},{5,4},{6,7},{7,6},{8,9},{9,8},{10,11... | collective-permute-start | bytes 196616 | tf_op jit(solution)/shard_map/ppermute | solution.py:19
  62.1 2.0 reshape.154
  65.3 3.1 collective-permute-done.45
  68.4 14.2 %collective-permute-start.7 = (bf16[128,16,128]{2,1,0:T(8,128)(2,1)S(1)}, bf16[128,16,128]{2,1,0:T(8,128)(2,1)S(1)}, u32[]{:S(2)}, u32[]{:S(2)}) collective-permute-start(bf16[128,16,128]{2,1,0:T(8,128)(2,1)S(1)} %copy-done.19), channel_id=1, source_target_pairs={{0,2},{1,3},{2,0},{3,1},{4,6},{5,7},{6,4},{7,5},{8,10},{9,11},{10,... | collective-permute-start | bytes 1572872 | tf_op jit(solution)/shard_map/ppermute | solution.py:19
  83.8 2.1 collective-permute-start.46
  86.9 18.5 %collective-permute-done.46.refs_1_ = bf16[64,256]{1,0:T(8,128)(2,1)S(1)} collective-permute-done((bf16[64,256]{1,0:T(8,128)(2,1)S(1)}, bf16[64,256]{1,0:T(8,128)(2,1)S(1)}, u32[]{:S(2)}, u32[]{:S(2)}) %collective-permute-start.46) | collective-permute-done | bytes 32800 | tf_op jit(solution)/shard_map/ppermute | solution.py:19
  107.1 2.3 collective-permute-start.48
  113.8 1.9 collective-permute-start.17
  116.7 5.9 %collective-permute-done.50.refs_5_ = bf16[64,256]{1,0:T(8,128)(2,1)S(1)} collective-permute-done((bf16[64,256]{1,0:T(8,128)(2,1)S(1)}, bf16[64,256]{1,0:T(8,128)(2,1)S(1)}, u32[]{:S(2)}, u32[]{:S(2)}) %collective-permute-start.50) | collective-permute-done | bytes 32800 | tf_op jit(solution)/shard_map/ppermute | solution.py:19
  123.9 36.2 %collective-permute-done.51.refs_6_ = bf16[64,256]{1,0:T(8,128)(2,1)S(1)} collective-permute-done((bf16[64,256]{1,0:T(8,128)(2,1)S(1)}, bf16[64,256]{1,0:T(8,128)(2,1)S(1)}, u32[]{:S(2)}, u32[]{:S(2)}) %collective-permute-start.51) | collective-permute-done | bytes 32800 | tf_op jit(solution)/shard_map/ppermute | solution.py:19
  160.1 2.1 collective-permute-start.52
  163.3 3.4 %collective-permute-done.52.refs_7_ = bf16[64,256]{1,0:T(8,128)(2,1)S(1)} collective-permute-done((bf16[64,256]{1,0:T(8,128)(2,1)S(1)}, bf16[64,256]{1,0:T(8,128)(2,1)S(1)}, u32[]{:S(2)}, u32[]{:S(2)}) %collective-permute-start.52) | collective-permute-done | bytes 32800 | tf_op jit(solution)/shard_map/ppermute | solution.py:19
  166.7 2.3 collective-permute-start.37
  169.1 2.0 collective-permute-start.38
  173.7 2.3 add.61
  178.4 2.5 collective-permute-start.41
  180.9 2.7 collective-permute-start.42
  183.6 1.8 collective-permute-start.9
  187.3 10.5 %collective-permute-done.41.refs_6_ = bf16[64,8,128]{2,1,0:T(8,128)(2,1)S(1)} collective-permute-done((bf16[64,8,128]{2,1,0:T(8,128)(2,1)S(1)}, bf16[64,8,128]{2,1,0:T(8,128)(2,1)S(1)}, u32[]{:S(2)}, u32[]{:S(2)}) %collective-permute-start.41) | collective-permute-done | bytes 131104 | tf_op jit(solution)/shard_map/ppermute | solution.py:19
  197.8 1.8 collective-permute-start.13
  199.6 11.6 %collective-permute-start.14 = (bf16[64,16,128]{2,1,0:T(8,128)(2,1)S(1)}, bf16[64,16,128]{2,1,0:T(8,128)(2,1)S(1)}, u32[]{:S(2)}, u32[]{:S(2)}) collective-permute-start(bf16[64,16,128]{2,1,0:T(8,128)(2,1)S(1)} %bitcast.171), channel_id=1, source_target_pairs={{0,18},{1,19},{2,16},{3,17},{16,2},{17,3},{18,0},{19,1},{4,22},{5,... | collective-permute-start | bytes 786440 | tf_op jit(solution)/shard_map/ppermute | solution.py:19
  213.0 4.3 %collective-permute-start.19 = (bf16[64,16,128]{2,1,0:T(8,128)(2,1)}, bf16[64,16,128]{2,1,0:T(8,128)(2,1)S(1)}, u32[]{:S(2)}, u32[]{:S(2)}) collective-permute-start(bf16[64,16,128]{2,1,0:T(8,128)(2,1)} %bitcast.59), channel_id=1, source_target_pairs={{0,19},{1,18},{2,17},{3,16},{16,3},{17,2},{18,1},{19,0},{4,23},{5,... | collective-permute-start | bytes 786440 | tf_op jit(solution)/shard_map/ppermute | solution.py:19
  218.8 15.6 %collective-permute-done.14.refs_1_ = bf16[64,16,128]{2,1,0:T(8,128)(2,1)S(1)} collective-permute-done((bf16[64,16,128]{2,1,0:T(8,128)(2,1)S(1)}, bf16[64,16,128]{2,1,0:T(8,128)(2,1)S(1)}, u32[]{:S(2)}, u32[]{:S(2)}) %collective-permute-start.14) | collective-permute-done | bytes 262176 | tf_op jit(solution)/shard_map/ppermute | solution.py:19
  237.8 4.0 %all-to-all-start.1 = ((bf16[64,8,256]{2,1,0:T(8,128)(2,1)}), bf16[64,8,256]{2,1,0:T(8,128)(2,1)}, u32[]{:S(2)}, u32[]{:S(2)}) async-start(bf16[64,8,256]{2,1,0:T(8,128)(2,1)} %copy.32), calls=%async_computation.1 | async-start | bytes 524288 | tf_op jit(solution)/shard_map/all_to_all | solution.py:417
  242.6 2.0 collective-permute-start.22
  246.9 9.7 %collective-permute-done.20.refs_1_ = bf16[64,16,128]{2,1,0:T(8,128)(2,1)S(1)} collective-permute-done((bf16[64,16,128]{2,1,0:T(8,128)(2,1)}, bf16[64,16,128]{2,1,0:T(8,128)(2,1)S(1)}, u32[]{:S(2)}, u32[]{:S(2)}) %collective-permute-start.20) | collective-permute-done | bytes 262176 | tf_op jit(solution)/shard_map/ppermute | solution.py:19
  256.6 2.7 collective-permute-start.24
  259.3 2.5 join.4
  261.8 4.7 %all-to-all-start = ((bf16[64,8,1024]{2,1,0:T(8,128)(2,1)}), bf16[64,8,1024]{2,1,0:T(8,128)(2,1)}, u32[]{:S(2)}, u32[]{:S(2)}) async-start(bf16[64,8,1024]{2,1,0:T(8,128)(2,1)} %join.4), calls=%async_computation | async-start | bytes 2097152 | tf_op jit(solution)/shard_map/all_to_all | solution.py:417
  269.3 3.2 %collective-permute-start.32 = (f32[1,96,1024]{2,1,0:T(8,128)}, f32[1,96,1024]{2,1,0:T(8,128)}, u32[]{:S(2)}, u32[]{:S(2)}) collective-permute-start(f32[1,96,1024]{2,1,0:T(8,128)} %slice.231), channel_id=1, source_target_pairs={{0,8},{4,12},{8,0},{12,4},{1,9},{5,13},{9,1},{13,5},{2,10},{6,14},... | collective-permute-start | bytes 1179656 | tf_op jit(solution)/shard_map/ppermute | solution.py:19
  278.0 2.6 collective-permute-start.10
  289.1 2.7 collective-permute-done.10.refs_1_
  291.8 3.3 %collective-permute-done.11.refs_2_ = bf16[64,16,128]{2,1,0:T(8,128)(2,1)} collective-permute-done((bf16[64,16,128]{2,1,0:T(8,128)(2,1)}, bf16[64,16,128]{2,1,0:T(8,128)(2,1)}, u32[]{:S(2)}, u32[]{:S(2)}) %collective-permute-start.11) | collective-permute-done | bytes 262176 | tf_op jit(solution)/shard_map/ppermute | solution.py:19
  295.1 2.4 collective-permute-done.12.refs_3_
  297.5 1.9 project.5
  304.1 2.1 join.7
  (216 shorter events, 77.3 us)
Async XLA Ops:
  2.9 28.0 %collective-permute-start = (bf16[16,512]{1,0:T(8,128)(2,1)S(1)}, bf16[16,512]{1,0:T(8,128)(2,1)S(1)}, u32[]{:S(2)}, u32[]{:S(2)}) collective-permute-start(bf16[16,512]{1,0:T(8,128)(2,1)S(1)} %get-tuple-element.134), channel_id=1, source_target_pairs={{0,1},{1,0},{2,3},{3,2},{4,5},{5,4},{6,7},{7,6},{8,9},{9,8},{10,11... | collective-permute-start | bytes 49160 | tf_op jit(solution)/shard_map/ppermute | solution.py:19
  6.0 25.0 %collective-permute-start.1 = (bf16[16,512]{1,0:T(8,128)(2,1)S(1)}, bf16[16,512]{1,0:T(8,128)(2,1)S(1)}, u32[]{:S(2)}, u32[]{:S(2)}) collective-permute-start(bf16[16,512]{1,0:T(8,128)(2,1)S(1)} %get-tuple-element.134), channel_id=1, source_target_pairs={{0,2},{1,3},{2,0},{3,1},{4,6},{5,7},{6,4},{7,5},{8,10},{9,11},{10,... | collective-permute-start | bytes 49160 | tf_op jit(solution)/shard_map/ppermute | solution.py:19
  8.6 23.0 %collective-permute-start.2 = (bf16[16,512]{1,0:T(8,128)(2,1)S(1)}, bf16[16,512]{1,0:T(8,128)(2,1)S(1)}, u32[]{:S(2)}, u32[]{:S(2)}) collective-permute-start(bf16[16,512]{1,0:T(8,128)(2,1)S(1)} %get-tuple-element.134), channel_id=1, source_target_pairs={{0,3},{1,2},{2,1},{3,0},{4,7},{5,6},{6,5},{7,4},{8,11},{9,10},{10,... | collective-permute-start | bytes 49160 | tf_op jit(solution)/shard_map/ppermute | solution.py:19
  23.4 148.5 %collective-permute-start.29 = (f32[2,96,4096]{2,1,0:T(8,128)}, f32[2,96,4096]{2,1,0:T(8,128)}, u32[]{:S(2)}, u32[]{:S(2)}) collective-permute-start(f32[2,96,4096]{2,1,0:T(8,128)} %bitcast.20), channel_id=1, source_target_pairs={{0,4},{4,0},{8,12},{12,8},{1,5},{5,1},{9,13},{13,9},{2,6},{6,2},{1... | collective-permute-start | bytes 9437192 | tf_op jit(solution)/shard_map/ppermute | solution.py:19
  25.3 24.6 %collective-permute-start.35 = (bf16[128,8,128]{2,1,0:T(8,128)(2,1)}, bf16[128,8,128]{2,1,0:T(8,128)(2,1)}, u32[]{:S(2)}, u32[]{:S(2)}) collective-permute-start(bf16[128,8,128]{2,1,0:T(8,128)(2,1)} %get-tuple-element.58), channel_id=1, source_target_pairs={{0,3},{1,2},{2,1},{3,0},{4,7},{5,6},{6,5},{7,4},{8,11},{9,10},{10,... | collective-permute-start | bytes 786440 | tf_op jit(solution)/shard_map/ppermute | solution.py:19
  30.9 22.6 %collective-permute-start.34 = (bf16[128,8,128]{2,1,0:T(8,128)(2,1)}, bf16[128,8,128]{2,1,0:T(8,128)(2,1)}, u32[]{:S(2)}, u32[]{:S(2)}) collective-permute-start(bf16[128,8,128]{2,1,0:T(8,128)(2,1)} %get-tuple-element.57), channel_id=1, source_target_pairs={{0,2},{1,3},{2,0},{3,1},{4,6},{5,7},{6,4},{7,5},{8,10},{9,11},{10,... | collective-permute-start | bytes 786440 | tf_op jit(solution)/shard_map/ppermute | solution.py:19
  31.0 22.9 %collective-permute-start.33 = (bf16[128,8,128]{2,1,0:T(8,128)(2,1)}, bf16[128,8,128]{2,1,0:T(8,128)(2,1)}, u32[]{:S(2)}, u32[]{:S(2)}) collective-permute-start(bf16[128,8,128]{2,1,0:T(8,128)(2,1)} %get-tuple-element.56), channel_id=1, source_target_pairs={{0,1},{1,0},{2,3},{3,2},{4,5},{5,4},{6,7},{7,6},{8,9},{9,8},{10,11... | collective-permute-start | bytes 786440 | tf_op jit(solution)/shard_map/ppermute | solution.py:19
  39.2 17.1 %collective-permute-start.5 = (bf16[2,128,512]{2,1,0:T(8,128)(2,1)}, bf16[2,128,512]{2,1,0:T(8,128)(2,1)}, u32[]{:S(2)}, u32[]{:S(2)}) collective-permute-start(bf16[2,128,512]{2,1,0:T(8,128)(2,1)} %pad_maximum_fusion.8), channel_id=1, source_target_pairs={{0,8},{4,12},{8,0},{12,4},{1,9},{5,13},{9,1},{13,5},{2,10},{6,14},... | collective-permute-start | bytes 786440 | tf_op jit(solution)/shard_map/ppermute | solution.py:19
  49.9 57.2 %collective-permute-start.8 = (bf16[128,16,128]{2,1,0:T(8,128)(2,1)}, bf16[128,16,128]{2,1,0:T(8,128)(2,1)}, u32[]{:S(2)}, u32[]{:S(2)}) collective-permute-start(bf16[128,16,128]{2,1,0:T(8,128)(2,1)} %copy-done.20), channel_id=1, source_target_pairs={{0,3},{1,2},{2,1},{3,0},{4,7},{5,6},{6,5},{7,4},{8,11},{9,10},{10,... | collective-permute-start | bytes 1572872 | tf_op jit(solution)/shard_map/ppermute | solution.py:19
  53.5 14.9 %collective-permute-start.45 = (bf16[128,256]{1,0:T(8,128)(2,1)}, bf16[128,256]{1,0:T(8,128)(2,1)}, u32[]{:S(2)}, u32[]{:S(2)}) collective-permute-start(bf16[128,256]{1,0:T(8,128)(2,1)} %copy-done.22), channel_id=1, source_target_pairs={{0,3},{1,2},{2,1},{3,0},{4,7},{5,6},{6,5},{7,4},{8,11},{9,10},{10,... | collective-permute-start | bytes 196616 | tf_op jit(solution)/shard_map/ppermute | solution.py:19
  53.9 28.6 %collective-permute-start.44 = (bf16[128,256]{1,0:T(8,128)(2,1)}, bf16[128,256]{1,0:T(8,128)(2,1)}, u32[]{:S(2)}, u32[]{:S(2)}) collective-permute-start(bf16[128,256]{1,0:T(8,128)(2,1)} %copy-done.21), channel_id=1, source_target_pairs={{0,2},{1,3},{2,0},{3,1},{4,6},{5,7},{6,4},{7,5},{8,10},{9,11},{10,... | collective-permute-start | bytes 196616 | tf_op jit(solution)/shard_map/ppermute | solution.py:19
  56.3 26.3 %collective-permute-start.43 = (bf16[128,256]{1,0:T(8,128)(2,1)S(1)}, bf16[128,256]{1,0:T(8,128)(2,1)}, u32[]{:S(2)}, u32[]{:S(2)}) collective-permute-start(bf16[128,256]{1,0:T(8,128)(2,1)S(1)} %get-tuple-element.60), channel_id=1, source_target_pairs={{0,1},{1,0},{2,3},{3,2},{4,5},{5,4},{6,7},{7,6},{8,9},{9,8},{10,11... | collective-permute-start | bytes 196616 | tf_op jit(solution)/shard_map/ppermute | solution.py:19
  68.4 41.0 %collective-permute-start.7 = (bf16[128,16,128]{2,1,0:T(8,128)(2,1)S(1)}, bf16[128,16,128]{2,1,0:T(8,128)(2,1)S(1)}, u32[]{:S(2)}, u32[]{:S(2)}) collective-permute-start(bf16[128,16,128]{2,1,0:T(8,128)(2,1)S(1)} %copy-done.19), channel_id=1, source_target_pairs={{0,2},{1,3},{2,0},{3,1},{4,6},{5,7},{6,4},{7,5},{8,10},{9,11},{10,... | collective-permute-start | bytes 1572872 | tf_op jit(solution)/shard_map/ppermute | solution.py:19
  82.6 28.3 %collective-permute-start.6 = (bf16[128,16,128]{2,1,0:T(8,128)(2,1)S(1)}, bf16[128,16,128]{2,1,0:T(8,128)(2,1)S(1)}, u32[]{:S(2)}, u32[]{:S(2)}) collective-permute-start(bf16[128,16,128]{2,1,0:T(8,128)(2,1)S(1)} %copy-done.17), channel_id=1, source_target_pairs={{0,1},{1,0},{2,3},{3,2},{4,5},{5,4},{6,7},{7,6},{8,9},{9,8},{10,11... | collective-permute-start | bytes 1572872 | tf_op jit(solution)/shard_map/ppermute | solution.py:19
  83.8 21.5 %collective-permute-start.46 = (bf16[64,256]{1,0:T(8,128)(2,1)S(1)}, bf16[64,256]{1,0:T(8,128)(2,1)S(1)}, u32[]{:S(2)}, u32[]{:S(2)}) collective-permute-start(bf16[64,256]{1,0:T(8,128)(2,1)S(1)} %get-tuple-element.129), channel_id=1, source_target_pairs={{0,1},{1,0},{2,3},{3,2},{16,17},{17,16},{18,19},{19,18},{4,5},{5,4... | collective-permute-start | bytes 98312 | tf_op jit(solution)/shard_map/ppermute | solution.py:19
  110.9 11.7 %collective-permute-start.50 = (bf16[64,256]{1,0:T(8,128)(2,1)S(1)}, bf16[64,256]{1,0:T(8,128)(2,1)S(1)}, u32[]{:S(2)}, u32[]{:S(2)}) collective-permute-start(bf16[64,256]{1,0:T(8,128)(2,1)S(1)} %get-tuple-element.125), channel_id=1, source_target_pairs={{0,17},{1,16},{2,19},{3,18},{16,1},{17,0},{18,3},{19,2},{4,21},{5,... | collective-permute-start | bytes 98312 | tf_op jit(solution)/shard_map/ppermute | solution.py:19
  112.2 54.5 %collective-permute-start.18 = (bf16[128,16,128]{2,1,0:T(8,128)(2,1)S(1)}, bf16[128,16,128]{2,1,0:T(8,128)(2,1)S(1)}, u32[]{:S(2)}, u32[]{:S(2)}) collective-permute-start(bf16[128,16,128]{2,1,0:T(8,128)(2,1)S(1)} %get-tuple-element.42), channel_id=1, source_target_pairs={{0,3},{1,2},{2,1},{3,0},{4,7},{5,6},{6,5},{7,4},{8,11},{9,10},{10,... | collective-permute-start | bytes 1572872 | tf_op jit(solution)/shard_map/ppermute | solution.py:19
  113.8 55.2 %collective-permute-start.17 = (bf16[128,16,128]{2,1,0:T(8,128)(2,1)S(1)}, bf16[128,16,128]{2,1,0:T(8,128)(2,1)S(1)}, u32[]{:S(2)}, u32[]{:S(2)}) collective-permute-start(bf16[128,16,128]{2,1,0:T(8,128)(2,1)S(1)} %get-tuple-element.41), channel_id=1, source_target_pairs={{0,2},{1,3},{2,0},{3,1},{4,6},{5,7},{6,4},{7,5},{8,10},{9,11},{10,... | collective-permute-start | bytes 1572872 | tf_op jit(solution)/shard_map/ppermute | solution.py:19
  115.7 55.4 %collective-permute-start.16 = (bf16[128,16,128]{2,1,0:T(8,128)(2,1)S(1)}, bf16[128,16,128]{2,1,0:T(8,128)(2,1)S(1)}, u32[]{:S(2)}, u32[]{:S(2)}) collective-permute-start(bf16[128,16,128]{2,1,0:T(8,128)(2,1)S(1)} %get-tuple-element.40), channel_id=1, source_target_pairs={{0,1},{1,0},{2,3},{3,2},{4,5},{5,4},{6,7},{7,6},{8,9},{9,8},{10,11... | collective-permute-start | bytes 1572872 | tf_op jit(solution)/shard_map/ppermute | solution.py:19
  122.6 37.5 %collective-permute-start.51 = (bf16[64,256]{1,0:T(8,128)(2,1)S(1)}, bf16[64,256]{1,0:T(8,128)(2,1)S(1)}, u32[]{:S(2)}, u32[]{:S(2)}) collective-permute-start(bf16[64,256]{1,0:T(8,128)(2,1)S(1)} %get-tuple-element.124), channel_id=1, source_target_pairs={{0,18},{1,19},{2,16},{3,17},{16,2},{17,3},{18,0},{19,1},{4,22},{5,... | collective-permute-start | bytes 98312 | tf_op jit(solution)/shard_map/ppermute | solution.py:19
  166.7 11.6 %collective-permute-start.37 = (bf16[64,8,128]{2,1,0:T(8,128)(2,1)S(1)}, bf16[64,8,128]{2,1,0:T(8,128)(2,1)S(1)}, u32[]{:S(2)}, u32[]{:S(2)}) collective-permute-start(bf16[64,8,128]{2,1,0:T(8,128)(2,1)S(1)} %bitcast.180), channel_id=1, source_target_pairs={{0,2},{1,3},{2,0},{3,1},{16,18},{17,19},{18,16},{19,17},{4,6},{5,7... | collective-permute-start | bytes 393224 | tf_op jit(solution)/shard_map/ppermute | solution.py:19
  169.1 11.8 %collective-permute-start.38 = (bf16[64,8,128]{2,1,0:T(8,128)(2,1)S(1)}, bf16[64,8,128]{2,1,0:T(8,128)(2,1)S(1)}, u32[]{:S(2)}, u32[]{:S(2)}) collective-permute-start(bf16[64,8,128]{2,1,0:T(8,128)(2,1)S(1)} %bitcast.179), channel_id=1, source_target_pairs={{0,3},{1,2},{2,1},{3,0},{16,19},{17,18},{18,17},{19,16},{4,7},{5,6... | collective-permute-start | bytes 393224 | tf_op jit(solution)/shard_map/ppermute | solution.py:19
  171.1 12.4 %collective-permute-start.39 = (bf16[64,8,128]{2,1,0:T(8,128)(2,1)S(1)}, bf16[64,8,128]{2,1,0:T(8,128)(2,1)S(1)}, u32[]{:S(2)}, u32[]{:S(2)}) collective-permute-start(bf16[64,8,128]{2,1,0:T(8,128)(2,1)S(1)} %bitcast.178), channel_id=1, source_target_pairs={{0,16},{1,17},{2,18},{3,19},{16,0},{17,1},{18,2},{19,3},{4,20},{5,... | collective-permute-start | bytes 393224 | tf_op jit(solution)/shard_map/ppermute | solution.py:19
  171.8 13.5 %collective-permute-start.40 = (bf16[64,8,128]{2,1,0:T(8,128)(2,1)S(1)}, bf16[64,8,128]{2,1,0:T(8,128)(2,1)S(1)}, u32[]{:S(2)}, u32[]{:S(2)}) collective-permute-start(bf16[64,8,128]{2,1,0:T(8,128)(2,1)S(1)} %bitcast.177), channel_id=1, source_target_pairs={{0,17},{1,16},{2,19},{3,18},{16,1},{17,0},{18,3},{19,2},{4,21},{5,... | collective-permute-start | bytes 393224 | tf_op jit(solution)/shard_map/ppermute | solution.py:19
  177.4 81.8 %collective-permute-start.31 = (f32[2,96,1024]{2,1,0:T(8,128)}, f32[2,96,1024]{2,1,0:T(8,128)}, u32[]{:S(2)}, u32[]{:S(2)}) collective-permute-start(f32[2,96,1024]{2,1,0:T(8,128)} %bitcast.23), channel_id=1, source_target_pairs={{0,4},{4,0},{8,12},{12,8},{1,5},{5,1},{9,13},{13,9},{2,6},{6,2},{1... | collective-permute-start | bytes 2359304 | tf_op jit(solution)/shard_map/ppermute | solution.py:19
  178.4 19.4 %collective-permute-start.41 = (bf16[64,8,128]{2,1,0:T(8,128)(2,1)S(1)}, bf16[64,8,128]{2,1,0:T(8,128)(2,1)S(1)}, u32[]{:S(2)}, u32[]{:S(2)}) collective-permute-start(bf16[64,8,128]{2,1,0:T(8,128)(2,1)S(1)} %bitcast.176), channel_id=1, source_target_pairs={{0,18},{1,19},{2,16},{3,17},{16,2},{17,3},{18,0},{19,1},{4,22},{5,... | collective-permute-start | bytes 393224 | tf_op jit(solution)/shard_map/ppermute | solution.py:19
  180.9 18.7 %collective-permute-start.42 = (bf16[64,8,128]{2,1,0:T(8,128)(2,1)S(1)}, bf16[64,8,128]{2,1,0:T(8,128)(2,1)S(1)}, u32[]{:S(2)}, u32[]{:S(2)}) collective-permute-start(bf16[64,8,128]{2,1,0:T(8,128)(2,1)S(1)} %bitcast.175), channel_id=1, source_target_pairs={{0,19},{1,18},{2,17},{3,16},{16,3},{17,2},{18,1},{19,0},{4,23},{5,... | collective-permute-start | bytes 393224 | tf_op jit(solution)/shard_map/ppermute | solution.py:19
  183.6 27.7 %collective-permute-start.9 = (bf16[64,16,128]{2,1,0:T(8,128)(2,1)S(1)}, bf16[64,16,128]{2,1,0:T(8,128)(2,1)S(1)}, u32[]{:S(2)}, u32[]{:S(2)}) collective-permute-start(bf16[64,16,128]{2,1,0:T(8,128)(2,1)S(1)} %bitcast.169), channel_id=1, source_target_pairs={{0,3},{1,2},{2,1},{3,0},{16,19},{17,18},{18,17},{19,16},{4,7},{5,6... | collective-permute-start | bytes 786440 | tf_op jit(solution)/shard_map/ppermute | solution.py:19
  185.3 123.4 %collective-permute-start.30 = (f32[1,96,4096]{2,1,0:T(8,128)}, f32[1,96,4096]{2,1,0:T(8,128)}, u32[]{:S(2)}, u32[]{:S(2)}) collective-permute-start(f32[1,96,4096]{2,1,0:T(8,128)} %slice.227), channel_id=1, source_target_pairs={{0,8},{4,12},{8,0},{12,4},{1,9},{5,13},{9,1},{13,5},{2,10},{6,14},... | collective-permute-start | bytes 4718600 | tf_op jit(solution)/shard_map/ppermute | solution.py:19
  197.8 15.2 %collective-permute-start.13 = (bf16[64,16,128]{2,1,0:T(8,128)(2,1)S(1)}, bf16[64,16,128]{2,1,0:T(8,128)(2,1)S(1)}, u32[]{:S(2)}, u32[]{:S(2)}) collective-permute-start(bf16[64,16,128]{2,1,0:T(8,128)(2,1)S(1)} %bitcast.172), channel_id=1, source_target_pairs={{0,19},{1,18},{2,17},{3,16},{16,3},{17,2},{18,1},{19,0},{4,23},{5,... | collective-permute-start | bytes 786440 | tf_op jit(solution)/shard_map/ppermute | solution.py:19
  199.6 34.8 %collective-permute-start.14 = (bf16[64,16,128]{2,1,0:T(8,128)(2,1)S(1)}, bf16[64,16,128]{2,1,0:T(8,128)(2,1)S(1)}, u32[]{:S(2)}, u32[]{:S(2)}) collective-permute-start(bf16[64,16,128]{2,1,0:T(8,128)(2,1)S(1)} %bitcast.171), channel_id=1, source_target_pairs={{0,18},{1,19},{2,16},{3,17},{16,2},{17,3},{18,0},{19,1},{4,22},{5,... | collective-permute-start | bytes 786440 | tf_op jit(solution)/shard_map/ppermute | solution.py:19
  211.2 23.8 %collective-permute-start.15 = (bf16[64,16,128]{2,1,0:T(8,128)(2,1)S(1)}, bf16[64,16,128]{2,1,0:T(8,128)(2,1)S(1)}, u32[]{:S(2)}, u32[]{:S(2)}) collective-permute-start(bf16[64,16,128]{2,1,0:T(8,128)(2,1)S(1)} %bitcast.170), channel_id=1, source_target_pairs={{0,16},{1,17},{2,18},{3,19},{16,0},{17,1},{18,2},{19,3},{4,20},{5,... | collective-permute-start | bytes 786440 | tf_op jit(solution)/shard_map/ppermute | solution.py:19
  213.0 29.7 %collective-permute-start.19 = (bf16[64,16,128]{2,1,0:T(8,128)(2,1)}, bf16[64,16,128]{2,1,0:T(8,128)(2,1)S(1)}, u32[]{:S(2)}, u32[]{:S(2)}) collective-permute-start(bf16[64,16,128]{2,1,0:T(8,128)(2,1)} %bitcast.59), channel_id=1, source_target_pairs={{0,19},{1,18},{2,17},{3,16},{16,3},{17,2},{18,1},{19,0},{4,23},{5,... | collective-permute-start | bytes 786440 | tf_op jit(solution)/shard_map/ppermute | solution.py:19
  235.1 21.5 %collective-permute-start.20 = (bf16[64,16,128]{2,1,0:T(8,128)(2,1)}, bf16[64,16,128]{2,1,0:T(8,128)(2,1)S(1)}, u32[]{:S(2)}, u32[]{:S(2)}) collective-permute-start(bf16[64,16,128]{2,1,0:T(8,128)(2,1)} %bitcast.61), channel_id=1, source_target_pairs={{0,18},{1,19},{2,16},{3,17},{16,2},{17,3},{18,0},{19,1},{4,22},{5,... | collective-permute-start | bytes 786440 | tf_op jit(solution)/shard_map/ppermute | solution.py:19
  235.8 20.8 %collective-permute-start.21 = (bf16[64,16,128]{2,1,0:T(8,128)(2,1)}, bf16[64,16,128]{2,1,0:T(8,128)(2,1)S(1)}, u32[]{:S(2)}, u32[]{:S(2)}) collective-permute-start(bf16[64,16,128]{2,1,0:T(8,128)(2,1)} %bitcast.63), channel_id=1, source_target_pairs={{0,16},{1,17},{2,18},{3,19},{16,0},{17,1},{18,2},{19,3},{4,20},{5,... | collective-permute-start | bytes 786440 | tf_op jit(solution)/shard_map/ppermute | solution.py:19
  237.8 23.9 %all-to-all-start.1 = ((bf16[64,8,256]{2,1,0:T(8,128)(2,1)}), bf16[64,8,256]{2,1,0:T(8,128)(2,1)}, u32[]{:S(2)}, u32[]{:S(2)}) async-start(bf16[64,8,256]{2,1,0:T(8,128)(2,1)} %copy.32), calls=%async_computation.1 | async-start | bytes 524288 | tf_op jit(solution)/shard_map/all_to_all | solution.py:417
  242.6 26.7 %collective-permute-start.22 = (bf16[64,16,128]{2,1,0:T(8,128)(2,1)}, bf16[64,16,128]{2,1,0:T(8,128)(2,1)S(1)}, u32[]{:S(2)}, u32[]{:S(2)}) collective-permute-start(bf16[64,16,128]{2,1,0:T(8,128)(2,1)} %bitcast.67), channel_id=1, source_target_pairs={{0,3},{1,2},{2,1},{3,0},{16,19},{17,18},{18,17},{19,16},{4,7},{5,6... | collective-permute-start | bytes 786440 | tf_op jit(solution)/shard_map/ppermute | solution.py:19
  256.6 21.5 %collective-permute-start.23 = (bf16[64,16,128]{2,1,0:T(8,128)(2,1)}, bf16[64,16,128]{2,1,0:T(8,128)(2,1)S(1)}, u32[]{:S(2)}, u32[]{:S(2)}) collective-permute-start(bf16[64,16,128]{2,1,0:T(8,128)(2,1)} %bitcast.69), channel_id=1, source_target_pairs={{0,2},{1,3},{2,0},{3,1},{16,18},{17,19},{18,16},{19,17},{4,6},{5,7... | collective-permute-start | bytes 786440 | tf_op jit(solution)/shard_map/ppermute | solution.py:19
  256.6 24.0 %collective-permute-start.24 = (bf16[64,16,128]{2,1,0:T(8,128)(2,1)}, bf16[64,16,128]{2,1,0:T(8,128)(2,1)S(1)}, u32[]{:S(2)}, u32[]{:S(2)}) collective-permute-start(bf16[64,16,128]{2,1,0:T(8,128)(2,1)} %bitcast.71), channel_id=1, source_target_pairs={{0,17},{1,16},{2,19},{3,18},{16,1},{17,0},{18,3},{19,2},{4,21},{5,... | collective-permute-start | bytes 786440 | tf_op jit(solution)/shard_map/ppermute | solution.py:19
  259.2 21.4 %collective-permute-start.25 = (bf16[64,16,128]{2,1,0:T(8,128)(2,1)}, bf16[64,16,128]{2,1,0:T(8,128)(2,1)S(1)}, u32[]{:S(2)}, u32[]{:S(2)}) collective-permute-start(bf16[64,16,128]{2,1,0:T(8,128)(2,1)} %bitcast.73), channel_id=1, source_target_pairs={{0,1},{1,0},{2,3},{3,2},{16,17},{17,16},{18,19},{19,18},{4,5},{5,4... | collective-permute-start | bytes 786440 | tf_op jit(solution)/shard_map/ppermute | solution.py:19
  261.8 45.5 %all-to-all-start = ((bf16[64,8,1024]{2,1,0:T(8,128)(2,1)}), bf16[64,8,1024]{2,1,0:T(8,128)(2,1)}, u32[]{:S(2)}, u32[]{:S(2)}) async-start(bf16[64,8,1024]{2,1,0:T(8,128)(2,1)} %join.4), calls=%async_computation | async-start | bytes 2097152 | tf_op jit(solution)/shard_map/all_to_all | solution.py:417
  269.3 36.9 %collective-permute-start.32 = (f32[1,96,1024]{2,1,0:T(8,128)}, f32[1,96,1024]{2,1,0:T(8,128)}, u32[]{:S(2)}, u32[]{:S(2)}) collective-permute-start(f32[1,96,1024]{2,1,0:T(8,128)} %slice.231), channel_id=1, source_target_pairs={{0,8},{4,12},{8,0},{12,4},{1,9},{5,13},{9,1},{13,5},{2,10},{6,14},... | collective-permute-start | bytes 1179656 | tf_op jit(solution)/shard_map/ppermute | solution.py:19
  278.0 13.8 %collective-permute-start.10 = (bf16[64,16,128]{2,1,0:T(8,128)(2,1)}, bf16[64,16,128]{2,1,0:T(8,128)(2,1)}, u32[]{:S(2)}, u32[]{:S(2)}) collective-permute-start(bf16[64,16,128]{2,1,0:T(8,128)(2,1)} %bitcast.43), channel_id=1, source_target_pairs={{0,2},{1,3},{2,0},{3,1},{16,18},{17,19},{18,16},{19,17},{4,6},{5,7... | collective-permute-start | bytes 786440 | tf_op jit(solution)/shard_map/ppermute | solution.py:19
  280.6 14.5 %collective-permute-start.11 = (bf16[64,16,128]{2,1,0:T(8,128)(2,1)}, bf16[64,16,128]{2,1,0:T(8,128)(2,1)}, u32[]{:S(2)}, u32[]{:S(2)}) collective-permute-start(bf16[64,16,128]{2,1,0:T(8,128)(2,1)} %bitcast.45), channel_id=1, source_target_pairs={{0,17},{1,16},{2,19},{3,18},{16,1},{17,0},{18,3},{19,2},{4,21},{5,... | collective-permute-start | bytes 786440 | tf_op jit(solution)/shard_map/ppermute | solution.py:19
  280.7 16.8 %collective-permute-start.12 = (bf16[64,16,128]{2,1,0:T(8,128)(2,1)}, bf16[64,16,128]{2,1,0:T(8,128)(2,1)}, u32[]{:S(2)}, u32[]{:S(2)}) collective-permute-start(bf16[64,16,128]{2,1,0:T(8,128)(2,1)} %bitcast.47), channel_id=1, source_target_pairs={{0,1},{1,0},{2,3},{3,2},{16,17},{17,16},{18,19},{19,18},{4,5},{5,4... | collective-permute-start | bytes 786440 | tf_op jit(solution)/shard_map/ppermute | solution.py:19
  299.4 12.6 %collective-permute-start.26 = (f32[16,96]{1,0:T(8,128)S(1)}, f32[16,96]{1,0:T(8,128)S(1)}, u32[]{:S(2)}, u32[]{:S(2)}) collective-permute-start(f32[16,96]{1,0:T(8,128)S(1)} %get-tuple-element.52), channel_id=1, source_target_pairs={{0,4},{4,0},{8,12},{12,8},{1,5},{5,1},{9,13},{13,9},{2,6},{6,2},{1... | collective-permute-start | bytes 18440 | tf_op jit(solution)/shard_map/ppermute | solution.py:19
  299.5 12.6 %collective-permute-start.27 = (f32[16,96]{1,0:T(8,128)S(1)}, f32[16,96]{1,0:T(8,128)S(1)}, u32[]{:S(2)}, u32[]{:S(2)}) collective-permute-start(f32[16,96]{1,0:T(8,128)S(1)} %get-tuple-element.53), channel_id=1, source_target_pairs={{0,8},{4,12},{8,0},{12,4},{1,9},{5,13},{9,1},{13,5},{2,10},{6,14},... | collective-permute-start | bytes 18440 | tf_op jit(solution)/shard_map/ppermute | solution.py:19
  300.0 12.1 %collective-permute-start.28 = (f32[16,96]{1,0:T(8,128)S(1)}, f32[16,96]{1,0:T(8,128)S(1)}, u32[]{:S(2)}, u32[]{:S(2)}) collective-permute-start(f32[16,96]{1,0:T(8,128)S(1)} %get-tuple-element.54), channel_id=1, source_target_pairs={{0,12},{4,8},{8,4},{12,0},{1,13},{5,9},{9,5},{13,1},{2,14},{6,10},... | collective-permute-start | bytes 18440 | tf_op jit(solution)/shard_map/ppermute | solution.py:19
  (41 other events, 212.5 us)

commit v5 on v4

--- a/solution.py
+++ b/solution.py
@@ -342,15 +342,13 @@
         "down": Head(down_factor_head, 2),
     }
 
-    def fetch(name, chunk, cuts):
-        got = {}
-        for cut_shifts in cuts:
-            for s, piece in zip(cut_shifts, heads[name].cut(chunk, cut_shifts)):
-                got[s] = swap(piece, "task", s) if s else piece
+    def fetch(name, chunk):
+        pieces = heads[name].cut(chunk, far_first + [0])
+        got = {s: swap(p, "task", s) if s else p for s, p in zip(far_first + [0], pieces)}
         return jnp.concatenate([got[s] for s in ring_shifts], axis=0)
 
     fetched = {}
-    fetched["query", 0] = fetch("query", 0, [far_first[: ring // 2], far_first[ring // 2 :] + [0]])
+    fetched["query", 0] = fetch("query", 0)
 
     share = own_tasks // parts
     embeddings = lax.dynamic_index_in_dim(
@@ -377,8 +375,8 @@
 
     chunks = heads["down"].chunks
     for chunk in range(chunks):
-        fetched["down", chunk] = fetch("down", chunk, [far_first + [0]])
-    fetched["value", 0] = fetch("value", 0, [far_first + [0]])
+        fetched["down", chunk] = fetch("down", chunk)
+    fetched["value", 0] = fetch("value", 0)
 
     def emit(name, chunk):
         matrix = fetched[name, chunk]

time: 315 us -> 314 us (level)
    pallas_call x4 -> x3, Pallas kernels: 7.2 us -> 5.48 us  [cut(): pl.pallas_call(functools.partial(cut_kernel, shifts, stride, start, width...]
where the time goes in v5:
time: 314 us; the launch traced here: 313 us
  waiting for transfers between devices  113 us (36%)
  starting transfers between devices  105 us (33%)
  local copies, waits for them, and re-layouts  43.1 us (14%)
  Pallas kernels  19.7 us (6%)
  matrix products  17.5 us (6%)
  other arithmetic  12.9 us (4%)
    ppermute x53, waiting for transfers between devices, swap(): return lax.ppermute(x, axes, [(a, a ^ shift) for a in range(total)])  113 us
    ppermute x53, starting transfers between devices, swap(): return lax.ppermute(x, axes, [(a, a ^ shift) for a in range(total)])  96.1 us
    unnamed x98, local copies, waits for them, and re-layouts  27.7 us
    dot_general x1, matrix products, local(): base_query = jnp.dot(turned, w_query, preferred_element_type=jnp.float32)  10.2 us
    all_to_all x2, starting transfers between devices, own_block(): lax.all_to_all(factors, 'tensor', split_axis=0, concat_axis=0, tiled=True)  8.64 us
    pallas_call x4, Pallas kernels, join(): pl.pallas_call(functools.partial(join_kernel, shifts, stride, start, widt...  7.24 us
    slice x4, local copies, waits for them, and re-layouts, reduce_blocks(): came = swap(partial[half:], axis, step)  6.97 us
  transfers between devices with their start and end apart: 55, of which 13 were waited for; matrix products, arithmetic and copies ran while one was open for 19% of the time, Pallas kernels for 6%

profile of v5, /device:TPU:0, one launch (start us, length us, event | category | flops | bytes accessed | tf_op | source)
XLA Modules:
  0.0 312.8 jit_solution(6214244078034870493)
XLA Ops:
  2.9 3.1 collective-permute-start
  6.0 2.6 collective-permute-start.1
  10.1 10.2 %fusion.9 = f32[384,4096]{1,0:T(8,128)S(1)} fusion(bf16[2048,4096]{1,0:T(8,128)(2,1)} %param.16, bf16[96,2048]{1,0:T(8,128)(2,1)S(1)} %get-tuple-element.106, bf16[96,2048]{1,0:T(8,128)(2,1)S(1)} %get-tuple-element.107, bf16[96,2048]{1,0:T(8,128)(2,1)S(1)} %get-tuple-element.108, bf16[96,2048]{1,0:T(8,128)(2,1)S(1)} %get-tuple-element.105), kind=kOutput, calls=%fused_computation.25 | convolution fusion | flops 6448742400 | bytes 24641536 | tf_op jit(solution)/shard_map/dot_general | solution.py:409
  20.3 3.5 %fusion.26 = (f32[192,4096]{1,0:T(8,128)}, f32[192,4096]{1,0:T(8,128)}) fusion(f32[384,4096]{1,0:T(8,128)S(1)} %fusion.9), kind=kLoop, calls=%fused_computation.82 | loop fusion | bytes 12582912 | tf_op jit(solution)/shard_map/slice | solution.py:297
  23.8 1.9 cut.5
  25.7 3.9 %collective-permute-start.35 = (bf16[128,8,128]{2,1,0:T(8,128)(2,1)}, bf16[128,8,128]{2,1,0:T(8,128)(2,1)}, u32[]{:S(2)}, u32[]{:S(2)}) collective-permute-start(bf16[128,8,128]{2,1,0:T(8,128)(2,1)} %get-tuple-element.58), channel_id=1, source_target_pairs={{0,3},{1,2},{2,1},{3,0},{4,7},{5,6},{6,5},{7,4},{8,11},{9,10},{10,... | collective-permute-start | bytes 786440 | tf_op jit(solution)/shard_map/ppermute | solution.py:19
  32.0 2.6 collective-permute-done.3
  34.7 1.8 fusion.8
  45.0 1.9 cut.4
  48.6 3.6 %collective-permute-start.8 = (bf16[128,16,128]{2,1,0:T(8,128)(2,1)}, bf16[128,16,128]{2,1,0:T(8,128)(2,1)}, u32[]{:S(2)}, u32[]{:S(2)}) collective-permute-start(bf16[128,16,128]{2,1,0:T(8,128)(2,1)} %copy-done.20), channel_id=1, source_target_pairs={{0,3},{1,2},{2,1},{3,0},{4,7},{5,6},{6,5},{7,4},{8,11},{9,10},{10,... | collective-permute-start | bytes 1572872 | tf_op jit(solution)/shard_map/ppermute | solution.py:19
  52.2 2.3 collective-permute-start.45
  54.5 2.2 pad_maximum_fusion.3
  56.7 2.1 collective-permute-start.43
  60.8 2.0 reshape.154
  64.0 3.0 collective-permute-done.45
  67.1 14.2 %collective-permute-start.7 = (bf16[128,16,128]{2,1,0:T(8,128)(2,1)S(1)}, bf16[128,16,128]{2,1,0:T(8,128)(2,1)S(1)}, u32[]{:S(2)}, u32[]{:S(2)}) collective-permute-start(bf16[128,16,128]{2,1,0:T(8,128)(2,1)S(1)} %copy-done.19), channel_id=1, source_target_pairs={{0,2},{1,3},{2,0},{3,1},{4,6},{5,7},{6,4},{7,5},{8,10},{9,11},{10,... | collective-permute-start | bytes 1572872 | tf_op jit(solution)/shard_map/ppermute | solution.py:19
  82.5 2.1 collective-permute-start.46
  85.6 18.5 %collective-permute-done.46.refs_1_ = bf16[64,256]{1,0:T(8,128)(2,1)S(1)} collective-permute-done((bf16[64,256]{1,0:T(8,128)(2,1)S(1)}, bf16[64,256]{1,0:T(8,128)(2,1)S(1)}, u32[]{:S(2)}, u32[]{:S(2)}) %collective-permute-start.46) | collective-permute-done | bytes 32800 | tf_op jit(solution)/shard_map/ppermute | solution.py:19
  105.8 2.3 collective-permute-start.48
  112.5 1.9 collective-permute-start.17
  115.4 5.9 %collective-permute-done.50.refs_5_ = bf16[64,256]{1,0:T(8,128)(2,1)S(1)} collective-permute-done((bf16[64,256]{1,0:T(8,128)(2,1)S(1)}, bf16[64,256]{1,0:T(8,128)(2,1)S(1)}, u32[]{:S(2)}, u32[]{:S(2)}) %collective-permute-start.50) | collective-permute-done | bytes 32800 | tf_op jit(solution)/shard_map/ppermute | solution.py:19
  122.5 36.3 %collective-permute-done.51.refs_6_ = bf16[64,256]{1,0:T(8,128)(2,1)S(1)} collective-permute-done((bf16[64,256]{1,0:T(8,128)(2,1)S(1)}, bf16[64,256]{1,0:T(8,128)(2,1)S(1)}, u32[]{:S(2)}, u32[]{:S(2)}) %collective-permute-start.51) | collective-permute-done | bytes 32800 | tf_op jit(solution)/shard_map/ppermute | solution.py:19
  158.8 2.0 collective-permute-start.52
  161.9 3.5 %collective-permute-done.52.refs_7_ = bf16[64,256]{1,0:T(8,128)(2,1)S(1)} collective-permute-done((bf16[64,256]{1,0:T(8,128)(2,1)S(1)}, bf16[64,256]{1,0:T(8,128)(2,1)S(1)}, u32[]{:S(2)}, u32[]{:S(2)}) %collective-permute-start.52) | collective-permute-done | bytes 32800 | tf_op jit(solution)/shard_map/ppermute | solution.py:19
  165.4 2.3 collective-permute-start.37
  167.7 2.1 collective-permute-start.38
  172.4 2.3 add.61
  177.1 2.5 collective-permute-start.41
  179.6 2.7 collective-permute-start.42
  184.0 2.0 collective-permute-start.30
  187.5 9.0 %collective-permute-done.41.refs_6_ = bf16[64,8,128]{2,1,0:T(8,128)(2,1)S(1)} collective-permute-done((bf16[64,8,128]{2,1,0:T(8,128)(2,1)S(1)}, bf16[64,8,128]{2,1,0:T(8,128)(2,1)S(1)}, u32[]{:S(2)}, u32[]{:S(2)}) %collective-permute-start.41) | collective-permute-done | bytes 131104 | tf_op jit(solution)/shard_map/ppermute | solution.py:19
  198.2 11.7 %collective-permute-start.14 = (bf16[64,16,128]{2,1,0:T(8,128)(2,1)S(1)}, bf16[64,16,128]{2,1,0:T(8,128)(2,1)S(1)}, u32[]{:S(2)}, u32[]{:S(2)}) collective-permute-start(bf16[64,16,128]{2,1,0:T(8,128)(2,1)S(1)} %bitcast.171), channel_id=1, source_target_pairs={{0,18},{1,19},{2,16},{3,17},{16,2},{17,3},{18,0},{19,1},{4,22},{5,... | collective-permute-start | bytes 786440 | tf_op jit(solution)/shard_map/ppermute | solution.py:19
  211.6 4.3 %collective-permute-start.19 = (bf16[64,16,128]{2,1,0:T(8,128)(2,1)}, bf16[64,16,128]{2,1,0:T(8,128)(2,1)S(1)}, u32[]{:S(2)}, u32[]{:S(2)}) collective-permute-start(bf16[64,16,128]{2,1,0:T(8,128)(2,1)} %bitcast.59), channel_id=1, source_target_pairs={{0,19},{1,18},{2,17},{3,16},{16,3},{17,2},{18,1},{19,0},{4,23},{5,... | collective-permute-start | bytes 786440 | tf_op jit(solution)/shard_map/ppermute | solution.py:19
  217.5 15.6 %collective-permute-done.14.refs_1_ = bf16[64,16,128]{2,1,0:T(8,128)(2,1)S(1)} collective-permute-done((bf16[64,16,128]{2,1,0:T(8,128)(2,1)S(1)}, bf16[64,16,128]{2,1,0:T(8,128)(2,1)S(1)}, u32[]{:S(2)}, u32[]{:S(2)}) %collective-permute-start.14) | collective-permute-done | bytes 262176 | tf_op jit(solution)/shard_map/ppermute | solution.py:19
  236.5 4.0 %all-to-all-start.1 = ((bf16[64,8,256]{2,1,0:T(8,128)(2,1)}), bf16[64,8,256]{2,1,0:T(8,128)(2,1)}, u32[]{:S(2)}, u32[]{:S(2)}) async-start(bf16[64,8,256]{2,1,0:T(8,128)(2,1)} %copy.32), calls=%async_computation.1 | async-start | bytes 524288 | tf_op jit(solution)/shard_map/all_to_all | solution.py:415
  241.3 1.9 collective-permute-start.22
  245.5 9.9 %collective-permute-done.20.refs_1_ = bf16[64,16,128]{2,1,0:T(8,128)(2,1)S(1)} collective-permute-done((bf16[64,16,128]{2,1,0:T(8,128)(2,1)}, bf16[64,16,128]{2,1,0:T(8,128)(2,1)S(1)}, u32[]{:S(2)}, u32[]{:S(2)}) %collective-permute-start.20) | collective-permute-done | bytes 262176 | tf_op jit(solution)/shard_map/ppermute | solution.py:19
  255.3 2.5 collective-permute-start.24
  257.9 2.5 join.4
  260.4 4.6 %all-to-all-start = ((bf16[64,8,1024]{2,1,0:T(8,128)(2,1)}), bf16[64,8,1024]{2,1,0:T(8,128)(2,1)}, u32[]{:S(2)}, u32[]{:S(2)}) async-start(bf16[64,8,1024]{2,1,0:T(8,128)(2,1)} %join.4), calls=%async_computation | async-start | bytes 2097152 | tf_op jit(solution)/shard_map/all_to_all | solution.py:415
  267.9 2.0 collective-permute-start.32
  275.4 2.4 collective-permute-start.10
  278.9 2.0 collective-permute-start.12
  288.3 1.9 collective-permute-done.10.refs_1_
  290.1 2.2 collective-permute-done.11.refs_2_
  292.3 3.9 %collective-permute-done.12.refs_3_ = bf16[64,16,128]{2,1,0:T(8,128)(2,1)} collective-permute-done((bf16[64,16,128]{2,1,0:T(8,128)(2,1)}, bf16[64,16,128]{2,1,0:T(8,128)(2,1)}, u32[]{:S(2)}, u32[]{:S(2)}) %collective-permute-start.12) | collective-permute-done | bytes 262176 | tf_op jit(solution)/shard_map/ppermute | solution.py:19
  296.2 1.9 project.5
  302.9 2.1 join.7
  (215 shorter events, 79.4 us)
Async XLA Ops:
  2.9 26.7 %collective-permute-start = (bf16[16,512]{1,0:T(8,128)(2,1)S(1)}, bf16[16,512]{1,0:T(8,128)(2,1)S(1)}, u32[]{:S(2)}, u32[]{:S(2)}) collective-permute-start(bf16[16,512]{1,0:T(8,128)(2,1)S(1)} %get-tuple-element.134), channel_id=1, source_target_pairs={{0,1},{1,0},{2,3},{3,2},{4,5},{5,4},{6,7},{7,6},{8,9},{9,8},{10,11... | collective-permute-start | bytes 49160 | tf_op jit(solution)/shard_map/ppermute | solution.py:19
  6.0 23.6 %collective-permute-start.1 = (bf16[16,512]{1,0:T(8,128)(2,1)S(1)}, bf16[16,512]{1,0:T(8,128)(2,1)S(1)}, u32[]{:S(2)}, u32[]{:S(2)}) collective-permute-start(bf16[16,512]{1,0:T(8,128)(2,1)S(1)} %get-tuple-element.134), channel_id=1, source_target_pairs={{0,2},{1,3},{2,0},{3,1},{4,6},{5,7},{6,4},{7,5},{8,10},{9,11},{10,... | collective-permute-start | bytes 49160 | tf_op jit(solution)/shard_map/ppermute | solution.py:19
  8.6 21.7 %collective-permute-start.2 = (bf16[16,512]{1,0:T(8,128)(2,1)S(1)}, bf16[16,512]{1,0:T(8,128)(2,1)S(1)}, u32[]{:S(2)}, u32[]{:S(2)}) collective-permute-start(bf16[16,512]{1,0:T(8,128)(2,1)S(1)} %get-tuple-element.134), channel_id=1, source_target_pairs={{0,3},{1,2},{2,1},{3,0},{4,7},{5,6},{6,5},{7,4},{8,11},{9,10},{10,... | collective-permute-start | bytes 49160 | tf_op jit(solution)/shard_map/ppermute | solution.py:19
  23.8 146.7 %collective-permute-start.29 = (f32[2,96,4096]{2,1,0:T(8,128)}, f32[2,96,4096]{2,1,0:T(8,128)}, u32[]{:S(2)}, u32[]{:S(2)}) collective-permute-start(f32[2,96,4096]{2,1,0:T(8,128)} %bitcast.20), channel_id=1, source_target_pairs={{0,4},{4,0},{8,12},{12,8},{1,5},{5,1},{9,13},{13,9},{2,6},{6,2},{1... | collective-permute-start | bytes 9437192 | tf_op jit(solution)/shard_map/ppermute | solution.py:19
  25.7 22.9 %collective-permute-start.35 = (bf16[128,8,128]{2,1,0:T(8,128)(2,1)}, bf16[128,8,128]{2,1,0:T(8,128)(2,1)}, u32[]{:S(2)}, u32[]{:S(2)}) collective-permute-start(bf16[128,8,128]{2,1,0:T(8,128)(2,1)} %get-tuple-element.58), channel_id=1, source_target_pairs={{0,3},{1,2},{2,1},{3,0},{4,7},{5,6},{6,5},{7,4},{8,11},{9,10},{10,... | collective-permute-start | bytes 786440 | tf_op jit(solution)/shard_map/ppermute | solution.py:19
  29.6 22.6 %collective-permute-start.34 = (bf16[128,8,128]{2,1,0:T(8,128)(2,1)}, bf16[128,8,128]{2,1,0:T(8,128)(2,1)}, u32[]{:S(2)}, u32[]{:S(2)}) collective-permute-start(bf16[128,8,128]{2,1,0:T(8,128)(2,1)} %get-tuple-element.57), channel_id=1, source_target_pairs={{0,2},{1,3},{2,0},{3,1},{4,6},{5,7},{6,4},{7,5},{8,10},{9,11},{10,... | collective-permute-start | bytes 786440 | tf_op jit(solution)/shard_map/ppermute | solution.py:19
  29.6 24.9 %collective-permute-start.33 = (bf16[128,8,128]{2,1,0:T(8,128)(2,1)}, bf16[128,8,128]{2,1,0:T(8,128)(2,1)}, u32[]{:S(2)}, u32[]{:S(2)}) collective-permute-start(bf16[128,8,128]{2,1,0:T(8,128)(2,1)} %get-tuple-element.56), channel_id=1, source_target_pairs={{0,1},{1,0},{2,3},{3,2},{4,5},{5,4},{6,7},{7,6},{8,9},{9,8},{10,11... | collective-permute-start | bytes 786440 | tf_op jit(solution)/shard_map/ppermute | solution.py:19
  37.9 18.8 %collective-permute-start.5 = (bf16[2,128,512]{2,1,0:T(8,128)(2,1)}, bf16[2,128,512]{2,1,0:T(8,128)(2,1)}, u32[]{:S(2)}, u32[]{:S(2)}) collective-permute-start(bf16[2,128,512]{2,1,0:T(8,128)(2,1)} %pad_maximum_fusion.8), channel_id=1, source_target_pairs={{0,8},{4,12},{8,0},{12,4},{1,9},{5,13},{9,1},{13,5},{2,10},{6,14},... | collective-permute-start | bytes 786440 | tf_op jit(solution)/shard_map/ppermute | solution.py:19
  48.6 57.2 %collective-permute-start.8 = (bf16[128,16,128]{2,1,0:T(8,128)(2,1)}, bf16[128,16,128]{2,1,0:T(8,128)(2,1)}, u32[]{:S(2)}, u32[]{:S(2)}) collective-permute-start(bf16[128,16,128]{2,1,0:T(8,128)(2,1)} %copy-done.20), channel_id=1, source_target_pairs={{0,3},{1,2},{2,1},{3,0},{4,7},{5,6},{6,5},{7,4},{8,11},{9,10},{10,... | collective-permute-start | bytes 1572872 | tf_op jit(solution)/shard_map/ppermute | solution.py:19
  52.2 14.9 %collective-permute-start.45 = (bf16[128,256]{1,0:T(8,128)(2,1)}, bf16[128,256]{1,0:T(8,128)(2,1)}, u32[]{:S(2)}, u32[]{:S(2)}) collective-permute-start(bf16[128,256]{1,0:T(8,128)(2,1)} %copy-done.22), channel_id=1, source_target_pairs={{0,3},{1,2},{2,1},{3,0},{4,7},{5,6},{6,5},{7,4},{8,11},{9,10},{10,... | collective-permute-start | bytes 196616 | tf_op jit(solution)/shard_map/ppermute | solution.py:19
  54.5 26.8 %collective-permute-start.44 = (bf16[128,256]{1,0:T(8,128)(2,1)}, bf16[128,256]{1,0:T(8,128)(2,1)}, u32[]{:S(2)}, u32[]{:S(2)}) collective-permute-start(bf16[128,256]{1,0:T(8,128)(2,1)} %copy-done.21), channel_id=1, source_target_pairs={{0,2},{1,3},{2,0},{3,1},{4,6},{5,7},{6,4},{7,5},{8,10},{9,11},{10,... | collective-permute-start | bytes 196616 | tf_op jit(solution)/shard_map/ppermute | solution.py:19
  56.7 24.6 %collective-permute-start.43 = (bf16[128,256]{1,0:T(8,128)(2,1)S(1)}, bf16[128,256]{1,0:T(8,128)(2,1)}, u32[]{:S(2)}, u32[]{:S(2)}) collective-permute-start(bf16[128,256]{1,0:T(8,128)(2,1)S(1)} %get-tuple-element.60), channel_id=1, source_target_pairs={{0,1},{1,0},{2,3},{3,2},{4,5},{5,4},{6,7},{7,6},{8,9},{9,8},{10,11... | collective-permute-start | bytes 196616 | tf_op jit(solution)/shard_map/ppermute | solution.py:19
  67.1 41.0 %collective-permute-start.7 = (bf16[128,16,128]{2,1,0:T(8,128)(2,1)S(1)}, bf16[128,16,128]{2,1,0:T(8,128)(2,1)S(1)}, u32[]{:S(2)}, u32[]{:S(2)}) collective-permute-start(bf16[128,16,128]{2,1,0:T(8,128)(2,1)S(1)} %copy-done.19), channel_id=1, source_target_pairs={{0,2},{1,3},{2,0},{3,1},{4,6},{5,7},{6,4},{7,5},{8,10},{9,11},{10,... | collective-permute-start | bytes 1572872 | tf_op jit(solution)/shard_map/ppermute | solution.py:19
  81.3 28.3 %collective-permute-start.6 = (bf16[128,16,128]{2,1,0:T(8,128)(2,1)S(1)}, bf16[128,16,128]{2,1,0:T(8,128)(2,1)S(1)}, u32[]{:S(2)}, u32[]{:S(2)}) collective-permute-start(bf16[128,16,128]{2,1,0:T(8,128)(2,1)S(1)} %copy-done.17), channel_id=1, source_target_pairs={{0,1},{1,0},{2,3},{3,2},{4,5},{5,4},{6,7},{7,6},{8,9},{9,8},{10,11... | collective-permute-start | bytes 1572872 | tf_op jit(solution)/shard_map/ppermute | solution.py:19
  82.5 21.5 %collective-permute-start.46 = (bf16[64,256]{1,0:T(8,128)(2,1)S(1)}, bf16[64,256]{1,0:T(8,128)(2,1)S(1)}, u32[]{:S(2)}, u32[]{:S(2)}) collective-permute-start(bf16[64,256]{1,0:T(8,128)(2,1)S(1)} %get-tuple-element.129), channel_id=1, source_target_pairs={{0,1},{1,0},{2,3},{3,2},{16,17},{17,16},{18,19},{19,18},{4,5},{5,4... | collective-permute-start | bytes 98312 | tf_op jit(solution)/shard_map/ppermute | solution.py:19
  109.6 11.7 %collective-permute-start.50 = (bf16[64,256]{1,0:T(8,128)(2,1)S(1)}, bf16[64,256]{1,0:T(8,128)(2,1)S(1)}, u32[]{:S(2)}, u32[]{:S(2)}) collective-permute-start(bf16[64,256]{1,0:T(8,128)(2,1)S(1)} %get-tuple-element.125), channel_id=1, source_target_pairs={{0,17},{1,16},{2,19},{3,18},{16,1},{17,0},{18,3},{19,2},{4,21},{5,... | collective-permute-start | bytes 98312 | tf_op jit(solution)/shard_map/ppermute | solution.py:19
  110.9 54.5 %collective-permute-start.18 = (bf16[128,16,128]{2,1,0:T(8,128)(2,1)S(1)}, bf16[128,16,128]{2,1,0:T(8,128)(2,1)S(1)}, u32[]{:S(2)}, u32[]{:S(2)}) collective-permute-start(bf16[128,16,128]{2,1,0:T(8,128)(2,1)S(1)} %get-tuple-element.42), channel_id=1, source_target_pairs={{0,3},{1,2},{2,1},{3,0},{4,7},{5,6},{6,5},{7,4},{8,11},{9,10},{10,... | collective-permute-start | bytes 1572872 | tf_op jit(solution)/shard_map/ppermute | solution.py:19
  112.5 55.2 %collective-permute-start.17 = (bf16[128,16,128]{2,1,0:T(8,128)(2,1)S(1)}, bf16[128,16,128]{2,1,0:T(8,128)(2,1)S(1)}, u32[]{:S(2)}, u32[]{:S(2)}) collective-permute-start(bf16[128,16,128]{2,1,0:T(8,128)(2,1)S(1)} %get-tuple-element.41), channel_id=1, source_target_pairs={{0,2},{1,3},{2,0},{3,1},{4,6},{5,7},{6,4},{7,5},{8,10},{9,11},{10,... | collective-permute-start | bytes 1572872 | tf_op jit(solution)/shard_map/ppermute | solution.py:19
  114.4 55.4 %collective-permute-start.16 = (bf16[128,16,128]{2,1,0:T(8,128)(2,1)S(1)}, bf16[128,16,128]{2,1,0:T(8,128)(2,1)S(1)}, u32[]{:S(2)}, u32[]{:S(2)}) collective-permute-start(bf16[128,16,128]{2,1,0:T(8,128)(2,1)S(1)} %get-tuple-element.40), channel_id=1, source_target_pairs={{0,1},{1,0},{2,3},{3,2},{4,5},{5,4},{6,7},{7,6},{8,9},{9,8},{10,11... | collective-permute-start | bytes 1572872 | tf_op jit(solution)/shard_map/ppermute | solution.py:19
  121.3 37.5 %collective-permute-start.51 = (bf16[64,256]{1,0:T(8,128)(2,1)S(1)}, bf16[64,256]{1,0:T(8,128)(2,1)S(1)}, u32[]{:S(2)}, u32[]{:S(2)}) collective-permute-start(bf16[64,256]{1,0:T(8,128)(2,1)S(1)} %get-tuple-element.124), channel_id=1, source_target_pairs={{0,18},{1,19},{2,16},{3,17},{16,2},{17,3},{18,0},{19,1},{4,22},{5,... | collective-permute-start | bytes 98312 | tf_op jit(solution)/shard_map/ppermute | solution.py:19
  165.4 11.6 %collective-permute-start.37 = (bf16[64,8,128]{2,1,0:T(8,128)(2,1)S(1)}, bf16[64,8,128]{2,1,0:T(8,128)(2,1)S(1)}, u32[]{:S(2)}, u32[]{:S(2)}) collective-permute-start(bf16[64,8,128]{2,1,0:T(8,128)(2,1)S(1)} %bitcast.180), channel_id=1, source_target_pairs={{0,2},{1,3},{2,0},{3,1},{16,18},{17,19},{18,16},{19,17},{4,6},{5,7... | collective-permute-start | bytes 393224 | tf_op jit(solution)/shard_map/ppermute | solution.py:19
  167.7 11.8 %collective-permute-start.38 = (bf16[64,8,128]{2,1,0:T(8,128)(2,1)S(1)}, bf16[64,8,128]{2,1,0:T(8,128)(2,1)S(1)}, u32[]{:S(2)}, u32[]{:S(2)}) collective-permute-start(bf16[64,8,128]{2,1,0:T(8,128)(2,1)S(1)} %bitcast.179), channel_id=1, source_target_pairs={{0,3},{1,2},{2,1},{3,0},{16,19},{17,18},{18,17},{19,16},{4,7},{5,6... | collective-permute-start | bytes 393224 | tf_op jit(solution)/shard_map/ppermute | solution.py:19
  169.8 12.4 %collective-permute-start.39 = (bf16[64,8,128]{2,1,0:T(8,128)(2,1)S(1)}, bf16[64,8,128]{2,1,0:T(8,128)(2,1)S(1)}, u32[]{:S(2)}, u32[]{:S(2)}) collective-permute-start(bf16[64,8,128]{2,1,0:T(8,128)(2,1)S(1)} %bitcast.178), channel_id=1, source_target_pairs={{0,16},{1,17},{2,18},{3,19},{16,0},{17,1},{18,2},{19,3},{4,20},{5,... | collective-permute-start | bytes 393224 | tf_op jit(solution)/shard_map/ppermute | solution.py:19
  170.5 13.5 %collective-permute-start.40 = (bf16[64,8,128]{2,1,0:T(8,128)(2,1)S(1)}, bf16[64,8,128]{2,1,0:T(8,128)(2,1)S(1)}, u32[]{:S(2)}, u32[]{:S(2)}) collective-permute-start(bf16[64,8,128]{2,1,0:T(8,128)(2,1)S(1)} %bitcast.177), channel_id=1, source_target_pairs={{0,17},{1,16},{2,19},{3,18},{16,1},{17,0},{18,3},{19,2},{4,21},{5,... | collective-permute-start | bytes 393224 | tf_op jit(solution)/shard_map/ppermute | solution.py:19
  176.1 81.7 %collective-permute-start.31 = (f32[2,96,1024]{2,1,0:T(8,128)}, f32[2,96,1024]{2,1,0:T(8,128)}, u32[]{:S(2)}, u32[]{:S(2)}) collective-permute-start(f32[2,96,1024]{2,1,0:T(8,128)} %bitcast.23), channel_id=1, source_target_pairs={{0,4},{4,0},{8,12},{12,8},{1,5},{5,1},{9,13},{13,9},{2,6},{6,2},{1... | collective-permute-start | bytes 2359304 | tf_op jit(solution)/shard_map/ppermute | solution.py:19
  177.1 19.4 %collective-permute-start.41 = (bf16[64,8,128]{2,1,0:T(8,128)(2,1)S(1)}, bf16[64,8,128]{2,1,0:T(8,128)(2,1)S(1)}, u32[]{:S(2)}, u32[]{:S(2)}) collective-permute-start(bf16[64,8,128]{2,1,0:T(8,128)(2,1)S(1)} %bitcast.176), channel_id=1, source_target_pairs={{0,18},{1,19},{2,16},{3,17},{16,2},{17,3},{18,0},{19,1},{4,22},{5,... | collective-permute-start | bytes 393224 | tf_op jit(solution)/shard_map/ppermute | solution.py:19
  179.6 18.7 %collective-permute-start.42 = (bf16[64,8,128]{2,1,0:T(8,128)(2,1)S(1)}, bf16[64,8,128]{2,1,0:T(8,128)(2,1)S(1)}, u32[]{:S(2)}, u32[]{:S(2)}) collective-permute-start(bf16[64,8,128]{2,1,0:T(8,128)(2,1)S(1)} %bitcast.175), channel_id=1, source_target_pairs={{0,19},{1,18},{2,17},{3,16},{16,3},{17,2},{18,1},{19,0},{4,23},{5,... | collective-permute-start | bytes 393224 | tf_op jit(solution)/shard_map/ppermute | solution.py:19
  182.2 27.7 %collective-permute-start.9 = (bf16[64,16,128]{2,1,0:T(8,128)(2,1)S(1)}, bf16[64,16,128]{2,1,0:T(8,128)(2,1)S(1)}, u32[]{:S(2)}, u32[]{:S(2)}) collective-permute-start(bf16[64,16,128]{2,1,0:T(8,128)(2,1)S(1)} %bitcast.169), channel_id=1, source_target_pairs={{0,3},{1,2},{2,1},{3,0},{16,19},{17,18},{18,17},{19,16},{4,7},{5,6... | collective-permute-start | bytes 786440 | tf_op jit(solution)/shard_map/ppermute | solution.py:19
  184.0 123.5 %collective-permute-start.30 = (f32[1,96,4096]{2,1,0:T(8,128)}, f32[1,96,4096]{2,1,0:T(8,128)}, u32[]{:S(2)}, u32[]{:S(2)}) collective-permute-start(f32[1,96,4096]{2,1,0:T(8,128)} %slice.227), channel_id=1, source_target_pairs={{0,8},{4,12},{8,0},{12,4},{1,9},{5,13},{9,1},{13,5},{2,10},{6,14},... | collective-permute-start | bytes 4718600 | tf_op jit(solution)/shard_map/ppermute | solution.py:19
  196.5 15.2 %collective-permute-start.13 = (bf16[64,16,128]{2,1,0:T(8,128)(2,1)S(1)}, bf16[64,16,128]{2,1,0:T(8,128)(2,1)S(1)}, u32[]{:S(2)}, u32[]{:S(2)}) collective-permute-start(bf16[64,16,128]{2,1,0:T(8,128)(2,1)S(1)} %bitcast.172), channel_id=1, source_target_pairs={{0,19},{1,18},{2,17},{3,16},{16,3},{17,2},{18,1},{19,0},{4,23},{5,... | collective-permute-start | bytes 786440 | tf_op jit(solution)/shard_map/ppermute | solution.py:19
  198.2 34.8 %collective-permute-start.14 = (bf16[64,16,128]{2,1,0:T(8,128)(2,1)S(1)}, bf16[64,16,128]{2,1,0:T(8,128)(2,1)S(1)}, u32[]{:S(2)}, u32[]{:S(2)}) collective-permute-start(bf16[64,16,128]{2,1,0:T(8,128)(2,1)S(1)} %bitcast.171), channel_id=1, source_target_pairs={{0,18},{1,19},{2,16},{3,17},{16,2},{17,3},{18,0},{19,1},{4,22},{5,... | collective-permute-start | bytes 786440 | tf_op jit(solution)/shard_map/ppermute | solution.py:19
  209.9 23.8 %collective-permute-start.15 = (bf16[64,16,128]{2,1,0:T(8,128)(2,1)S(1)}, bf16[64,16,128]{2,1,0:T(8,128)(2,1)S(1)}, u32[]{:S(2)}, u32[]{:S(2)}) collective-permute-start(bf16[64,16,128]{2,1,0:T(8,128)(2,1)S(1)} %bitcast.170), channel_id=1, source_target_pairs={{0,16},{1,17},{2,18},{3,19},{16,0},{17,1},{18,2},{19,3},{4,20},{5,... | collective-permute-start | bytes 786440 | tf_op jit(solution)/shard_map/ppermute | solution.py:19
  211.6 29.7 %collective-permute-start.19 = (bf16[64,16,128]{2,1,0:T(8,128)(2,1)}, bf16[64,16,128]{2,1,0:T(8,128)(2,1)S(1)}, u32[]{:S(2)}, u32[]{:S(2)}) collective-permute-start(bf16[64,16,128]{2,1,0:T(8,128)(2,1)} %bitcast.59), channel_id=1, source_target_pairs={{0,19},{1,18},{2,17},{3,16},{16,3},{17,2},{18,1},{19,0},{4,23},{5,... | collective-permute-start | bytes 786440 | tf_op jit(solution)/shard_map/ppermute | solution.py:19
  233.7 21.6 %collective-permute-start.20 = (bf16[64,16,128]{2,1,0:T(8,128)(2,1)}, bf16[64,16,128]{2,1,0:T(8,128)(2,1)S(1)}, u32[]{:S(2)}, u32[]{:S(2)}) collective-permute-start(bf16[64,16,128]{2,1,0:T(8,128)(2,1)} %bitcast.61), channel_id=1, source_target_pairs={{0,18},{1,19},{2,16},{3,17},{16,2},{17,3},{18,0},{19,1},{4,22},{5,... | collective-permute-start | bytes 786440 | tf_op jit(solution)/shard_map/ppermute | solution.py:19
  234.4 20.9 %collective-permute-start.21 = (bf16[64,16,128]{2,1,0:T(8,128)(2,1)}, bf16[64,16,128]{2,1,0:T(8,128)(2,1)S(1)}, u32[]{:S(2)}, u32[]{:S(2)}) collective-permute-start(bf16[64,16,128]{2,1,0:T(8,128)(2,1)} %bitcast.63), channel_id=1, source_target_pairs={{0,16},{1,17},{2,18},{3,19},{16,0},{17,1},{18,2},{19,3},{4,20},{5,... | collective-permute-start | bytes 786440 | tf_op jit(solution)/shard_map/ppermute | solution.py:19
  236.5 23.8 %all-to-all-start.1 = ((bf16[64,8,256]{2,1,0:T(8,128)(2,1)}), bf16[64,8,256]{2,1,0:T(8,128)(2,1)}, u32[]{:S(2)}, u32[]{:S(2)}) async-start(bf16[64,8,256]{2,1,0:T(8,128)(2,1)} %copy.32), calls=%async_computation.1 | async-start | bytes 524288 | tf_op jit(solution)/shard_map/all_to_all | solution.py:415
  241.3 26.6 %collective-permute-start.22 = (bf16[64,16,128]{2,1,0:T(8,128)(2,1)}, bf16[64,16,128]{2,1,0:T(8,128)(2,1)S(1)}, u32[]{:S(2)}, u32[]{:S(2)}) collective-permute-start(bf16[64,16,128]{2,1,0:T(8,128)(2,1)} %bitcast.67), channel_id=1, source_target_pairs={{0,3},{1,2},{2,1},{3,0},{16,19},{17,18},{18,17},{19,16},{4,7},{5,6... | collective-permute-start | bytes 786440 | tf_op jit(solution)/shard_map/ppermute | solution.py:19
  255.3 20.1 %collective-permute-start.23 = (bf16[64,16,128]{2,1,0:T(8,128)(2,1)}, bf16[64,16,128]{2,1,0:T(8,128)(2,1)S(1)}, u32[]{:S(2)}, u32[]{:S(2)}) collective-permute-start(bf16[64,16,128]{2,1,0:T(8,128)(2,1)} %bitcast.69), channel_id=1, source_target_pairs={{0,2},{1,3},{2,0},{3,1},{16,18},{17,19},{18,16},{19,17},{4,6},{5,7... | collective-permute-start | bytes 786440 | tf_op jit(solution)/shard_map/ppermute | solution.py:19
  255.3 22.5 %collective-permute-start.24 = (bf16[64,16,128]{2,1,0:T(8,128)(2,1)}, bf16[64,16,128]{2,1,0:T(8,128)(2,1)S(1)}, u32[]{:S(2)}, u32[]{:S(2)}) collective-permute-start(bf16[64,16,128]{2,1,0:T(8,128)(2,1)} %bitcast.71), channel_id=1, source_target_pairs={{0,17},{1,16},{2,19},{3,18},{16,1},{17,0},{18,3},{19,2},{4,21},{5,... | collective-permute-start | bytes 786440 | tf_op jit(solution)/shard_map/ppermute | solution.py:19
  257.9 21.0 %collective-permute-start.25 = (bf16[64,16,128]{2,1,0:T(8,128)(2,1)}, bf16[64,16,128]{2,1,0:T(8,128)(2,1)S(1)}, u32[]{:S(2)}, u32[]{:S(2)}) collective-permute-start(bf16[64,16,128]{2,1,0:T(8,128)(2,1)} %bitcast.73), channel_id=1, source_target_pairs={{0,1},{1,0},{2,3},{3,2},{16,17},{17,16},{18,19},{19,18},{4,5},{5,4... | collective-permute-start | bytes 786440 | tf_op jit(solution)/shard_map/ppermute | solution.py:19
  260.4 45.6 %all-to-all-start = ((bf16[64,8,1024]{2,1,0:T(8,128)(2,1)}), bf16[64,8,1024]{2,1,0:T(8,128)(2,1)}, u32[]{:S(2)}, u32[]{:S(2)}) async-start(bf16[64,8,1024]{2,1,0:T(8,128)(2,1)} %join.4), calls=%async_computation | async-start | bytes 2097152 | tf_op jit(solution)/shard_map/all_to_all | solution.py:415
  267.9 37.0 %collective-permute-start.32 = (f32[1,96,1024]{2,1,0:T(8,128)}, f32[1,96,1024]{2,1,0:T(8,128)}, u32[]{:S(2)}, u32[]{:S(2)}) collective-permute-start(f32[1,96,1024]{2,1,0:T(8,128)} %slice.231), channel_id=1, source_target_pairs={{0,8},{4,12},{8,0},{12,4},{1,9},{5,13},{9,1},{13,5},{2,10},{6,14},... | collective-permute-start | bytes 1179656 | tf_op jit(solution)/shard_map/ppermute | solution.py:19
  275.4 14.7 %collective-permute-start.10 = (bf16[64,16,128]{2,1,0:T(8,128)(2,1)}, bf16[64,16,128]{2,1,0:T(8,128)(2,1)}, u32[]{:S(2)}, u32[]{:S(2)}) collective-permute-start(bf16[64,16,128]{2,1,0:T(8,128)(2,1)} %bitcast.43), channel_id=1, source_target_pairs={{0,2},{1,3},{2,0},{3,1},{16,18},{17,19},{18,16},{19,17},{4,6},{5,7... | collective-permute-start | bytes 786440 | tf_op jit(solution)/shard_map/ppermute | solution.py:19
  277.9 14.5 %collective-permute-start.11 = (bf16[64,16,128]{2,1,0:T(8,128)(2,1)}, bf16[64,16,128]{2,1,0:T(8,128)(2,1)}, u32[]{:S(2)}, u32[]{:S(2)}) collective-permute-start(bf16[64,16,128]{2,1,0:T(8,128)(2,1)} %bitcast.45), channel_id=1, source_target_pairs={{0,17},{1,16},{2,19},{3,18},{16,1},{17,0},{18,3},{19,2},{4,21},{5,... | collective-permute-start | bytes 786440 | tf_op jit(solution)/shard_map/ppermute | solution.py:19
  278.9 17.4 %collective-permute-start.12 = (bf16[64,16,128]{2,1,0:T(8,128)(2,1)}, bf16[64,16,128]{2,1,0:T(8,128)(2,1)}, u32[]{:S(2)}, u32[]{:S(2)}) collective-permute-start(bf16[64,16,128]{2,1,0:T(8,128)(2,1)} %bitcast.47), channel_id=1, source_target_pairs={{0,1},{1,0},{2,3},{3,2},{16,17},{17,16},{18,19},{19,18},{4,5},{5,4... | collective-permute-start | bytes 786440 | tf_op jit(solution)/shard_map/ppermute | solution.py:19
  298.2 12.6 %collective-permute-start.26 = (f32[16,96]{1,0:T(8,128)S(1)}, f32[16,96]{1,0:T(8,128)S(1)}, u32[]{:S(2)}, u32[]{:S(2)}) collective-permute-start(f32[16,96]{1,0:T(8,128)S(1)} %get-tuple-element.52), channel_id=1, source_target_pairs={{0,4},{4,0},{8,12},{12,8},{1,5},{5,1},{9,13},{13,9},{2,6},{6,2},{1... | collective-permute-start | bytes 18440 | tf_op jit(solution)/shard_map/ppermute | solution.py:19
  298.3 12.6 %collective-permute-start.27 = (f32[16,96]{1,0:T(8,128)S(1)}, f32[16,96]{1,0:T(8,128)S(1)}, u32[]{:S(2)}, u32[]{:S(2)}) collective-permute-start(f32[16,96]{1,0:T(8,128)S(1)} %get-tuple-element.53), channel_id=1, source_target_pairs={{0,8},{4,12},{8,0},{12,4},{1,9},{5,13},{9,1},{13,5},{2,10},{6,14},... | collective-permute-start | bytes 18440 | tf_op jit(solution)/shard_map/ppermute | solution.py:19
  298.7 12.1 %collective-permute-start.28 = (f32[16,96]{1,0:T(8,128)S(1)}, f32[16,96]{1,0:T(8,128)S(1)}, u32[]{:S(2)}, u32[]{:S(2)}) collective-permute-start(f32[16,96]{1,0:T(8,128)S(1)} %get-tuple-element.54), channel_id=1, source_target_pairs={{0,12},{4,8},{8,4},{12,0},{1,13},{5,9},{9,5},{13,1},{2,14},{6,10},... | collective-permute-start | bytes 18440 | tf_op jit(solution)/shard_map/ppermute | solution.py:19
  (41 other events, 217.6 us)

commit v6 on v5

--- a/solution.py
+++ b/solution.py
@@ -62,7 +62,7 @@
     return pl.pallas_call(
         functools.partial(cut_kernel, shifts, stride, start, width),
         in_specs=[pl.BlockSpec(memory_space=pl.ANY)],
-        out_specs=[pl.BlockSpec(memory_space=pl.ANY)] * len(shifts),
+        out_specs=[pl.BlockSpec(memory_space=pltpu.HBM)] * len(shifts),
         out_shape=[jax.ShapeDtypeStruct(shape, head.dtype)] * len(shifts),
         scratch_shapes=vmem_scratch(len(shifts), shape, head.dtype),
         compiler_params=SMALL,
@@ -357,7 +357,13 @@
     hidden = jax.nn.silu(
         jnp.dot(embeddings, embedding_weight, preferred_element_type=jnp.float32)
     ).astype(jnp.bfloat16)
-    ring_hidden = jnp.stack([hidden] + [swap(hidden, "task", s) for s in ring_shifts[1:]])
+    far, came = ring // 2, [0, ring // 2]
+    ring_hidden = jnp.concatenate([hidden[None], swap(hidden[None], "task", far)])
+    while far > 1:
+        far //= 2
+        ring_hidden = jnp.concatenate([ring_hidden, swap(ring_hidden, "task", far)])
+        came = came + [s ^ far for s in came]
+    ring_hidden = jnp.stack([ring_hidden[came.index(s)] for s in ring_shifts])
     group_hidden = jnp.concatenate(
         [ring_hidden] + [swap(ring_hidden, "groups", s) for s in range(1, groups)]
     )
@@ -389,9 +395,8 @@
         return {s: swap(made[s], PLACES, s) if s else made[s] for s in sent}
 
     crossing = [s for s in reversed(shifts) if s % ring >= ring // 2]
-    early = [s for s in crossing if s >= ring] + [s for s in reversed(shifts) if s % ring == 0]
-    late = [s for s in crossing if s < ring]
-    late = late + [s for s in reversed(shifts) if 0 < s % ring < ring // 2]
+    late = crossing[-1:]
+    early = crossing[:-1] + [s for s in reversed(shifts) if s % ring < ring // 2]
     emitted = {}
     for name, chunk in [("query", 0), ("value", 0)] + [("down", c) for c in range(chunks)]:
         made = emit(name, chunk)
@@ -456,7 +461,7 @@
             for s in range(parts)
         ]
     shares = [low_rank[0]] + [swap(low_rank[s], "tensor", s) for s in range(1, parts)]
-    query, value = finish(shares, bounds, [base_query, base_value, own_query, own_value], steps=4)
+    query, value = finish(shares, bounds, [base_query, base_value, own_query, own_value], steps=8)
     return query, value, down_factors, query_up_factors, value_up_factors
 
 

time: 314 us -> 323 us (1.029)
  starting transfers between devices: 105 us -> 149 us
  waiting for transfers between devices: 113 us -> 75.5 us
    ppermute x53 -> x52, starting transfers between devices: 96.1 us -> 141 us  [swap(): return lax.ppermute(x, axes, [(a, a ^ shift) for a in range(total)])]
    ppermute x53 -> x52, waiting for transfers between devices: 113 us -> 75.5 us  [swap(): return lax.ppermute(x, axes, [(a, a ^ shift) for a in range(total)])]
    unnamed x98 -> x99, local copies, waits for them, and re-layouts: 27.7 us -> 28.4 us
  transfers between devices with their start and end apart: 55 -> 54, of which waited for: 13 -> 12; matrix products, arithmetic and copies ran while one was open for 19% -> 18% of each run, Pallas kernels for 6% -> 6%
where the time goes in v6:
time: 323 us; the launch traced here: 322 us
  starting transfers between devices  149 us (46%)
  waiting for transfers between devices  75.5 us (23%)
  local copies, waits for them, and re-layouts  43.8 us (14%)
  Pallas kernels  21.5 us (7%)
  matrix products  16.6 us (5%)
  other arithmetic  13 us (4%)
    ppermute x52, starting transfers between devices, swap(): return lax.ppermute(x, axes, [(a, a ^ shift) for a in range(total)])  141 us
    ppermute x52, waiting for transfers between devices, swap(): return lax.ppermute(x, axes, [(a, a ^ shift) for a in range(total)])  75.5 us
    unnamed x99, local copies, waits for them, and re-layouts  28.4 us
    dot_general x1, matrix products, local(): base_query = jnp.dot(turned, w_query, preferred_element_type=jnp.float32)  10.2 us
    all_to_all x2, starting transfers between devices, own_block(): lax.all_to_all(factors, 'tensor', split_axis=0, concat_axis=0, tiled=True)  8.69 us
    pallas_call x4, Pallas kernels, join(): pl.pallas_call(functools.partial(join_kernel, shifts, stride, start, widt...  8.11 us
    slice x4, local copies, waits for them, and re-layouts, reduce_blocks(): came = swap(partial[half:], axis, step)  6.95 us
  transfers between devices with their start and end apart: 54, of which 12 were waited for; matrix products, arithmetic and copies ran while one was open for 18% of the time, Pallas kernels for 6%

profile of v6, /device:TPU:0, one launch (start us, length us, event | category | flops | bytes accessed | tf_op | source)
XLA Modules:
  0.0 321.6 jit_solution(12893145045115723690)
XLA Ops:
  2.9 4.1 %collective-permute-start = (bf16[1,16,512]{2,1,0:T(8,128)(2,1)S(1)}, bf16[1,16,512]{2,1,0:T(8,128)(2,1)S(1)}, u32[]{:S(2)}, u32[]{:S(2)}) collective-permute-start(bf16[1,16,512]{2,1,0:T(8,128)(2,1)S(1)} %get-tuple-element.137), channel_id=1, source_target_pairs={{0,2},{1,3},{2,0},{3,1},{4,6},{5,7},{6,4},{7,5},{8,10},{9,11},{10,... | collective-permute-start | bytes 49160 | tf_op jit(solution)/shard_map/ppermute | solution.py:19
  8.5 10.2 %fusion.9 = f32[384,4096]{1,0:T(8,128)S(1)} fusion(bf16[2048,4096]{1,0:T(8,128)(2,1)} %param.16, bf16[96,2048]{1,0:T(8,128)(2,1)S(1)} %get-tuple-element.106, bf16[96,2048]{1,0:T(8,128)(2,1)S(1)} %get-tuple-element.107, bf16[96,2048]{1,0:T(8,128)(2,1)S(1)} %get-tuple-element.108, bf16[96,2048]{1,0:T(8,128)(2,1)S(1)} %get-tuple-element.105), kind=kOutput, calls=%fused_computation.25 | convolution fusion | flops 6448742400 | bytes 24641536 | tf_op jit(solution)/shard_map/dot_general | solution.py:414
  18.7 1.6 collective-permute-start.1
  20.4 3.5 %fusion.29 = (f32[192,4096]{1,0:T(8,128)}, f32[192,4096]{1,0:T(8,128)}) fusion(f32[384,4096]{1,0:T(8,128)S(1)} %fusion.9), kind=kLoop, calls=%fused_computation.84 | loop fusion | bytes 12582912 | tf_op jit(solution)/shard_map/slice | solution.py:297
  23.9 1.9 cut.5
  25.9 1.9 collective-permute-start.33
  27.8 2.5 collective-permute-start.32
  31.9 2.7 collective-permute-done.2
  34.6 1.8 fusion.8
  40.7 1.7 cut.3
  44.8 1.9 cut.4
  48.7 3.4 %collective-permute-done.33 = bf16[128,8,128]{2,1,0:T(8,128)(2,1)} collective-permute-done((bf16[128,8,128]{2,1,0:T(8,128)(2,1)}, bf16[128,8,128]{2,1,0:T(8,128)(2,1)}, u32[]{:S(2)}, u32[]{:S(2)}) %collective-permute-start.33) | collective-permute-done | bytes 262176 | tf_op jit(solution)/shard_map/ppermute | solution.py:19
  53.5 2.2 pad_maximum_fusion.3
  55.7 2.0 collective-permute-start.43
  59.6 2.0 reshape.154
  63.7 14.3 %collective-permute-done.44 = bf16[128,256]{1,0:T(8,128)(2,1)S(1)} collective-permute-done((bf16[128,256]{1,0:T(8,128)(2,1)}, bf16[128,256]{1,0:T(8,128)(2,1)S(1)}, u32[]{:S(2)}, u32[]{:S(2)}) %collective-permute-start.44) | collective-permute-done | bytes 65568 | tf_op jit(solution)/shard_map/ppermute | solution.py:19
  78.0 23.7 %collective-permute-start.5 = (bf16[128,16,128]{2,1,0:T(8,128)(2,1)S(1)}, bf16[128,16,128]{2,1,0:T(8,128)(2,1)S(1)}, u32[]{:S(2)}, u32[]{:S(2)}) collective-permute-start(bf16[128,16,128]{2,1,0:T(8,128)(2,1)S(1)} %copy-done.17), channel_id=1, source_target_pairs={{0,1},{1,0},{2,3},{3,2},{4,5},{5,4},{6,7},{7,6},{8,9},{9,8},{10,11... | collective-permute-start | bytes 1572872 | tf_op jit(solution)/shard_map/ppermute | solution.py:19
  103.1 11.7 %collective-permute-done.42 = bf16[128,256]{1,0:T(8,128)(2,1)S(1)} collective-permute-done((bf16[128,256]{1,0:T(8,128)(2,1)S(1)}, bf16[128,256]{1,0:T(8,128)(2,1)S(1)}, u32[]{:S(2)}, u32[]{:S(2)}) %collective-permute-start.42) | collective-permute-done | bytes 65568 | tf_op jit(solution)/shard_map/ppermute | solution.py:19
  121.5 9.9 %collective-permute-done.17 = bf16[128,16,128]{2,1,0:T(8,128)(2,1)S(1)} collective-permute-done((bf16[128,16,128]{2,1,0:T(8,128)(2,1)S(1)}, bf16[128,16,128]{2,1,0:T(8,128)(2,1)S(1)}, u32[]{:S(2)}, u32[]{:S(2)}) %collective-permute-start.17) | collective-permute-done | bytes 524320 | tf_op jit(solution)/shard_map/ppermute | solution.py:19
  131.4 20.9 %collective-permute-start.46 = (bf16[64,256]{1,0:T(8,128)(2,1)S(1)}, bf16[64,256]{1,0:T(8,128)(2,1)S(1)}, u32[]{:S(2)}, u32[]{:S(2)}) collective-permute-start(bf16[64,256]{1,0:T(8,128)(2,1)S(1)} %get-tuple-element.128), channel_id=1, source_target_pairs={{0,2},{1,3},{2,0},{3,1},{16,18},{17,19},{18,16},{19,17},{4,6},{5,7... | collective-permute-start | bytes 98312 | tf_op jit(solution)/shard_map/ppermute | solution.py:19
  152.3 10.5 %collective-permute-done.16 = bf16[128,16,128]{2,1,0:T(8,128)(2,1)S(1)} collective-permute-done((bf16[128,16,128]{2,1,0:T(8,128)(2,1)S(1)}, bf16[128,16,128]{2,1,0:T(8,128)(2,1)S(1)}, u32[]{:S(2)}, u32[]{:S(2)}) %collective-permute-start.16) | collective-permute-done | bytes 524320 | tf_op jit(solution)/shard_map/ppermute | solution.py:19
  166.9 4.1 %collective-permute-start.50 = (bf16[64,256]{1,0:T(8,128)(2,1)S(1)}, bf16[64,256]{1,0:T(8,128)(2,1)S(1)}, u32[]{:S(2)}, u32[]{:S(2)}) collective-permute-start(bf16[64,256]{1,0:T(8,128)(2,1)S(1)} %get-tuple-element.124), channel_id=1, source_target_pairs={{0,18},{1,19},{2,16},{3,17},{16,2},{17,3},{18,0},{19,1},{4,22},{5,... | collective-permute-start | bytes 98312 | tf_op jit(solution)/shard_map/ppermute | solution.py:19
  173.4 3.2 collective-permute-start.36
  181.1 2.3 add.61
  184.9 4.1 %collective-permute-start.40 = (bf16[64,8,128]{2,1,0:T(8,128)(2,1)S(1)}, bf16[64,8,128]{2,1,0:T(8,128)(2,1)S(1)}, u32[]{:S(2)}, u32[]{:S(2)}) collective-permute-start(bf16[64,8,128]{2,1,0:T(8,128)(2,1)S(1)} %bitcast.172), channel_id=1, source_target_pairs={{0,18},{1,19},{2,16},{3,17},{16,2},{17,3},{18,0},{19,1},{4,22},{5,... | collective-permute-start | bytes 393224 | tf_op jit(solution)/shard_map/ppermute | solution.py:19
  190.2 3.6 %collective-permute-start.9 = (bf16[64,16,128]{2,1,0:T(8,128)(2,1)S(1)}, bf16[64,16,128]{2,1,0:T(8,128)(2,1)S(1)}, u32[]{:S(2)}, u32[]{:S(2)}) collective-permute-start(bf16[64,16,128]{2,1,0:T(8,128)(2,1)S(1)} %bitcast.165), channel_id=1, source_target_pairs={{0,19},{1,18},{2,17},{3,16},{16,3},{17,2},{18,1},{19,0},{4,23},{5,... | collective-permute-start | bytes 786440 | tf_op jit(solution)/shard_map/ppermute | solution.py:19
  196.6 10.7 %collective-permute-done.40.refs_6_ = bf16[64,8,128]{2,1,0:T(8,128)(2,1)S(1)} collective-permute-done((bf16[64,8,128]{2,1,0:T(8,128)(2,1)S(1)}, bf16[64,8,128]{2,1,0:T(8,128)(2,1)S(1)}, u32[]{:S(2)}, u32[]{:S(2)}) %collective-permute-start.40) | collective-permute-done | bytes 131104 | tf_op jit(solution)/shard_map/ppermute | solution.py:19
  207.4 17.4 %collective-permute-start.12 = (bf16[64,16,128]{2,1,0:T(8,128)(2,1)S(1)}, bf16[64,16,128]{2,1,0:T(8,128)(2,1)S(1)}, u32[]{:S(2)}, u32[]{:S(2)}) collective-permute-start(bf16[64,16,128]{2,1,0:T(8,128)(2,1)S(1)} %bitcast.166), channel_id=1, source_target_pairs={{0,17},{1,16},{2,19},{3,18},{16,1},{17,0},{18,3},{19,2},{4,21},{5,... | collective-permute-start | bytes 786440 | tf_op jit(solution)/shard_map/ppermute | solution.py:19
  226.5 3.4 %collective-permute-done.10.refs_1_ = bf16[64,16,128]{2,1,0:T(8,128)(2,1)S(1)} collective-permute-done((bf16[64,16,128]{2,1,0:T(8,128)(2,1)S(1)}, bf16[64,16,128]{2,1,0:T(8,128)(2,1)S(1)}, u32[]{:S(2)}, u32[]{:S(2)}) %collective-permute-start.10) | collective-permute-done | bytes 262176 | tf_op jit(solution)/shard_map/ppermute | solution.py:19
  229.9 2.4 collective-permute-start.18
  234.6 11.5 %collective-permute-start.19 = (bf16[64,16,128]{2,1,0:T(8,128)(2,1)}, bf16[64,16,128]{2,1,0:T(8,128)(2,1)S(1)}, u32[]{:S(2)}, u32[]{:S(2)}) collective-permute-start(bf16[64,16,128]{2,1,0:T(8,128)(2,1)} %bitcast.58), channel_id=1, source_target_pairs={{0,18},{1,19},{2,16},{3,17},{16,2},{17,3},{18,0},{19,1},{4,22},{5,... | collective-permute-start | bytes 786440 | tf_op jit(solution)/shard_map/ppermute | solution.py:19
  250.0 4.1 %all-to-all-start.1 = ((bf16[64,8,256]{2,1,0:T(8,128)(2,1)}), bf16[64,8,256]{2,1,0:T(8,128)(2,1)}, u32[]{:S(2)}, u32[]{:S(2)}) async-start(bf16[64,8,256]{2,1,0:T(8,128)(2,1)} %copy.32), calls=%async_computation.1 | async-start | bytes 524288 | tf_op jit(solution)/shard_map/all_to_all | solution.py:420
  254.8 3.9 %collective-permute-start.21 = (bf16[64,16,128]{2,1,0:T(8,128)(2,1)}, bf16[64,16,128]{2,1,0:T(8,128)(2,1)S(1)}, u32[]{:S(2)}, u32[]{:S(2)}) collective-permute-start(bf16[64,16,128]{2,1,0:T(8,128)(2,1)} %bitcast.62), channel_id=1, source_target_pairs={{0,17},{1,16},{2,19},{3,18},{16,1},{17,0},{18,3},{19,2},{4,21},{5,... | collective-permute-start | bytes 786440 | tf_op jit(solution)/shard_map/ppermute | solution.py:19
  260.9 2.8 collective-permute-done.19.refs_1_
  264.3 4.3 %collective-permute-start.23 = (bf16[64,16,128]{2,1,0:T(8,128)(2,1)}, bf16[64,16,128]{2,1,0:T(8,128)(2,1)S(1)}, u32[]{:S(2)}, u32[]{:S(2)}) collective-permute-start(bf16[64,16,128]{2,1,0:T(8,128)(2,1)} %bitcast.66), channel_id=1, source_target_pairs={{0,1},{1,0},{2,3},{3,2},{16,17},{17,16},{18,19},{19,18},{4,5},{5,4... | collective-permute-start | bytes 786440 | tf_op jit(solution)/shard_map/ppermute | solution.py:19
  269.4 2.5 join.4
  271.9 4.6 %all-to-all-start = ((bf16[64,8,1024]{2,1,0:T(8,128)(2,1)}), bf16[64,8,1024]{2,1,0:T(8,128)(2,1)}, u32[]{:S(2)}, u32[]{:S(2)}) async-start(bf16[64,8,1024]{2,1,0:T(8,128)(2,1)} %join.4), calls=%async_computation | async-start | bytes 2097152 | tf_op jit(solution)/shard_map/all_to_all | solution.py:420
  279.5 1.7 collective-permute-start.31
  281.6 1.7 copy.36
  283.3 1.7 copy.41
  285.0 1.7 copy.42
  286.7 2.2 collective-permute-start.8
  296.9 5.3 %collective-permute-done.14.refs_5_ = bf16[64,16,128]{2,1,0:T(8,128)(2,1)} collective-permute-done((bf16[64,16,128]{2,1,0:T(8,128)(2,1)}, bf16[64,16,128]{2,1,0:T(8,128)(2,1)}, u32[]{:S(2)}, u32[]{:S(2)}) %collective-permute-start.14) | collective-permute-done | bytes 262176 | tf_op jit(solution)/shard_map/ppermute | solution.py:19
  302.3 2.1 project.4
  309.6 2.3 join.6.refs_1_
  311.9 1.7 join.7
  316.3 1.7 copy-done.25
  319.6 1.8 finish.1
  (216 shorter events, 76.3 us)
Async XLA Ops:
  2.9 15.8 %collective-permute-start = (bf16[1,16,512]{2,1,0:T(8,128)(2,1)S(1)}, bf16[1,16,512]{2,1,0:T(8,128)(2,1)S(1)}, u32[]{:S(2)}, u32[]{:S(2)}) collective-permute-start(bf16[1,16,512]{2,1,0:T(8,128)(2,1)S(1)} %get-tuple-element.137), channel_id=1, source_target_pairs={{0,2},{1,3},{2,0},{3,1},{4,6},{5,7},{6,4},{7,5},{8,10},{9,11},{10,... | collective-permute-start | bytes 49160 | tf_op jit(solution)/shard_map/ppermute | solution.py:19
  18.7 11.5 %collective-permute-start.1 = (bf16[2,16,512]{2,1,0:T(8,128)(2,1)S(1)}, bf16[2,16,512]{2,1,0:T(8,128)(2,1)S(1)}, u32[]{:S(2)}, u32[]{:S(2)}) collective-permute-start(bf16[2,16,512]{2,1,0:T(8,128)(2,1)S(1)} %pad_maximum_fusion.10), channel_id=1, source_target_pairs={{0,1},{1,0},{2,3},{3,2},{4,5},{5,4},{6,7},{7,6},{8,9},{9,8},{10,11... | collective-permute-start | bytes 98312 | tf_op jit(solution)/shard_map/ppermute | solution.py:19
  23.9 155.3 %collective-permute-start.28 = (f32[2,96,4096]{2,1,0:T(8,128)}, f32[2,96,4096]{2,1,0:T(8,128)}, u32[]{:S(2)}, u32[]{:S(2)}) collective-permute-start(f32[2,96,4096]{2,1,0:T(8,128)} %bitcast.17), channel_id=1, source_target_pairs={{0,4},{4,0},{8,12},{12,8},{1,5},{5,1},{9,13},{13,9},{2,6},{6,2},{1... | collective-permute-start | bytes 9437192 | tf_op jit(solution)/shard_map/ppermute | solution.py:19
  25.8 22.7 %collective-permute-start.34 = (bf16[128,8,128]{2,1,0:T(8,128)(2,1)}, bf16[128,8,128]{2,1,0:T(8,128)(2,1)}, u32[]{:S(2)}, u32[]{:S(2)}) collective-permute-start(bf16[128,8,128]{2,1,0:T(8,128)(2,1)} %get-tuple-element.58), channel_id=1, source_target_pairs={{0,3},{1,2},{2,1},{3,0},{4,7},{5,6},{6,5},{7,4},{8,11},{9,10},{10,... | collective-permute-start | bytes 786440 | tf_op jit(solution)/shard_map/ppermute | solution.py:19
  25.9 26.2 %collective-permute-start.33 = (bf16[128,8,128]{2,1,0:T(8,128)(2,1)}, bf16[128,8,128]{2,1,0:T(8,128)(2,1)}, u32[]{:S(2)}, u32[]{:S(2)}) collective-permute-start(bf16[128,8,128]{2,1,0:T(8,128)(2,1)} %get-tuple-element.57), channel_id=1, source_target_pairs={{0,2},{1,3},{2,0},{3,1},{4,6},{5,7},{6,4},{7,5},{8,10},{9,11},{10,... | collective-permute-start | bytes 786440 | tf_op jit(solution)/shard_map/ppermute | solution.py:19
  27.8 24.3 %collective-permute-start.32 = (bf16[128,8,128]{2,1,0:T(8,128)(2,1)}, bf16[128,8,128]{2,1,0:T(8,128)(2,1)}, u32[]{:S(2)}, u32[]{:S(2)}) collective-permute-start(bf16[128,8,128]{2,1,0:T(8,128)(2,1)} %get-tuple-element.56), channel_id=1, source_target_pairs={{0,1},{1,0},{2,3},{3,2},{4,5},{5,4},{6,7},{7,6},{8,9},{9,8},{10,11... | collective-permute-start | bytes 786440 | tf_op jit(solution)/shard_map/ppermute | solution.py:19
  37.9 17.8 %collective-permute-start.4 = (bf16[2,128,512]{2,1,0:T(8,128)(2,1)}, bf16[2,128,512]{2,1,0:T(8,128)(2,1)}, u32[]{:S(2)}, u32[]{:S(2)}) collective-permute-start(bf16[2,128,512]{2,1,0:T(8,128)(2,1)} %pad_maximum_fusion.8), channel_id=1, source_target_pairs={{0,8},{4,12},{8,0},{12,4},{1,9},{5,13},{9,1},{13,5},{2,10},{6,14},... | collective-permute-start | bytes 786440 | tf_op jit(solution)/shard_map/ppermute | solution.py:19
  48.5 67.6 %collective-permute-start.7 = (bf16[128,16,128]{2,1,0:T(8,128)(2,1)}, bf16[128,16,128]{2,1,0:T(8,128)(2,1)}, u32[]{:S(2)}, u32[]{:S(2)}) collective-permute-start(bf16[128,16,128]{2,1,0:T(8,128)(2,1)} %copy-done.19), channel_id=1, source_target_pairs={{0,3},{1,2},{2,1},{3,0},{4,7},{5,6},{6,5},{7,4},{8,11},{9,10},{10,... | collective-permute-start | bytes 1572872 | tf_op jit(solution)/shard_map/ppermute | solution.py:19
  52.1 65.8 %collective-permute-start.6 = (bf16[128,16,128]{2,1,0:T(8,128)(2,1)}, bf16[128,16,128]{2,1,0:T(8,128)(2,1)}, u32[]{:S(2)}, u32[]{:S(2)}) collective-permute-start(bf16[128,16,128]{2,1,0:T(8,128)(2,1)} %copy-done.18), channel_id=1, source_target_pairs={{0,2},{1,3},{2,0},{3,1},{4,6},{5,7},{6,4},{7,5},{8,10},{9,11},{10,... | collective-permute-start | bytes 1572872 | tf_op jit(solution)/shard_map/ppermute | solution.py:19
  52.1 25.9 %collective-permute-start.44 = (bf16[128,256]{1,0:T(8,128)(2,1)}, bf16[128,256]{1,0:T(8,128)(2,1)S(1)}, u32[]{:S(2)}, u32[]{:S(2)}) collective-permute-start(bf16[128,256]{1,0:T(8,128)(2,1)} %copy-done.22), channel_id=1, source_target_pairs={{0,3},{1,2},{2,1},{3,0},{4,7},{5,6},{6,5},{7,4},{8,11},{9,10},{10,... | collective-permute-start | bytes 196616 | tf_op jit(solution)/shard_map/ppermute | solution.py:19
  55.7 46.5 %collective-permute-start.43 = (bf16[128,256]{1,0:T(8,128)(2,1)S(1)}, bf16[128,256]{1,0:T(8,128)(2,1)S(1)}, u32[]{:S(2)}, u32[]{:S(2)}) collective-permute-start(bf16[128,256]{1,0:T(8,128)(2,1)S(1)} %copy-done.21), channel_id=1, source_target_pairs={{0,2},{1,3},{2,0},{3,1},{4,6},{5,7},{6,4},{7,5},{8,10},{9,11},{10,... | collective-permute-start | bytes 196616 | tf_op jit(solution)/shard_map/ppermute | solution.py:19
  78.0 41.6 %collective-permute-start.5 = (bf16[128,16,128]{2,1,0:T(8,128)(2,1)S(1)}, bf16[128,16,128]{2,1,0:T(8,128)(2,1)S(1)}, u32[]{:S(2)}, u32[]{:S(2)}) collective-permute-start(bf16[128,16,128]{2,1,0:T(8,128)(2,1)S(1)} %copy-done.17), channel_id=1, source_target_pairs={{0,1},{1,0},{2,3},{3,2},{4,5},{5,4},{6,7},{7,6},{8,9},{9,8},{10,11... | collective-permute-start | bytes 1572872 | tf_op jit(solution)/shard_map/ppermute | solution.py:19
  102.1 12.6 %collective-permute-start.42 = (bf16[128,256]{1,0:T(8,128)(2,1)S(1)}, bf16[128,256]{1,0:T(8,128)(2,1)S(1)}, u32[]{:S(2)}, u32[]{:S(2)}) collective-permute-start(bf16[128,256]{1,0:T(8,128)(2,1)S(1)} %get-tuple-element.60), channel_id=1, source_target_pairs={{0,1},{1,0},{2,3},{3,2},{4,5},{5,4},{6,7},{7,6},{8,9},{9,8},{10,11... | collective-permute-start | bytes 196616 | tf_op jit(solution)/shard_map/ppermute | solution.py:19
  114.7 16.7 %collective-permute-start.17 = (bf16[128,16,128]{2,1,0:T(8,128)(2,1)S(1)}, bf16[128,16,128]{2,1,0:T(8,128)(2,1)S(1)}, u32[]{:S(2)}, u32[]{:S(2)}) collective-permute-start(bf16[128,16,128]{2,1,0:T(8,128)(2,1)S(1)} %get-tuple-element.42), channel_id=1, source_target_pairs={{0,3},{1,2},{2,1},{3,0},{4,7},{5,6},{6,5},{7,4},{8,11},{9,10},{10,... | collective-permute-start | bytes 1572872 | tf_op jit(solution)/shard_map/ppermute | solution.py:19
  116.1 46.8 %collective-permute-start.16 = (bf16[128,16,128]{2,1,0:T(8,128)(2,1)S(1)}, bf16[128,16,128]{2,1,0:T(8,128)(2,1)S(1)}, u32[]{:S(2)}, u32[]{:S(2)}) collective-permute-start(bf16[128,16,128]{2,1,0:T(8,128)(2,1)S(1)} %get-tuple-element.41), channel_id=1, source_target_pairs={{0,2},{1,3},{2,0},{3,1},{4,6},{5,7},{6,4},{7,5},{8,10},{9,11},{10,... | collective-permute-start | bytes 1572872 | tf_op jit(solution)/shard_map/ppermute | solution.py:19
  118.0 47.4 %collective-permute-start.15 = (bf16[128,16,128]{2,1,0:T(8,128)(2,1)S(1)}, bf16[128,16,128]{2,1,0:T(8,128)(2,1)S(1)}, u32[]{:S(2)}, u32[]{:S(2)}) collective-permute-start(bf16[128,16,128]{2,1,0:T(8,128)(2,1)S(1)} %get-tuple-element.40), channel_id=1, source_target_pairs={{0,1},{1,0},{2,3},{3,2},{4,5},{5,4},{6,7},{7,6},{8,9},{9,8},{10,11... | collective-permute-start | bytes 1572872 | tf_op jit(solution)/shard_map/ppermute | solution.py:19
  119.5 47.4 %collective-permute-start.45 = (bf16[64,256]{1,0:T(8,128)(2,1)S(1)}, bf16[64,256]{1,0:T(8,128)(2,1)S(1)}, u32[]{:S(2)}, u32[]{:S(2)}) collective-permute-start(bf16[64,256]{1,0:T(8,128)(2,1)S(1)} %get-tuple-element.129), channel_id=1, source_target_pairs={{0,1},{1,0},{2,3},{3,2},{16,17},{17,16},{18,19},{19,18},{4,5},{5,4... | collective-permute-start | bytes 98312 | tf_op jit(solution)/shard_map/ppermute | solution.py:19
  131.4 35.5 %collective-permute-start.46 = (bf16[64,256]{1,0:T(8,128)(2,1)S(1)}, bf16[64,256]{1,0:T(8,128)(2,1)S(1)}, u32[]{:S(2)}, u32[]{:S(2)}) collective-permute-start(bf16[64,256]{1,0:T(8,128)(2,1)S(1)} %get-tuple-element.128), channel_id=1, source_target_pairs={{0,2},{1,3},{2,0},{3,1},{16,18},{17,19},{18,16},{19,17},{4,6},{5,7... | collective-permute-start | bytes 98312 | tf_op jit(solution)/shard_map/ppermute | solution.py:19
  162.9 8.2 %collective-permute-start.47 = (bf16[64,256]{1,0:T(8,128)(2,1)S(1)}, bf16[64,256]{1,0:T(8,128)(2,1)S(1)}, u32[]{:S(2)}, u32[]{:S(2)}) collective-permute-start(bf16[64,256]{1,0:T(8,128)(2,1)S(1)} %get-tuple-element.127), channel_id=1, source_target_pairs={{0,3},{1,2},{2,1},{3,0},{16,19},{17,18},{18,17},{19,16},{4,7},{5,6... | collective-permute-start | bytes 98312 | tf_op jit(solution)/shard_map/ppermute | solution.py:19
  166.9 9.6 %collective-permute-start.50 = (bf16[64,256]{1,0:T(8,128)(2,1)S(1)}, bf16[64,256]{1,0:T(8,128)(2,1)S(1)}, u32[]{:S(2)}, u32[]{:S(2)}) collective-permute-start(bf16[64,256]{1,0:T(8,128)(2,1)S(1)} %get-tuple-element.124), channel_id=1, source_target_pairs={{0,18},{1,19},{2,16},{3,17},{16,2},{17,3},{18,0},{19,1},{4,22},{5,... | collective-permute-start | bytes 98312 | tf_op jit(solution)/shard_map/ppermute | solution.py:19
  173.3 11.6 %collective-permute-start.35 = (bf16[64,8,128]{2,1,0:T(8,128)(2,1)S(1)}, bf16[64,8,128]{2,1,0:T(8,128)(2,1)S(1)}, u32[]{:S(2)}, u32[]{:S(2)}) collective-permute-start(bf16[64,8,128]{2,1,0:T(8,128)(2,1)S(1)} %bitcast.177), channel_id=1, source_target_pairs={{0,1},{1,0},{2,3},{3,2},{16,17},{17,16},{18,19},{19,18},{4,5},{5,4... | collective-permute-start | bytes 393224 | tf_op jit(solution)/shard_map/ppermute | solution.py:19
  173.4 11.5 %collective-permute-start.36 = (bf16[64,8,128]{2,1,0:T(8,128)(2,1)S(1)}, bf16[64,8,128]{2,1,0:T(8,128)(2,1)S(1)}, u32[]{:S(2)}, u32[]{:S(2)}) collective-permute-start(bf16[64,8,128]{2,1,0:T(8,128)(2,1)S(1)} %bitcast.176), channel_id=1, source_target_pairs={{0,2},{1,3},{2,0},{3,1},{16,18},{17,19},{18,16},{19,17},{4,6},{5,7... | collective-permute-start | bytes 393224 | tf_op jit(solution)/shard_map/ppermute | solution.py:19
  176.5 12.5 %collective-permute-start.37 = (bf16[64,8,128]{2,1,0:T(8,128)(2,1)S(1)}, bf16[64,8,128]{2,1,0:T(8,128)(2,1)S(1)}, u32[]{:S(2)}, u32[]{:S(2)}) collective-permute-start(bf16[64,8,128]{2,1,0:T(8,128)(2,1)S(1)} %bitcast.175), channel_id=1, source_target_pairs={{0,3},{1,2},{2,1},{3,0},{16,19},{17,18},{18,17},{19,16},{4,7},{5,6... | collective-permute-start | bytes 393224 | tf_op jit(solution)/shard_map/ppermute | solution.py:19
  177.7 12.4 %collective-permute-start.38 = (bf16[64,8,128]{2,1,0:T(8,128)(2,1)S(1)}, bf16[64,8,128]{2,1,0:T(8,128)(2,1)S(1)}, u32[]{:S(2)}, u32[]{:S(2)}) collective-permute-start(bf16[64,8,128]{2,1,0:T(8,128)(2,1)S(1)} %bitcast.174), channel_id=1, source_target_pairs={{0,16},{1,17},{2,18},{3,19},{16,0},{17,1},{18,2},{19,3},{4,20},{5,... | collective-permute-start | bytes 393224 | tf_op jit(solution)/shard_map/ppermute | solution.py:19
  179.3 14.5 %collective-permute-start.39 = (bf16[64,8,128]{2,1,0:T(8,128)(2,1)S(1)}, bf16[64,8,128]{2,1,0:T(8,128)(2,1)S(1)}, u32[]{:S(2)}, u32[]{:S(2)}) collective-permute-start(bf16[64,8,128]{2,1,0:T(8,128)(2,1)S(1)} %bitcast.173), channel_id=1, source_target_pairs={{0,17},{1,16},{2,19},{3,18},{16,1},{17,0},{18,3},{19,2},{4,21},{5,... | collective-permute-start | bytes 393224 | tf_op jit(solution)/shard_map/ppermute | solution.py:19
  184.8 83.8 %collective-permute-start.30 = (f32[2,96,1024]{2,1,0:T(8,128)}, f32[2,96,1024]{2,1,0:T(8,128)}, u32[]{:S(2)}, u32[]{:S(2)}) collective-permute-start(f32[2,96,1024]{2,1,0:T(8,128)} %bitcast.20), channel_id=1, source_target_pairs={{0,4},{4,0},{8,12},{12,8},{1,5},{5,1},{9,13},{13,9},{2,6},{6,2},{1... | collective-permute-start | bytes 2359304 | tf_op jit(solution)/shard_map/ppermute | solution.py:19
  184.9 22.5 %collective-permute-start.40 = (bf16[64,8,128]{2,1,0:T(8,128)(2,1)S(1)}, bf16[64,8,128]{2,1,0:T(8,128)(2,1)S(1)}, u32[]{:S(2)}, u32[]{:S(2)}) collective-permute-start(bf16[64,8,128]{2,1,0:T(8,128)(2,1)S(1)} %bitcast.172), channel_id=1, source_target_pairs={{0,18},{1,19},{2,16},{3,17},{16,2},{17,3},{18,0},{19,1},{4,22},{5,... | collective-permute-start | bytes 393224 | tf_op jit(solution)/shard_map/ppermute | solution.py:19
  189.0 18.4 %collective-permute-start.41 = (bf16[64,8,128]{2,1,0:T(8,128)(2,1)S(1)}, bf16[64,8,128]{2,1,0:T(8,128)(2,1)S(1)}, u32[]{:S(2)}, u32[]{:S(2)}) collective-permute-start(bf16[64,8,128]{2,1,0:T(8,128)(2,1)S(1)} %bitcast.171), channel_id=1, source_target_pairs={{0,19},{1,18},{2,17},{3,16},{16,3},{17,2},{18,1},{19,0},{4,23},{5,... | collective-permute-start | bytes 393224 | tf_op jit(solution)/shard_map/ppermute | solution.py:19
  190.2 17.2 %collective-permute-start.9 = (bf16[64,16,128]{2,1,0:T(8,128)(2,1)S(1)}, bf16[64,16,128]{2,1,0:T(8,128)(2,1)S(1)}, u32[]{:S(2)}, u32[]{:S(2)}) collective-permute-start(bf16[64,16,128]{2,1,0:T(8,128)(2,1)S(1)} %bitcast.165), channel_id=1, source_target_pairs={{0,19},{1,18},{2,17},{3,16},{16,3},{17,2},{18,1},{19,0},{4,23},{5,... | collective-permute-start | bytes 786440 | tf_op jit(solution)/shard_map/ppermute | solution.py:19
  193.7 122.5 %collective-permute-start.29 = (f32[1,96,4096]{2,1,0:T(8,128)}, f32[1,96,4096]{2,1,0:T(8,128)}, u32[]{:S(2)}, u32[]{:S(2)}) collective-permute-start(f32[1,96,4096]{2,1,0:T(8,128)} %slice.237), channel_id=1, source_target_pairs={{0,8},{4,12},{8,0},{12,4},{1,9},{5,13},{9,1},{13,5},{2,10},{6,14},... | collective-permute-start | bytes 4718600 | tf_op jit(solution)/shard_map/ppermute | solution.py:19
  207.4 22.5 %collective-permute-start.10 = (bf16[64,16,128]{2,1,0:T(8,128)(2,1)S(1)}, bf16[64,16,128]{2,1,0:T(8,128)(2,1)S(1)}, u32[]{:S(2)}, u32[]{:S(2)}) collective-permute-start(bf16[64,16,128]{2,1,0:T(8,128)(2,1)S(1)} %bitcast.168), channel_id=1, source_target_pairs={{0,18},{1,19},{2,16},{3,17},{16,2},{17,3},{18,0},{19,1},{4,22},{5,... | collective-permute-start | bytes 786440 | tf_op jit(solution)/shard_map/ppermute | solution.py:19
  207.4 26.5 %collective-permute-start.11 = (bf16[64,16,128]{2,1,0:T(8,128)(2,1)S(1)}, bf16[64,16,128]{2,1,0:T(8,128)(2,1)S(1)}, u32[]{:S(2)}, u32[]{:S(2)}) collective-permute-start(bf16[64,16,128]{2,1,0:T(8,128)(2,1)S(1)} %bitcast.167), channel_id=1, source_target_pairs={{0,3},{1,2},{2,1},{3,0},{16,19},{17,18},{18,17},{19,16},{4,7},{5,6... | collective-permute-start | bytes 786440 | tf_op jit(solution)/shard_map/ppermute | solution.py:19
  207.4 38.7 %collective-permute-start.12 = (bf16[64,16,128]{2,1,0:T(8,128)(2,1)S(1)}, bf16[64,16,128]{2,1,0:T(8,128)(2,1)S(1)}, u32[]{:S(2)}, u32[]{:S(2)}) collective-permute-start(bf16[64,16,128]{2,1,0:T(8,128)(2,1)S(1)} %bitcast.166), channel_id=1, source_target_pairs={{0,17},{1,16},{2,19},{3,18},{16,1},{17,0},{18,3},{19,2},{4,21},{5,... | collective-permute-start | bytes 786440 | tf_op jit(solution)/shard_map/ppermute | solution.py:19
  229.9 24.9 %collective-permute-start.18 = (bf16[64,16,128]{2,1,0:T(8,128)(2,1)}, bf16[64,16,128]{2,1,0:T(8,128)(2,1)S(1)}, u32[]{:S(2)}, u32[]{:S(2)}) collective-permute-start(bf16[64,16,128]{2,1,0:T(8,128)(2,1)} %bitcast.56), channel_id=1, source_target_pairs={{0,19},{1,18},{2,17},{3,16},{16,3},{17,2},{18,1},{19,0},{4,23},{5,... | collective-permute-start | bytes 786440 | tf_op jit(solution)/shard_map/ppermute | solution.py:19
  234.6 29.1 %collective-permute-start.19 = (bf16[64,16,128]{2,1,0:T(8,128)(2,1)}, bf16[64,16,128]{2,1,0:T(8,128)(2,1)S(1)}, u32[]{:S(2)}, u32[]{:S(2)}) collective-permute-start(bf16[64,16,128]{2,1,0:T(8,128)(2,1)} %bitcast.58), channel_id=1, source_target_pairs={{0,18},{1,19},{2,16},{3,17},{16,2},{17,3},{18,0},{19,1},{4,22},{5,... | collective-permute-start | bytes 786440 | tf_op jit(solution)/shard_map/ppermute | solution.py:19
  246.8 17.5 %collective-permute-start.20 = (bf16[64,16,128]{2,1,0:T(8,128)(2,1)}, bf16[64,16,128]{2,1,0:T(8,128)(2,1)S(1)}, u32[]{:S(2)}, u32[]{:S(2)}) collective-permute-start(bf16[64,16,128]{2,1,0:T(8,128)(2,1)} %bitcast.60), channel_id=1, source_target_pairs={{0,3},{1,2},{2,1},{3,0},{16,19},{17,18},{18,17},{19,16},{4,7},{5,6... | collective-permute-start | bytes 786440 | tf_op jit(solution)/shard_map/ppermute | solution.py:19
  250.0 21.9 %all-to-all-start.1 = ((bf16[64,8,256]{2,1,0:T(8,128)(2,1)}), bf16[64,8,256]{2,1,0:T(8,128)(2,1)}, u32[]{:S(2)}, u32[]{:S(2)}) async-start(bf16[64,8,256]{2,1,0:T(8,128)(2,1)} %copy.32), calls=%async_computation.1 | async-start | bytes 524288 | tf_op jit(solution)/shard_map/all_to_all | solution.py:420
  254.8 24.7 %collective-permute-start.21 = (bf16[64,16,128]{2,1,0:T(8,128)(2,1)}, bf16[64,16,128]{2,1,0:T(8,128)(2,1)S(1)}, u32[]{:S(2)}, u32[]{:S(2)}) collective-permute-start(bf16[64,16,128]{2,1,0:T(8,128)(2,1)} %bitcast.62), channel_id=1, source_target_pairs={{0,17},{1,16},{2,19},{3,18},{16,1},{17,0},{18,3},{19,2},{4,21},{5,... | collective-permute-start | bytes 786440 | tf_op jit(solution)/shard_map/ppermute | solution.py:19
  263.7 23.0 %collective-permute-start.22 = (bf16[64,16,128]{2,1,0:T(8,128)(2,1)}, bf16[64,16,128]{2,1,0:T(8,128)(2,1)S(1)}, u32[]{:S(2)}, u32[]{:S(2)}) collective-permute-start(bf16[64,16,128]{2,1,0:T(8,128)(2,1)} %bitcast.64), channel_id=1, source_target_pairs={{0,16},{1,17},{2,18},{3,19},{16,0},{17,1},{18,2},{19,3},{4,20},{5,... | collective-permute-start | bytes 786440 | tf_op jit(solution)/shard_map/ppermute | solution.py:19
  264.3 24.6 %collective-permute-start.23 = (bf16[64,16,128]{2,1,0:T(8,128)(2,1)}, bf16[64,16,128]{2,1,0:T(8,128)(2,1)S(1)}, u32[]{:S(2)}, u32[]{:S(2)}) collective-permute-start(bf16[64,16,128]{2,1,0:T(8,128)(2,1)} %bitcast.66), channel_id=1, source_target_pairs={{0,1},{1,0},{2,3},{3,2},{16,17},{17,16},{18,19},{19,18},{4,5},{5,4... | collective-permute-start | bytes 786440 | tf_op jit(solution)/shard_map/ppermute | solution.py:19
  268.6 21.7 %collective-permute-start.24 = (bf16[64,16,128]{2,1,0:T(8,128)(2,1)}, bf16[64,16,128]{2,1,0:T(8,128)(2,1)S(1)}, u32[]{:S(2)}, u32[]{:S(2)}) collective-permute-start(bf16[64,16,128]{2,1,0:T(8,128)(2,1)} %bitcast.70), channel_id=1, source_target_pairs={{0,2},{1,3},{2,0},{3,1},{16,18},{17,19},{18,16},{19,17},{4,6},{5,7... | collective-permute-start | bytes 786440 | tf_op jit(solution)/shard_map/ppermute | solution.py:19
  271.9 42.8 %all-to-all-start = ((bf16[64,8,1024]{2,1,0:T(8,128)(2,1)}), bf16[64,8,1024]{2,1,0:T(8,128)(2,1)}, u32[]{:S(2)}, u32[]{:S(2)}) async-start(bf16[64,8,1024]{2,1,0:T(8,128)(2,1)} %join.4), calls=%async_computation | async-start | bytes 2097152 | tf_op jit(solution)/shard_map/all_to_all | solution.py:420
  279.5 34.2 %collective-permute-start.31 = (f32[1,96,1024]{2,1,0:T(8,128)}, f32[1,96,1024]{2,1,0:T(8,128)}, u32[]{:S(2)}, u32[]{:S(2)}) collective-permute-start(f32[1,96,1024]{2,1,0:T(8,128)} %slice.241), channel_id=1, source_target_pairs={{0,8},{4,12},{8,0},{12,4},{1,9},{5,13},{9,1},{13,5},{2,10},{6,14},... | collective-permute-start | bytes 1179656 | tf_op jit(solution)/shard_map/ppermute | solution.py:19
  286.7 17.8 %collective-permute-start.8 = (bf16[64,16,128]{2,1,0:T(8,128)(2,1)}, bf16[64,16,128]{2,1,0:T(8,128)(2,1)}, u32[]{:S(2)}, u32[]{:S(2)}) collective-permute-start(bf16[64,16,128]{2,1,0:T(8,128)(2,1)} %bitcast.38), channel_id=1, source_target_pairs={{0,2},{1,3},{2,0},{3,1},{16,18},{17,19},{18,16},{19,17},{4,6},{5,7... | collective-permute-start | bytes 786440 | tf_op jit(solution)/shard_map/ppermute | solution.py:19
  290.4 11.9 %collective-permute-start.14 = (bf16[64,16,128]{2,1,0:T(8,128)(2,1)}, bf16[64,16,128]{2,1,0:T(8,128)(2,1)}, u32[]{:S(2)}, u32[]{:S(2)}) collective-permute-start(bf16[64,16,128]{2,1,0:T(8,128)(2,1)} %bitcast.50), channel_id=1, source_target_pairs={{0,1},{1,0},{2,3},{3,2},{16,17},{17,16},{18,19},{19,18},{4,5},{5,4... | collective-permute-start | bytes 786440 | tf_op jit(solution)/shard_map/ppermute | solution.py:19
  306.0 13.5 %collective-permute-start.25 = (f32[16,96]{1,0:T(8,128)S(1)}, f32[16,96]{1,0:T(8,128)S(1)}, u32[]{:S(2)}, u32[]{:S(2)}) collective-permute-start(f32[16,96]{1,0:T(8,128)S(1)} %get-tuple-element.52), channel_id=1, source_target_pairs={{0,4},{4,0},{8,12},{12,8},{1,5},{5,1},{9,13},{13,9},{2,6},{6,2},{1... | collective-permute-start | bytes 18440 | tf_op jit(solution)/shard_map/ppermute | solution.py:19
  306.1 13.4 %collective-permute-start.26 = (f32[16,96]{1,0:T(8,128)S(1)}, f32[16,96]{1,0:T(8,128)S(1)}, u32[]{:S(2)}, u32[]{:S(2)}) collective-permute-start(f32[16,96]{1,0:T(8,128)S(1)} %get-tuple-element.53), channel_id=1, source_target_pairs={{0,8},{4,12},{8,0},{12,4},{1,9},{5,13},{9,1},{13,5},{2,10},{6,14},... | collective-permute-start | bytes 18440 | tf_op jit(solution)/shard_map/ppermute | solution.py:19
  306.6 13.0 %collective-permute-start.27 = (f32[16,96]{1,0:T(8,128)S(1)}, f32[16,96]{1,0:T(8,128)S(1)}, u32[]{:S(2)}, u32[]{:S(2)}) collective-permute-start(f32[16,96]{1,0:T(8,128)S(1)} %get-tuple-element.54), channel_id=1, source_target_pairs={{0,12},{4,8},{8,4},{12,0},{1,13},{5,9},{9,5},{13,1},{2,14},{6,10},... | collective-permute-start | bytes 18440 | tf_op jit(solution)/shard_map/ppermute | solution.py:19
  (41 other events, 243.7 us)

commit v7 on v6

--- a/solution.py
+++ b/solution.py
@@ -394,9 +394,11 @@
     def send(made, sent):
         return {s: swap(made[s], PLACES, s) if s else made[s] for s in sent}
 
-    crossing = [s for s in reversed(shifts) if s % ring >= ring // 2]
+    crossing = [s for s in shifts if s % ring >= ring // 2]
+    crossing = sorted(crossing, key=lambda s: -(s // ring))
     late = crossing[-1:]
-    early = crossing[:-1] + [s for s in reversed(shifts) if s % ring < ring // 2]
+    near = [s for s in reversed(shifts) if s % ring < ring // 2]
+    early = sorted(near, key=lambda s: s % ring == 0) + crossing[:-1]
     emitted = {}
     for name, chunk in [("query", 0), ("value", 0)] + [("down", c) for c in range(chunks)]:
         made = emit(name, chunk)
@@ -444,7 +446,9 @@
                     some, half, head.stride, start, head.width, tokens, bounds, low_rank,
                     half is late,
                 )
-                down_factors = head.join(some, half, chunk, down_factors)
+            down_factors = head.join(
+                [pieces[s] for s in early + late], early + late, chunk, down_factors
+            )
     else:
         down_factors = head.join(ordered(emitted["down", 0]), shifts)
         projected = jnp.einsum(
@@ -461,7 +465,7 @@
             for s in range(parts)
         ]
     shares = [low_rank[0]] + [swap(low_rank[s], "tensor", s) for s in range(1, parts)]
-    query, value = finish(shares, bounds, [base_query, base_value, own_query, own_value], steps=8)
+    query, value = finish(shares, bounds, [base_query, base_value, own_query, own_value], steps=4)
     return query, value, down_factors, query_up_factors, value_up_factors
 
 

time: 323 us -> 336 us (1.040)
  waiting for transfers between devices: 75.5 us -> 112 us
  starting transfers between devices: 149 us -> 127 us
    ppermute x52, waiting for transfers between devices: 75.5 us -> 112 us  [swap(): return lax.ppermute(x, axes, [(a, a ^ shift) for a in range(total)])]
    ppermute x52, starting transfers between devices: 141 us -> 118 us  [swap(): return lax.ppermute(x, axes, [(a, a ^ shift) for a in range(total)])]
    pallas_call x4 -> x3, Pallas kernels: 8.11 us -> 6.66 us  [join(): pl.pallas_call(functools.partial(join_kernel, shifts, stride, start, widt...]
  transfers between devices with their start and end apart: 54 -> 54, of which waited for: 12 -> 14; matrix products, arithmetic and copies ran while one was open for 18% -> 18% of each run, Pallas kernels for 6% -> 5%
where the time goes in v7:
time: 336 us; the launch traced here: 334 us
  starting transfers between devices  127 us (38%)
  waiting for transfers between devices  112 us (33%)
  local copies, waits for them, and re-layouts  43.9 us (13%)
  Pallas kernels  20 us (6%)
  matrix products  16.6 us (5%)
  other arithmetic  13 us (4%)
    ppermute x52, starting transfers between devices, swap(): return lax.ppermute(x, axes, [(a, a ^ shift) for a in range(total)])  118 us
    ppermute x52, waiting for transfers between devices, swap(): return lax.ppermute(x, axes, [(a, a ^ shift) for a in range(total)])  112 us
    unnamed x99, local copies, waits for them, and re-layouts  28.5 us
    dot_general x1, matrix products, local(): base_query = jnp.dot(turned, w_query, preferred_element_type=jnp.float32)  10.2 us
    all_to_all x2, starting transfers between devices, own_block(): lax.all_to_all(factors, 'tensor', split_axis=0, concat_axis=0, tiled=True)  8.69 us
    slice x4, local copies, waits for them, and re-layouts, reduce_blocks(): came = swap(partial[half:], axis, step)  6.95 us
  transfers between devices with their start and end apart: 54, of which 14 were waited for; matrix products, arithmetic and copies ran while one was open for 18% of the time, Pallas kernels for 5%

profile of v7, /device:TPU:0, one launch (start us, length us, event | category | flops | bytes accessed | tf_op | source)
XLA Modules:
  0.0 334.3 jit_solution(7346232776868343752)
XLA Ops:
  2.9 4.1 %collective-permute-start = (bf16[1,16,512]{2,1,0:T(8,128)(2,1)S(1)}, bf16[1,16,512]{2,1,0:T(8,128)(2,1)S(1)}, u32[]{:S(2)}, u32[]{:S(2)}) collective-permute-start(bf16[1,16,512]{2,1,0:T(8,128)(2,1)S(1)} %get-tuple-element.137), channel_id=1, source_target_pairs={{0,2},{1,3},{2,0},{3,1},{4,6},{5,7},{6,4},{7,5},{8,10},{9,11},{10,... | collective-permute-start | bytes 49160 | tf_op jit(solution)/shard_map/ppermute | solution.py:19
  8.5 10.2 %fusion.9 = f32[384,4096]{1,0:T(8,128)S(1)} fusion(bf16[2048,4096]{1,0:T(8,128)(2,1)} %param.16, bf16[96,2048]{1,0:T(8,128)(2,1)S(1)} %get-tuple-element.106, bf16[96,2048]{1,0:T(8,128)(2,1)S(1)} %get-tuple-element.107, bf16[96,2048]{1,0:T(8,128)(2,1)S(1)} %get-tuple-element.108, bf16[96,2048]{1,0:T(8,128)(2,1)S(1)} %get-tuple-element.105), kind=kOutput, calls=%fused_computation.25 | convolution fusion | flops 6448742400 | bytes 24641536 | tf_op jit(solution)/shard_map/dot_general | solution.py:416
  18.7 1.6 collective-permute-start.1
  20.4 3.5 %fusion.29 = (f32[192,4096]{1,0:T(8,128)}, f32[192,4096]{1,0:T(8,128)}) fusion(f32[384,4096]{1,0:T(8,128)S(1)} %fusion.9), kind=kLoop, calls=%fused_computation.84 | loop fusion | bytes 12582912 | tf_op jit(solution)/shard_map/slice | solution.py:297
  23.9 1.9 cut.5
  25.9 1.9 collective-permute-start.33
  27.8 2.5 collective-permute-start.32
  31.9 2.7 collective-permute-done.2
  34.6 1.8 fusion.8
  40.7 1.7 cut.3
  44.8 1.9 cut.4
  48.7 3.4 %collective-permute-done.33 = bf16[128,8,128]{2,1,0:T(8,128)(2,1)} collective-permute-done((bf16[128,8,128]{2,1,0:T(8,128)(2,1)}, bf16[128,8,128]{2,1,0:T(8,128)(2,1)}, u32[]{:S(2)}, u32[]{:S(2)}) %collective-permute-start.33) | collective-permute-done | bytes 262176 | tf_op jit(solution)/shard_map/ppermute | solution.py:19
  53.5 2.2 pad_maximum_fusion.3
  55.7 2.0 collective-permute-start.43
  59.6 2.0 reshape.154
  63.7 14.3 %collective-permute-done.44 = bf16[128,256]{1,0:T(8,128)(2,1)S(1)} collective-permute-done((bf16[128,256]{1,0:T(8,128)(2,1)}, bf16[128,256]{1,0:T(8,128)(2,1)S(1)}, u32[]{:S(2)}, u32[]{:S(2)}) %collective-permute-start.44) | collective-permute-done | bytes 65568 | tf_op jit(solution)/shard_map/ppermute | solution.py:19
  78.0 23.7 %collective-permute-start.5 = (bf16[128,16,128]{2,1,0:T(8,128)(2,1)S(1)}, bf16[128,16,128]{2,1,0:T(8,128)(2,1)S(1)}, u32[]{:S(2)}, u32[]{:S(2)}) collective-permute-start(bf16[128,16,128]{2,1,0:T(8,128)(2,1)S(1)} %copy-done.17), channel_id=1, source_target_pairs={{0,1},{1,0},{2,3},{3,2},{4,5},{5,4},{6,7},{7,6},{8,9},{9,8},{10,11... | collective-permute-start | bytes 1572872 | tf_op jit(solution)/shard_map/ppermute | solution.py:19
  103.1 11.7 %collective-permute-done.42 = bf16[128,256]{1,0:T(8,128)(2,1)S(1)} collective-permute-done((bf16[128,256]{1,0:T(8,128)(2,1)S(1)}, bf16[128,256]{1,0:T(8,128)(2,1)S(1)}, u32[]{:S(2)}, u32[]{:S(2)}) %collective-permute-start.42) | collective-permute-done | bytes 65568 | tf_op jit(solution)/shard_map/ppermute | solution.py:19
  121.5 9.9 %collective-permute-done.17 = bf16[128,16,128]{2,1,0:T(8,128)(2,1)S(1)} collective-permute-done((bf16[128,16,128]{2,1,0:T(8,128)(2,1)S(1)}, bf16[128,16,128]{2,1,0:T(8,128)(2,1)S(1)}, u32[]{:S(2)}, u32[]{:S(2)}) %collective-permute-start.17) | collective-permute-done | bytes 524320 | tf_op jit(solution)/shard_map/ppermute | solution.py:19
  131.4 20.9 %collective-permute-start.46 = (bf16[64,256]{1,0:T(8,128)(2,1)S(1)}, bf16[64,256]{1,0:T(8,128)(2,1)S(1)}, u32[]{:S(2)}, u32[]{:S(2)}) collective-permute-start(bf16[64,256]{1,0:T(8,128)(2,1)S(1)} %get-tuple-element.128), channel_id=1, source_target_pairs={{0,2},{1,3},{2,0},{3,1},{16,18},{17,19},{18,16},{19,17},{4,6},{5,7... | collective-permute-start | bytes 98312 | tf_op jit(solution)/shard_map/ppermute | solution.py:19
  152.3 10.5 %collective-permute-done.16 = bf16[128,16,128]{2,1,0:T(8,128)(2,1)S(1)} collective-permute-done((bf16[128,16,128]{2,1,0:T(8,128)(2,1)S(1)}, bf16[128,16,128]{2,1,0:T(8,128)(2,1)S(1)}, u32[]{:S(2)}, u32[]{:S(2)}) %collective-permute-start.16) | collective-permute-done | bytes 524320 | tf_op jit(solution)/shard_map/ppermute | solution.py:19
  166.9 4.1 %collective-permute-start.50 = (bf16[64,256]{1,0:T(8,128)(2,1)S(1)}, bf16[64,256]{1,0:T(8,128)(2,1)S(1)}, u32[]{:S(2)}, u32[]{:S(2)}) collective-permute-start(bf16[64,256]{1,0:T(8,128)(2,1)S(1)} %get-tuple-element.124), channel_id=1, source_target_pairs={{0,18},{1,19},{2,16},{3,17},{16,2},{17,3},{18,0},{19,1},{4,22},{5,... | collective-permute-start | bytes 98312 | tf_op jit(solution)/shard_map/ppermute | solution.py:19
  173.4 3.2 collective-permute-start.36
  181.2 2.3 add.61
  184.9 4.1 %collective-permute-start.40 = (bf16[64,8,128]{2,1,0:T(8,128)(2,1)S(1)}, bf16[64,8,128]{2,1,0:T(8,128)(2,1)S(1)}, u32[]{:S(2)}, u32[]{:S(2)}) collective-permute-start(bf16[64,8,128]{2,1,0:T(8,128)(2,1)S(1)} %bitcast.172), channel_id=1, source_target_pairs={{0,18},{1,19},{2,16},{3,17},{16,2},{17,3},{18,0},{19,1},{4,22},{5,... | collective-permute-start | bytes 393224 | tf_op jit(solution)/shard_map/ppermute | solution.py:19
  193.2 5.9 %collective-permute-done.40.refs_6_ = bf16[64,8,128]{2,1,0:T(8,128)(2,1)S(1)} collective-permute-done((bf16[64,8,128]{2,1,0:T(8,128)(2,1)S(1)}, bf16[64,8,128]{2,1,0:T(8,128)(2,1)S(1)}, u32[]{:S(2)}, u32[]{:S(2)}) %collective-permute-start.40) | collective-permute-done | bytes 131104 | tf_op jit(solution)/shard_map/ppermute | solution.py:19
  199.7 4.8 %collective-permute-done.9.refs_0_ = bf16[64,16,128]{2,1,0:T(8,128)(2,1)S(1)} collective-permute-done((bf16[64,16,128]{2,1,0:T(8,128)(2,1)S(1)}, bf16[64,16,128]{2,1,0:T(8,128)(2,1)S(1)}, u32[]{:S(2)}, u32[]{:S(2)}) %collective-permute-start.9) | collective-permute-done | bytes 262176 | tf_op jit(solution)/shard_map/ppermute | solution.py:19
  204.5 2.5 collective-permute-start.12
  208.5 3.8 %collective-permute-done.10.refs_1_ = bf16[64,16,128]{2,1,0:T(8,128)(2,1)S(1)} collective-permute-done((bf16[64,16,128]{2,1,0:T(8,128)(2,1)S(1)}, bf16[64,16,128]{2,1,0:T(8,128)(2,1)S(1)}, u32[]{:S(2)}, u32[]{:S(2)}) %collective-permute-start.10) | collective-permute-done | bytes 262176 | tf_op jit(solution)/shard_map/ppermute | solution.py:19
  214.6 11.0 %collective-permute-start.19 = (bf16[64,16,128]{2,1,0:T(8,128)(2,1)}, bf16[64,16,128]{2,1,0:T(8,128)(2,1)S(1)}, u32[]{:S(2)}, u32[]{:S(2)}) collective-permute-start(bf16[64,16,128]{2,1,0:T(8,128)(2,1)} %bitcast.58), channel_id=1, source_target_pairs={{0,1},{1,0},{2,3},{3,2},{16,17},{17,16},{18,19},{19,18},{4,5},{5,4... | collective-permute-start | bytes 786440 | tf_op jit(solution)/shard_map/ppermute | solution.py:19
  227.9 4.1 %all-to-all-start.1 = ((bf16[64,8,256]{2,1,0:T(8,128)(2,1)}), bf16[64,8,256]{2,1,0:T(8,128)(2,1)}, u32[]{:S(2)}, u32[]{:S(2)}) async-start(bf16[64,8,256]{2,1,0:T(8,128)(2,1)} %copy.31), calls=%async_computation.1 | async-start | bytes 524288 | tf_op jit(solution)/shard_map/all_to_all | solution.py:422
  235.0 3.3 collective-permute-start.22
  239.4 2.3 collective-permute-start.24
  241.8 2.5 join.3
  244.3 4.6 %all-to-all-start = ((bf16[64,8,1024]{2,1,0:T(8,128)(2,1)}), bf16[64,8,1024]{2,1,0:T(8,128)(2,1)}, u32[]{:S(2)}, u32[]{:S(2)}) async-start(bf16[64,8,1024]{2,1,0:T(8,128)(2,1)} %join.3), calls=%async_computation | async-start | bytes 2097152 | tf_op jit(solution)/shard_map/all_to_all | solution.py:422
  251.8 13.6 %collective-permute-done.21.refs_4_ = bf16[64,16,128]{2,1,0:T(8,128)(2,1)S(1)} collective-permute-done((bf16[64,16,128]{2,1,0:T(8,128)(2,1)}, bf16[64,16,128]{2,1,0:T(8,128)(2,1)S(1)}, u32[]{:S(2)}, u32[]{:S(2)}) %collective-permute-start.21) | collective-permute-done | bytes 262176 | tf_op jit(solution)/shard_map/ppermute | solution.py:19
  265.4 1.7 collective-permute-start.31
  267.4 1.7 copy.35
  269.1 1.7 copy.41
  270.8 1.7 copy.42
  273.9 14.5 %collective-permute-done.23.refs_6_ = bf16[64,16,128]{2,1,0:T(8,128)(2,1)S(1)} collective-permute-done((bf16[64,16,128]{2,1,0:T(8,128)(2,1)}, bf16[64,16,128]{2,1,0:T(8,128)(2,1)S(1)}, u32[]{:S(2)}, u32[]{:S(2)}) %collective-permute-start.23) | collective-permute-done | bytes 262176 | tf_op jit(solution)/shard_map/ppermute | solution.py:19
  288.4 5.2 %collective-permute-start.14 = (bf16[64,16,128]{2,1,0:T(8,128)(2,1)}, bf16[64,16,128]{2,1,0:T(8,128)(2,1)}, u32[]{:S(2)}, u32[]{:S(2)}) collective-permute-start(bf16[64,16,128]{2,1,0:T(8,128)(2,1)} %bitcast.52), channel_id=1, source_target_pairs={{0,2},{1,3},{2,0},{3,1},{16,18},{17,19},{18,16},{19,17},{4,6},{5,7... | collective-permute-start | bytes 786440 | tf_op jit(solution)/shard_map/ppermute | solution.py:19
  300.7 15.9 %collective-permute-done.14.refs_6_ = bf16[64,16,128]{2,1,0:T(8,128)(2,1)} collective-permute-done((bf16[64,16,128]{2,1,0:T(8,128)(2,1)}, bf16[64,16,128]{2,1,0:T(8,128)(2,1)}, u32[]{:S(2)}, u32[]{:S(2)}) %collective-permute-start.14) | collective-permute-done | bytes 262176 | tf_op jit(solution)/shard_map/ppermute | solution.py:19
  316.6 2.1 project.4
  320.5 1.7 collective-permute-start.26
  323.9 2.6 join.5
  329.1 1.7 copy-done.25
  332.4 1.7 finish.1
  (215 shorter events, 74.0 us)
Async XLA Ops:
  2.9 15.8 %collective-permute-start = (bf16[1,16,512]{2,1,0:T(8,128)(2,1)S(1)}, bf16[1,16,512]{2,1,0:T(8,128)(2,1)S(1)}, u32[]{:S(2)}, u32[]{:S(2)}) collective-permute-start(bf16[1,16,512]{2,1,0:T(8,128)(2,1)S(1)} %get-tuple-element.137), channel_id=1, source_target_pairs={{0,2},{1,3},{2,0},{3,1},{4,6},{5,7},{6,4},{7,5},{8,10},{9,11},{10,... | collective-permute-start | bytes 49160 | tf_op jit(solution)/shard_map/ppermute | solution.py:19
  18.7 11.5 %collective-permute-start.1 = (bf16[2,16,512]{2,1,0:T(8,128)(2,1)S(1)}, bf16[2,16,512]{2,1,0:T(8,128)(2,1)S(1)}, u32[]{:S(2)}, u32[]{:S(2)}) collective-permute-start(bf16[2,16,512]{2,1,0:T(8,128)(2,1)S(1)} %pad_maximum_fusion.10), channel_id=1, source_target_pairs={{0,1},{1,0},{2,3},{3,2},{4,5},{5,4},{6,7},{7,6},{8,9},{9,8},{10,11... | collective-permute-start | bytes 98312 | tf_op jit(solution)/shard_map/ppermute | solution.py:19
  23.9 155.4 %collective-permute-start.28 = (f32[2,96,4096]{2,1,0:T(8,128)}, f32[2,96,4096]{2,1,0:T(8,128)}, u32[]{:S(2)}, u32[]{:S(2)}) collective-permute-start(f32[2,96,4096]{2,1,0:T(8,128)} %bitcast.17), channel_id=1, source_target_pairs={{0,4},{4,0},{8,12},{12,8},{1,5},{5,1},{9,13},{13,9},{2,6},{6,2},{1... | collective-permute-start | bytes 9437192 | tf_op jit(solution)/shard_map/ppermute | solution.py:19
  25.8 22.7 %collective-permute-start.34 = (bf16[128,8,128]{2,1,0:T(8,128)(2,1)}, bf16[128,8,128]{2,1,0:T(8,128)(2,1)}, u32[]{:S(2)}, u32[]{:S(2)}) collective-permute-start(bf16[128,8,128]{2,1,0:T(8,128)(2,1)} %get-tuple-element.58), channel_id=1, source_target_pairs={{0,3},{1,2},{2,1},{3,0},{4,7},{5,6},{6,5},{7,4},{8,11},{9,10},{10,... | collective-permute-start | bytes 786440 | tf_op jit(solution)/shard_map/ppermute | solution.py:19
  25.9 26.2 %collective-permute-start.33 = (bf16[128,8,128]{2,1,0:T(8,128)(2,1)}, bf16[128,8,128]{2,1,0:T(8,128)(2,1)}, u32[]{:S(2)}, u32[]{:S(2)}) collective-permute-start(bf16[128,8,128]{2,1,0:T(8,128)(2,1)} %get-tuple-element.57), channel_id=1, source_target_pairs={{0,2},{1,3},{2,0},{3,1},{4,6},{5,7},{6,4},{7,5},{8,10},{9,11},{10,... | collective-permute-start | bytes 786440 | tf_op jit(solution)/shard_map/ppermute | solution.py:19
  27.8 24.3 %collective-permute-start.32 = (bf16[128,8,128]{2,1,0:T(8,128)(2,1)}, bf16[128,8,128]{2,1,0:T(8,128)(2,1)}, u32[]{:S(2)}, u32[]{:S(2)}) collective-permute-start(bf16[128,8,128]{2,1,0:T(8,128)(2,1)} %get-tuple-element.56), channel_id=1, source_target_pairs={{0,1},{1,0},{2,3},{3,2},{4,5},{5,4},{6,7},{7,6},{8,9},{9,8},{10,11... | collective-permute-start | bytes 786440 | tf_op jit(solution)/shard_map/ppermute | solution.py:19
  37.9 17.8 %collective-permute-start.4 = (bf16[2,128,512]{2,1,0:T(8,128)(2,1)}, bf16[2,128,512]{2,1,0:T(8,128)(2,1)}, u32[]{:S(2)}, u32[]{:S(2)}) collective-permute-start(bf16[2,128,512]{2,1,0:T(8,128)(2,1)} %pad_maximum_fusion.8), channel_id=1, source_target_pairs={{0,8},{4,12},{8,0},{12,4},{1,9},{5,13},{9,1},{13,5},{2,10},{6,14},... | collective-permute-start | bytes 786440 | tf_op jit(solution)/shard_map/ppermute | solution.py:19
  48.5 67.6 %collective-permute-start.7 = (bf16[128,16,128]{2,1,0:T(8,128)(2,1)}, bf16[128,16,128]{2,1,0:T(8,128)(2,1)}, u32[]{:S(2)}, u32[]{:S(2)}) collective-permute-start(bf16[128,16,128]{2,1,0:T(8,128)(2,1)} %copy-done.19), channel_id=1, source_target_pairs={{0,3},{1,2},{2,1},{3,0},{4,7},{5,6},{6,5},{7,4},{8,11},{9,10},{10,... | collective-permute-start | bytes 1572872 | tf_op jit(solution)/shard_map/ppermute | solution.py:19
  52.1 65.8 %collective-permute-start.6 = (bf16[128,16,128]{2,1,0:T(8,128)(2,1)}, bf16[128,16,128]{2,1,0:T(8,128)(2,1)}, u32[]{:S(2)}, u32[]{:S(2)}) collective-permute-start(bf16[128,16,128]{2,1,0:T(8,128)(2,1)} %copy-done.18), channel_id=1, source_target_pairs={{0,2},{1,3},{2,0},{3,1},{4,6},{5,7},{6,4},{7,5},{8,10},{9,11},{10,... | collective-permute-start | bytes 1572872 | tf_op jit(solution)/shard_map/ppermute | solution.py:19
  52.1 25.9 %collective-permute-start.44 = (bf16[128,256]{1,0:T(8,128)(2,1)}, bf16[128,256]{1,0:T(8,128)(2,1)S(1)}, u32[]{:S(2)}, u32[]{:S(2)}) collective-permute-start(bf16[128,256]{1,0:T(8,128)(2,1)} %copy-done.22), channel_id=1, source_target_pairs={{0,3},{1,2},{2,1},{3,0},{4,7},{5,6},{6,5},{7,4},{8,11},{9,10},{10,... | collective-permute-start | bytes 196616 | tf_op jit(solution)/shard_map/ppermute | solution.py:19
  55.7 46.5 %collective-permute-start.43 = (bf16[128,256]{1,0:T(8,128)(2,1)S(1)}, bf16[128,256]{1,0:T(8,128)(2,1)S(1)}, u32[]{:S(2)}, u32[]{:S(2)}) collective-permute-start(bf16[128,256]{1,0:T(8,128)(2,1)S(1)} %copy-done.21), channel_id=1, source_target_pairs={{0,2},{1,3},{2,0},{3,1},{4,6},{5,7},{6,4},{7,5},{8,10},{9,11},{10,... | collective-permute-start | bytes 196616 | tf_op jit(solution)/shard_map/ppermute | solution.py:19
  78.0 41.6 %collective-permute-start.5 = (bf16[128,16,128]{2,1,0:T(8,128)(2,1)S(1)}, bf16[128,16,128]{2,1,0:T(8,128)(2,1)S(1)}, u32[]{:S(2)}, u32[]{:S(2)}) collective-permute-start(bf16[128,16,128]{2,1,0:T(8,128)(2,1)S(1)} %copy-done.17), channel_id=1, source_target_pairs={{0,1},{1,0},{2,3},{3,2},{4,5},{5,4},{6,7},{7,6},{8,9},{9,8},{10,11... | collective-permute-start | bytes 1572872 | tf_op jit(solution)/shard_map/ppermute | solution.py:19
  102.1 12.6 %collective-permute-start.42 = (bf16[128,256]{1,0:T(8,128)(2,1)S(1)}, bf16[128,256]{1,0:T(8,128)(2,1)S(1)}, u32[]{:S(2)}, u32[]{:S(2)}) collective-permute-start(bf16[128,256]{1,0:T(8,128)(2,1)S(1)} %get-tuple-element.60), channel_id=1, source_target_pairs={{0,1},{1,0},{2,3},{3,2},{4,5},{5,4},{6,7},{7,6},{8,9},{9,8},{10,11... | collective-permute-start | bytes 196616 | tf_op jit(solution)/shard_map/ppermute | solution.py:19
  114.7 16.7 %collective-permute-start.17 = (bf16[128,16,128]{2,1,0:T(8,128)(2,1)S(1)}, bf16[128,16,128]{2,1,0:T(8,128)(2,1)S(1)}, u32[]{:S(2)}, u32[]{:S(2)}) collective-permute-start(bf16[128,16,128]{2,1,0:T(8,128)(2,1)S(1)} %get-tuple-element.42), channel_id=1, source_target_pairs={{0,3},{1,2},{2,1},{3,0},{4,7},{5,6},{6,5},{7,4},{8,11},{9,10},{10,... | collective-permute-start | bytes 1572872 | tf_op jit(solution)/shard_map/ppermute | solution.py:19
  116.1 46.8 %collective-permute-start.16 = (bf16[128,16,128]{2,1,0:T(8,128)(2,1)S(1)}, bf16[128,16,128]{2,1,0:T(8,128)(2,1)S(1)}, u32[]{:S(2)}, u32[]{:S(2)}) collective-permute-start(bf16[128,16,128]{2,1,0:T(8,128)(2,1)S(1)} %get-tuple-element.41), channel_id=1, source_target_pairs={{0,2},{1,3},{2,0},{3,1},{4,6},{5,7},{6,4},{7,5},{8,10},{9,11},{10,... | collective-permute-start | bytes 1572872 | tf_op jit(solution)/shard_map/ppermute | solution.py:19
  118.0 47.4 %collective-permute-start.15 = (bf16[128,16,128]{2,1,0:T(8,128)(2,1)S(1)}, bf16[128,16,128]{2,1,0:T(8,128)(2,1)S(1)}, u32[]{:S(2)}, u32[]{:S(2)}) collective-permute-start(bf16[128,16,128]{2,1,0:T(8,128)(2,1)S(1)} %get-tuple-element.40), channel_id=1, source_target_pairs={{0,1},{1,0},{2,3},{3,2},{4,5},{5,4},{6,7},{7,6},{8,9},{9,8},{10,11... | collective-permute-start | bytes 1572872 | tf_op jit(solution)/shard_map/ppermute | solution.py:19
  119.5 47.4 %collective-permute-start.45 = (bf16[64,256]{1,0:T(8,128)(2,1)S(1)}, bf16[64,256]{1,0:T(8,128)(2,1)S(1)}, u32[]{:S(2)}, u32[]{:S(2)}) collective-permute-start(bf16[64,256]{1,0:T(8,128)(2,1)S(1)} %get-tuple-element.129), channel_id=1, source_target_pairs={{0,1},{1,0},{2,3},{3,2},{16,17},{17,16},{18,19},{19,18},{4,5},{5,4... | collective-permute-start | bytes 98312 | tf_op jit(solution)/shard_map/ppermute | solution.py:19
  131.4 35.5 %collective-permute-start.46 = (bf16[64,256]{1,0:T(8,128)(2,1)S(1)}, bf16[64,256]{1,0:T(8,128)(2,1)S(1)}, u32[]{:S(2)}, u32[]{:S(2)}) collective-permute-start(bf16[64,256]{1,0:T(8,128)(2,1)S(1)} %get-tuple-element.128), channel_id=1, source_target_pairs={{0,2},{1,3},{2,0},{3,1},{16,18},{17,19},{18,16},{19,17},{4,6},{5,7... | collective-permute-start | bytes 98312 | tf_op jit(solution)/shard_map/ppermute | solution.py:19
  166.9 9.6 %collective-permute-start.50 = (bf16[64,256]{1,0:T(8,128)(2,1)S(1)}, bf16[64,256]{1,0:T(8,128)(2,1)S(1)}, u32[]{:S(2)}, u32[]{:S(2)}) collective-permute-start(bf16[64,256]{1,0:T(8,128)(2,1)S(1)} %get-tuple-element.124), channel_id=1, source_target_pairs={{0,18},{1,19},{2,16},{3,17},{16,2},{17,3},{18,0},{19,1},{4,22},{5,... | collective-permute-start | bytes 98312 | tf_op jit(solution)/shard_map/ppermute | solution.py:19
  173.3 11.6 %collective-permute-start.35 = (bf16[64,8,128]{2,1,0:T(8,128)(2,1)S(1)}, bf16[64,8,128]{2,1,0:T(8,128)(2,1)S(1)}, u32[]{:S(2)}, u32[]{:S(2)}) collective-permute-start(bf16[64,8,128]{2,1,0:T(8,128)(2,1)S(1)} %bitcast.177), channel_id=1, source_target_pairs={{0,1},{1,0},{2,3},{3,2},{16,17},{17,16},{18,19},{19,18},{4,5},{5,4... | collective-permute-start | bytes 393224 | tf_op jit(solution)/shard_map/ppermute | solution.py:19
  173.4 11.5 %collective-permute-start.36 = (bf16[64,8,128]{2,1,0:T(8,128)(2,1)S(1)}, bf16[64,8,128]{2,1,0:T(8,128)(2,1)S(1)}, u32[]{:S(2)}, u32[]{:S(2)}) collective-permute-start(bf16[64,8,128]{2,1,0:T(8,128)(2,1)S(1)} %bitcast.176), channel_id=1, source_target_pairs={{0,2},{1,3},{2,0},{3,1},{16,18},{17,19},{18,16},{19,17},{4,6},{5,7... | collective-permute-start | bytes 393224 | tf_op jit(solution)/shard_map/ppermute | solution.py:19
  176.5 12.5 %collective-permute-start.37 = (bf16[64,8,128]{2,1,0:T(8,128)(2,1)S(1)}, bf16[64,8,128]{2,1,0:T(8,128)(2,1)S(1)}, u32[]{:S(2)}, u32[]{:S(2)}) collective-permute-start(bf16[64,8,128]{2,1,0:T(8,128)(2,1)S(1)} %bitcast.175), channel_id=1, source_target_pairs={{0,3},{1,2},{2,1},{3,0},{16,19},{17,18},{18,17},{19,16},{4,7},{5,6... | collective-permute-start | bytes 393224 | tf_op jit(solution)/shard_map/ppermute | solution.py:19
  177.7 12.4 %collective-permute-start.38 = (bf16[64,8,128]{2,1,0:T(8,128)(2,1)S(1)}, bf16[64,8,128]{2,1,0:T(8,128)(2,1)S(1)}, u32[]{:S(2)}, u32[]{:S(2)}) collective-permute-start(bf16[64,8,128]{2,1,0:T(8,128)(2,1)S(1)} %bitcast.174), channel_id=1, source_target_pairs={{0,16},{1,17},{2,18},{3,19},{16,0},{17,1},{18,2},{19,3},{4,20},{5,... | collective-permute-start | bytes 393224 | tf_op jit(solution)/shard_map/ppermute | solution.py:19
  179.3 10.9 %collective-permute-start.39 = (bf16[64,8,128]{2,1,0:T(8,128)(2,1)S(1)}, bf16[64,8,128]{2,1,0:T(8,128)(2,1)S(1)}, u32[]{:S(2)}, u32[]{:S(2)}) collective-permute-start(bf16[64,8,128]{2,1,0:T(8,128)(2,1)S(1)} %bitcast.173), channel_id=1, source_target_pairs={{0,17},{1,16},{2,19},{3,18},{16,1},{17,0},{18,3},{19,2},{4,21},{5,... | collective-permute-start | bytes 393224 | tf_op jit(solution)/shard_map/ppermute | solution.py:19
  184.9 54.6 %collective-permute-start.30 = (f32[2,96,1024]{2,1,0:T(8,128)}, f32[2,96,1024]{2,1,0:T(8,128)}, u32[]{:S(2)}, u32[]{:S(2)}) collective-permute-start(f32[2,96,1024]{2,1,0:T(8,128)} %bitcast.20), channel_id=1, source_target_pairs={{0,4},{4,0},{8,12},{12,8},{1,5},{5,1},{9,13},{13,9},{2,6},{6,2},{1... | collective-permute-start | bytes 2359304 | tf_op jit(solution)/shard_map/ppermute | solution.py:19
  184.9 14.2 %collective-permute-start.40 = (bf16[64,8,128]{2,1,0:T(8,128)(2,1)S(1)}, bf16[64,8,128]{2,1,0:T(8,128)(2,1)S(1)}, u32[]{:S(2)}, u32[]{:S(2)}) collective-permute-start(bf16[64,8,128]{2,1,0:T(8,128)(2,1)S(1)} %bitcast.172), channel_id=1, source_target_pairs={{0,18},{1,19},{2,16},{3,17},{16,2},{17,3},{18,0},{19,1},{4,22},{5,... | collective-permute-start | bytes 393224 | tf_op jit(solution)/shard_map/ppermute | solution.py:19
  189.0 10.0 %collective-permute-start.41 = (bf16[64,8,128]{2,1,0:T(8,128)(2,1)S(1)}, bf16[64,8,128]{2,1,0:T(8,128)(2,1)S(1)}, u32[]{:S(2)}, u32[]{:S(2)}) collective-permute-start(bf16[64,8,128]{2,1,0:T(8,128)(2,1)S(1)} %bitcast.171), channel_id=1, source_target_pairs={{0,19},{1,18},{2,17},{3,16},{16,3},{17,2},{18,1},{19,0},{4,23},{5,... | collective-permute-start | bytes 393224 | tf_op jit(solution)/shard_map/ppermute | solution.py:19
  190.2 14.3 %collective-permute-start.9 = (bf16[64,16,128]{2,1,0:T(8,128)(2,1)S(1)}, bf16[64,16,128]{2,1,0:T(8,128)(2,1)S(1)}, u32[]{:S(2)}, u32[]{:S(2)}) collective-permute-start(bf16[64,16,128]{2,1,0:T(8,128)(2,1)S(1)} %bitcast.165), channel_id=1, source_target_pairs={{0,17},{1,16},{2,19},{3,18},{16,1},{17,0},{18,3},{19,2},{4,21},{5,... | collective-permute-start | bytes 786440 | tf_op jit(solution)/shard_map/ppermute | solution.py:19
  190.2 138.9 %collective-permute-start.29 = (f32[1,96,4096]{2,1,0:T(8,128)}, f32[1,96,4096]{2,1,0:T(8,128)}, u32[]{:S(2)}, u32[]{:S(2)}) collective-permute-start(f32[1,96,4096]{2,1,0:T(8,128)} %slice.237), channel_id=1, source_target_pairs={{0,8},{4,12},{8,0},{12,4},{1,9},{5,13},{9,1},{13,5},{2,10},{6,14},... | collective-permute-start | bytes 4718600 | tf_op jit(solution)/shard_map/ppermute | solution.py:19
  199.0 13.3 %collective-permute-start.10 = (bf16[64,16,128]{2,1,0:T(8,128)(2,1)S(1)}, bf16[64,16,128]{2,1,0:T(8,128)(2,1)S(1)}, u32[]{:S(2)}, u32[]{:S(2)}) collective-permute-start(bf16[64,16,128]{2,1,0:T(8,128)(2,1)S(1)} %bitcast.168), channel_id=1, source_target_pairs={{0,1},{1,0},{2,3},{3,2},{16,17},{17,16},{18,19},{19,18},{4,5},{5,4... | collective-permute-start | bytes 786440 | tf_op jit(solution)/shard_map/ppermute | solution.py:19
  199.0 14.8 %collective-permute-start.11 = (bf16[64,16,128]{2,1,0:T(8,128)(2,1)S(1)}, bf16[64,16,128]{2,1,0:T(8,128)(2,1)S(1)}, u32[]{:S(2)}, u32[]{:S(2)}) collective-permute-start(bf16[64,16,128]{2,1,0:T(8,128)(2,1)S(1)} %bitcast.167), channel_id=1, source_target_pairs={{0,16},{1,17},{2,18},{3,19},{16,0},{17,1},{18,2},{19,3},{4,20},{5,... | collective-permute-start | bytes 786440 | tf_op jit(solution)/shard_map/ppermute | solution.py:19
  204.5 21.1 %collective-permute-start.12 = (bf16[64,16,128]{2,1,0:T(8,128)(2,1)S(1)}, bf16[64,16,128]{2,1,0:T(8,128)(2,1)S(1)}, u32[]{:S(2)}, u32[]{:S(2)}) collective-permute-start(bf16[64,16,128]{2,1,0:T(8,128)(2,1)S(1)} %bitcast.166), channel_id=1, source_target_pairs={{0,18},{1,19},{2,16},{3,17},{16,2},{17,3},{18,0},{19,1},{4,22},{5,... | collective-permute-start | bytes 786440 | tf_op jit(solution)/shard_map/ppermute | solution.py:19
  212.3 20.4 %collective-permute-start.18 = (bf16[64,16,128]{2,1,0:T(8,128)(2,1)}, bf16[64,16,128]{2,1,0:T(8,128)(2,1)S(1)}, u32[]{:S(2)}, u32[]{:S(2)}) collective-permute-start(bf16[64,16,128]{2,1,0:T(8,128)(2,1)} %bitcast.56), channel_id=1, source_target_pairs={{0,17},{1,16},{2,19},{3,18},{16,1},{17,0},{18,3},{19,2},{4,21},{5,... | collective-permute-start | bytes 786440 | tf_op jit(solution)/shard_map/ppermute | solution.py:19
  214.6 20.4 %collective-permute-start.19 = (bf16[64,16,128]{2,1,0:T(8,128)(2,1)}, bf16[64,16,128]{2,1,0:T(8,128)(2,1)S(1)}, u32[]{:S(2)}, u32[]{:S(2)}) collective-permute-start(bf16[64,16,128]{2,1,0:T(8,128)(2,1)} %bitcast.58), channel_id=1, source_target_pairs={{0,1},{1,0},{2,3},{3,2},{16,17},{17,16},{18,19},{19,18},{4,5},{5,4... | collective-permute-start | bytes 786440 | tf_op jit(solution)/shard_map/ppermute | solution.py:19
  226.2 12.0 %collective-permute-start.20 = (bf16[64,16,128]{2,1,0:T(8,128)(2,1)}, bf16[64,16,128]{2,1,0:T(8,128)(2,1)S(1)}, u32[]{:S(2)}, u32[]{:S(2)}) collective-permute-start(bf16[64,16,128]{2,1,0:T(8,128)(2,1)} %bitcast.60), channel_id=1, source_target_pairs={{0,16},{1,17},{2,18},{3,19},{16,0},{17,1},{18,2},{19,3},{4,20},{5,... | collective-permute-start | bytes 786440 | tf_op jit(solution)/shard_map/ppermute | solution.py:19
  227.9 16.3 %all-to-all-start.1 = ((bf16[64,8,256]{2,1,0:T(8,128)(2,1)}), bf16[64,8,256]{2,1,0:T(8,128)(2,1)}, u32[]{:S(2)}, u32[]{:S(2)}) async-start(bf16[64,8,256]{2,1,0:T(8,128)(2,1)} %copy.31), calls=%async_computation.1 | async-start | bytes 524288 | tf_op jit(solution)/shard_map/all_to_all | solution.py:422
  232.8 32.6 %collective-permute-start.21 = (bf16[64,16,128]{2,1,0:T(8,128)(2,1)}, bf16[64,16,128]{2,1,0:T(8,128)(2,1)S(1)}, u32[]{:S(2)}, u32[]{:S(2)}) collective-permute-start(bf16[64,16,128]{2,1,0:T(8,128)(2,1)} %bitcast.64), channel_id=1, source_target_pairs={{0,18},{1,19},{2,16},{3,17},{16,2},{17,3},{18,0},{19,1},{4,22},{5,... | collective-permute-start | bytes 786440 | tf_op jit(solution)/shard_map/ppermute | solution.py:19
  235.0 37.5 %collective-permute-start.22 = (bf16[64,16,128]{2,1,0:T(8,128)(2,1)}, bf16[64,16,128]{2,1,0:T(8,128)(2,1)S(1)}, u32[]{:S(2)}, u32[]{:S(2)}) collective-permute-start(bf16[64,16,128]{2,1,0:T(8,128)(2,1)} %bitcast.66), channel_id=1, source_target_pairs={{0,19},{1,18},{2,17},{3,16},{16,3},{17,2},{18,1},{19,0},{4,23},{5,... | collective-permute-start | bytes 786440 | tf_op jit(solution)/shard_map/ppermute | solution.py:19
  238.3 50.1 %collective-permute-start.23 = (bf16[64,16,128]{2,1,0:T(8,128)(2,1)}, bf16[64,16,128]{2,1,0:T(8,128)(2,1)S(1)}, u32[]{:S(2)}, u32[]{:S(2)}) collective-permute-start(bf16[64,16,128]{2,1,0:T(8,128)(2,1)} %bitcast.68), channel_id=1, source_target_pairs={{0,2},{1,3},{2,0},{3,1},{16,18},{17,19},{18,16},{19,17},{4,6},{5,7... | collective-permute-start | bytes 786440 | tf_op jit(solution)/shard_map/ppermute | solution.py:19
  239.4 49.0 %collective-permute-start.24 = (bf16[64,16,128]{2,1,0:T(8,128)(2,1)}, bf16[64,16,128]{2,1,0:T(8,128)(2,1)S(1)}, u32[]{:S(2)}, u32[]{:S(2)}) collective-permute-start(bf16[64,16,128]{2,1,0:T(8,128)(2,1)} %bitcast.70), channel_id=1, source_target_pairs={{0,3},{1,2},{2,1},{3,0},{16,19},{17,18},{18,17},{19,16},{4,7},{5,6... | collective-permute-start | bytes 786440 | tf_op jit(solution)/shard_map/ppermute | solution.py:19
  244.3 83.3 %all-to-all-start = ((bf16[64,8,1024]{2,1,0:T(8,128)(2,1)}), bf16[64,8,1024]{2,1,0:T(8,128)(2,1)}, u32[]{:S(2)}, u32[]{:S(2)}) async-start(bf16[64,8,1024]{2,1,0:T(8,128)(2,1)} %join.3), calls=%async_computation | async-start | bytes 2097152 | tf_op jit(solution)/shard_map/all_to_all | solution.py:422
  265.4 61.1 %collective-permute-start.31 = (f32[1,96,1024]{2,1,0:T(8,128)}, f32[1,96,1024]{2,1,0:T(8,128)}, u32[]{:S(2)}, u32[]{:S(2)}) collective-permute-start(f32[1,96,1024]{2,1,0:T(8,128)} %slice.241), channel_id=1, source_target_pairs={{0,8},{4,12},{8,0},{12,4},{1,9},{5,13},{9,1},{13,5},{2,10},{6,14},... | collective-permute-start | bytes 1179656 | tf_op jit(solution)/shard_map/ppermute | solution.py:19
  272.5 46.2 %collective-permute-start.8 = (bf16[64,16,128]{2,1,0:T(8,128)(2,1)}, bf16[64,16,128]{2,1,0:T(8,128)(2,1)}, u32[]{:S(2)}, u32[]{:S(2)}) collective-permute-start(bf16[64,16,128]{2,1,0:T(8,128)(2,1)} %bitcast.38), channel_id=1, source_target_pairs={{0,3},{1,2},{2,1},{3,0},{16,19},{17,18},{18,17},{19,16},{4,7},{5,6... | collective-permute-start | bytes 786440 | tf_op jit(solution)/shard_map/ppermute | solution.py:19
  288.4 12.3 %collective-permute-start.13 = (bf16[64,16,128]{2,1,0:T(8,128)(2,1)}, bf16[64,16,128]{2,1,0:T(8,128)(2,1)}, u32[]{:S(2)}, u32[]{:S(2)}) collective-permute-start(bf16[64,16,128]{2,1,0:T(8,128)(2,1)} %bitcast.50), channel_id=1, source_target_pairs={{0,19},{1,18},{2,17},{3,16},{16,3},{17,2},{18,1},{19,0},{4,23},{5,... | collective-permute-start | bytes 786440 | tf_op jit(solution)/shard_map/ppermute | solution.py:19
  288.4 28.1 %collective-permute-start.14 = (bf16[64,16,128]{2,1,0:T(8,128)(2,1)}, bf16[64,16,128]{2,1,0:T(8,128)(2,1)}, u32[]{:S(2)}, u32[]{:S(2)}) collective-permute-start(bf16[64,16,128]{2,1,0:T(8,128)(2,1)} %bitcast.52), channel_id=1, source_target_pairs={{0,2},{1,3},{2,0},{3,1},{16,18},{17,19},{18,16},{19,17},{4,6},{5,7... | collective-permute-start | bytes 786440 | tf_op jit(solution)/shard_map/ppermute | solution.py:19
  320.3 12.1 %collective-permute-start.25 = (f32[16,96]{1,0:T(8,128)S(1)}, f32[16,96]{1,0:T(8,128)S(1)}, u32[]{:S(2)}, u32[]{:S(2)}) collective-permute-start(f32[16,96]{1,0:T(8,128)S(1)} %get-tuple-element.52), channel_id=1, source_target_pairs={{0,4},{4,0},{8,12},{12,8},{1,5},{5,1},{9,13},{13,9},{2,6},{6,2},{1... | collective-permute-start | bytes 18440 | tf_op jit(solution)/shard_map/ppermute | solution.py:19
  320.5 11.9 %collective-permute-start.26 = (f32[16,96]{1,0:T(8,128)S(1)}, f32[16,96]{1,0:T(8,128)S(1)}, u32[]{:S(2)}, u32[]{:S(2)}) collective-permute-start(f32[16,96]{1,0:T(8,128)S(1)} %get-tuple-element.53), channel_id=1, source_target_pairs={{0,8},{4,12},{8,0},{12,4},{1,9},{5,13},{9,1},{13,5},{2,10},{6,14},... | collective-permute-start | bytes 18440 | tf_op jit(solution)/shard_map/ppermute | solution.py:19
  322.1 10.3 %collective-permute-start.27 = (f32[16,96]{1,0:T(8,128)S(1)}, f32[16,96]{1,0:T(8,128)S(1)}, u32[]{:S(2)}, u32[]{:S(2)}) collective-permute-start(f32[16,96]{1,0:T(8,128)S(1)} %get-tuple-element.54), channel_id=1, source_target_pairs={{0,12},{4,8},{8,4},{12,0},{1,13},{5,9},{9,5},{13,1},{2,14},{6,10},... | collective-permute-start | bytes 18440 | tf_op jit(solution)/shard_map/ppermute | solution.py:19
  (41 other events, 311.6 us)

commit v8 on v7

--- a/solution.py
+++ b/solution.py
@@ -342,13 +342,20 @@
         "down": Head(down_factor_head, 2),
     }
 
-    def fetch(name, chunk):
-        pieces = heads[name].cut(chunk, far_first + [0])
-        got = {s: swap(p, "task", s) if s else p for s, p in zip(far_first + [0], pieces)}
+    def fetch(name, chunk, ahead=()):
+        head, got = heads[name], {}
+        for s in ahead:
+            start = (place() ^ s) * head.stride
+            piece = lax.dynamic_slice_in_dim(head.head, start, head.width, axis=2)
+            got[s] = swap(piece, "task", s)
+        rest = [s for s in far_first + [0] if s not in ahead]
+        for s, piece in zip(rest, head.cut(chunk, rest)):
+            got[s] = swap(piece, "task", s) if s else piece
         return jnp.concatenate([got[s] for s in ring_shifts], axis=0)
 
     fetched = {}
-    fetched["query", 0] = fetch("query", 0)
+    ahead = far_first[:1] if heads["query"].by_lane else []
+    fetched["query", 0] = fetch("query", 0, ahead)
 
     share = own_tasks // parts
     embeddings = lax.dynamic_index_in_dim(
@@ -395,7 +402,7 @@
         return {s: swap(made[s], PLACES, s) if s else made[s] for s in sent}
 
     crossing = [s for s in shifts if s % ring >= ring // 2]
-    crossing = sorted(crossing, key=lambda s: -(s // ring))
+    crossing = sorted(crossing, key=lambda s: (s < ring, s if s < ring else -s))
     late = crossing[-1:]
     near = [s for s in reversed(shifts) if s % ring < ring // 2]
     early = sorted(near, key=lambda s: s % ring == 0) + crossing[:-1]

time: 336 us -> 331 us (0.985)
  waiting for transfers between devices: 112 us -> 89.4 us
  starting transfers between devices: 127 us -> 141 us
    ppermute x52, waiting for transfers between devices: 112 us -> 89.3 us  [swap(): return lax.ppermute(x, axes, [(a, a ^ shift) for a in range(total)])]
    ppermute x52, starting transfers between devices: 118 us -> 132 us  [swap(): return lax.ppermute(x, axes, [(a, a ^ shift) for a in range(total)])]
    unnamed x99 -> x97, local copies, waits for them, and re-layouts: 28.5 us -> 28.4 us
  transfers between devices with their start and end apart: 54 -> 54, of which waited for: 14 -> 14; matrix products, arithmetic and copies ran while one was open for 18% -> 19% of each run, Pallas kernels for 5% -> 6%
where the time goes in v8:
time: 331 us; the launch traced here: 329 us
  starting transfers between devices  141 us (43%)
  waiting for transfers between devices  89.4 us (27%)
  local copies, waits for them, and re-layouts  45.1 us (14%)
  Pallas kernels  19.9 us (6%)
  matrix products  18.7 us (6%)
  other arithmetic  13.9 us (4%)
    ppermute x52, starting transfers between devices, swap(): return lax.ppermute(x, axes, [(a, a ^ shift) for a in range(total)])  132 us
    ppermute x52, waiting for transfers between devices, swap(): return lax.ppermute(x, axes, [(a, a ^ shift) for a in range(total)])  89.3 us
    unnamed x97, local copies, waits for them, and re-layouts  28.4 us
    dot_general x1, matrix products, local(): base_query = jnp.dot(turned, w_query, preferred_element_type=jnp.float32)  10.2 us
    all_to_all x2, starting transfers between devices, own_block(): lax.all_to_all(factors, 'tensor', split_axis=0, concat_axis=0, tiled=True)  8.65 us
    pallas_call x3, Pallas kernels, join(): pl.pallas_call(functools.partial(join_kernel, shifts, stride, start, widt...  6.66 us
  transfers between devices with their start and end apart: 54, of which 14 were waited for; matrix products, arithmetic and copies ran while one was open for 19% of the time, Pallas kernels for 6%

profile of v8, /device:TPU:0, one launch (start us, length us, event | category | flops | bytes accessed | tf_op | source)
XLA Modules:
  0.0 329.3 jit_solution(18007073983978245290)
XLA Ops:
  2.9 4.1 %collective-permute-start = (bf16[1,16,512]{2,1,0:T(8,128)(2,1)S(1)}, bf16[1,16,512]{2,1,0:T(8,128)(2,1)S(1)}, u32[]{:S(2)}, u32[]{:S(2)}) collective-permute-start(bf16[1,16,512]{2,1,0:T(8,128)(2,1)S(1)} %get-tuple-element.135), channel_id=1, source_target_pairs={{0,2},{1,3},{2,0},{3,1},{4,6},{5,7},{6,4},{7,5},{8,10},{9,11},{10,... | collective-permute-start | bytes 49160 | tf_op jit(solution)/shard_map/ppermute | solution.py:19
  8.5 10.2 %fusion.9 = f32[384,4096]{1,0:T(8,128)S(1)} fusion(bf16[2048,4096]{1,0:T(8,128)(2,1)} %param.16, bf16[96,2048]{1,0:T(8,128)(2,1)S(1)} %get-tuple-element.104, bf16[96,2048]{1,0:T(8,128)(2,1)S(1)} %get-tuple-element.105, bf16[96,2048]{1,0:T(8,128)(2,1)S(1)} %get-tuple-element.106, bf16[96,2048]{1,0:T(8,128)(2,1)S(1)} %get-tuple-element.103), kind=kOutput, calls=%fused_computation.25 | convolution fusion | flops 6448742400 | bytes 24641536 | tf_op jit(solution)/shard_map/dot_general | solution.py:423
  18.7 3.1 fusion.29
  25.1 1.8 cut.5
  26.9 2.0 collective-permute-start.33
  28.9 2.5 collective-permute-start.32
  33.0 2.7 collective-permute-done.2
  35.8 4.0 %fusion.8 = f32[384,1024]{1,0:T(8,128)S(1)} fusion(bf16[2048,1024]{1,0:T(8,128)(2,1)} %param.17, bf16[96,2048]{1,0:T(8,128)(2,1)S(1)} %get-tuple-element.104, bf16[96,2048]{1,0:T(8,128)(2,1)S(1)} %get-tuple-element.105, bf16[96,2048]{1,0:T(8,128)(2,1)S(1)} %get-tuple-element.106, bf16[96,2048]{1,0:T(8,128)(2,1)S(1)} %get-tuple-element.103), kind=kOutput, calls=%fused_computation.24 | convolution fusion | flops 1616904192 | bytes 7340032 | tf_op jit(solution)/shard_map/dot_general | solution.py:424
  49.0 1.9 cut.4
  54.1 2.4 collective-permute-start.44
  56.5 2.2 pad_maximum_fusion.3
  58.8 2.0 collective-permute-start.43
  62.6 2.0 reshape.154
  66.7 15.4 %collective-permute-done.44 = bf16[128,256]{1,0:T(8,128)(2,1)S(1)} collective-permute-done((bf16[128,256]{1,0:T(8,128)(2,1)}, bf16[128,256]{1,0:T(8,128)(2,1)S(1)}, u32[]{:S(2)}, u32[]{:S(2)}) %collective-permute-start.44) | collective-permute-done | bytes 65568 | tf_op jit(solution)/shard_map/ppermute | solution.py:19
  82.1 23.4 %collective-permute-start.5 = (bf16[128,16,128]{2,1,0:T(8,128)(2,1)S(1)}, bf16[128,16,128]{2,1,0:T(8,128)(2,1)S(1)}, u32[]{:S(2)}, u32[]{:S(2)}) collective-permute-start(bf16[128,16,128]{2,1,0:T(8,128)(2,1)S(1)} %copy-done.17), channel_id=1, source_target_pairs={{0,1},{1,0},{2,3},{3,2},{4,5},{5,4},{6,7},{7,6},{8,9},{9,8},{10,11... | collective-permute-start | bytes 1572872 | tf_op jit(solution)/shard_map/ppermute | solution.py:19
  106.7 11.5 %collective-permute-done.42 = bf16[128,256]{1,0:T(8,128)(2,1)S(1)} collective-permute-done((bf16[128,256]{1,0:T(8,128)(2,1)S(1)}, bf16[128,256]{1,0:T(8,128)(2,1)S(1)}, u32[]{:S(2)}, u32[]{:S(2)}) %collective-permute-start.42) | collective-permute-done | bytes 65568 | tf_op jit(solution)/shard_map/ppermute | solution.py:19
  120.9 2.0 collective-permute-start.15
  124.5 10.3 %collective-permute-done.17 = bf16[128,16,128]{2,1,0:T(8,128)(2,1)S(1)} collective-permute-done((bf16[128,16,128]{2,1,0:T(8,128)(2,1)S(1)}, bf16[128,16,128]{2,1,0:T(8,128)(2,1)S(1)}, u32[]{:S(2)}, u32[]{:S(2)}) %collective-permute-start.17) | collective-permute-done | bytes 524320 | tf_op jit(solution)/shard_map/ppermute | solution.py:19
  134.9 21.1 %collective-permute-start.46 = (bf16[64,256]{1,0:T(8,128)(2,1)S(1)}, bf16[64,256]{1,0:T(8,128)(2,1)S(1)}, u32[]{:S(2)}, u32[]{:S(2)}) collective-permute-start(bf16[64,256]{1,0:T(8,128)(2,1)S(1)} %get-tuple-element.126), channel_id=1, source_target_pairs={{0,2},{1,3},{2,0},{3,1},{16,18},{17,19},{18,16},{19,17},{4,6},{5,7... | collective-permute-start | bytes 98312 | tf_op jit(solution)/shard_map/ppermute | solution.py:19
  155.9 9.1 %collective-permute-done.16 = bf16[128,16,128]{2,1,0:T(8,128)(2,1)S(1)} collective-permute-done((bf16[128,16,128]{2,1,0:T(8,128)(2,1)S(1)}, bf16[128,16,128]{2,1,0:T(8,128)(2,1)S(1)}, u32[]{:S(2)}, u32[]{:S(2)}) %collective-permute-start.16) | collective-permute-done | bytes 524320 | tf_op jit(solution)/shard_map/ppermute | solution.py:19
  169.4 3.8 %collective-permute-start.50 = (bf16[64,256]{1,0:T(8,128)(2,1)S(1)}, bf16[64,256]{1,0:T(8,128)(2,1)S(1)}, u32[]{:S(2)}, u32[]{:S(2)}) collective-permute-start(bf16[64,256]{1,0:T(8,128)(2,1)S(1)} %get-tuple-element.122), channel_id=1, source_target_pairs={{0,18},{1,19},{2,16},{3,17},{16,2},{17,3},{18,0},{19,1},{4,22},{5,... | collective-permute-start | bytes 98312 | tf_op jit(solution)/shard_map/ppermute | solution.py:19
  175.8 2.8 collective-permute-start.36
  183.6 2.3 add.67
  187.3 3.8 %collective-permute-start.40 = (bf16[64,8,128]{2,1,0:T(8,128)(2,1)S(1)}, bf16[64,8,128]{2,1,0:T(8,128)(2,1)S(1)}, u32[]{:S(2)}, u32[]{:S(2)}) collective-permute-start(bf16[64,8,128]{2,1,0:T(8,128)(2,1)S(1)} %bitcast.172), channel_id=1, source_target_pairs={{0,18},{1,19},{2,16},{3,17},{16,2},{17,3},{18,0},{19,1},{4,22},{5,... | collective-permute-start | bytes 393224 | tf_op jit(solution)/shard_map/ppermute | solution.py:19
  195.2 6.1 %collective-permute-done.40.refs_6_ = bf16[64,8,128]{2,1,0:T(8,128)(2,1)S(1)} collective-permute-done((bf16[64,8,128]{2,1,0:T(8,128)(2,1)S(1)}, bf16[64,8,128]{2,1,0:T(8,128)(2,1)S(1)}, u32[]{:S(2)}, u32[]{:S(2)}) %collective-permute-start.40) | collective-permute-done | bytes 131104 | tf_op jit(solution)/shard_map/ppermute | solution.py:19
  201.2 2.0 collective-permute-start.11
  203.2 3.4 %collective-permute-done.9.refs_0_ = bf16[64,16,128]{2,1,0:T(8,128)(2,1)S(1)} collective-permute-done((bf16[64,16,128]{2,1,0:T(8,128)(2,1)S(1)}, bf16[64,16,128]{2,1,0:T(8,128)(2,1)S(1)}, u32[]{:S(2)}, u32[]{:S(2)}) %collective-permute-start.9) | collective-permute-done | bytes 262176 | tf_op jit(solution)/shard_map/ppermute | solution.py:19
  206.6 2.5 collective-permute-start.12
  211.9 2.1 collective-permute-start.18
  223.1 4.0 %all-to-all-start.1 = ((bf16[64,8,256]{2,1,0:T(8,128)(2,1)}), bf16[64,8,256]{2,1,0:T(8,128)(2,1)}, u32[]{:S(2)}, u32[]{:S(2)}) async-start(bf16[64,8,256]{2,1,0:T(8,128)(2,1)} %copy.31), calls=%async_computation.1 | async-start | bytes 524288 | tf_op jit(solution)/shard_map/all_to_all | solution.py:429
  227.9 2.2 collective-permute-start.21
  232.4 5.9 %collective-permute-start.22 = (bf16[64,16,128]{2,1,0:T(8,128)(2,1)}, bf16[64,16,128]{2,1,0:T(8,128)(2,1)S(1)}, u32[]{:S(2)}, u32[]{:S(2)}) collective-permute-start(bf16[64,16,128]{2,1,0:T(8,128)(2,1)} %bitcast.66), channel_id=1, source_target_pairs={{0,18},{1,19},{2,16},{3,17},{16,2},{17,3},{18,0},{19,1},{4,22},{5,... | collective-permute-start | bytes 786440 | tf_op jit(solution)/shard_map/ppermute | solution.py:19
  239.5 2.5 join.3
  242.0 4.6 %all-to-all-start = ((bf16[64,8,1024]{2,1,0:T(8,128)(2,1)}), bf16[64,8,1024]{2,1,0:T(8,128)(2,1)}, u32[]{:S(2)}, u32[]{:S(2)}) async-start(bf16[64,8,1024]{2,1,0:T(8,128)(2,1)} %join.3), calls=%async_computation | async-start | bytes 2097152 | tf_op jit(solution)/shard_map/all_to_all | solution.py:429
  249.5 2.0 collective-permute-start.31
  251.9 1.7 copy.35
  253.6 1.7 copy.41
  255.3 1.7 copy.42
  257.0 10.6 %collective-permute-done.22.refs_5_ = bf16[64,16,128]{2,1,0:T(8,128)(2,1)S(1)} collective-permute-done((bf16[64,16,128]{2,1,0:T(8,128)(2,1)}, bf16[64,16,128]{2,1,0:T(8,128)(2,1)S(1)}, u32[]{:S(2)}, u32[]{:S(2)}) %collective-permute-start.22) | collective-permute-done | bytes 262176 | tf_op jit(solution)/shard_map/ppermute | solution.py:19
  267.6 2.1 collective-permute-start.8
  269.7 2.4 collective-permute-done.23.refs_6_
  272.1 6.4 %collective-permute-start.13 = (bf16[64,16,128]{2,1,0:T(8,128)(2,1)}, bf16[64,16,128]{2,1,0:T(8,128)(2,1)}, u32[]{:S(2)}, u32[]{:S(2)}) collective-permute-start(bf16[64,16,128]{2,1,0:T(8,128)(2,1)} %bitcast.50), channel_id=1, source_target_pairs={{0,18},{1,19},{2,16},{3,17},{16,2},{17,3},{18,0},{19,1},{4,22},{5,... | collective-permute-start | bytes 786440 | tf_op jit(solution)/shard_map/ppermute | solution.py:19
  278.5 12.0 %collective-permute-start.14 = (bf16[64,16,128]{2,1,0:T(8,128)(2,1)}, bf16[64,16,128]{2,1,0:T(8,128)(2,1)}, u32[]{:S(2)}, u32[]{:S(2)}) collective-permute-start(bf16[64,16,128]{2,1,0:T(8,128)(2,1)} %bitcast.52), channel_id=1, source_target_pairs={{0,2},{1,3},{2,0},{3,1},{16,18},{17,19},{18,16},{19,17},{4,6},{5,7... | collective-permute-start | bytes 786440 | tf_op jit(solution)/shard_map/ppermute | solution.py:19
  297.0 10.1 %collective-permute-done.13.refs_5_ = bf16[64,16,128]{2,1,0:T(8,128)(2,1)} collective-permute-done((bf16[64,16,128]{2,1,0:T(8,128)(2,1)}, bf16[64,16,128]{2,1,0:T(8,128)(2,1)}, u32[]{:S(2)}, u32[]{:S(2)}) %collective-permute-start.13) | collective-permute-done | bytes 262176 | tf_op jit(solution)/shard_map/ppermute | solution.py:19
  307.1 4.5 %collective-permute-done.14.refs_6_ = bf16[64,16,128]{2,1,0:T(8,128)(2,1)} collective-permute-done((bf16[64,16,128]{2,1,0:T(8,128)(2,1)}, bf16[64,16,128]{2,1,0:T(8,128)(2,1)}, u32[]{:S(2)}, u32[]{:S(2)}) %collective-permute-start.14) | collective-permute-done | bytes 262176 | tf_op jit(solution)/shard_map/ppermute | solution.py:19
  311.5 2.1 project.4
  318.8 2.6 join.5
  327.4 1.7 finish.1
  (214 shorter events, 84.5 us)
Async XLA Ops:
  2.9 18.9 %collective-permute-start = (bf16[1,16,512]{2,1,0:T(8,128)(2,1)S(1)}, bf16[1,16,512]{2,1,0:T(8,128)(2,1)S(1)}, u32[]{:S(2)}, u32[]{:S(2)}) collective-permute-start(bf16[1,16,512]{2,1,0:T(8,128)(2,1)S(1)} %get-tuple-element.135), channel_id=1, source_target_pairs={{0,2},{1,3},{2,0},{3,1},{4,6},{5,7},{6,4},{7,5},{8,10},{9,11},{10,... | collective-permute-start | bytes 49160 | tf_op jit(solution)/shard_map/ppermute | solution.py:19
  21.8 159.9 %collective-permute-start.28 = (f32[2,96,4096]{2,1,0:T(8,128)}, f32[2,96,4096]{2,1,0:T(8,128)}, u32[]{:S(2)}, u32[]{:S(2)}) collective-permute-start(f32[2,96,4096]{2,1,0:T(8,128)} %bitcast.17), channel_id=1, source_target_pairs={{0,4},{4,0},{8,12},{12,8},{1,5},{5,1},{9,13},{13,9},{2,6},{6,2},{1... | collective-permute-start | bytes 9437192 | tf_op jit(solution)/shard_map/ppermute | solution.py:19
  21.8 9.6 %collective-permute-start.1 = (bf16[2,16,512]{2,1,0:T(8,128)(2,1)S(1)}, bf16[2,16,512]{2,1,0:T(8,128)(2,1)S(1)}, u32[]{:S(2)}, u32[]{:S(2)}) collective-permute-start(bf16[2,16,512]{2,1,0:T(8,128)(2,1)S(1)} %pad_maximum_fusion.10), channel_id=1, source_target_pairs={{0,1},{1,0},{2,3},{3,2},{4,5},{5,4},{6,7},{7,6},{8,9},{9,8},{10,11... | collective-permute-start | bytes 98312 | tf_op jit(solution)/shard_map/ppermute | solution.py:19
  25.1 27.5 %collective-permute-start.34 = (bf16[128,8,128]{2,1,0:T(8,128)(2,1)}, bf16[128,8,128]{2,1,0:T(8,128)(2,1)}, u32[]{:S(2)}, u32[]{:S(2)}) collective-permute-start(bf16[128,8,128]{2,1,0:T(8,128)(2,1)} %constant_dynamic-slice_fusion), channel_id=1, source_target_pairs={{0,3},{1,2},{2,1},{3,0},{4,7},{5,6},{6,5},{7,4},{8,11},{9,10},{10,... | collective-permute-start | bytes 786440 | tf_op jit(solution)/shard_map/ppermute | solution.py:19
  26.9 25.9 %collective-permute-start.33 = (bf16[128,8,128]{2,1,0:T(8,128)(2,1)}, bf16[128,8,128]{2,1,0:T(8,128)(2,1)}, u32[]{:S(2)}, u32[]{:S(2)}) collective-permute-start(bf16[128,8,128]{2,1,0:T(8,128)(2,1)} %get-tuple-element.56), channel_id=1, source_target_pairs={{0,2},{1,3},{2,0},{3,1},{4,6},{5,7},{6,4},{7,5},{8,10},{9,11},{10,... | collective-permute-start | bytes 786440 | tf_op jit(solution)/shard_map/ppermute | solution.py:19
  28.9 25.2 %collective-permute-start.32 = (bf16[128,8,128]{2,1,0:T(8,128)(2,1)}, bf16[128,8,128]{2,1,0:T(8,128)(2,1)}, u32[]{:S(2)}, u32[]{:S(2)}) collective-permute-start(bf16[128,8,128]{2,1,0:T(8,128)(2,1)} %get-tuple-element.55), channel_id=1, source_target_pairs={{0,1},{1,0},{2,3},{3,2},{4,5},{5,4},{6,7},{7,6},{8,9},{9,8},{10,11... | collective-permute-start | bytes 786440 | tf_op jit(solution)/shard_map/ppermute | solution.py:19
  42.1 16.7 %collective-permute-start.4 = (bf16[2,128,512]{2,1,0:T(8,128)(2,1)}, bf16[2,128,512]{2,1,0:T(8,128)(2,1)}, u32[]{:S(2)}, u32[]{:S(2)}) collective-permute-start(bf16[2,128,512]{2,1,0:T(8,128)(2,1)} %pad_maximum_fusion.8), channel_id=1, source_target_pairs={{0,8},{4,12},{8,0},{12,4},{1,9},{5,13},{9,1},{13,5},{2,10},{6,14},... | collective-permute-start | bytes 786440 | tf_op jit(solution)/shard_map/ppermute | solution.py:19
  52.6 67.1 %collective-permute-start.7 = (bf16[128,16,128]{2,1,0:T(8,128)(2,1)}, bf16[128,16,128]{2,1,0:T(8,128)(2,1)}, u32[]{:S(2)}, u32[]{:S(2)}) collective-permute-start(bf16[128,16,128]{2,1,0:T(8,128)(2,1)} %copy-done.19), channel_id=1, source_target_pairs={{0,3},{1,2},{2,1},{3,0},{4,7},{5,6},{6,5},{7,4},{8,11},{9,10},{10,... | collective-permute-start | bytes 1572872 | tf_op jit(solution)/shard_map/ppermute | solution.py:19
  52.9 68.1 %collective-permute-start.6 = (bf16[128,16,128]{2,1,0:T(8,128)(2,1)}, bf16[128,16,128]{2,1,0:T(8,128)(2,1)}, u32[]{:S(2)}, u32[]{:S(2)}) collective-permute-start(bf16[128,16,128]{2,1,0:T(8,128)(2,1)} %copy-done.18), channel_id=1, source_target_pairs={{0,2},{1,3},{2,0},{3,1},{4,6},{5,7},{6,4},{7,5},{8,10},{9,11},{10,... | collective-permute-start | bytes 1572872 | tf_op jit(solution)/shard_map/ppermute | solution.py:19
  54.1 28.0 %collective-permute-start.44 = (bf16[128,256]{1,0:T(8,128)(2,1)}, bf16[128,256]{1,0:T(8,128)(2,1)S(1)}, u32[]{:S(2)}, u32[]{:S(2)}) collective-permute-start(bf16[128,256]{1,0:T(8,128)(2,1)} %copy-done.22), channel_id=1, source_target_pairs={{0,3},{1,2},{2,1},{3,0},{4,7},{5,6},{6,5},{7,4},{8,11},{9,10},{10,... | collective-permute-start | bytes 196616 | tf_op jit(solution)/shard_map/ppermute | solution.py:19
  58.8 47.0 %collective-permute-start.43 = (bf16[128,256]{1,0:T(8,128)(2,1)S(1)}, bf16[128,256]{1,0:T(8,128)(2,1)S(1)}, u32[]{:S(2)}, u32[]{:S(2)}) collective-permute-start(bf16[128,256]{1,0:T(8,128)(2,1)S(1)} %copy-done.21), channel_id=1, source_target_pairs={{0,2},{1,3},{2,0},{3,1},{4,6},{5,7},{6,4},{7,5},{8,10},{9,11},{10,... | collective-permute-start | bytes 196616 | tf_op jit(solution)/shard_map/ppermute | solution.py:19
  82.1 40.8 %collective-permute-start.5 = (bf16[128,16,128]{2,1,0:T(8,128)(2,1)S(1)}, bf16[128,16,128]{2,1,0:T(8,128)(2,1)S(1)}, u32[]{:S(2)}, u32[]{:S(2)}) collective-permute-start(bf16[128,16,128]{2,1,0:T(8,128)(2,1)S(1)} %copy-done.17), channel_id=1, source_target_pairs={{0,1},{1,0},{2,3},{3,2},{4,5},{5,4},{6,7},{7,6},{8,9},{9,8},{10,11... | collective-permute-start | bytes 1572872 | tf_op jit(solution)/shard_map/ppermute | solution.py:19
  105.8 12.4 %collective-permute-start.42 = (bf16[128,256]{1,0:T(8,128)(2,1)S(1)}, bf16[128,256]{1,0:T(8,128)(2,1)S(1)}, u32[]{:S(2)}, u32[]{:S(2)}) collective-permute-start(bf16[128,256]{1,0:T(8,128)(2,1)S(1)} %get-tuple-element.58), channel_id=1, source_target_pairs={{0,1},{1,0},{2,3},{3,2},{4,5},{5,4},{6,7},{7,6},{8,9},{9,8},{10,11... | collective-permute-start | bytes 196616 | tf_op jit(solution)/shard_map/ppermute | solution.py:19
  118.2 16.7 %collective-permute-start.17 = (bf16[128,16,128]{2,1,0:T(8,128)(2,1)S(1)}, bf16[128,16,128]{2,1,0:T(8,128)(2,1)S(1)}, u32[]{:S(2)}, u32[]{:S(2)}) collective-permute-start(bf16[128,16,128]{2,1,0:T(8,128)(2,1)S(1)} %get-tuple-element.41), channel_id=1, source_target_pairs={{0,3},{1,2},{2,1},{3,0},{4,7},{5,6},{6,5},{7,4},{8,11},{9,10},{10,... | collective-permute-start | bytes 1572872 | tf_op jit(solution)/shard_map/ppermute | solution.py:19
  119.7 45.3 %collective-permute-start.16 = (bf16[128,16,128]{2,1,0:T(8,128)(2,1)S(1)}, bf16[128,16,128]{2,1,0:T(8,128)(2,1)S(1)}, u32[]{:S(2)}, u32[]{:S(2)}) collective-permute-start(bf16[128,16,128]{2,1,0:T(8,128)(2,1)S(1)} %get-tuple-element.40), channel_id=1, source_target_pairs={{0,2},{1,3},{2,0},{3,1},{4,6},{5,7},{6,4},{7,5},{8,10},{9,11},{10,... | collective-permute-start | bytes 1572872 | tf_op jit(solution)/shard_map/ppermute | solution.py:19
  120.9 46.9 %collective-permute-start.15 = (bf16[128,16,128]{2,1,0:T(8,128)(2,1)S(1)}, bf16[128,16,128]{2,1,0:T(8,128)(2,1)S(1)}, u32[]{:S(2)}, u32[]{:S(2)}) collective-permute-start(bf16[128,16,128]{2,1,0:T(8,128)(2,1)S(1)} %get-tuple-element.39), channel_id=1, source_target_pairs={{0,1},{1,0},{2,3},{3,2},{4,5},{5,4},{6,7},{7,6},{8,9},{9,8},{10,11... | collective-permute-start | bytes 1572872 | tf_op jit(solution)/shard_map/ppermute | solution.py:19
  123.0 46.4 %collective-permute-start.45 = (bf16[64,256]{1,0:T(8,128)(2,1)S(1)}, bf16[64,256]{1,0:T(8,128)(2,1)S(1)}, u32[]{:S(2)}, u32[]{:S(2)}) collective-permute-start(bf16[64,256]{1,0:T(8,128)(2,1)S(1)} %get-tuple-element.127), channel_id=1, source_target_pairs={{0,1},{1,0},{2,3},{3,2},{16,17},{17,16},{18,19},{19,18},{4,5},{5,4... | collective-permute-start | bytes 98312 | tf_op jit(solution)/shard_map/ppermute | solution.py:19
  134.9 34.5 %collective-permute-start.46 = (bf16[64,256]{1,0:T(8,128)(2,1)S(1)}, bf16[64,256]{1,0:T(8,128)(2,1)S(1)}, u32[]{:S(2)}, u32[]{:S(2)}) collective-permute-start(bf16[64,256]{1,0:T(8,128)(2,1)S(1)} %get-tuple-element.126), channel_id=1, source_target_pairs={{0,2},{1,3},{2,0},{3,1},{16,18},{17,19},{18,16},{19,17},{4,6},{5,7... | collective-permute-start | bytes 98312 | tf_op jit(solution)/shard_map/ppermute | solution.py:19
  169.4 9.3 %collective-permute-start.50 = (bf16[64,256]{1,0:T(8,128)(2,1)S(1)}, bf16[64,256]{1,0:T(8,128)(2,1)S(1)}, u32[]{:S(2)}, u32[]{:S(2)}) collective-permute-start(bf16[64,256]{1,0:T(8,128)(2,1)S(1)} %get-tuple-element.122), channel_id=1, source_target_pairs={{0,18},{1,19},{2,16},{3,17},{16,2},{17,3},{18,0},{19,1},{4,22},{5,... | collective-permute-start | bytes 98312 | tf_op jit(solution)/shard_map/ppermute | solution.py:19
  175.7 11.6 %collective-permute-start.35 = (bf16[64,8,128]{2,1,0:T(8,128)(2,1)S(1)}, bf16[64,8,128]{2,1,0:T(8,128)(2,1)S(1)}, u32[]{:S(2)}, u32[]{:S(2)}) collective-permute-start(bf16[64,8,128]{2,1,0:T(8,128)(2,1)S(1)} %bitcast.177), channel_id=1, source_target_pairs={{0,1},{1,0},{2,3},{3,2},{16,17},{17,16},{18,19},{19,18},{4,5},{5,4... | collective-permute-start | bytes 393224 | tf_op jit(solution)/shard_map/ppermute | solution.py:19
  175.8 11.5 %collective-permute-start.36 = (bf16[64,8,128]{2,1,0:T(8,128)(2,1)S(1)}, bf16[64,8,128]{2,1,0:T(8,128)(2,1)S(1)}, u32[]{:S(2)}, u32[]{:S(2)}) collective-permute-start(bf16[64,8,128]{2,1,0:T(8,128)(2,1)S(1)} %bitcast.176), channel_id=1, source_target_pairs={{0,2},{1,3},{2,0},{3,1},{16,18},{17,19},{18,16},{19,17},{4,6},{5,7... | collective-permute-start | bytes 393224 | tf_op jit(solution)/shard_map/ppermute | solution.py:19
  178.7 12.5 %collective-permute-start.37 = (bf16[64,8,128]{2,1,0:T(8,128)(2,1)S(1)}, bf16[64,8,128]{2,1,0:T(8,128)(2,1)S(1)}, u32[]{:S(2)}, u32[]{:S(2)}) collective-permute-start(bf16[64,8,128]{2,1,0:T(8,128)(2,1)S(1)} %bitcast.175), channel_id=1, source_target_pairs={{0,3},{1,2},{2,1},{3,0},{16,19},{17,18},{18,17},{19,16},{4,7},{5,6... | collective-permute-start | bytes 393224 | tf_op jit(solution)/shard_map/ppermute | solution.py:19
  180.2 12.4 %collective-permute-start.38 = (bf16[64,8,128]{2,1,0:T(8,128)(2,1)S(1)}, bf16[64,8,128]{2,1,0:T(8,128)(2,1)S(1)}, u32[]{:S(2)}, u32[]{:S(2)}) collective-permute-start(bf16[64,8,128]{2,1,0:T(8,128)(2,1)S(1)} %bitcast.174), channel_id=1, source_target_pairs={{0,16},{1,17},{2,18},{3,19},{16,0},{17,1},{18,2},{19,3},{4,20},{5,... | collective-permute-start | bytes 393224 | tf_op jit(solution)/shard_map/ppermute | solution.py:19
  181.7 11.5 %collective-permute-start.39 = (bf16[64,8,128]{2,1,0:T(8,128)(2,1)S(1)}, bf16[64,8,128]{2,1,0:T(8,128)(2,1)S(1)}, u32[]{:S(2)}, u32[]{:S(2)}) collective-permute-start(bf16[64,8,128]{2,1,0:T(8,128)(2,1)S(1)} %bitcast.173), channel_id=1, source_target_pairs={{0,17},{1,16},{2,19},{3,18},{16,1},{17,0},{18,3},{19,2},{4,21},{5,... | collective-permute-start | bytes 393224 | tf_op jit(solution)/shard_map/ppermute | solution.py:19
  187.3 50.9 %collective-permute-start.30 = (f32[2,96,1024]{2,1,0:T(8,128)}, f32[2,96,1024]{2,1,0:T(8,128)}, u32[]{:S(2)}, u32[]{:S(2)}) collective-permute-start(f32[2,96,1024]{2,1,0:T(8,128)} %bitcast.20), channel_id=1, source_target_pairs={{0,4},{4,0},{8,12},{12,8},{1,5},{5,1},{9,13},{13,9},{2,6},{6,2},{1... | collective-permute-start | bytes 2359304 | tf_op jit(solution)/shard_map/ppermute | solution.py:19
  187.3 13.9 %collective-permute-start.40 = (bf16[64,8,128]{2,1,0:T(8,128)(2,1)S(1)}, bf16[64,8,128]{2,1,0:T(8,128)(2,1)S(1)}, u32[]{:S(2)}, u32[]{:S(2)}) collective-permute-start(bf16[64,8,128]{2,1,0:T(8,128)(2,1)S(1)} %bitcast.172), channel_id=1, source_target_pairs={{0,18},{1,19},{2,16},{3,17},{16,2},{17,3},{18,0},{19,1},{4,22},{5,... | collective-permute-start | bytes 393224 | tf_op jit(solution)/shard_map/ppermute | solution.py:19
  191.2 10.1 %collective-permute-start.41 = (bf16[64,8,128]{2,1,0:T(8,128)(2,1)S(1)}, bf16[64,8,128]{2,1,0:T(8,128)(2,1)S(1)}, u32[]{:S(2)}, u32[]{:S(2)}) collective-permute-start(bf16[64,8,128]{2,1,0:T(8,128)(2,1)S(1)} %bitcast.171), channel_id=1, source_target_pairs={{0,19},{1,18},{2,17},{3,16},{16,3},{17,2},{18,1},{19,0},{4,23},{5,... | collective-permute-start | bytes 393224 | tf_op jit(solution)/shard_map/ppermute | solution.py:19
  192.6 14.0 %collective-permute-start.9 = (bf16[64,16,128]{2,1,0:T(8,128)(2,1)S(1)}, bf16[64,16,128]{2,1,0:T(8,128)(2,1)S(1)}, u32[]{:S(2)}, u32[]{:S(2)}) collective-permute-start(bf16[64,16,128]{2,1,0:T(8,128)(2,1)S(1)} %bitcast.165), channel_id=1, source_target_pairs={{0,17},{1,16},{2,19},{3,18},{16,1},{17,0},{18,3},{19,2},{4,21},{5,... | collective-permute-start | bytes 786440 | tf_op jit(solution)/shard_map/ppermute | solution.py:19
  193.2 130.8 %collective-permute-start.29 = (f32[1,96,4096]{2,1,0:T(8,128)}, f32[1,96,4096]{2,1,0:T(8,128)}, u32[]{:S(2)}, u32[]{:S(2)}) collective-permute-start(f32[1,96,4096]{2,1,0:T(8,128)} %slice.237), channel_id=1, source_target_pairs={{0,8},{4,12},{8,0},{12,4},{1,9},{5,13},{9,1},{13,5},{2,10},{6,14},... | collective-permute-start | bytes 4718600 | tf_op jit(solution)/shard_map/ppermute | solution.py:19
  201.2 10.7 %collective-permute-start.10 = (bf16[64,16,128]{2,1,0:T(8,128)(2,1)S(1)}, bf16[64,16,128]{2,1,0:T(8,128)(2,1)S(1)}, u32[]{:S(2)}, u32[]{:S(2)}) collective-permute-start(bf16[64,16,128]{2,1,0:T(8,128)(2,1)S(1)} %bitcast.168), channel_id=1, source_target_pairs={{0,1},{1,0},{2,3},{3,2},{16,17},{17,16},{18,19},{19,18},{4,5},{5,4... | collective-permute-start | bytes 786440 | tf_op jit(solution)/shard_map/ppermute | solution.py:19
  201.2 14.3 %collective-permute-start.11 = (bf16[64,16,128]{2,1,0:T(8,128)(2,1)S(1)}, bf16[64,16,128]{2,1,0:T(8,128)(2,1)S(1)}, u32[]{:S(2)}, u32[]{:S(2)}) collective-permute-start(bf16[64,16,128]{2,1,0:T(8,128)(2,1)S(1)} %bitcast.167), channel_id=1, source_target_pairs={{0,16},{1,17},{2,18},{3,19},{16,0},{17,1},{18,2},{19,3},{4,20},{5,... | collective-permute-start | bytes 786440 | tf_op jit(solution)/shard_map/ppermute | solution.py:19
  206.6 12.4 %collective-permute-start.12 = (bf16[64,16,128]{2,1,0:T(8,128)(2,1)S(1)}, bf16[64,16,128]{2,1,0:T(8,128)(2,1)S(1)}, u32[]{:S(2)}, u32[]{:S(2)}) collective-permute-start(bf16[64,16,128]{2,1,0:T(8,128)(2,1)S(1)} %bitcast.166), channel_id=1, source_target_pairs={{0,19},{1,18},{2,17},{3,16},{16,3},{17,2},{18,1},{19,0},{4,23},{5,... | collective-permute-start | bytes 786440 | tf_op jit(solution)/shard_map/ppermute | solution.py:19
  211.9 16.0 %collective-permute-start.18 = (bf16[64,16,128]{2,1,0:T(8,128)(2,1)}, bf16[64,16,128]{2,1,0:T(8,128)(2,1)S(1)}, u32[]{:S(2)}, u32[]{:S(2)}) collective-permute-start(bf16[64,16,128]{2,1,0:T(8,128)(2,1)} %bitcast.56), channel_id=1, source_target_pairs={{0,17},{1,16},{2,19},{3,18},{16,1},{17,0},{18,3},{19,2},{4,21},{5,... | collective-permute-start | bytes 786440 | tf_op jit(solution)/shard_map/ppermute | solution.py:19
  216.2 16.2 %collective-permute-start.19 = (bf16[64,16,128]{2,1,0:T(8,128)(2,1)}, bf16[64,16,128]{2,1,0:T(8,128)(2,1)S(1)}, u32[]{:S(2)}, u32[]{:S(2)}) collective-permute-start(bf16[64,16,128]{2,1,0:T(8,128)(2,1)} %bitcast.58), channel_id=1, source_target_pairs={{0,1},{1,0},{2,3},{3,2},{16,17},{17,16},{18,19},{19,18},{4,5},{5,4... | collective-permute-start | bytes 786440 | tf_op jit(solution)/shard_map/ppermute | solution.py:19
  219.7 18.5 %collective-permute-start.20 = (bf16[64,16,128]{2,1,0:T(8,128)(2,1)}, bf16[64,16,128]{2,1,0:T(8,128)(2,1)S(1)}, u32[]{:S(2)}, u32[]{:S(2)}) collective-permute-start(bf16[64,16,128]{2,1,0:T(8,128)(2,1)} %bitcast.60), channel_id=1, source_target_pairs={{0,16},{1,17},{2,18},{3,19},{16,0},{17,1},{18,2},{19,3},{4,20},{5,... | collective-permute-start | bytes 786440 | tf_op jit(solution)/shard_map/ppermute | solution.py:19
  223.1 18.9 %all-to-all-start.1 = ((bf16[64,8,256]{2,1,0:T(8,128)(2,1)}), bf16[64,8,256]{2,1,0:T(8,128)(2,1)}, u32[]{:S(2)}, u32[]{:S(2)}) async-start(bf16[64,8,256]{2,1,0:T(8,128)(2,1)} %copy.31), calls=%async_computation.1 | async-start | bytes 524288 | tf_op jit(solution)/shard_map/all_to_all | solution.py:429
  227.9 21.6 %collective-permute-start.21 = (bf16[64,16,128]{2,1,0:T(8,128)(2,1)}, bf16[64,16,128]{2,1,0:T(8,128)(2,1)S(1)}, u32[]{:S(2)}, u32[]{:S(2)}) collective-permute-start(bf16[64,16,128]{2,1,0:T(8,128)(2,1)} %bitcast.64), channel_id=1, source_target_pairs={{0,19},{1,18},{2,17},{3,16},{16,3},{17,2},{18,1},{19,0},{4,23},{5,... | collective-permute-start | bytes 786440 | tf_op jit(solution)/shard_map/ppermute | solution.py:19
  232.4 35.2 %collective-permute-start.22 = (bf16[64,16,128]{2,1,0:T(8,128)(2,1)}, bf16[64,16,128]{2,1,0:T(8,128)(2,1)S(1)}, u32[]{:S(2)}, u32[]{:S(2)}) collective-permute-start(bf16[64,16,128]{2,1,0:T(8,128)(2,1)} %bitcast.66), channel_id=1, source_target_pairs={{0,18},{1,19},{2,16},{3,17},{16,2},{17,3},{18,0},{19,1},{4,22},{5,... | collective-permute-start | bytes 786440 | tf_op jit(solution)/shard_map/ppermute | solution.py:19
  238.2 33.9 %collective-permute-start.23 = (bf16[64,16,128]{2,1,0:T(8,128)(2,1)}, bf16[64,16,128]{2,1,0:T(8,128)(2,1)S(1)}, u32[]{:S(2)}, u32[]{:S(2)}) collective-permute-start(bf16[64,16,128]{2,1,0:T(8,128)(2,1)} %bitcast.68), channel_id=1, source_target_pairs={{0,2},{1,3},{2,0},{3,1},{16,18},{17,19},{18,16},{19,17},{4,6},{5,7... | collective-permute-start | bytes 786440 | tf_op jit(solution)/shard_map/ppermute | solution.py:19
  238.2 40.3 %collective-permute-start.24 = (bf16[64,16,128]{2,1,0:T(8,128)(2,1)}, bf16[64,16,128]{2,1,0:T(8,128)(2,1)S(1)}, u32[]{:S(2)}, u32[]{:S(2)}) collective-permute-start(bf16[64,16,128]{2,1,0:T(8,128)(2,1)} %bitcast.70), channel_id=1, source_target_pairs={{0,3},{1,2},{2,1},{3,0},{16,19},{17,18},{18,17},{19,16},{4,7},{5,6... | collective-permute-start | bytes 786440 | tf_op jit(solution)/shard_map/ppermute | solution.py:19
  242.0 80.5 %all-to-all-start = ((bf16[64,8,1024]{2,1,0:T(8,128)(2,1)}), bf16[64,8,1024]{2,1,0:T(8,128)(2,1)}, u32[]{:S(2)}, u32[]{:S(2)}) async-start(bf16[64,8,1024]{2,1,0:T(8,128)(2,1)} %join.3), calls=%async_computation | async-start | bytes 2097152 | tf_op jit(solution)/shard_map/all_to_all | solution.py:429
  249.5 71.9 %collective-permute-start.31 = (f32[1,96,1024]{2,1,0:T(8,128)}, f32[1,96,1024]{2,1,0:T(8,128)}, u32[]{:S(2)}, u32[]{:S(2)}) collective-permute-start(f32[1,96,1024]{2,1,0:T(8,128)} %slice.241), channel_id=1, source_target_pairs={{0,8},{4,12},{8,0},{12,4},{1,9},{5,13},{9,1},{13,5},{2,10},{6,14},... | collective-permute-start | bytes 1179656 | tf_op jit(solution)/shard_map/ppermute | solution.py:19
  267.6 46.1 %collective-permute-start.8 = (bf16[64,16,128]{2,1,0:T(8,128)(2,1)}, bf16[64,16,128]{2,1,0:T(8,128)(2,1)}, u32[]{:S(2)}, u32[]{:S(2)}) collective-permute-start(bf16[64,16,128]{2,1,0:T(8,128)(2,1)} %bitcast.38), channel_id=1, source_target_pairs={{0,3},{1,2},{2,1},{3,0},{16,19},{17,18},{18,17},{19,16},{4,7},{5,6... | collective-permute-start | bytes 786440 | tf_op jit(solution)/shard_map/ppermute | solution.py:19
  272.1 34.9 %collective-permute-start.13 = (bf16[64,16,128]{2,1,0:T(8,128)(2,1)}, bf16[64,16,128]{2,1,0:T(8,128)(2,1)}, u32[]{:S(2)}, u32[]{:S(2)}) collective-permute-start(bf16[64,16,128]{2,1,0:T(8,128)(2,1)} %bitcast.50), channel_id=1, source_target_pairs={{0,18},{1,19},{2,16},{3,17},{16,2},{17,3},{18,0},{19,1},{4,22},{5,... | collective-permute-start | bytes 786440 | tf_op jit(solution)/shard_map/ppermute | solution.py:19
  278.5 33.0 %collective-permute-start.14 = (bf16[64,16,128]{2,1,0:T(8,128)(2,1)}, bf16[64,16,128]{2,1,0:T(8,128)(2,1)}, u32[]{:S(2)}, u32[]{:S(2)}) collective-permute-start(bf16[64,16,128]{2,1,0:T(8,128)(2,1)} %bitcast.52), channel_id=1, source_target_pairs={{0,2},{1,3},{2,0},{3,1},{16,18},{17,19},{18,16},{19,17},{4,6},{5,7... | collective-permute-start | bytes 786440 | tf_op jit(solution)/shard_map/ppermute | solution.py:19
  315.3 12.1 %collective-permute-start.25 = (f32[16,96]{1,0:T(8,128)S(1)}, f32[16,96]{1,0:T(8,128)S(1)}, u32[]{:S(2)}, u32[]{:S(2)}) collective-permute-start(f32[16,96]{1,0:T(8,128)S(1)} %get-tuple-element.51), channel_id=1, source_target_pairs={{0,4},{4,0},{8,12},{12,8},{1,5},{5,1},{9,13},{13,9},{2,6},{6,2},{1... | collective-permute-start | bytes 18440 | tf_op jit(solution)/shard_map/ppermute | solution.py:19
  315.4 11.9 %collective-permute-start.26 = (f32[16,96]{1,0:T(8,128)S(1)}, f32[16,96]{1,0:T(8,128)S(1)}, u32[]{:S(2)}, u32[]{:S(2)}) collective-permute-start(f32[16,96]{1,0:T(8,128)S(1)} %get-tuple-element.52), channel_id=1, source_target_pairs={{0,8},{4,12},{8,0},{12,4},{1,9},{5,13},{9,1},{13,5},{2,10},{6,14},... | collective-permute-start | bytes 18440 | tf_op jit(solution)/shard_map/ppermute | solution.py:19
  317.1 10.3 %collective-permute-start.27 = (f32[16,96]{1,0:T(8,128)S(1)}, f32[16,96]{1,0:T(8,128)S(1)}, u32[]{:S(2)}, u32[]{:S(2)}) collective-permute-start(f32[16,96]{1,0:T(8,128)S(1)} %get-tuple-element.53), channel_id=1, source_target_pairs={{0,12},{4,8},{8,4},{12,0},{1,13},{5,9},{9,5},{13,1},{2,14},{6,10},... | collective-permute-start | bytes 18440 | tf_op jit(solution)/shard_map/ppermute | solution.py:19
  (40 other events, 289.2 us)

commit v9 on v8

--- a/solution.py
+++ b/solution.py
@@ -471,8 +471,9 @@
             lax.dynamic_index_in_dim(projected, tensor ^ s, 0, keepdims=False)
             for s in range(parts)
         ]
-    shares = [low_rank[0]] + [swap(low_rank[s], "tensor", s) for s in range(1, parts)]
-    query, value = finish(shares, bounds, [base_query, base_value, own_query, own_value], steps=4)
+    turns = sorted(range(1, parts), key=lambda s: s == 1)
+    shares = [low_rank[0]] + [swap(low_rank[s], "tensor", s) for s in turns]
+    query, value = finish(shares, bounds, [base_query, base_value, own_query, own_value], steps=2)
     return query, value, down_factors, query_up_factors, value_up_factors
 
 

time: 331 us -> 331 us (level)
  no operation moved by 1% of the time
where the time goes in v9:
time: 331 us; the launch traced here: 329 us
  starting transfers between devices  141 us (43%)
  waiting for transfers between devices  89.4 us (27%)
  local copies, waits for them, and re-layouts  45.1 us (14%)
  Pallas kernels  19.9 us (6%)
  matrix products  18.7 us (6%)
  other arithmetic  13.9 us (4%)
    ppermute x52, starting transfers between devices, swap(): return lax.ppermute(x, axes, [(a, a ^ shift) for a in range(total)])  132 us
    ppermute x52, waiting for transfers between devices, swap(): return lax.ppermute(x, axes, [(a, a ^ shift) for a in range(total)])  89.3 us
    unnamed x97, local copies, waits for them, and re-layouts  28.4 us
    dot_general x1, matrix products, local(): base_query = jnp.dot(turned, w_query, preferred_element_type=jnp.float32)  10.2 us
    all_to_all x2, starting transfers between devices, own_block(): lax.all_to_all(factors, 'tensor', split_axis=0, concat_axis=0, tiled=True)  8.65 us
    pallas_call x3, Pallas kernels, join(): pl.pallas_call(functools.partial(join_kernel, shifts, stride, start, widt...  6.66 us
  transfers between devices with their start and end apart: 54, of which 14 were waited for; matrix products, arithmetic and copies ran while one was open for 19% of the time, Pallas kernels for 6%

profile of v9, /device:TPU:0, one launch (start us, length us, event | category | flops | bytes accessed | tf_op | source)
XLA Modules:
  0.0 329.5 jit_solution(684053891135455453)
XLA Ops:
  2.9 4.1 %collective-permute-start = (bf16[1,16,512]{2,1,0:T(8,128)(2,1)S(1)}, bf16[1,16,512]{2,1,0:T(8,128)(2,1)S(1)}, u32[]{:S(2)}, u32[]{:S(2)}) collective-permute-start(bf16[1,16,512]{2,1,0:T(8,128)(2,1)S(1)} %get-tuple-element.135), channel_id=1, source_target_pairs={{0,2},{1,3},{2,0},{3,1},{4,6},{5,7},{6,4},{7,5},{8,10},{9,11},{10,... | collective-permute-start | bytes 49160 | tf_op jit(solution)/shard_map/ppermute | solution.py:19
  8.5 10.2 %fusion.9 = f32[384,4096]{1,0:T(8,128)S(1)} fusion(bf16[2048,4096]{1,0:T(8,128)(2,1)} %param.16, bf16[96,2048]{1,0:T(8,128)(2,1)S(1)} %get-tuple-element.104, bf16[96,2048]{1,0:T(8,128)(2,1)S(1)} %get-tuple-element.105, bf16[96,2048]{1,0:T(8,128)(2,1)S(1)} %get-tuple-element.106, bf16[96,2048]{1,0:T(8,128)(2,1)S(1)} %get-tuple-element.103), kind=kOutput, calls=%fused_computation.25 | convolution fusion | flops 6448742400 | bytes 24641536 | tf_op jit(solution)/shard_map/dot_general | solution.py:423
  18.7 3.1 fusion.29
  25.1 1.8 cut.5
  26.9 2.0 collective-permute-start.33
  28.9 2.5 collective-permute-start.32
  33.0 2.7 collective-permute-done.2
  35.8 4.0 %fusion.8 = f32[384,1024]{1,0:T(8,128)S(1)} fusion(bf16[2048,1024]{1,0:T(8,128)(2,1)} %param.17, bf16[96,2048]{1,0:T(8,128)(2,1)S(1)} %get-tuple-element.104, bf16[96,2048]{1,0:T(8,128)(2,1)S(1)} %get-tuple-element.105, bf16[96,2048]{1,0:T(8,128)(2,1)S(1)} %get-tuple-element.106, bf16[96,2048]{1,0:T(8,128)(2,1)S(1)} %get-tuple-element.103), kind=kOutput, calls=%fused_computation.24 | convolution fusion | flops 1616904192 | bytes 7340032 | tf_op jit(solution)/shard_map/dot_general | solution.py:424
  49.0 1.9 cut.4
  54.1 2.4 collective-permute-start.44
  56.5 2.2 pad_maximum_fusion.3
  58.8 2.0 collective-permute-start.43
  62.6 2.0 reshape.154
  66.7 15.4 %collective-permute-done.44 = bf16[128,256]{1,0:T(8,128)(2,1)S(1)} collective-permute-done((bf16[128,256]{1,0:T(8,128)(2,1)}, bf16[128,256]{1,0:T(8,128)(2,1)S(1)}, u32[]{:S(2)}, u32[]{:S(2)}) %collective-permute-start.44) | collective-permute-done | bytes 65568 | tf_op jit(solution)/shard_map/ppermute | solution.py:19
  82.1 23.4 %collective-permute-start.5 = (bf16[128,16,128]{2,1,0:T(8,128)(2,1)S(1)}, bf16[128,16,128]{2,1,0:T(8,128)(2,1)S(1)}, u32[]{:S(2)}, u32[]{:S(2)}) collective-permute-start(bf16[128,16,128]{2,1,0:T(8,128)(2,1)S(1)} %copy-done.17), channel_id=1, source_target_pairs={{0,1},{1,0},{2,3},{3,2},{4,5},{5,4},{6,7},{7,6},{8,9},{9,8},{10,11... | collective-permute-start | bytes 1572872 | tf_op jit(solution)/shard_map/ppermute | solution.py:19
  106.7 11.5 %collective-permute-done.42 = bf16[128,256]{1,0:T(8,128)(2,1)S(1)} collective-permute-done((bf16[128,256]{1,0:T(8,128)(2,1)S(1)}, bf16[128,256]{1,0:T(8,128)(2,1)S(1)}, u32[]{:S(2)}, u32[]{:S(2)}) %collective-permute-start.42) | collective-permute-done | bytes 65568 | tf_op jit(solution)/shard_map/ppermute | solution.py:19
  120.9 2.0 collective-permute-start.15
  124.5 10.3 %collective-permute-done.17 = bf16[128,16,128]{2,1,0:T(8,128)(2,1)S(1)} collective-permute-done((bf16[128,16,128]{2,1,0:T(8,128)(2,1)S(1)}, bf16[128,16,128]{2,1,0:T(8,128)(2,1)S(1)}, u32[]{:S(2)}, u32[]{:S(2)}) %collective-permute-start.17) | collective-permute-done | bytes 524320 | tf_op jit(solution)/shard_map/ppermute | solution.py:19
  134.9 21.1 %collective-permute-start.46 = (bf16[64,256]{1,0:T(8,128)(2,1)S(1)}, bf16[64,256]{1,0:T(8,128)(2,1)S(1)}, u32[]{:S(2)}, u32[]{:S(2)}) collective-permute-start(bf16[64,256]{1,0:T(8,128)(2,1)S(1)} %get-tuple-element.126), channel_id=1, source_target_pairs={{0,2},{1,3},{2,0},{3,1},{16,18},{17,19},{18,16},{19,17},{4,6},{5,7... | collective-permute-start | bytes 98312 | tf_op jit(solution)/shard_map/ppermute | solution.py:19
  155.9 9.1 %collective-permute-done.16 = bf16[128,16,128]{2,1,0:T(8,128)(2,1)S(1)} collective-permute-done((bf16[128,16,128]{2,1,0:T(8,128)(2,1)S(1)}, bf16[128,16,128]{2,1,0:T(8,128)(2,1)S(1)}, u32[]{:S(2)}, u32[]{:S(2)}) %collective-permute-start.16) | collective-permute-done | bytes 524320 | tf_op jit(solution)/shard_map/ppermute | solution.py:19
  169.4 3.8 %collective-permute-start.50 = (bf16[64,256]{1,0:T(8,128)(2,1)S(1)}, bf16[64,256]{1,0:T(8,128)(2,1)S(1)}, u32[]{:S(2)}, u32[]{:S(2)}) collective-permute-start(bf16[64,256]{1,0:T(8,128)(2,1)S(1)} %get-tuple-element.122), channel_id=1, source_target_pairs={{0,18},{1,19},{2,16},{3,17},{16,2},{17,3},{18,0},{19,1},{4,22},{5,... | collective-permute-start | bytes 98312 | tf_op jit(solution)/shard_map/ppermute | solution.py:19
  175.8 2.8 collective-permute-start.36
  183.6 2.3 add.67
  187.3 3.8 %collective-permute-start.40 = (bf16[64,8,128]{2,1,0:T(8,128)(2,1)S(1)}, bf16[64,8,128]{2,1,0:T(8,128)(2,1)S(1)}, u32[]{:S(2)}, u32[]{:S(2)}) collective-permute-start(bf16[64,8,128]{2,1,0:T(8,128)(2,1)S(1)} %bitcast.172), channel_id=1, source_target_pairs={{0,18},{1,19},{2,16},{3,17},{16,2},{17,3},{18,0},{19,1},{4,22},{5,... | collective-permute-start | bytes 393224 | tf_op jit(solution)/shard_map/ppermute | solution.py:19
  195.2 6.1 %collective-permute-done.40.refs_6_ = bf16[64,8,128]{2,1,0:T(8,128)(2,1)S(1)} collective-permute-done((bf16[64,8,128]{2,1,0:T(8,128)(2,1)S(1)}, bf16[64,8,128]{2,1,0:T(8,128)(2,1)S(1)}, u32[]{:S(2)}, u32[]{:S(2)}) %collective-permute-start.40) | collective-permute-done | bytes 131104 | tf_op jit(solution)/shard_map/ppermute | solution.py:19
  201.2 2.0 collective-permute-start.11
  203.2 3.4 %collective-permute-done.9.refs_0_ = bf16[64,16,128]{2,1,0:T(8,128)(2,1)S(1)} collective-permute-done((bf16[64,16,128]{2,1,0:T(8,128)(2,1)S(1)}, bf16[64,16,128]{2,1,0:T(8,128)(2,1)S(1)}, u32[]{:S(2)}, u32[]{:S(2)}) %collective-permute-start.9) | collective-permute-done | bytes 262176 | tf_op jit(solution)/shard_map/ppermute | solution.py:19
  206.6 2.5 collective-permute-start.12
  211.9 2.1 collective-permute-start.18
  223.1 4.0 %all-to-all-start.1 = ((bf16[64,8,256]{2,1,0:T(8,128)(2,1)}), bf16[64,8,256]{2,1,0:T(8,128)(2,1)}, u32[]{:S(2)}, u32[]{:S(2)}) async-start(bf16[64,8,256]{2,1,0:T(8,128)(2,1)} %copy.31), calls=%async_computation.1 | async-start | bytes 524288 | tf_op jit(solution)/shard_map/all_to_all | solution.py:429
  227.9 2.2 collective-permute-start.21
  232.4 5.9 %collective-permute-start.22 = (bf16[64,16,128]{2,1,0:T(8,128)(2,1)}, bf16[64,16,128]{2,1,0:T(8,128)(2,1)S(1)}, u32[]{:S(2)}, u32[]{:S(2)}) collective-permute-start(bf16[64,16,128]{2,1,0:T(8,128)(2,1)} %bitcast.66), channel_id=1, source_target_pairs={{0,18},{1,19},{2,16},{3,17},{16,2},{17,3},{18,0},{19,1},{4,22},{5,... | collective-permute-start | bytes 786440 | tf_op jit(solution)/shard_map/ppermute | solution.py:19
  239.5 2.5 join.3
  242.0 4.6 %all-to-all-start = ((bf16[64,8,1024]{2,1,0:T(8,128)(2,1)}), bf16[64,8,1024]{2,1,0:T(8,128)(2,1)}, u32[]{:S(2)}, u32[]{:S(2)}) async-start(bf16[64,8,1024]{2,1,0:T(8,128)(2,1)} %join.3), calls=%async_computation | async-start | bytes 2097152 | tf_op jit(solution)/shard_map/all_to_all | solution.py:429
  249.5 2.0 collective-permute-start.31
  251.9 1.7 copy.35
  253.6 1.7 copy.41
  255.3 1.7 copy.42
  257.0 10.6 %collective-permute-done.22.refs_5_ = bf16[64,16,128]{2,1,0:T(8,128)(2,1)S(1)} collective-permute-done((bf16[64,16,128]{2,1,0:T(8,128)(2,1)}, bf16[64,16,128]{2,1,0:T(8,128)(2,1)S(1)}, u32[]{:S(2)}, u32[]{:S(2)}) %collective-permute-start.22) | collective-permute-done | bytes 262176 | tf_op jit(solution)/shard_map/ppermute | solution.py:19
  267.6 2.1 collective-permute-start.8
  269.7 2.4 collective-permute-done.23.refs_6_
  272.1 6.4 %collective-permute-start.13 = (bf16[64,16,128]{2,1,0:T(8,128)(2,1)}, bf16[64,16,128]{2,1,0:T(8,128)(2,1)}, u32[]{:S(2)}, u32[]{:S(2)}) collective-permute-start(bf16[64,16,128]{2,1,0:T(8,128)(2,1)} %bitcast.50), channel_id=1, source_target_pairs={{0,18},{1,19},{2,16},{3,17},{16,2},{17,3},{18,0},{19,1},{4,22},{5,... | collective-permute-start | bytes 786440 | tf_op jit(solution)/shard_map/ppermute | solution.py:19
  278.5 12.0 %collective-permute-start.14 = (bf16[64,16,128]{2,1,0:T(8,128)(2,1)}, bf16[64,16,128]{2,1,0:T(8,128)(2,1)}, u32[]{:S(2)}, u32[]{:S(2)}) collective-permute-start(bf16[64,16,128]{2,1,0:T(8,128)(2,1)} %bitcast.52), channel_id=1, source_target_pairs={{0,2},{1,3},{2,0},{3,1},{16,18},{17,19},{18,16},{19,17},{4,6},{5,7... | collective-permute-start | bytes 786440 | tf_op jit(solution)/shard_map/ppermute | solution.py:19
  297.0 10.1 %collective-permute-done.13.refs_5_ = bf16[64,16,128]{2,1,0:T(8,128)(2,1)} collective-permute-done((bf16[64,16,128]{2,1,0:T(8,128)(2,1)}, bf16[64,16,128]{2,1,0:T(8,128)(2,1)}, u32[]{:S(2)}, u32[]{:S(2)}) %collective-permute-start.13) | collective-permute-done | bytes 262176 | tf_op jit(solution)/shard_map/ppermute | solution.py:19
  307.1 4.5 %collective-permute-done.14.refs_6_ = bf16[64,16,128]{2,1,0:T(8,128)(2,1)} collective-permute-done((bf16[64,16,128]{2,1,0:T(8,128)(2,1)}, bf16[64,16,128]{2,1,0:T(8,128)(2,1)}, u32[]{:S(2)}, u32[]{:S(2)}) %collective-permute-start.14) | collective-permute-done | bytes 262176 | tf_op jit(solution)/shard_map/ppermute | solution.py:19
  311.5 2.1 project.4
  315.3 1.7 collective-permute-start.25
  319.1 2.6 join.5
  (214 shorter events, 84.7 us)
Async XLA Ops:
  2.9 18.9 %collective-permute-start = (bf16[1,16,512]{2,1,0:T(8,128)(2,1)S(1)}, bf16[1,16,512]{2,1,0:T(8,128)(2,1)S(1)}, u32[]{:S(2)}, u32[]{:S(2)}) collective-permute-start(bf16[1,16,512]{2,1,0:T(8,128)(2,1)S(1)} %get-tuple-element.135), channel_id=1, source_target_pairs={{0,2},{1,3},{2,0},{3,1},{4,6},{5,7},{6,4},{7,5},{8,10},{9,11},{10,... | collective-permute-start | bytes 49160 | tf_op jit(solution)/shard_map/ppermute | solution.py:19
  21.8 159.9 %collective-permute-start.28 = (f32[2,96,4096]{2,1,0:T(8,128)}, f32[2,96,4096]{2,1,0:T(8,128)}, u32[]{:S(2)}, u32[]{:S(2)}) collective-permute-start(f32[2,96,4096]{2,1,0:T(8,128)} %bitcast.17), channel_id=1, source_target_pairs={{0,4},{4,0},{8,12},{12,8},{1,5},{5,1},{9,13},{13,9},{2,6},{6,2},{1... | collective-permute-start | bytes 9437192 | tf_op jit(solution)/shard_map/ppermute | solution.py:19
  21.8 9.6 %collective-permute-start.1 = (bf16[2,16,512]{2,1,0:T(8,128)(2,1)S(1)}, bf16[2,16,512]{2,1,0:T(8,128)(2,1)S(1)}, u32[]{:S(2)}, u32[]{:S(2)}) collective-permute-start(bf16[2,16,512]{2,1,0:T(8,128)(2,1)S(1)} %pad_maximum_fusion.10), channel_id=1, source_target_pairs={{0,1},{1,0},{2,3},{3,2},{4,5},{5,4},{6,7},{7,6},{8,9},{9,8},{10,11... | collective-permute-start | bytes 98312 | tf_op jit(solution)/shard_map/ppermute | solution.py:19
  25.1 27.5 %collective-permute-start.34 = (bf16[128,8,128]{2,1,0:T(8,128)(2,1)}, bf16[128,8,128]{2,1,0:T(8,128)(2,1)}, u32[]{:S(2)}, u32[]{:S(2)}) collective-permute-start(bf16[128,8,128]{2,1,0:T(8,128)(2,1)} %constant_dynamic-slice_fusion), channel_id=1, source_target_pairs={{0,3},{1,2},{2,1},{3,0},{4,7},{5,6},{6,5},{7,4},{8,11},{9,10},{10,... | collective-permute-start | bytes 786440 | tf_op jit(solution)/shard_map/ppermute | solution.py:19
  26.9 25.9 %collective-permute-start.33 = (bf16[128,8,128]{2,1,0:T(8,128)(2,1)}, bf16[128,8,128]{2,1,0:T(8,128)(2,1)}, u32[]{:S(2)}, u32[]{:S(2)}) collective-permute-start(bf16[128,8,128]{2,1,0:T(8,128)(2,1)} %get-tuple-element.56), channel_id=1, source_target_pairs={{0,2},{1,3},{2,0},{3,1},{4,6},{5,7},{6,4},{7,5},{8,10},{9,11},{10,... | collective-permute-start | bytes 786440 | tf_op jit(solution)/shard_map/ppermute | solution.py:19
  28.9 25.2 %collective-permute-start.32 = (bf16[128,8,128]{2,1,0:T(8,128)(2,1)}, bf16[128,8,128]{2,1,0:T(8,128)(2,1)}, u32[]{:S(2)}, u32[]{:S(2)}) collective-permute-start(bf16[128,8,128]{2,1,0:T(8,128)(2,1)} %get-tuple-element.55), channel_id=1, source_target_pairs={{0,1},{1,0},{2,3},{3,2},{4,5},{5,4},{6,7},{7,6},{8,9},{9,8},{10,11... | collective-permute-start | bytes 786440 | tf_op jit(solution)/shard_map/ppermute | solution.py:19
  42.1 16.7 %collective-permute-start.4 = (bf16[2,128,512]{2,1,0:T(8,128)(2,1)}, bf16[2,128,512]{2,1,0:T(8,128)(2,1)}, u32[]{:S(2)}, u32[]{:S(2)}) collective-permute-start(bf16[2,128,512]{2,1,0:T(8,128)(2,1)} %pad_maximum_fusion.8), channel_id=1, source_target_pairs={{0,8},{4,12},{8,0},{12,4},{1,9},{5,13},{9,1},{13,5},{2,10},{6,14},... | collective-permute-start | bytes 786440 | tf_op jit(solution)/shard_map/ppermute | solution.py:19
  52.6 67.1 %collective-permute-start.7 = (bf16[128,16,128]{2,1,0:T(8,128)(2,1)}, bf16[128,16,128]{2,1,0:T(8,128)(2,1)}, u32[]{:S(2)}, u32[]{:S(2)}) collective-permute-start(bf16[128,16,128]{2,1,0:T(8,128)(2,1)} %copy-done.19), channel_id=1, source_target_pairs={{0,3},{1,2},{2,1},{3,0},{4,7},{5,6},{6,5},{7,4},{8,11},{9,10},{10,... | collective-permute-start | bytes 1572872 | tf_op jit(solution)/shard_map/ppermute | solution.py:19
  52.9 68.1 %collective-permute-start.6 = (bf16[128,16,128]{2,1,0:T(8,128)(2,1)}, bf16[128,16,128]{2,1,0:T(8,128)(2,1)}, u32[]{:S(2)}, u32[]{:S(2)}) collective-permute-start(bf16[128,16,128]{2,1,0:T(8,128)(2,1)} %copy-done.18), channel_id=1, source_target_pairs={{0,2},{1,3},{2,0},{3,1},{4,6},{5,7},{6,4},{7,5},{8,10},{9,11},{10,... | collective-permute-start | bytes 1572872 | tf_op jit(solution)/shard_map/ppermute | solution.py:19
  54.1 28.0 %collective-permute-start.44 = (bf16[128,256]{1,0:T(8,128)(2,1)}, bf16[128,256]{1,0:T(8,128)(2,1)S(1)}, u32[]{:S(2)}, u32[]{:S(2)}) collective-permute-start(bf16[128,256]{1,0:T(8,128)(2,1)} %copy-done.22), channel_id=1, source_target_pairs={{0,3},{1,2},{2,1},{3,0},{4,7},{5,6},{6,5},{7,4},{8,11},{9,10},{10,... | collective-permute-start | bytes 196616 | tf_op jit(solution)/shard_map/ppermute | solution.py:19
  58.8 47.0 %collective-permute-start.43 = (bf16[128,256]{1,0:T(8,128)(2,1)S(1)}, bf16[128,256]{1,0:T(8,128)(2,1)S(1)}, u32[]{:S(2)}, u32[]{:S(2)}) collective-permute-start(bf16[128,256]{1,0:T(8,128)(2,1)S(1)} %copy-done.21), channel_id=1, source_target_pairs={{0,2},{1,3},{2,0},{3,1},{4,6},{5,7},{6,4},{7,5},{8,10},{9,11},{10,... | collective-permute-start | bytes 196616 | tf_op jit(solution)/shard_map/ppermute | solution.py:19
  82.1 40.8 %collective-permute-start.5 = (bf16[128,16,128]{2,1,0:T(8,128)(2,1)S(1)}, bf16[128,16,128]{2,1,0:T(8,128)(2,1)S(1)}, u32[]{:S(2)}, u32[]{:S(2)}) collective-permute-start(bf16[128,16,128]{2,1,0:T(8,128)(2,1)S(1)} %copy-done.17), channel_id=1, source_target_pairs={{0,1},{1,0},{2,3},{3,2},{4,5},{5,4},{6,7},{7,6},{8,9},{9,8},{10,11... | collective-permute-start | bytes 1572872 | tf_op jit(solution)/shard_map/ppermute | solution.py:19
  105.8 12.4 %collective-permute-start.42 = (bf16[128,256]{1,0:T(8,128)(2,1)S(1)}, bf16[128,256]{1,0:T(8,128)(2,1)S(1)}, u32[]{:S(2)}, u32[]{:S(2)}) collective-permute-start(bf16[128,256]{1,0:T(8,128)(2,1)S(1)} %get-tuple-element.58), channel_id=1, source_target_pairs={{0,1},{1,0},{2,3},{3,2},{4,5},{5,4},{6,7},{7,6},{8,9},{9,8},{10,11... | collective-permute-start | bytes 196616 | tf_op jit(solution)/shard_map/ppermute | solution.py:19
  118.2 16.7 %collective-permute-start.17 = (bf16[128,16,128]{2,1,0:T(8,128)(2,1)S(1)}, bf16[128,16,128]{2,1,0:T(8,128)(2,1)S(1)}, u32[]{:S(2)}, u32[]{:S(2)}) collective-permute-start(bf16[128,16,128]{2,1,0:T(8,128)(2,1)S(1)} %get-tuple-element.41), channel_id=1, source_target_pairs={{0,3},{1,2},{2,1},{3,0},{4,7},{5,6},{6,5},{7,4},{8,11},{9,10},{10,... | collective-permute-start | bytes 1572872 | tf_op jit(solution)/shard_map/ppermute | solution.py:19
  119.7 45.3 %collective-permute-start.16 = (bf16[128,16,128]{2,1,0:T(8,128)(2,1)S(1)}, bf16[128,16,128]{2,1,0:T(8,128)(2,1)S(1)}, u32[]{:S(2)}, u32[]{:S(2)}) collective-permute-start(bf16[128,16,128]{2,1,0:T(8,128)(2,1)S(1)} %get-tuple-element.40), channel_id=1, source_target_pairs={{0,2},{1,3},{2,0},{3,1},{4,6},{5,7},{6,4},{7,5},{8,10},{9,11},{10,... | collective-permute-start | bytes 1572872 | tf_op jit(solution)/shard_map/ppermute | solution.py:19
  120.9 46.9 %collective-permute-start.15 = (bf16[128,16,128]{2,1,0:T(8,128)(2,1)S(1)}, bf16[128,16,128]{2,1,0:T(8,128)(2,1)S(1)}, u32[]{:S(2)}, u32[]{:S(2)}) collective-permute-start(bf16[128,16,128]{2,1,0:T(8,128)(2,1)S(1)} %get-tuple-element.39), channel_id=1, source_target_pairs={{0,1},{1,0},{2,3},{3,2},{4,5},{5,4},{6,7},{7,6},{8,9},{9,8},{10,11... | collective-permute-start | bytes 1572872 | tf_op jit(solution)/shard_map/ppermute | solution.py:19
  123.0 46.4 %collective-permute-start.45 = (bf16[64,256]{1,0:T(8,128)(2,1)S(1)}, bf16[64,256]{1,0:T(8,128)(2,1)S(1)}, u32[]{:S(2)}, u32[]{:S(2)}) collective-permute-start(bf16[64,256]{1,0:T(8,128)(2,1)S(1)} %get-tuple-element.127), channel_id=1, source_target_pairs={{0,1},{1,0},{2,3},{3,2},{16,17},{17,16},{18,19},{19,18},{4,5},{5,4... | collective-permute-start | bytes 98312 | tf_op jit(solution)/shard_map/ppermute | solution.py:19
  134.9 34.5 %collective-permute-start.46 = (bf16[64,256]{1,0:T(8,128)(2,1)S(1)}, bf16[64,256]{1,0:T(8,128)(2,1)S(1)}, u32[]{:S(2)}, u32[]{:S(2)}) collective-permute-start(bf16[64,256]{1,0:T(8,128)(2,1)S(1)} %get-tuple-element.126), channel_id=1, source_target_pairs={{0,2},{1,3},{2,0},{3,1},{16,18},{17,19},{18,16},{19,17},{4,6},{5,7... | collective-permute-start | bytes 98312 | tf_op jit(solution)/shard_map/ppermute | solution.py:19
  169.4 9.3 %collective-permute-start.50 = (bf16[64,256]{1,0:T(8,128)(2,1)S(1)}, bf16[64,256]{1,0:T(8,128)(2,1)S(1)}, u32[]{:S(2)}, u32[]{:S(2)}) collective-permute-start(bf16[64,256]{1,0:T(8,128)(2,1)S(1)} %get-tuple-element.122), channel_id=1, source_target_pairs={{0,18},{1,19},{2,16},{3,17},{16,2},{17,3},{18,0},{19,1},{4,22},{5,... | collective-permute-start | bytes 98312 | tf_op jit(solution)/shard_map/ppermute | solution.py:19
  175.7 11.6 %collective-permute-start.35 = (bf16[64,8,128]{2,1,0:T(8,128)(2,1)S(1)}, bf16[64,8,128]{2,1,0:T(8,128)(2,1)S(1)}, u32[]{:S(2)}, u32[]{:S(2)}) collective-permute-start(bf16[64,8,128]{2,1,0:T(8,128)(2,1)S(1)} %bitcast.177), channel_id=1, source_target_pairs={{0,1},{1,0},{2,3},{3,2},{16,17},{17,16},{18,19},{19,18},{4,5},{5,4... | collective-permute-start | bytes 393224 | tf_op jit(solution)/shard_map/ppermute | solution.py:19
  175.8 11.5 %collective-permute-start.36 = (bf16[64,8,128]{2,1,0:T(8,128)(2,1)S(1)}, bf16[64,8,128]{2,1,0:T(8,128)(2,1)S(1)}, u32[]{:S(2)}, u32[]{:S(2)}) collective-permute-start(bf16[64,8,128]{2,1,0:T(8,128)(2,1)S(1)} %bitcast.176), channel_id=1, source_target_pairs={{0,2},{1,3},{2,0},{3,1},{16,18},{17,19},{18,16},{19,17},{4,6},{5,7... | collective-permute-start | bytes 393224 | tf_op jit(solution)/shard_map/ppermute | solution.py:19
  178.7 12.5 %collective-permute-start.37 = (bf16[64,8,128]{2,1,0:T(8,128)(2,1)S(1)}, bf16[64,8,128]{2,1,0:T(8,128)(2,1)S(1)}, u32[]{:S(2)}, u32[]{:S(2)}) collective-permute-start(bf16[64,8,128]{2,1,0:T(8,128)(2,1)S(1)} %bitcast.175), channel_id=1, source_target_pairs={{0,3},{1,2},{2,1},{3,0},{16,19},{17,18},{18,17},{19,16},{4,7},{5,6... | collective-permute-start | bytes 393224 | tf_op jit(solution)/shard_map/ppermute | solution.py:19
  180.2 12.4 %collective-permute-start.38 = (bf16[64,8,128]{2,1,0:T(8,128)(2,1)S(1)}, bf16[64,8,128]{2,1,0:T(8,128)(2,1)S(1)}, u32[]{:S(2)}, u32[]{:S(2)}) collective-permute-start(bf16[64,8,128]{2,1,0:T(8,128)(2,1)S(1)} %bitcast.174), channel_id=1, source_target_pairs={{0,16},{1,17},{2,18},{3,19},{16,0},{17,1},{18,2},{19,3},{4,20},{5,... | collective-permute-start | bytes 393224 | tf_op jit(solution)/shard_map/ppermute | solution.py:19
  181.7 11.5 %collective-permute-start.39 = (bf16[64,8,128]{2,1,0:T(8,128)(2,1)S(1)}, bf16[64,8,128]{2,1,0:T(8,128)(2,1)S(1)}, u32[]{:S(2)}, u32[]{:S(2)}) collective-permute-start(bf16[64,8,128]{2,1,0:T(8,128)(2,1)S(1)} %bitcast.173), channel_id=1, source_target_pairs={{0,17},{1,16},{2,19},{3,18},{16,1},{17,0},{18,3},{19,2},{4,21},{5,... | collective-permute-start | bytes 393224 | tf_op jit(solution)/shard_map/ppermute | solution.py:19
  187.3 50.9 %collective-permute-start.30 = (f32[2,96,1024]{2,1,0:T(8,128)}, f32[2,96,1024]{2,1,0:T(8,128)}, u32[]{:S(2)}, u32[]{:S(2)}) collective-permute-start(f32[2,96,1024]{2,1,0:T(8,128)} %bitcast.20), channel_id=1, source_target_pairs={{0,4},{4,0},{8,12},{12,8},{1,5},{5,1},{9,13},{13,9},{2,6},{6,2},{1... | collective-permute-start | bytes 2359304 | tf_op jit(solution)/shard_map/ppermute | solution.py:19
  187.3 13.9 %collective-permute-start.40 = (bf16[64,8,128]{2,1,0:T(8,128)(2,1)S(1)}, bf16[64,8,128]{2,1,0:T(8,128)(2,1)S(1)}, u32[]{:S(2)}, u32[]{:S(2)}) collective-permute-start(bf16[64,8,128]{2,1,0:T(8,128)(2,1)S(1)} %bitcast.172), channel_id=1, source_target_pairs={{0,18},{1,19},{2,16},{3,17},{16,2},{17,3},{18,0},{19,1},{4,22},{5,... | collective-permute-start | bytes 393224 | tf_op jit(solution)/shard_map/ppermute | solution.py:19
  191.2 10.1 %collective-permute-start.41 = (bf16[64,8,128]{2,1,0:T(8,128)(2,1)S(1)}, bf16[64,8,128]{2,1,0:T(8,128)(2,1)S(1)}, u32[]{:S(2)}, u32[]{:S(2)}) collective-permute-start(bf16[64,8,128]{2,1,0:T(8,128)(2,1)S(1)} %bitcast.171), channel_id=1, source_target_pairs={{0,19},{1,18},{2,17},{3,16},{16,3},{17,2},{18,1},{19,0},{4,23},{5,... | collective-permute-start | bytes 393224 | tf_op jit(solution)/shard_map/ppermute | solution.py:19
  192.6 14.0 %collective-permute-start.9 = (bf16[64,16,128]{2,1,0:T(8,128)(2,1)S(1)}, bf16[64,16,128]{2,1,0:T(8,128)(2,1)S(1)}, u32[]{:S(2)}, u32[]{:S(2)}) collective-permute-start(bf16[64,16,128]{2,1,0:T(8,128)(2,1)S(1)} %bitcast.165), channel_id=1, source_target_pairs={{0,17},{1,16},{2,19},{3,18},{16,1},{17,0},{18,3},{19,2},{4,21},{5,... | collective-permute-start | bytes 786440 | tf_op jit(solution)/shard_map/ppermute | solution.py:19
  193.2 131.1 %collective-permute-start.29 = (f32[1,96,4096]{2,1,0:T(8,128)}, f32[1,96,4096]{2,1,0:T(8,128)}, u32[]{:S(2)}, u32[]{:S(2)}) collective-permute-start(f32[1,96,4096]{2,1,0:T(8,128)} %slice.237), channel_id=1, source_target_pairs={{0,8},{4,12},{8,0},{12,4},{1,9},{5,13},{9,1},{13,5},{2,10},{6,14},... | collective-permute-start | bytes 4718600 | tf_op jit(solution)/shard_map/ppermute | solution.py:19
  201.2 10.7 %collective-permute-start.10 = (bf16[64,16,128]{2,1,0:T(8,128)(2,1)S(1)}, bf16[64,16,128]{2,1,0:T(8,128)(2,1)S(1)}, u32[]{:S(2)}, u32[]{:S(2)}) collective-permute-start(bf16[64,16,128]{2,1,0:T(8,128)(2,1)S(1)} %bitcast.168), channel_id=1, source_target_pairs={{0,1},{1,0},{2,3},{3,2},{16,17},{17,16},{18,19},{19,18},{4,5},{5,4... | collective-permute-start | bytes 786440 | tf_op jit(solution)/shard_map/ppermute | solution.py:19
  201.2 14.3 %collective-permute-start.11 = (bf16[64,16,128]{2,1,0:T(8,128)(2,1)S(1)}, bf16[64,16,128]{2,1,0:T(8,128)(2,1)S(1)}, u32[]{:S(2)}, u32[]{:S(2)}) collective-permute-start(bf16[64,16,128]{2,1,0:T(8,128)(2,1)S(1)} %bitcast.167), channel_id=1, source_target_pairs={{0,16},{1,17},{2,18},{3,19},{16,0},{17,1},{18,2},{19,3},{4,20},{5,... | collective-permute-start | bytes 786440 | tf_op jit(solution)/shard_map/ppermute | solution.py:19
  206.6 12.4 %collective-permute-start.12 = (bf16[64,16,128]{2,1,0:T(8,128)(2,1)S(1)}, bf16[64,16,128]{2,1,0:T(8,128)(2,1)S(1)}, u32[]{:S(2)}, u32[]{:S(2)}) collective-permute-start(bf16[64,16,128]{2,1,0:T(8,128)(2,1)S(1)} %bitcast.166), channel_id=1, source_target_pairs={{0,19},{1,18},{2,17},{3,16},{16,3},{17,2},{18,1},{19,0},{4,23},{5,... | collective-permute-start | bytes 786440 | tf_op jit(solution)/shard_map/ppermute | solution.py:19
  211.9 16.0 %collective-permute-start.18 = (bf16[64,16,128]{2,1,0:T(8,128)(2,1)}, bf16[64,16,128]{2,1,0:T(8,128)(2,1)S(1)}, u32[]{:S(2)}, u32[]{:S(2)}) collective-permute-start(bf16[64,16,128]{2,1,0:T(8,128)(2,1)} %bitcast.56), channel_id=1, source_target_pairs={{0,17},{1,16},{2,19},{3,18},{16,1},{17,0},{18,3},{19,2},{4,21},{5,... | collective-permute-start | bytes 786440 | tf_op jit(solution)/shard_map/ppermute | solution.py:19
  216.2 16.2 %collective-permute-start.19 = (bf16[64,16,128]{2,1,0:T(8,128)(2,1)}, bf16[64,16,128]{2,1,0:T(8,128)(2,1)S(1)}, u32[]{:S(2)}, u32[]{:S(2)}) collective-permute-start(bf16[64,16,128]{2,1,0:T(8,128)(2,1)} %bitcast.58), channel_id=1, source_target_pairs={{0,1},{1,0},{2,3},{3,2},{16,17},{17,16},{18,19},{19,18},{4,5},{5,4... | collective-permute-start | bytes 786440 | tf_op jit(solution)/shard_map/ppermute | solution.py:19
  219.7 18.5 %collective-permute-start.20 = (bf16[64,16,128]{2,1,0:T(8,128)(2,1)}, bf16[64,16,128]{2,1,0:T(8,128)(2,1)S(1)}, u32[]{:S(2)}, u32[]{:S(2)}) collective-permute-start(bf16[64,16,128]{2,1,0:T(8,128)(2,1)} %bitcast.60), channel_id=1, source_target_pairs={{0,16},{1,17},{2,18},{3,19},{16,0},{17,1},{18,2},{19,3},{4,20},{5,... | collective-permute-start | bytes 786440 | tf_op jit(solution)/shard_map/ppermute | solution.py:19
  223.1 18.9 %all-to-all-start.1 = ((bf16[64,8,256]{2,1,0:T(8,128)(2,1)}), bf16[64,8,256]{2,1,0:T(8,128)(2,1)}, u32[]{:S(2)}, u32[]{:S(2)}) async-start(bf16[64,8,256]{2,1,0:T(8,128)(2,1)} %copy.31), calls=%async_computation.1 | async-start | bytes 524288 | tf_op jit(solution)/shard_map/all_to_all | solution.py:429
  227.9 21.6 %collective-permute-start.21 = (bf16[64,16,128]{2,1,0:T(8,128)(2,1)}, bf16[64,16,128]{2,1,0:T(8,128)(2,1)S(1)}, u32[]{:S(2)}, u32[]{:S(2)}) collective-permute-start(bf16[64,16,128]{2,1,0:T(8,128)(2,1)} %bitcast.64), channel_id=1, source_target_pairs={{0,19},{1,18},{2,17},{3,16},{16,3},{17,2},{18,1},{19,0},{4,23},{5,... | collective-permute-start | bytes 786440 | tf_op jit(solution)/shard_map/ppermute | solution.py:19
  232.4 35.2 %collective-permute-start.22 = (bf16[64,16,128]{2,1,0:T(8,128)(2,1)}, bf16[64,16,128]{2,1,0:T(8,128)(2,1)S(1)}, u32[]{:S(2)}, u32[]{:S(2)}) collective-permute-start(bf16[64,16,128]{2,1,0:T(8,128)(2,1)} %bitcast.66), channel_id=1, source_target_pairs={{0,18},{1,19},{2,16},{3,17},{16,2},{17,3},{18,0},{19,1},{4,22},{5,... | collective-permute-start | bytes 786440 | tf_op jit(solution)/shard_map/ppermute | solution.py:19
  238.2 33.9 %collective-permute-start.23 = (bf16[64,16,128]{2,1,0:T(8,128)(2,1)}, bf16[64,16,128]{2,1,0:T(8,128)(2,1)S(1)}, u32[]{:S(2)}, u32[]{:S(2)}) collective-permute-start(bf16[64,16,128]{2,1,0:T(8,128)(2,1)} %bitcast.68), channel_id=1, source_target_pairs={{0,2},{1,3},{2,0},{3,1},{16,18},{17,19},{18,16},{19,17},{4,6},{5,7... | collective-permute-start | bytes 786440 | tf_op jit(solution)/shard_map/ppermute | solution.py:19
  238.2 40.3 %collective-permute-start.24 = (bf16[64,16,128]{2,1,0:T(8,128)(2,1)}, bf16[64,16,128]{2,1,0:T(8,128)(2,1)S(1)}, u32[]{:S(2)}, u32[]{:S(2)}) collective-permute-start(bf16[64,16,128]{2,1,0:T(8,128)(2,1)} %bitcast.70), channel_id=1, source_target_pairs={{0,3},{1,2},{2,1},{3,0},{16,19},{17,18},{18,17},{19,16},{4,7},{5,6... | collective-permute-start | bytes 786440 | tf_op jit(solution)/shard_map/ppermute | solution.py:19
  242.0 80.8 %all-to-all-start = ((bf16[64,8,1024]{2,1,0:T(8,128)(2,1)}), bf16[64,8,1024]{2,1,0:T(8,128)(2,1)}, u32[]{:S(2)}, u32[]{:S(2)}) async-start(bf16[64,8,1024]{2,1,0:T(8,128)(2,1)} %join.3), calls=%async_computation | async-start | bytes 2097152 | tf_op jit(solution)/shard_map/all_to_all | solution.py:429
  249.5 72.2 %collective-permute-start.31 = (f32[1,96,1024]{2,1,0:T(8,128)}, f32[1,96,1024]{2,1,0:T(8,128)}, u32[]{:S(2)}, u32[]{:S(2)}) collective-permute-start(f32[1,96,1024]{2,1,0:T(8,128)} %slice.241), channel_id=1, source_target_pairs={{0,8},{4,12},{8,0},{12,4},{1,9},{5,13},{9,1},{13,5},{2,10},{6,14},... | collective-permute-start | bytes 1179656 | tf_op jit(solution)/shard_map/ppermute | solution.py:19
  267.6 46.1 %collective-permute-start.8 = (bf16[64,16,128]{2,1,0:T(8,128)(2,1)}, bf16[64,16,128]{2,1,0:T(8,128)(2,1)}, u32[]{:S(2)}, u32[]{:S(2)}) collective-permute-start(bf16[64,16,128]{2,1,0:T(8,128)(2,1)} %bitcast.38), channel_id=1, source_target_pairs={{0,3},{1,2},{2,1},{3,0},{16,19},{17,18},{18,17},{19,16},{4,7},{5,6... | collective-permute-start | bytes 786440 | tf_op jit(solution)/shard_map/ppermute | solution.py:19
  272.1 34.9 %collective-permute-start.13 = (bf16[64,16,128]{2,1,0:T(8,128)(2,1)}, bf16[64,16,128]{2,1,0:T(8,128)(2,1)}, u32[]{:S(2)}, u32[]{:S(2)}) collective-permute-start(bf16[64,16,128]{2,1,0:T(8,128)(2,1)} %bitcast.50), channel_id=1, source_target_pairs={{0,18},{1,19},{2,16},{3,17},{16,2},{17,3},{18,0},{19,1},{4,22},{5,... | collective-permute-start | bytes 786440 | tf_op jit(solution)/shard_map/ppermute | solution.py:19
  278.5 33.0 %collective-permute-start.14 = (bf16[64,16,128]{2,1,0:T(8,128)(2,1)}, bf16[64,16,128]{2,1,0:T(8,128)(2,1)}, u32[]{:S(2)}, u32[]{:S(2)}) collective-permute-start(bf16[64,16,128]{2,1,0:T(8,128)(2,1)} %bitcast.52), channel_id=1, source_target_pairs={{0,2},{1,3},{2,0},{3,1},{16,18},{17,19},{18,16},{19,17},{4,6},{5,7... | collective-permute-start | bytes 786440 | tf_op jit(solution)/shard_map/ppermute | solution.py:19
  315.3 12.3 %collective-permute-start.25 = (f32[16,96]{1,0:T(8,128)S(1)}, f32[16,96]{1,0:T(8,128)S(1)}, u32[]{:S(2)}, u32[]{:S(2)}) collective-permute-start(f32[16,96]{1,0:T(8,128)S(1)} %get-tuple-element.51), channel_id=1, source_target_pairs={{0,8},{4,12},{8,0},{12,4},{1,9},{5,13},{9,1},{13,5},{2,10},{6,14},... | collective-permute-start | bytes 18440 | tf_op jit(solution)/shard_map/ppermute | solution.py:19
  317.0 10.7 %collective-permute-start.26 = (f32[16,96]{1,0:T(8,128)S(1)}, f32[16,96]{1,0:T(8,128)S(1)}, u32[]{:S(2)}, u32[]{:S(2)}) collective-permute-start(f32[16,96]{1,0:T(8,128)S(1)} %get-tuple-element.52), channel_id=1, source_target_pairs={{0,12},{4,8},{8,4},{12,0},{1,13},{5,9},{9,5},{13,1},{2,14},{6,10},... | collective-permute-start | bytes 18440 | tf_op jit(solution)/shard_map/ppermute | solution.py:19
  317.0 10.7 %collective-permute-start.27 = (f32[16,96]{1,0:T(8,128)S(1)}, f32[16,96]{1,0:T(8,128)S(1)}, u32[]{:S(2)}, u32[]{:S(2)}) collective-permute-start(f32[16,96]{1,0:T(8,128)S(1)} %get-tuple-element.53), channel_id=1, source_target_pairs={{0,4},{4,0},{8,12},{12,8},{1,5},{5,1},{9,13},{13,9},{2,6},{6,2},{1... | collective-permute-start | bytes 18440 | tf_op jit(solution)/shard_map/ppermute | solution.py:19
  (40 other events, 289.1 us)
